TPU v7x, 128 devices: a whole 4x4x4 slice. The times are simulated.
128 devices in a mesh: row: 16 (over z, y), col: 8 (over x, core).
Axes of the slice: x: 4, y: 4, z: 4, core: 2. Of those that a mesh axis runs over, the one named last changes fastest.
Arguments:
- covariance: float32 [4, 16, 256, 8, 8, 256], P(None, 'row', None, None, 'col'), as said below
- check_weights: float32 [4, 16, 256], P(None, 'row'), may hold values from 0.05 to 0.5
Outputs:
- trailing: float32 [4, 16, 256, 8, 8, 256], P(None, 'row', None, None, 'col')
- panels: float32 [4, 16, 256, 512], P(None, 'row')
- checksum: float32 [8, 8, 256], P(None, 'col')
Inputs may be any that keep to these rules, and one draw needn't show every extreme that they name: covariance is symmetric with smallest eigenvalue at least 0.5: an exponential kernel of jittered grid sites plus a nugget plus a small symmetric rough part.
All inputs are finite; a program needn't handle non-finite values.
Results may differ from a plain program's by a relative error of at most 0.0003.
Values sent between devices are 32-bit elements; how exact they have to be, the bound alone decides.
No kernel may reach another device: no remote copies, remote signals or barrier semaphores. Data moves between devices by JAX's collectives and lax.ppermute only.
A program may use at most 128 MiB of HBM per device.

v0:
```python
import jax
import jax.numpy as jnp
from jax import lax
from jax.sharding import PartitionSpec as P

HIGHEST = lax.Precision.HIGHEST


def from_root(value, axis, source):
    kept = jnp.where(lax.axis_index(axis) == source, value, 0).astype(value.dtype)
    return lax.psum(kept, axis)


def shards(covariance, check_weights):
    rows_size = lax.axis_size("row")
    cols_size = lax.axis_size("col")
    row_tiles = covariance.shape[0]
    width = covariance.shape[2]
    col_tiles = covariance.shape[3]
    matrix = covariance.reshape(row_tiles, width, col_tiles, width)
    row_index = lax.axis_index("row")
    col_index = lax.axis_index("col")
    global_rows = jnp.arange(row_tiles, dtype=jnp.int32) * rows_size + row_index
    global_cols = jnp.arange(col_tiles, dtype=jnp.int32) * cols_size + col_index
    panel_list = []
    for step in range(2):
        corner = matrix[step // rows_size, :, step // cols_size, :]
        corner = from_root(corner, "row", step % rows_size)
        corner = jnp.where(col_index == step % cols_size, corner, jnp.eye(width, dtype=jnp.float32))
        factor = jnp.linalg.cholesky(corner)
        column = matrix[:, :, step // cols_size, :].reshape(row_tiles * width, width)
        solved = jax.scipy.linalg.solve_triangular(factor, column.T, lower=True).T
        solved = solved.reshape(row_tiles, width, width)
        solved = jnp.where((global_rows >= step)[:, None, None], solved, 0.0)
        solved = from_root(solved, "col", step % cols_size)
        whole = lax.all_gather(solved, "row", axis=0, tiled=True)
        picked = global_cols % rows_size * row_tiles + global_cols // rows_size
        across = jnp.take(whole, picked, axis=0)
        matrix = matrix - jnp.einsum("iak,jbk->iajb", solved, across, precision=HIGHEST)
        panel_list.append(solved)
    keep = (global_rows >= 2)[:, None, None, None] & (global_cols >= 2)[None, None, :, None]
    trailing = jnp.where(keep, matrix, 0.0)
    weights = check_weights.reshape(row_tiles, width)
    partial_sums = jnp.einsum("ia,iajb->jb", weights, trailing, precision=HIGHEST)
    checksum = lax.psum(partial_sums, "row")
    panels = jnp.concatenate(panel_list, axis=2)
    return (
        trailing.reshape(row_tiles, 1, width, col_tiles, 1, width),
        panels.reshape(row_tiles, 1, width, 2 * width),
        checksum.reshape(col_tiles, 1, width),
    )


def solution(mesh):
    in_specs = (P(None, "row", None, None, "col", None), P(None, "row", None))
    out_specs = (
        P(None, "row", None, None, "col", None),
        P(None, "row", None, None),
        P(None, "col", None),
    )
    return jax.shard_map(shards, mesh=mesh, in_specs=in_specs, out_specs=out_specs, check_vma=False)
```

profile of v0, /device:TPU:1, one launch (start us, length us, event | category | flops | bytes accessed | tf_op | source)
XLA Modules:
  0.0 784.4 jit_solution(16580449472333877571)
XLA Ops:
  7.2 20.6 %copy.25 = f32[4,1,256,8,1,256]{2,5,3,0,4,1:T(8,128)} copy(f32[4,1,256,8,1,256]{5,4,3,2,1,0:T(1,128)} %param.7) | data formatting | bytes 16777216 | tf_op args[0]
  27.8 1.7 fusion.15
  29.5 1.3 slice.67
  31.5 84.5 %all-reduce.6.cloned.1.call-done = f32[256,256]{0,1:T(8,128)} async-done(((f32[256,256]{0,1:T(8,128)}), f32[256,256]{0,1:T(8,128)}) %all-reduce.6.cloned.1.call-update) | async-done | bytes 262160 | tf_op jit(solution)/shard_map/psum | solution.py:11
  116.3 11.7 %cholesky.130 = f32[128,128]{1,0:T(8,128)S(1)} custom-call(f32[128,128]{1,0:T(8,128)S(1)} %cholesky.194), custom_call_target="Cholesky" | custom-call | tf_op jit(solution)/shard_map/jit(cholesky)/cholesky | solution.py:30
  128.0 9.8 %custom-call.13 = f32[1,128,128]{1,2,0:T(8,128)S(1)} custom-call(f32[1,128,128]{2,1,0:T(8,128)S(1)} %get-tuple-element.58), custom_call_target="InvertDiagBlocksLowerTriangular" | custom-call | tf_op jit(solution)/shard_map/jit(cholesky)/cholesky | solution.py:30
  138.3 11.7 %cholesky.147 = f32[128,128]{1,0:T(8,128)S(1)} custom-call(f32[128,128]{1,0:T(8,128)S(1)} %convolution_subtract_fusion.4), custom_call_target="Cholesky" | custom-call | tf_op jit(solution)/shard_map/jit(cholesky)/cholesky | solution.py:30
  150.1 0.7 compare_reduce_fusion.2
  152.3 4.6 while.4
  152.8 0.6 fusion.48
  153.4 1.4 bitcast_dynamic-update-slice_fusion.4
  154.8 0.6 fusion.48
  155.4 1.4 bitcast_dynamic-update-slice_fusion.4
  156.8 19.7 %custom-call.14 = f32[2,128,128]{1,2,0:T(8,128)S(1)} custom-call(f32[2,128,128]{2,1,0:T(8,128)S(1)} %get-tuple-element.20), custom_call_target="InvertDiagBlocksLowerTriangular" | custom-call | tf_op jit(solution)/shard_map/jit(_solve_triangular)/triangular_solve | solution.py:32
  176.5 0.6 fusion.12
  177.7 0.6 fusion.23
  178.8 1.2 select_select_fusion.1
  180.1 60.9 %all-reduce.8.cloned.1.call-done = f32[4,256,256]{2,1,0:T(8,128)} async-done(((f32[4,256,256]{2,1,0:T(8,128)}), f32[4,256,256]{2,1,0:T(8,128)}) %all-reduce.8.cloned.1.call-update) | async-done | bytes 1048592 | tf_op jit(solution)/shard_map/psum | solution.py:11
  241.1 115.0 %all-gather.3.cloned.1.call-done = f32[64,256,256]{2,1,0:T(8,128)} async-done(((f32[4,256,256]{2,1,0:T(8,128)}), f32[64,256,256]{2,1,0:T(8,128)}) %all-gather.3.cloned.1.call-update) | async-done | bytes 16777232 | tf_op jit(solution)/shard_map/all_gather | solution.py:36
  356.1 7.8 gather_fusion
  363.9 9.6 %convolution_subtract_fusion = f32[4,256,8,256]{1,3,2,0:T(8,128)S(1)} fusion(f32[8,256,256]{2,1,0:T(8,128)} %gather_fusion, f32[4,256,256]{2,1,0:T(8,128)S(1)} %copy-done.3, pred[8]{0:T(512)(128)(4,1)S(1)} %compare_and_fusion, f32[4,1,256,8,1,256]{2,5,3,0,4,1:T(8,128)} %copy.25), kind=kOutput, calls=%fused_computation.7 | convolution fusion | flops 6445072384 | bytes 19922952 | tf_op jit(solution)/shard_map/iak,jbk->iajb/dot_general | solution.py:39
  373.5 3.4 copy-done.2
  376.9 0.7 fusion.14
  377.9 1.0 slice-done
  379.5 81.0 %all-reduce.10.cloned.1.call-done = f32[256,256]{0,1:T(8,128)} async-done(((f32[256,256]{0,1:T(8,128)}), f32[256,256]{0,1:T(8,128)}) %all-reduce.10.cloned.1.call-update) | async-done | bytes 262160 | tf_op jit(solution)/shard_map/psum | solution.py:11
  460.6 1.0 convert_select_fusion
  461.7 1.0 fusion.16
  462.7 11.7 %cholesky.164 = f32[128,128]{1,0:T(8,128)S(1)} custom-call(f32[128,128]{1,0:T(8,128)S(1)} %cholesky.197), custom_call_target="Cholesky" | custom-call | tf_op jit(solution)/shard_map/jit(cholesky)/cholesky | solution.py:30
  474.5 0.6 compare_reduce_fusion.1
  475.1 9.8 %custom-call.15 = f32[1,128,128]{1,2,0:T(8,128)S(1)} custom-call(f32[1,128,128]{2,1,0:T(8,128)S(1)} %get-tuple-element.54), custom_call_target="InvertDiagBlocksLowerTriangular" | custom-call | tf_op jit(solution)/shard_map/jit(cholesky)/cholesky | solution.py:30
  485.4 11.7 %cholesky.181 = f32[128,128]{1,0:T(8,128)S(1)} custom-call(f32[128,128]{1,0:T(8,128)S(1)} %convolution_subtract_fusion.3), custom_call_target="Cholesky" | custom-call | tf_op jit(solution)/shard_map/jit(cholesky)/cholesky | solution.py:30
  497.2 0.7 compare_reduce_fusion
  499.3 4.3 while.5
  499.6 0.6 fusion.49
  500.1 1.4 bitcast_dynamic-update-slice_fusion.5
  502.2 1.4 bitcast_dynamic-update-slice_fusion.5
  503.6 19.7 %custom-call.16 = f32[2,128,128]{1,2,0:T(8,128)S(1)} custom-call(f32[2,128,128]{2,1,0:T(8,128)S(1)} %get-tuple-element.21), custom_call_target="InvertDiagBlocksLowerTriangular" | custom-call | tf_op jit(solution)/shard_map/jit(_solve_triangular)/triangular_solve | solution.py:32
  523.3 0.6 fusion.10
  524.5 0.6 fusion.19
  525.6 1.2 select_select_fusion
  526.9 59.1 %all-reduce.12.cloned.1.call-done = f32[4,256,256]{2,1,0:T(8,128)} async-done(((f32[4,256,256]{2,1,0:T(8,128)}), f32[4,256,256]{2,1,0:T(8,128)}) %all-reduce.12.cloned.1.call-update) | async-done | bytes 1048592 | tf_op jit(solution)/shard_map/psum | solution.py:11
  586.1 2.8 maximum_bitcast_fusion
  588.9 111.9 %all-gather.5.cloned.1.call-done = f32[64,256,256]{2,1,0:T(8,128)} async-done(((f32[4,256,256]{2,1,0:T(8,128)}), f32[64,256,256]{2,1,0:T(8,128)}) %all-gather.5.cloned.1.call-update) | async-done | bytes 16777232 | tf_op jit(solution)/shard_map/all_gather | solution.py:36
  700.7 6.4 gather_fusion.1
  707.2 9.6 %subtract_select_fusion = f32[4,256,8,256]{1,3,2,0:T(8,128)S(1)} fusion(f32[4,256,8,256]{1,3,2,0:T(8,128)} %copy-done.2, pred[4,8]{1,0:T(4,128)(4,1)S(1)} %broadcast_and_fusion, f32[8,256,256]{2,1,0:T(8,128)S(1)} %gather_fusion.1, f32[4,256,256]{2,1,0:T(8,128)S(1)} %copy-done.4, pred[8]{0:T(512)(128)(4,1)S(1)} %compare_and_fusion), kind=kOutput, calls=%fused_computation.6 | convolution fusion | flops 6447169536 | bytes 19922984 | tf_op jit(solution)/shard_map/iak,jbk->iajb/dot_general | solution.py:39
  716.8 7.2 fusion.28
  724.0 32.7 %psum.39 = f32[8,1,256]{2,1,0:T(1,128)} all-reduce(f32[8,1,256]{2,1,0:T(1,128)S(1)} %reshape.113), channel_id=1, replica_groups=mesh['row'=16,'col'=8] {'row'}, use_global_device_ids=true, to_apply=%region_8.12 | all-reduce | flops 2048 | bytes 16384 | tf_op jit(solution)/shard_map/psum | solution.py:45
  756.7 20.5 %copy.36 = f32[4,1,256,8,1,256]{5,4,3,2,1,0:T(1,128)} copy(f32[4,1,256,8,1,256]{2,5,3,0,4,1:T(8,128)} %bitcast.106) | data formatting | bytes 16777216
  (69 shorter events, 6.3 us)
Async XLA Ops:
  7.2 709.6 %copy-start = (f32[4,1,256]{2,1,0:T(1,128)S(1)}, f32[4,1,256]{2,1,0:T(1,128)}, u32[]{:S(2)}) copy-start(f32[4,1,256]{2,1,0:T(1,128)} %param.8) | copy-start | bytes 12292
  7.2 108.8 %all-reduce.6.cloned.1.call-start = ((), (), s32[]{:S(2)}) async-start(), calls=%async_computation | async-start | bytes 524288 | tf_op jit(solution)/shard_map/psum | solution.py:11
  29.5 211.5 %all-reduce.8.cloned.1.call-start = ((), (), s32[]{:S(2)}) async-start(), calls=%async_computation.1 | async-start | bytes 2097152 | tf_op jit(solution)/shard_map/psum | solution.py:11
  180.0 176.1 %all-gather.3.cloned.1.call-start = ((), (), s32[]{:S(2)}) async-start(), calls=%async_computation.2 | async-start | bytes 17825792 | tf_op jit(solution)/shard_map/all_gather | solution.py:36
  241.0 219.6 %all-reduce.10.cloned.1.call-start = ((), (), s32[]{:S(2)}) async-start(), calls=%async_computation.3 | async-start | bytes 524288 | tf_op jit(solution)/shard_map/psum | solution.py:11
  241.1 122.8 %copy-start.3 = (f32[4,256,256]{2,1,0:T(8,128)S(1)}, f32[4,256,256]{2,1,0:T(8,128)}, u32[]{:S(2)}) copy-start(f32[4,256,256]{2,1,0:T(8,128)} %all-reduce.8.cloned.1.call-done) | copy-start | bytes 3145732
  373.5 3.4 copy-start.2
  377.6 1.2 slice-start
  377.7 208.3 %all-reduce.12.cloned.1.call-start = ((), (), s32[]{:S(2)}) async-start(), calls=%async_computation.4 | async-start | bytes 2097152 | tf_op jit(solution)/shard_map/psum | solution.py:11
  526.8 173.9 %all-gather.5.cloned.1.call-start = ((), (), s32[]{:S(2)}) async-start(), calls=%async_computation.5 | async-start | bytes 17825792 | tf_op jit(solution)/shard_map/all_gather | solution.py:36
  588.9 118.3 %copy-start.4 = (f32[4,256,256]{2,1,0:T(8,128)S(1)}, f32[4,256,256]{2,1,0:T(8,128)}, u32[]{:S(2)}) copy-start(f32[4,256,256]{2,1,0:T(8,128)} %all-reduce.12.cloned.1.call-done) | copy-start | bytes 3145732
  716.8 7.2 copy-start.1
Sparse Core Ops, SparseCore 0:
  29.6 86.3 all-reduce.5
  180.1 60.7 all-reduce.7
  243.3 112.7 all-gather.2
  377.8 82.7 all-reduce.9
  526.9 58.9 all-reduce.11
  587.9 112.7 all-gather.4
where the time goes:
time: 800 us; the launch traced here: 784 us
  waiting for transfers between devices  512 us (64%)
  other arithmetic  118 us (15%)
  local copies, waits for them, and re-layouts  71.5 us (9%)
  blocking collectives  32.7 us (4%)
  matrix products  31 us (4%)
  between operations  17.6 us (2%)
    psum x4, waiting for transfers between devices, from_root(): return lax.psum(kept, axis)  285 us
    all_gather x2, waiting for transfers between devices, shards(): whole = lax.all_gather(solved, 'row', axis=0, tiled=True)  227 us
    another operation x13, other arithmetic, shards(): factor = jnp.linalg.cholesky(corner)  68.7 us
    unnamed x12, local copies, waits for them, and re-layouts  44.5 us
    another operation x5, other arithmetic, shards(): solved = jax.scipy.linalg.solve_triangular(factor, column.T, lower=True).T  39.4 us
    psum x1, blocking collectives, shards(): checksum = lax.psum(partial_sums, 'row')  32.7 us
    dot_general x2, matrix products, shards(): jnp.einsum('iak,jbk->iajb', solved, across, precision=HIGHEST)  19.2 us
  transfers between devices with their start and end apart: 6, of which 6 were waited for; matrix products, arithmetic and copies ran while one was open for 1% of the time, Pallas kernels for 0%

commit v1 on v0

v1 whole, which is shorter than its diff:
```python
import functools

import jax
import jax.numpy as jnp
from jax import lax
from jax.experimental import pallas as pl
from jax.experimental.pallas import tpu as pltpu
from jax.sharding import PartitionSpec as P

HIGHEST = lax.Precision.HIGHEST
F32 = jnp.float32
BF16 = jnp.bfloat16
NB = 256
NT = (((1,), (1,)), ((), ()))
NN = (((1,), (0,)), ((), ()))


def dot6(a, b, dims):
    return lax.dot_general(a, b, dims, precision=HIGHEST, preferred_element_type=F32)


def halves(value):
    high = value.astype(BF16)
    return high, (value - high.astype(F32)).astype(BF16)


def dot3(a, b, dims):
    total = lax.dot_general(a[0], b[0], dims, preferred_element_type=F32)
    total += lax.dot_general(a[0], b[1], dims, preferred_element_type=F32)
    return total + lax.dot_general(a[1], b[0], dims, preferred_element_type=F32)


def splat_row(ref, row, lanes):
    return jnp.broadcast_to(ref[row : row + 1, lanes], (8, 128))


def splat_lane(value, lane):
    return jnp.broadcast_to(value[:, lane : lane + 1], (8, 128))


def invert_factor(m, put):
    left, right = slice(0, 128), slice(128, 256)
    for block in range(16):
        base = 8 * block
        rows = [[splat_row(m, base + a, side) for a in range(8)] for side in (left, right)]
        b = {(a, k): splat_lane(rows[0][a], base + k) for a in range(8) for k in range(a + 1)}
        n = {}
        inverse, root = [], []
        for i in range(8):
            inverse.append(1.0 / b[i, i])
            root.append(lax.rsqrt(b[i, i]))
            for k in range(i + 1, 8):
                ratio = b[k, i] * inverse[i]
                for j in range(i + 1, k + 1):
                    b[k, j] = b[k, j] - ratio * b[j, i]
                for j in range(i):
                    n[k, j] = n[k, j] - ratio * n[i, j]
                n[k, i] = -ratio
        solved = []
        for side in range(2):
            upper = []
            for i in range(8):
                value = rows[side][i]
                for j in range(i):
                    value = value + n[i, j] * rows[side][j]
                upper.append(value)
            if side == 1:
                for i in range(8):
                    put(base + i, root[i] * upper[i])
            scaled = [inverse[i] * upper[i] for i in range(8)]
            out = []
            for i in range(8):
                value = scaled[i]
                for k in range(i + 1, 8):
                    value = value + n[k, i] * scaled[k]
                out.append(value)
            solved.append(out)
        for other in range(block + 1, 16):
            span = slice(8 * other, 8 * other + 8)
            a_part, n_part = m[span, left], m[span, right]
            columns = [splat_lane(a_part, base + i) for i in range(8)]
            for i in range(8):
                a_part = a_part - columns[i] * solved[0][i]
                n_part = n_part - columns[i] * solved[1][i]
            m[span, left] = a_part
            m[span, right] = n_part


def factor_tile(source, out, m, part):
    eye = (lax.broadcasted_iota(jnp.int32, (128, 128), 0) == lax.broadcasted_iota(jnp.int32, (128, 128), 1)).astype(F32)
    m[:, 0:128] = source[0:128, 0:128]

    def body(i, carry):
        m[:, 128:256] = eye

        def put(row, value):
            part[i, row : row + 1, :] = value[0:1, :]

        invert_factor(m, put)

        @pl.when(i == 0)
        def _():
            low = dot6(source[128:256, 0:128], part[0], NT)
            m[:, 0:128] = source[128:256, 128:256] - dot6(low, low, NT)
            part[2] = low

        return carry

    lax.fori_loop(0, 2, body, 0)
    out[0:128, 0:128] = part[0]
    out[0:128, 128:256] = jnp.zeros((128, 128), F32)
    out[128:256, 128:256] = part[1]
    out[128:256, 0:128] = -dot6(part[1], dot6(part[2], part[0], NN), NN)


def first_kernel(c00, w00, m, part):
    factor_tile(c00, w00, m, part)


def second_kernel(w00, c10, c11, l10, w11, schur, m, part):
    low = dot6(c10[...], w00[...], NT)
    l10[...] = low
    schur[...] = c11[...] - dot6(low, low, NT)
    factor_tile(schur, w11, m, part)


TILE = jax.ShapeDtypeStruct((NB, NB), F32)
WORK = [pltpu.VMEM((128, 256), F32), pltpu.VMEM((3, 128, 128), F32)]
VMEM = pl.BlockSpec(memory_space=pltpu.VMEM)
SMEM = pl.BlockSpec(memory_space=pltpu.SMEM)


def first_factor(c00):
    return pl.pallas_call(
        first_kernel, out_shape=TILE, in_specs=[VMEM], out_specs=VMEM, scratch_shapes=WORK, name="first_factor",
        cost_estimate=pl.CostEstimate(flops=20_000_000_000, bytes_accessed=1_000_000, transcendentals=0),
    )(c00)


def second_factor(w00, c10, c11):
    return pl.pallas_call(
        second_kernel, out_shape=(TILE, TILE), in_specs=[VMEM] * 3, out_specs=(VMEM, VMEM),
        scratch_shapes=[pltpu.VMEM((NB, NB), F32)] + WORK, name="second_factor",
        cost_estimate=pl.CostEstimate(flops=20_000_000_000, bytes_accessed=1_000_000, transcendentals=0),
    )(w00, c10, c11)


def corner_kernel(a, corner, pieces):
    for q in range(16):
        value = a[:, q, :]
        pieces[q // 2, :, 128 * (q % 2) : 128 * (q % 2) + 128] = value
        if q < 2:
            corner[:, 128 * q : 128 * q + 128] = value


def corner_call(flat):
    return pl.pallas_call(
        corner_kernel, grid=(2,),
        out_shape=(TILE, jax.ShapeDtypeStruct((8, NB, NB), F32)),
        in_specs=[pl.BlockSpec((128, 16, 128), lambda i: (i, 0, 0))],
        out_specs=(pl.BlockSpec((128, NB), lambda i: (i, 0)), pl.BlockSpec((8, 128, NB), lambda i: (0, i, 0))),
        name="corner_tiles",
    )(flat)


def column_kernel(weights, a, column, sums):
    step = pl.program_id(0)
    for q in range(2):
        column[:, 128 * q : 128 * q + 128] = a[:, q, :]

    @pl.when(step == 0)
    def _():
        sums[...] = jnp.zeros_like(sums)

    def body(i, total):
        for j in range(8):
            row = 8 * i + j
            total = total + weights[step * 128 + row] * a[row]
        return total

    sums[...] += lax.fori_loop(0, 16, body, jnp.zeros((16, 128), F32))


def column_call(weights, flat):
    return pl.pallas_call(
        column_kernel, grid=(8,),
        out_shape=(jax.ShapeDtypeStruct((1024, NB), F32), jax.ShapeDtypeStruct((16, 128), F32)),
        in_specs=[SMEM, pl.BlockSpec((128, 16, 128), lambda i: (i, 0, 0))],
        out_specs=(pl.BlockSpec((128, NB), lambda i: (i, 0)), pl.BlockSpec((16, 128), lambda i: (0, 0))),
        name="first_column",
    )(weights, flat)


def update_kernel(place, flat, row_panel, across, w00, l10, w11, sums, out, panels, checksum, high, low, factors):
    step = pl.program_id(0)
    row_index, col_index = place[0], place[1]

    def solve(first, second, dims):
        kept = [(factors[0, k], factors[1, k]) for k in range(3)]
        if dims == NN:
            top = dot3(kept[0], halves(first), NN)
            return top, dot3(kept[2], halves(second - dot3(kept[1], halves(top), NN)), NN)
        left = dot3(halves(first), kept[0], NT)
        return left, dot3(halves(second - dot3(halves(left), kept[1], NT)), kept[2], NT)

    @pl.when(step == 0)
    def _():
        for k, ref in enumerate((w00, l10, w11)):
            factors[0, k], factors[1, k] = halves(ref[...])
        y0 = dot6(jnp.broadcast_to(sums[2:3, 0:256], (8, 256)), w00[...], NT)
        y1 = dot6(jnp.broadcast_to(sums[2:3, 256:512], (8, 256)) - dot6(y0, l10[...], NT), w11[...], NT)
        y = halves(jnp.concatenate([y0, y1], axis=1))
        for u in range(8):
            top, bottom = solve(across[2 * u], across[2 * u + 1], NN)
            high[u, 0:256], low[u, 0:256] = halves(top)
            high[u, 256:512], low[u, 256:512] = halves(bottom)
            taken = dot3(y, (high[u], low[u]), NN)[0:1]
            whole = sums[3 + u : 4 + u, 0:256]
            kept = jnp.where((u == 0) & (col_index < 2), 0.0, whole - taken)
            checksum[u : u + 1, :] = kept

    left, right = solve(row_panel[:, 0:256], row_panel[:, 256:512], NT)
    right = jnp.where((step < 2) & (row_index == 0), 0.0, right)
    panels[:, 0:256] = left
    panels[:, 256:512] = right
    mine = halves(jnp.concatenate([left, right], axis=1))
    top_rows = (step < 2) & (row_index < 2)
    for u in range(8):
        product = dot3(mine, (high[u], low[u]), NN)
        gone = top_rows | (col_index < 2) if u == 0 else top_rows
        for h in range(2):
            q = 2 * u + h
            value = flat[:, q, :] - product[:, 128 * h : 128 * h + 128]
            out[:, q, :] = jnp.where(gone, 0.0, value)


def update_call(place, flat, row_panel, across, w00, l10, w11, sums):
    full = lambda *shape: pl.BlockSpec(shape, lambda i: (0,) * len(shape))
    return pl.pallas_call(
        update_kernel, grid=(8,),
        out_shape=(
            jax.ShapeDtypeStruct((1024, 16, 128), F32),
            jax.ShapeDtypeStruct((1024, 512), F32),
            jax.ShapeDtypeStruct((8, 256), F32),
        ),
        in_specs=[
            SMEM,
            pl.BlockSpec((128, 16, 128), lambda i: (i, 0, 0)),
            pl.BlockSpec((128, 512), lambda i: (i, 0)),
            full(16, NB, NB), full(NB, NB), full(NB, NB), full(NB, NB), full(16, 512),
        ],
        out_specs=(
            pl.BlockSpec((128, 16, 128), lambda i: (i, 0, 0)),
            pl.BlockSpec((128, 512), lambda i: (i, 0)),
            full(8, 256),
        ),
        scratch_shapes=[pltpu.VMEM((8, 512, 256), BF16), pltpu.VMEM((8, 512, 256), BF16), pltpu.VMEM((2, 3, NB, NB), BF16)],
        name="trailing_update",
    )(place, flat, row_panel, across, w00, l10, w11, sums)


def where_is(device):
    row, col = divmod(device, 8)
    return [row // 4, row % 4, col // 2, col % 2]


def device_at(z, y, x, core):
    return ((z % 4) * 4 + y % 4) * 8 + (x % 4) * 2 + core


def moved(device, dim, by):
    at = where_is(device)
    at[dim] += by
    return device_at(*at)


def spread(value, sources, dims):
    holders = list(sources)
    for dim in dims:
        first = [(h, moved(h, dim, 1)) for h in holders]
        value = value + lax.ppermute(value, ("row", "col"), first)
        second = [(h, moved(h, dim, -1)) for h in holders] + [(moved(h, dim, 1), moved(h, dim, 2)) for h in holders]
        value = value + lax.ppermute(value, ("row", "col"), second)
        holders = [moved(h, dim, k) for h in holders for k in range(4)]
    return value


def shards(covariance, check_weights):
    row = lax.axis_index("row")
    col = lax.axis_index("col")
    core = col % 2
    flat = covariance.reshape(1024, 16, 128)
    tiles = jnp.arange(4, dtype=jnp.int32) * 16 + row
    weights = jnp.where((tiles >= 2)[:, None], check_weights.reshape(4, NB), 0.0).reshape(1024)

    corner, pieces = corner_call(flat)
    c00 = jnp.where((row == 0) & (col == 0), corner, 0.0)
    c00 = spread(c00, [device_at(0, 0, 0, 0)], (2, 1, 0))
    swap_cores = [(c, c ^ 1) for c in range(8)]
    c00 = c00 + lax.ppermute(c00, "col", [(c, c + 1) for c in (0, 2, 4, 6)])
    below = jnp.where((row == 1) & (col < 2), corner, 0.0)
    below = spread(below, [device_at(0, 1, 0, 0), device_at(0, 1, 0, 1)], (0, 2, 1))
    other = lax.ppermute(below, "col", swap_cores)
    c10 = jnp.where(core == 0, below, other)
    c11 = jnp.where(core == 0, other, below)

    piece = jnp.where(row < 2, pieces[0], 0.0)
    for j in range(1, 8):
        piece = piece + lax.ppermute(pieces[j], "row", [(0, 2 * j), (1, 2 * j + 1)])
    across = lax.all_gather(piece, "row", axis=0)

    column, sums = column_call(weights, flat)
    mine = jnp.where(col < 2, column, 0.0)
    mine = mine + lax.ppermute(mine, "col", [(0, 2), (1, 3)]) + lax.ppermute(mine, "col", [(0, 6), (1, 7)])
    upper = mine[0:512] + lax.ppermute(mine[0:512], "col", [(2, 4), (3, 5)])
    lower = mine[512:1024] + lax.ppermute(mine[512:1024], "col", [(6, 4), (7, 5)])
    mine = jnp.concatenate([upper, lower], axis=0)
    theirs = lax.ppermute(mine, "col", swap_cores)
    row_panel = jnp.concatenate([jnp.where(core == 0, mine, theirs), jnp.where(core == 0, theirs, mine)], axis=1)

    panel_sums = jnp.dot(weights[None], row_panel, precision=HIGHEST)
    total = jnp.concatenate([sums, panel_sums.reshape(4, 128), jnp.zeros((4, 128), F32)], axis=0)
    for d in (1, 3, 4, 12):
        total = total + lax.ppermute(total, "row", [(r, r ^ d) for r in range(16)])
    wide = jnp.zeros((16, 512), F32).at[2, :].set(total[16:20].reshape(512)).at[3:11, 0:256].set(total[0:16].reshape(8, 256))

    w00 = first_factor(c00)
    l10, w11 = second_factor(w00, c10, c11)
    place = jnp.stack([row, col]).astype(jnp.int32)
    trailing, panels, checksum = update_call(place, flat, row_panel, across, w00, l10, w11, wide)
    return (
        trailing.reshape(4, 1, NB, 8, 1, NB),
        panels.reshape(4, 1, NB, 512),
        checksum.reshape(8, 1, NB),
    )


def solution(mesh):
    in_specs = (P(None, "row", None, None, "col", None), P(None, "row", None))
    out_specs = (
        P(None, "row", None, None, "col", None),
        P(None, "row", None, None),
        P(None, "col", None),
    )
    return jax.shard_map(shards, mesh=mesh, in_specs=in_specs, out_specs=out_specs, check_vma=False)
```

time: 800 us -> 186 us (0.23); the launches traced: 784 us -> 183 us
  waiting for transfers between devices: 512 us -> 9.77 us
  other arithmetic: 118 us -> 14 us
  starting transfers between devices: 0.42 us -> 75.2 us
  local copies, waits for them, and re-layouts: 71.5 us -> 6.09 us
  Pallas kernels: 0 us -> 62.6 us
  blocking collectives: 32.7 us -> 0 us
  matrix products: 31 us -> 1.09 us
    psum x4 -> x0, waiting for transfers between devices: 285 us -> none  [from_root(): return lax.psum(kept, axis)]
    all_gather x2 -> x1, waiting for transfers between devices: 227 us -> 0.02 us  [shards(): across = lax.all_gather(piece, 'row', axis=0)]
    another operation x18 -> x1, other arithmetic: 108 us -> 0.58 us  [shards(): place = jnp.stack([row, col]).astype(jnp.int32)]
    ppermute x0 -> x30, starting transfers between devices: none -> 75.1 us  [the longest x7 19.1 us: shards(): piece = piece + lax.ppermute(pieces[j], 'row', [(0, 2 * j), (1, 2 * j + 1)])]
    pallas_call x0 -> x5, Pallas kernels: none -> 62.6 us  [the longest x1 31.4 us: update_call(): pl.pallas_call(update_kernel, grid=(8,), out_shape=(jax.ShapeDtypeStruct(...]
    unnamed x12 -> x19, local copies, waits for them, and re-layouts: 44.5 us -> 2.61 us
    psum x1 -> x0, blocking collectives: 32.7 us -> none  [shards(): checksum = lax.psum(partial_sums, 'row')]
    dot_general x3 -> x1, matrix products: 26.4 us -> 1.09 us  [shards(): panel_sums = jnp.dot(weights[None], row_panel, precision=HIGHEST)]
  transfers between devices with their start and end apart: 6 -> 31, of which waited for: 6 -> 4; matrix products, arithmetic and copies ran while one was open for 1% -> 9% of each run, Pallas kernels for 0% -> 15%
where the time goes in v1:
time: 186 us; the launch traced here: 183 us
  starting transfers between devices  75.2 us (40%)
  Pallas kernels  62.6 us (34%)
  between operations  14.5 us (8%)
  other arithmetic  14 us (8%)
  waiting for transfers between devices  9.77 us (5%)
  local copies, waits for them, and re-layouts  6.09 us (3%)
    pallas_call x1, Pallas kernels, update_call(): pl.pallas_call(update_kernel, grid=(8,), out_shape=(jax.ShapeDtypeStruct(...  31.4 us
    ppermute x7, starting transfers between devices, shards(): piece = piece + lax.ppermute(pieces[j], 'row', [(0, 2 * j), (1, 2 * j + 1)])  19.1 us
    ppermute x4, starting transfers between devices, shards(): total = total + lax.ppermute(total, 'row', [(r, r ^ d) for r in range(16)])  13.9 us
    ppermute x1, starting transfers between devices, shards(): other = lax.ppermute(below, 'col', swap_cores)  13.3 us
    ppermute x1, starting transfers between devices, shards(): theirs = lax.ppermute(mine, 'col', swap_cores)  12.1 us
    pallas_call x1, Pallas kernels, second_factor(): pl.pallas_call(second_kernel, out_shape=(TILE, TILE), in_specs=[VMEM] * 3...  10.6 us
    pallas_call x1, Pallas kernels, first_factor(): pl.pallas_call(first_kernel, out_shape=TILE, in_specs=[VMEM], out_specs=V...  9.33 us
    pallas_call x1, Pallas kernels, column_call(): pl.pallas_call(column_kernel, grid=(8,), out_shape=(jax.ShapeDtypeStruct(...  7.91 us
  transfers between devices with their start and end apart: 31, of which 4 were waited for; matrix products, arithmetic and copies ran while one was open for 9% of the time, Pallas kernels for 15%

profile of v1, /device:TPU:1, one launch (start us, length us, event | category | flops | bytes accessed | tf_op | source)
XLA Modules:
  0.0 183.2 jit_solution(262785448663740603)
XLA Ops:
  7.2 3.4 %corner_tiles.1 = (f32[256,256]{1,0:T(8,128)}, f32[8,256,256]{2,1,0:T(8,128)}) custom-call(f32[1024,16,128]{2,1,0:T(8,128)} %bitcast.50), custom_call_target="tpu_custom_call" | custom-call | tf_op jit(solution)/shard_map/corner_tiles/pallas_call | solution.py:157
  10.6 2.6 %slice_bitcast_fusion.6 = (f32[256,256]{1,0:T(8,128)}, f32[256,256]{1,0:T(8,128)}, f32[256,256]{1,0:T(8,128)}, f32[256,256]{1,0:T(8,128)S(1)}, f32[256,256]{1,0:...) fusion(f32[8,256,256]{2,1,0:T(8,128)} %get-tuple-element.37), kind=kLoop, calls=%fused_computation.22 | loop fusion | bytes 3670016 | tf_op jit(solution)/shard_map/squeeze | solution.py:309
  13.2 6.3 %collective-permute-start.5 = (f32[256,256]{1,0:T(8,128)}, f32[256,256]{1,0:T(8,128)}, u32[]{:S(2)}, u32[]{:S(2)}) collective-permute-start(f32[256,256]{1,0:T(8,128)} %get-tuple-element.50), channel_id=1, source_target_pairs={{0,16},{8,24},{1,17},{9,25},{2,18},{10,26},{3,19},{11,27},{4,20},{... | collective-permute-start | bytes 786440 | tf_op jit(solution)/shard_map/ppermute | solution.py:309
  20.2 7.9 %first_column.1 = (f32[1024,256]{1,0:T(8,128)}, f32[16,128]{1,0:T(8,128)}) custom-call(f32[1024]{0:T(1024)} %broadcast_select_fusion.7.weights, f32[1024,16,128]{2,1,0:T(8,128)} %bitcast.51), custom_call_target="tpu_custom_call" | custom-call | tf_op jit(solution)/shard_map/first_column/pallas_call | solution.py:185
  28.1 2.4 %broadcast_select_fusion = f32[1024,256]{1,0:T(8,128)} fusion(f32[1024,256]{1,0:T(8,128)} %get-tuple-element.36, pred[]{:T(512)S(6)} %lt.14), kind=kLoop, calls=%fused_computation.6 | loop fusion | flops 262144 | bytes 2097153 | tf_op jit(solution)/shard_map/jit(_where)/select_n | solution.py:313
  30.5 3.3 %collective-permute-start.1 = (f32[1024,256]{1,0:T(8,128)}, f32[1024,256]{1,0:T(8,128)S(1)}, u32[]{:S(2)}, u32[]{:S(2)}) collective-permute-start(f32[1024,256]{1,0:T(8,128)} %broadcast_select_fusion), channel_id=1, source_target_pairs={{0,6},{1,7},{8,14},{9,15},{16,22},{17,23},{24,30},{25,31},{32,38},... | collective-permute-start | bytes 3145736 | tf_op jit(solution)/shard_map/ppermute | solution.py:314
  33.8 1.4 collective-permute-start
  35.2 4.2 %collective-permute-start.11 = (f32[256,256]{1,0:T(8,128)S(1)}, f32[256,256]{1,0:T(8,128)S(1)}, u32[]{:S(2)}, u32[]{:S(2)}) collective-permute-start(f32[256,256]{1,0:T(8,128)S(1)} %copy-done.2), channel_id=1, source_target_pairs={{0,112},{8,120},{1,113},{9,121},{2,114},{10,122},{3,115},{11,123},... | collective-permute-start | bytes 786440 | tf_op jit(solution)/shard_map/ppermute | solution.py:309
  39.3 1.3 collective-permute-start.10
  40.7 1.3 collective-permute-start.9
  42.0 2.0 %collective-permute-done.11 = f32[256,256]{1,0:T(8,128)S(1)} collective-permute-done((f32[256,256]{1,0:T(8,128)S(1)}, f32[256,256]{1,0:T(8,128)S(1)}, u32[]{:S(2)}, u32[]{:S(2)}) %collective-permute-start.11) | collective-permute-done | bytes 262176 | tf_op jit(solution)/shard_map/ppermute | solution.py:309
  44.0 2.0 %collective-permute-start.8 = (f32[256,256]{1,0:T(8,128)}, f32[256,256]{1,0:T(8,128)}, u32[]{:S(2)}, u32[]{:S(2)}) collective-permute-start(f32[256,256]{1,0:T(8,128)} %get-tuple-element.54), channel_id=1, source_target_pairs={{0,64},{8,72},{1,65},{9,73},{2,66},{10,74},{3,67},{11,75},{4,68},{... | collective-permute-start | bytes 786440 | tf_op jit(solution)/shard_map/ppermute | solution.py:309
  46.0 2.0 %collective-permute-start.7 = (f32[256,256]{1,0:T(8,128)}, f32[256,256]{1,0:T(8,128)}, u32[]{:S(2)}, u32[]{:S(2)}) collective-permute-start(f32[256,256]{1,0:T(8,128)} %get-tuple-element.55), channel_id=1, source_target_pairs={{0,48},{8,56},{1,49},{9,57},{2,50},{10,58},{3,51},{11,59},{4,52},{... | collective-permute-start | bytes 786440 | tf_op jit(solution)/shard_map/ppermute | solution.py:309
  47.9 1.6 collective-permute-done.9
  49.6 0.7 copy-done.5
  50.3 2.0 %collective-permute-start.6 = (f32[256,256]{1,0:T(8,128)}, f32[256,256]{1,0:T(8,128)}, u32[]{:S(2)}, u32[]{:S(2)}) collective-permute-start(f32[256,256]{1,0:T(8,128)} %get-tuple-element.56), channel_id=1, source_target_pairs={{0,32},{8,40},{1,33},{9,41},{2,34},{10,42},{3,35},{11,43},{4,36},{... | collective-permute-start | bytes 786440 | tf_op jit(solution)/shard_map/ppermute | solution.py:309
  52.3 1.7 broadcast_select_fusion.3
  54.0 1.4 collective-permute-start.12
  55.3 2.4 %fusion.8 = f32[256,256]{1,0:T(8,128)} fusion(f32[256,256]{1,0:T(8,128)} %copy-done.3, f32[256,256]{1,0:T(8,128)} %copy-done.4, f32[256,256]{1,0:T(8,128)} %copy-done.5, f32[256,256]{1,0:T(8,128)} %collective-permute-done.8, f32[256,256]{1,0:T(8,128)} %collective-permute-done.7, f32[256,256]{1,0:T(8,128)} %collective-permute-done.6, ...), kind=kLoop, calls=%fused_computation.15 | loop fusion | flops 524288 | bytes 2359297 | tf_op jit(solution)/shard_map/add | solution.py:309
  58.0 0.7 collective-permute-start.2
  58.7 0.7 collective-permute-start.3
  60.1 1.1 add.118
  61.2 0.7 collective-permute-start.13
  61.9 0.7 collective-permute-start.20
  62.7 0.7 collective-permute-start.14
  63.5 1.0 pad_maximum_fusion.1
  64.6 12.1 %collective-permute-start.4 = (f32[1024,256]{1,0:T(8,128)}, f32[1024,256]{1,0:T(8,128)S(1)}, u32[]{:S(2)}, u32[]{:S(2)}) collective-permute-start(f32[1024,256]{1,0:T(8,128)} %pad_maximum_fusion.1), channel_id=1, source_target_pairs={{0,1},{1,0},{2,3},{3,2},{4,5},{5,4},{6,7},{7,6},{8,9},{9,8},{10,11... | collective-permute-start | bytes 3145736 | tf_op jit(solution)/shard_map/ppermute | solution.py:318
  76.7 0.7 collective-permute-start.21
  77.4 0.7 collective-permute-start.15
  78.2 0.7 collective-permute-start.22
  78.9 0.7 collective-permute-start.16
  79.7 0.7 collective-permute-start.23
  81.3 1.3 collective-permute-start.24
  82.7 1.3 collective-permute-start.18
  84.1 1.7 fusion.10
  85.8 1.1 fusion
  87.0 9.3 %collective-permute-start.26 = (f32[24,128]{1,0:T(8,128)S(1)}, f32[24,128]{1,0:T(8,128)S(1)}, u32[]{:S(2)}, u32[]{:S(2)}) collective-permute-start(f32[24,128]{1,0:T(8,128)S(1)} %maximum_maximum_fusion), channel_id=1, source_target_pairs={{0,8},{8,0},{16,24},{24,16},{32,40},{40,32},{48,56},{56,48},{64,72... | collective-permute-start | bytes 36872 | tf_op jit(solution)/shard_map/ppermute | solution.py:324
  96.9 4.6 %collective-permute-done.24 = f32[256,256]{1,0:T(8,128)S(1)} collective-permute-done((f32[256,256]{1,0:T(8,128)S(1)}, f32[256,256]{1,0:T(8,128)S(1)}, u32[]{:S(2)}, u32[]{:S(2)}) %collective-permute-start.24) | collective-permute-done | bytes 262176 | tf_op jit(solution)/shard_map/ppermute | solution.py:283
  101.5 13.3 %collective-permute-start.25 = (f32[256,256]{1,0:T(8,128)S(1)}, f32[256,256]{1,0:T(8,128)S(1)}, u32[]{:S(2)}, u32[]{:S(2)}) collective-permute-start(f32[256,256]{1,0:T(8,128)S(1)} %add.130), channel_id=1, source_target_pairs={{0,1},{1,0},{2,3},{3,2},{4,5},{5,4},{6,7},{7,6},{8,9},{9,8},{10,11... | collective-permute-start | bytes 786440 | tf_op jit(solution)/shard_map/ppermute | solution.py:303
  114.9 0.7 add.124.c00
  115.7 2.7 %collective-permute-start.27 = (f32[24,128]{1,0:T(8,128)S(1)}, f32[24,128]{1,0:T(8,128)S(1)}, u32[]{:S(2)}, u32[]{:S(2)}) collective-permute-start(f32[24,128]{1,0:T(8,128)S(1)} %fusion.9), channel_id=1, source_target_pairs={{0,24},{8,16},{16,8},{24,0},{32,56},{40,48},{48,40},{56,32},{64,88... | collective-permute-start | bytes 36872 | tf_op jit(solution)/shard_map/ppermute | solution.py:324
  118.4 9.3 %first_factor.1.w00 = f32[256,256]{1,0:T(8,128)} custom-call(f32[256,256]{1,0:T(8,128)} %add.124.c00), custom_call_target="tpu_custom_call" | custom-call | flops 20000000000 | bytes 1000000 | tf_op jit(solution)/shard_map/first_factor/pallas_call | solution.py:134
  128.0 0.8 broadcast_select_fusion.5
  128.8 1.5 collective-permute-done.28
  130.3 1.6 collective-permute-start.29
  131.9 10.6 %second_factor.1 = (f32[256,256]{1,0:T(8,128)}, f32[256,256]{1,0:T(8,128)}) custom-call(f32[256,256]{1,0:T(8,128)} %first_factor.1.w00, f32[256,256]{1,0:T(8,128)} %get-tuple-element.64.c10, f32[256,256]{1,0:T(8,128)} %get-tuple-element.63.c11), custom_call_target="tpu_custom_call" | custom-call | flops 20000000000 | bytes 1000000 | tf_op jit(solution)/shard_map/second_factor/pallas_call | solution.py:141
  143.7 31.4 %trailing_update.1 = (f32[1024,16,128]{2,1,0:T(8,128)}, f32[1024,512]{1,0:T(8,128)}, f32[8,256]{1,0:T(8,128)}) custom-call(s32[2]{0:T(128)} %pad_add_fusion.place, f32[1024,16,128]{2,1,0:T(8,128)} %bitcast.52, f32[1024,512]{1,0:T(8,128)} %get-tuple-element.49.row_panel, f32[16,256,256]{2,1,0:T(8,128)} %bitcast.53, f32[256,256]{1,0:T(8,128)} %first_factor.1.w00, ...), custom_call_target="tpu_custom_call" | custom-call | tf_op jit(solution)/shard_map/trailing_update/pallas_call | solution.py:239
  175.1 1.3 copy.7
  (83 shorter events, 5.5 us)
Async XLA Ops:
  7.2 136.0 %all-gather.3.cloned.1.call-start = ((), (), s32[]{:S(2)}) async-start(), calls=%async_computation | async-start | bytes 4456448 | tf_op jit(solution)/shard_map/all_gather | solution.py:310
  10.6 9.1 %copy-start.8 = (f32[4,1,256]{2,1,0:T(1,128)S(1)}, f32[4,1,256]{2,1,0:T(1,128)}, u32[]{:S(2)}) copy-start(f32[4,1,256]{2,1,0:T(1,128)} %param.7) | copy-start | bytes 12292
  13.2 27.4 %collective-permute-start.5 = (f32[256,256]{1,0:T(8,128)}, f32[256,256]{1,0:T(8,128)}, u32[]{:S(2)}, u32[]{:S(2)}) collective-permute-start(f32[256,256]{1,0:T(8,128)} %get-tuple-element.50), channel_id=1, source_target_pairs={{0,16},{8,24},{1,17},{9,25},{2,18},{10,26},{3,19},{11,27},{4,20},{... | collective-permute-start | bytes 786440 | tf_op jit(solution)/shard_map/ppermute | solution.py:309
  28.1 7.0 %copy-start.2 = (f32[256,256]{1,0:T(8,128)S(1)}, f32[256,256]{1,0:T(8,128)}, u32[]{:S(2)}) copy-start(f32[256,256]{1,0:T(8,128)} %get-tuple-element.51) | copy-start | bytes 786436
  28.1 11.2 %copy-start.1 = (f32[256,256]{1,0:T(8,128)S(1)}, f32[256,256]{1,0:T(8,128)}, u32[]{:S(2)}) copy-start(f32[256,256]{1,0:T(8,128)} %get-tuple-element.52) | copy-start | bytes 786436
  30.5 27.2 %copy-start = (f32[1024,256]{1,0:T(8,128)S(1)}, f32[1024,256]{1,0:T(8,128)}, u32[]{:S(2)}) copy-start(f32[1024,256]{1,0:T(8,128)} %get-tuple-element.36) | copy-start | bytes 3145732
  30.5 27.2 %collective-permute-start.1 = (f32[1024,256]{1,0:T(8,128)}, f32[1024,256]{1,0:T(8,128)S(1)}, u32[]{:S(2)}, u32[]{:S(2)}) collective-permute-start(f32[1024,256]{1,0:T(8,128)} %broadcast_select_fusion), channel_id=1, source_target_pairs={{0,6},{1,7},{8,14},{9,15},{16,22},{17,23},{24,30},{25,31},{32,38},... | collective-permute-start | bytes 3145736 | tf_op jit(solution)/shard_map/ppermute | solution.py:314
  33.8 23.9 %collective-permute-start = (f32[1024,256]{1,0:T(8,128)}, f32[1024,256]{1,0:T(8,128)S(1)}, u32[]{:S(2)}, u32[]{:S(2)}) collective-permute-start(f32[1024,256]{1,0:T(8,128)} %broadcast_select_fusion), channel_id=1, source_target_pairs={{0,2},{1,3},{8,10},{9,11},{16,18},{17,19},{24,26},{25,27},{32,34},... | collective-permute-start | bytes 3145736 | tf_op jit(solution)/shard_map/ppermute | solution.py:314
  35.2 8.8 %collective-permute-start.11 = (f32[256,256]{1,0:T(8,128)S(1)}, f32[256,256]{1,0:T(8,128)S(1)}, u32[]{:S(2)}, u32[]{:S(2)}) collective-permute-start(f32[256,256]{1,0:T(8,128)S(1)} %copy-done.2), channel_id=1, source_target_pairs={{0,112},{8,120},{1,113},{9,121},{2,114},{10,122},{3,115},{11,123},... | collective-permute-start | bytes 786440 | tf_op jit(solution)/shard_map/ppermute | solution.py:309
  39.3 6.6 %collective-permute-start.10 = (f32[256,256]{1,0:T(8,128)S(1)}, f32[256,256]{1,0:T(8,128)S(1)}, u32[]{:S(2)}, u32[]{:S(2)}) collective-permute-start(f32[256,256]{1,0:T(8,128)S(1)} %copy-done.1), channel_id=1, source_target_pairs={{0,96},{8,104},{1,97},{9,105},{2,98},{10,106},{3,99},{11,107},{4,1... | collective-permute-start | bytes 786440 | tf_op jit(solution)/shard_map/ppermute | solution.py:309
  40.7 8.9 %collective-permute-start.9 = (f32[256,256]{1,0:T(8,128)S(1)}, f32[256,256]{1,0:T(8,128)S(1)}, u32[]{:S(2)}, u32[]{:S(2)}) collective-permute-start(f32[256,256]{1,0:T(8,128)S(1)} %get-tuple-element.53), channel_id=1, source_target_pairs={{0,80},{8,88},{1,81},{9,89},{2,82},{10,90},{3,83},{11,91},{4,84},{... | collective-permute-start | bytes 786440 | tf_op jit(solution)/shard_map/ppermute | solution.py:309
  43.9 5.6 %copy-start.3 = (f32[256,256]{1,0:T(8,128)}, f32[256,256]{1,0:T(8,128)S(1)}, u32[]{:S(2)}) copy-start(f32[256,256]{1,0:T(8,128)S(1)} %collective-permute-done.11) | copy-start | bytes 786436
  44.0 10.0 %collective-permute-start.8 = (f32[256,256]{1,0:T(8,128)}, f32[256,256]{1,0:T(8,128)}, u32[]{:S(2)}, u32[]{:S(2)}) collective-permute-start(f32[256,256]{1,0:T(8,128)} %get-tuple-element.54), channel_id=1, source_target_pairs={{0,64},{8,72},{1,65},{9,73},{2,66},{10,74},{3,67},{11,75},{4,68},{... | collective-permute-start | bytes 786440 | tf_op jit(solution)/shard_map/ppermute | solution.py:309
  45.9 3.6 %copy-start.4 = (f32[256,256]{1,0:T(8,128)}, f32[256,256]{1,0:T(8,128)S(1)}, u32[]{:S(2)}) copy-start(f32[256,256]{1,0:T(8,128)S(1)} %collective-permute-done.10) | copy-start | bytes 786436
  46.0 9.4 %collective-permute-start.7 = (f32[256,256]{1,0:T(8,128)}, f32[256,256]{1,0:T(8,128)}, u32[]{:S(2)}, u32[]{:S(2)}) collective-permute-start(f32[256,256]{1,0:T(8,128)} %get-tuple-element.55), channel_id=1, source_target_pairs={{0,48},{8,56},{1,49},{9,57},{2,50},{10,58},{3,51},{11,59},{4,52},{... | collective-permute-start | bytes 786440 | tf_op jit(solution)/shard_map/ppermute | solution.py:309
  49.6 0.7 copy-start.5
  50.3 5.1 %collective-permute-start.6 = (f32[256,256]{1,0:T(8,128)}, f32[256,256]{1,0:T(8,128)}, u32[]{:S(2)}, u32[]{:S(2)}) collective-permute-start(f32[256,256]{1,0:T(8,128)} %get-tuple-element.56), channel_id=1, source_target_pairs={{0,32},{8,40},{1,33},{9,41},{2,34},{10,42},{3,35},{11,43},{4,36},{... | collective-permute-start | bytes 786440 | tf_op jit(solution)/shard_map/ppermute | solution.py:309
  54.0 6.2 %collective-permute-start.12 = (f32[256,256]{1,0:T(8,128)}, f32[256,256]{1,0:T(8,128)}, u32[]{:S(2)}, u32[]{:S(2)}) collective-permute-start(f32[256,256]{1,0:T(8,128)} %get-tuple-element.66), channel_id=1, source_target_pairs={{0,2}} | collective-permute-start | bytes 786440 | tf_op jit(solution)/shard_map/ppermute | solution.py:281
  58.0 5.3 %collective-permute-start.2 = (f32[512,256]{1,0:T(8,128)S(1)}, f32[512,256]{1,0:T(8,128)S(1)}, u32[]{:S(2)}, u32[]{:S(2)}) collective-permute-start(f32[512,256]{1,0:T(8,128)S(1)} %get-tuple-element.61), channel_id=1, source_target_pairs={{2,4},{3,5},{10,12},{11,13},{18,20},{19,21},{26,28},{27,29},{34,36... | collective-permute-start | bytes 1572872 | tf_op jit(solution)/shard_map/ppermute | solution.py:315
  58.7 4.6 %collective-permute-start.3 = (f32[512,256]{1,0:T(8,128)S(1)}, f32[512,256]{1,0:T(8,128)S(1)}, u32[]{:S(2)}, u32[]{:S(2)}) collective-permute-start(f32[512,256]{1,0:T(8,128)S(1)} %get-tuple-element.62), channel_id=1, source_target_pairs={{6,4},{7,5},{14,12},{15,13},{22,20},{23,21},{30,28},{31,29},{38,36... | collective-permute-start | bytes 1572872 | tf_op jit(solution)/shard_map/ppermute | solution.py:316
  59.4 2.5 %collective-permute-start.19 = (f32[256,256]{1,0:T(8,128)S(1)}, f32[256,256]{1,0:T(8,128)S(1)}, u32[]{:S(2)}, u32[]{:S(2)}) collective-permute-start(f32[256,256]{1,0:T(8,128)S(1)} %get-tuple-element.65), channel_id=1, source_target_pairs={{8,40},{9,41}} | collective-permute-start | bytes 786440 | tf_op jit(solution)/shard_map/ppermute | solution.py:281
  61.2 1.4 collective-permute-start.13
  61.9 14.7 %collective-permute-start.20 = (f32[256,256]{1,0:T(8,128)S(1)}, f32[256,256]{1,0:T(8,128)S(1)}, u32[]{:S(2)}, u32[]{:S(2)}) collective-permute-start(f32[256,256]{1,0:T(8,128)S(1)} %add.125), channel_id=1, source_target_pairs={{8,104},{9,105},{40,72},{41,73}} | collective-permute-start | bytes 786440 | tf_op jit(solution)/shard_map/ppermute | solution.py:283
  62.7 14.7 %collective-permute-start.14 = (f32[256,256]{1,0:T(8,128)S(1)}, f32[256,256]{1,0:T(8,128)S(1)}, u32[]{:S(2)}, u32[]{:S(2)}) collective-permute-start(f32[256,256]{1,0:T(8,128)S(1)} %add.119), channel_id=1, source_target_pairs={{0,8},{2,10},{4,12},{6,14}} | collective-permute-start | bytes 786440 | tf_op jit(solution)/shard_map/ppermute | solution.py:281
  64.6 19.4 %collective-permute-start.4 = (f32[1024,256]{1,0:T(8,128)}, f32[1024,256]{1,0:T(8,128)S(1)}, u32[]{:S(2)}, u32[]{:S(2)}) collective-permute-start(f32[1024,256]{1,0:T(8,128)} %pad_maximum_fusion.1), channel_id=1, source_target_pairs={{0,1},{1,0},{2,3},{3,2},{4,5},{5,4},{6,7},{7,6},{8,9},{9,8},{10,11... | collective-permute-start | bytes 3145736 | tf_op jit(solution)/shard_map/ppermute | solution.py:318
  76.7 1.4 collective-permute-start.21
  77.4 1.4 collective-permute-start.15
  78.2 1.4 collective-permute-start.22
  78.9 1.4 collective-permute-start.16
  79.7 1.6 collective-permute-start.23
  80.4 2.2 %collective-permute-start.17 = (f32[256,256]{1,0:T(8,128)S(1)}, f32[256,256]{1,0:T(8,128)S(1)}, u32[]{:S(2)}, u32[]{:S(2)}) collective-permute-start(f32[256,256]{1,0:T(8,128)S(1)} %add.122), channel_id=1, source_target_pairs={{0,96},{8,104},{16,112},{24,120},{2,98},{10,106},{18,114},{26,122}... | collective-permute-start | bytes 786440 | tf_op jit(solution)/shard_map/ppermute | solution.py:283
  81.3 20.2 %collective-permute-start.24 = (f32[256,256]{1,0:T(8,128)S(1)}, f32[256,256]{1,0:T(8,128)S(1)}, u32[]{:S(2)}, u32[]{:S(2)}) collective-permute-start(f32[256,256]{1,0:T(8,128)S(1)} %add.129), channel_id=1, source_target_pairs={{8,0},{10,2},{12,4},{14,6},{40,32},{42,34},{44,36},{46,38},{72,64}... | collective-permute-start | bytes 786440 | tf_op jit(solution)/shard_map/ppermute | solution.py:283
  82.7 32.2 %collective-permute-start.18 = (f32[256,256]{1,0:T(8,128)S(1)}, f32[256,256]{1,0:T(8,128)S(1)}, u32[]{:S(2)}, u32[]{:S(2)}) collective-permute-start(f32[256,256]{1,0:T(8,128)S(1)} %add.123), channel_id=1, source_target_pairs={{0,1},{2,3},{4,5},{6,7},{8,9},{10,11},{12,13},{14,15},{16,17},{18,... | collective-permute-start | bytes 786440 | tf_op jit(solution)/shard_map/ppermute | solution.py:300
  85.8 1.1 copy-start.7
  87.0 28.6 %collective-permute-start.26 = (f32[24,128]{1,0:T(8,128)S(1)}, f32[24,128]{1,0:T(8,128)S(1)}, u32[]{:S(2)}, u32[]{:S(2)}) collective-permute-start(f32[24,128]{1,0:T(8,128)S(1)} %maximum_maximum_fusion), channel_id=1, source_target_pairs={{0,8},{8,0},{16,24},{24,16},{32,40},{40,32},{48,56},{56,48},{64,72... | collective-permute-start | bytes 36872 | tf_op jit(solution)/shard_map/ppermute | solution.py:324
  101.5 26.4 %collective-permute-start.25 = (f32[256,256]{1,0:T(8,128)S(1)}, f32[256,256]{1,0:T(8,128)S(1)}, u32[]{:S(2)}, u32[]{:S(2)}) collective-permute-start(f32[256,256]{1,0:T(8,128)S(1)} %add.130), channel_id=1, source_target_pairs={{0,1},{1,0},{2,3},{3,2},{4,5},{5,4},{6,7},{7,6},{8,9},{9,8},{10,11... | collective-permute-start | bytes 786440 | tf_op jit(solution)/shard_map/ppermute | solution.py:303
  115.7 12.1 %collective-permute-start.27 = (f32[24,128]{1,0:T(8,128)S(1)}, f32[24,128]{1,0:T(8,128)S(1)}, u32[]{:S(2)}, u32[]{:S(2)}) collective-permute-start(f32[24,128]{1,0:T(8,128)S(1)} %fusion.9), channel_id=1, source_target_pairs={{0,24},{8,16},{16,8},{24,0},{32,56},{40,48},{48,40},{56,32},{64,88... | collective-permute-start | bytes 36872 | tf_op jit(solution)/shard_map/ppermute | solution.py:324
  127.7 2.5 %collective-permute-start.28 = (f32[24,128]{1,0:T(8,128)S(1)}, f32[24,128]{1,0:T(8,128)S(1)}, u32[]{:S(2)}, u32[]{:S(2)}) collective-permute-start(f32[24,128]{1,0:T(8,128)S(1)} %add.132), channel_id=1, source_target_pairs={{0,32},{8,40},{16,48},{24,56},{32,0},{40,8},{48,16},{56,24},{64,96... | collective-permute-start | bytes 36872 | tf_op jit(solution)/shard_map/ppermute | solution.py:324
  130.3 12.2 %collective-permute-start.29 = (f32[24,128]{1,0:T(8,128)S(1)}, f32[24,128]{1,0:T(8,128)S(1)}, u32[]{:S(2)}, u32[]{:S(2)}) collective-permute-start(f32[24,128]{1,0:T(8,128)S(1)} %add.133), channel_id=1, source_target_pairs={{0,96},{8,104},{16,112},{24,120},{32,64},{40,72},{48,80},{56,88},{... | collective-permute-start | bytes 36872 | tf_op jit(solution)/shard_map/ppermute | solution.py:324
  143.1 0.6 copy-start.6
Sparse Core Ops, SparseCore 0:
  57.8 57.8 all-gather.2

commit v2 on v1

v2 whole, which is shorter than its diff:
```python
import functools

import jax
import jax.numpy as jnp
from jax import lax
from jax.experimental import pallas as pl
from jax.experimental.pallas import tpu as pltpu
from jax.sharding import PartitionSpec as P

HIGHEST = lax.Precision.HIGHEST
F32 = jnp.float32
BF16 = jnp.bfloat16
NB = 256
NT = (((1,), (1,)), ((), ()))
NN = (((1,), (0,)), ((), ()))


def dot6(a, b, dims):
    return lax.dot_general(a, b, dims, precision=HIGHEST, preferred_element_type=F32)


def halves(value):
    high = value.astype(BF16)
    return high, (value - high.astype(F32)).astype(BF16)


def dot3(a, b, dims):
    total = lax.dot_general(a[0], b[0], dims, preferred_element_type=F32)
    total += lax.dot_general(a[0], b[1], dims, preferred_element_type=F32)
    return total + lax.dot_general(a[1], b[0], dims, preferred_element_type=F32)


def splat_row(ref, row, lanes):
    return jnp.broadcast_to(ref[row : row + 1, lanes], (8, 128))


def splat_lane(value, lane):
    return jnp.broadcast_to(value[:, lane : lane + 1], (8, 128))


def invert_factor(m, put):
    left, right = slice(0, 128), slice(128, 256)
    for block in range(16):
        base = 8 * block
        rows = [[splat_row(m, base + a, side) for a in range(8)] for side in (left, right)]
        b = {(a, k): splat_lane(rows[0][a], base + k) for a in range(8) for k in range(a + 1)}
        n = {}
        inverse, root = [], []
        for i in range(8):
            inverse.append(1.0 / b[i, i])
            root.append(lax.rsqrt(b[i, i]))
            for k in range(i + 1, 8):
                ratio = b[k, i] * inverse[i]
                for j in range(i + 1, k + 1):
                    b[k, j] = b[k, j] - ratio * b[j, i]
                for j in range(i):
                    n[k, j] = n[k, j] - ratio * n[i, j]
                n[k, i] = -ratio
        solved = []
        for side in range(2):
            upper = []
            for i in range(8):
                value = rows[side][i]
                for j in range(i):
                    value = value + n[i, j] * rows[side][j]
                upper.append(value)
            if side == 1:
                for i in range(8):
                    put(base + i, root[i] * upper[i])
            scaled = [inverse[i] * upper[i] for i in range(8)]
            out = []
            for i in range(8):
                value = scaled[i]
                for k in range(i + 1, 8):
                    value = value + n[k, i] * scaled[k]
                out.append(value)
            solved.append(out)
        for other in range(block + 1, 16):
            span = slice(8 * other, 8 * other + 8)
            a_part, n_part = m[span, left], m[span, right]
            columns = [splat_lane(a_part, base + i) for i in range(8)]
            for i in range(8):
                a_part = a_part - columns[i] * solved[0][i]
                n_part = n_part - columns[i] * solved[1][i]
            m[span, left] = a_part
            m[span, right] = n_part


def factor_tile(source, out, m, part):
    eye = (lax.broadcasted_iota(jnp.int32, (128, 128), 0) == lax.broadcasted_iota(jnp.int32, (128, 128), 1)).astype(F32)
    m[:, 0:128] = source[0:128, 0:128]

    def body(i, carry):
        m[:, 128:256] = eye

        def put(row, value):
            part[i, row : row + 1, :] = value[0:1, :]

        invert_factor(m, put)

        @pl.when(i == 0)
        def _():
            low = dot6(source[128:256, 0:128], part[0], NT)
            m[:, 0:128] = source[128:256, 128:256] - dot6(low, low, NT)
            part[2] = low

        return carry

    lax.fori_loop(0, 2, body, 0)
    out[0:128, 0:128] = part[0]
    out[0:128, 128:256] = jnp.zeros((128, 128), F32)
    out[128:256, 128:256] = part[1]
    out[128:256, 0:128] = -dot6(part[1], dot6(part[2], part[0], NN), NN)


def first_kernel(c00, w00, m, part):
    factor_tile(c00, w00, m, part)


def second_kernel(w00, c10, c11, l10, w11, schur, m, part):
    low = dot6(c10[...], w00[...], NT)
    l10[...] = low
    schur[...] = c11[...] - dot6(low, low, NT)
    factor_tile(schur, w11, m, part)


TILE = jax.ShapeDtypeStruct((NB, NB), F32)
WORK = [pltpu.VMEM((128, 256), F32), pltpu.VMEM((3, 128, 128), F32)]
VMEM = pl.BlockSpec(memory_space=pltpu.VMEM)
SMEM = pl.BlockSpec(memory_space=pltpu.SMEM)


def first_factor(c00):
    return pl.pallas_call(
        first_kernel, out_shape=TILE, in_specs=[VMEM], out_specs=VMEM, scratch_shapes=WORK, name="first_factor",
        cost_estimate=pl.CostEstimate(flops=20_000_000_000, bytes_accessed=1_000_000, transcendentals=0),
    )(c00)


def second_factor(w00, c10, c11):
    return pl.pallas_call(
        second_kernel, out_shape=(TILE, TILE), in_specs=[VMEM] * 3, out_specs=(VMEM, VMEM),
        scratch_shapes=[pltpu.VMEM((NB, NB), F32)] + WORK, name="second_factor",
        cost_estimate=pl.CostEstimate(flops=20_000_000_000, bytes_accessed=1_000_000, transcendentals=0),
    )(w00, c10, c11)


def corner_kernel(a, *pieces):
    for q in range(16):
        pieces[q // 2][:, 128 * (q % 2) : 128 * (q % 2) + 128] = a[:, q, :]


def corner_call(flat):
    return pl.pallas_call(
        corner_kernel, grid=(2,), out_shape=(TILE,) * 8,
        in_specs=[pl.BlockSpec((128, 16, 128), lambda i: (i, 0, 0))],
        out_specs=(pl.BlockSpec((128, NB), lambda i: (i, 0)),) * 8,
        name="corner_tiles",
    )(flat)


def column_kernel(weights, a, column, sums):
    step = pl.program_id(0)

    @pl.when(step < 8)
    def _():
        for q in range(2):
            column[:, 128 * q : 128 * q + 128] = a[:, q, :]

    @pl.when(step == 0)
    def _():
        sums[...] = jnp.zeros_like(sums)

    @pl.when(step < 8)
    def _():
        def body(i, total):
            for j in range(8):
                row = 8 * i + j
                total = total + weights[step * 128 + row] * a[row]
            return total

        sums[...] += lax.fori_loop(0, 16, body, jnp.zeros((16, 128), F32))

    @pl.when(step == 8)
    def _():
        for q in range(2):
            column[0:8, 128 * q : 128 * q + 128] = jnp.broadcast_to(sums[q : q + 1, :], (8, 128))


def column_call(weights, flat):
    return pl.pallas_call(
        column_kernel, grid=(9,),
        out_shape=(jax.ShapeDtypeStruct((1032, NB), F32), jax.ShapeDtypeStruct((16, 128), F32)),
        in_specs=[SMEM, pl.BlockSpec((128, 16, 128), lambda i: (jnp.minimum(i, 7), 0, 0))],
        out_specs=(pl.BlockSpec((128, NB), lambda i: (i, 0)), pl.BlockSpec((16, 128), lambda i: (0, 0))),
        name="first_column",
    )(weights, flat)


def panel_kernel(place, mine, theirs, sums, w00, l10, w11, panels, high, low, taken, factors):
    step = pl.program_id(0)
    even = place[1] % 2 == 0

    @pl.when(step == 0)
    def _():
        for k, ref in enumerate((w00, l10, w11)):
            factors[0, k], factors[1, k] = halves(ref[...])
        v0 = jnp.broadcast_to(jnp.concatenate([sums[16:17], sums[17:18]], axis=1), (8, NB))
        v1 = jnp.broadcast_to(jnp.concatenate([sums[18:19], sums[19:20]], axis=1), (8, NB))
        y0 = dot6(v0, w00[...], NT)
        y1 = dot6(v1 - dot6(y0, l10[...], NT), w11[...], NT)
        z1 = dot6(y1, w11[...], NN)
        taken[:, 256:512] = z1
        taken[:, 0:256] = dot6(y0 - dot6(z1, l10[...], NN), w00[...], NN)

    f00, f10, f11 = [(factors[0, k], factors[1, k]) for k in range(3)]
    own, other = mine[...], theirs[...]
    first = jnp.where(even, own, other)
    second = jnp.where(even, other, own)
    left = dot3(halves(first), f00, NT)
    right = dot3(halves(second - dot3(halves(left), f10, NT)), f11, NT)
    panels[:, 0:256] = left
    panels[:, 256:512] = jnp.where((step * 512 < 256) & (place[0] == 0) & (lax.broadcasted_iota(jnp.int32, (512, 1), 0) < 256), 0.0, right)
    last = dot3(halves(right), f11, NN)
    last_halves = halves(last)
    high[:, 256:512], low[:, 256:512] = last_halves
    high[:, 0:256], low[:, 0:256] = halves(dot3(halves(left - dot3(last_halves, f10, NN)), f00, NN))


def panel_call(place, mine, theirs, sums, w00, l10, w11):
    full = lambda *shape: pl.BlockSpec(shape, lambda i: (0,) * len(shape))
    part = lambda n: pl.BlockSpec((512, n), lambda i: (i, 0))
    return pl.pallas_call(
        panel_kernel, grid=(2,),
        out_shape=(
            jax.ShapeDtypeStruct((1024, 512), F32),
            jax.ShapeDtypeStruct((1024, 512), BF16),
            jax.ShapeDtypeStruct((1024, 512), BF16),
            jax.ShapeDtypeStruct((8, 512), F32),
        ),
        in_specs=[SMEM, part(NB), part(NB), full(24, 128), full(NB, NB), full(NB, NB), full(NB, NB)],
        out_specs=(part(512), part(512), part(512), full(8, 512)),
        scratch_shapes=[pltpu.VMEM((2, 3, NB, NB), BF16)],
        name="panel_solve",
        cost_estimate=pl.CostEstimate(flops=8_000_000_000, bytes_accessed=8_000_000, transcendentals=0),
    )(place, mine, theirs, sums, w00, l10, w11)


def update_kernel(place, flat, across, high, low, sums, taken, out, checksum, right_high, right_low):
    group, step = pl.program_id(0), pl.program_id(1)
    row_index, col_index = place[0], place[1]

    @pl.when(step == 0)
    def _():
        y = halves(taken[...])
        for u in range(4):
            for h in range(2):
                span = slice(NB * h, NB * h + NB)
                right_high[u, span], right_low[u, span] = halves(across[2 * u + h])
            part = dot3(y, (right_high[u], right_low[u]), NN)[0:1]
            for h in range(2):
                q = 2 * u + h
                kept = sums[pl.ds(8 * group + q, 1), :] - part[:, 128 * h : 128 * h + 128]
                if u == 0:
                    kept = jnp.where((group == 0) & (col_index < 2), 0.0, kept)
                checksum[pl.ds(8 * group + q, 1), :] = kept

    rows = flat.shape[0]
    top = (step * rows + lax.broadcasted_iota(jnp.int32, (rows, 1), 0) < NB) & (row_index < 2)
    for u in range(4):
        product = dot3((high[...], low[...]), (right_high[u], right_low[u]), NN)
        gone = top | ((group == 0) & (col_index < 2)) if u == 0 else top
        for h in range(2):
            q = 2 * u + h
            value = flat[:, q, :] - product[:, 128 * h : 128 * h + 128]
            out[:, q, :] = jnp.where(gone, 0.0, value)


def update_call(place, flat, across, high, low, sums, taken):
    rows = 256
    full = lambda *shape: pl.BlockSpec(shape, lambda g, i: (0,) * len(shape))
    return pl.pallas_call(
        update_kernel, grid=(2, 1024 // rows),
        out_shape=(jax.ShapeDtypeStruct((1024, 16, 128), F32), jax.ShapeDtypeStruct((16, 128), F32)),
        in_specs=[
            SMEM,
            pl.BlockSpec((rows, 8, 128), lambda g, i: (i, g, 0)),
            pl.BlockSpec((8, NB, NB), lambda g, i: (g, 0, 0)),
            pl.BlockSpec((rows, 512), lambda g, i: (i, 0)),
            pl.BlockSpec((rows, 512), lambda g, i: (i, 0)),
            full(24, 128),
            full(8, 512),
        ],
        out_specs=(pl.BlockSpec((rows, 8, 128), lambda g, i: (i, g, 0)), full(16, 128)),
        scratch_shapes=[pltpu.VMEM((4, 512, NB), BF16), pltpu.VMEM((4, 512, NB), BF16)],
        name="trailing_update",
    )(place, flat, across, high, low, sums, taken)


def where_is(device):
    row, col = divmod(device, 8)
    return [row // 4, row % 4, col // 2, col % 2]


def device_at(z, y, x, core):
    return ((z % 4) * 4 + y % 4) * 8 + (x % 4) * 2 + core


def moved(device, dim, by):
    at = where_is(device)
    at[dim] += by
    return device_at(*at)


def spread(value, sources, dims, start, here):
    holders = list(sources)
    stages = []
    for dim in dims:
        away = (here[dim] - start[dim]) % 4
        pairs = [(h, moved(h, dim, 1)) for h in holders]
        value = jnp.where(away == 1, lax.ppermute(value, ("row", "col"), pairs), value)
        stages.append(value)
        pairs = [(h, moved(h, dim, -1)) for h in holders] + [(moved(h, dim, 1), moved(h, dim, 2)) for h in holders]
        value = jnp.where(away >= 2, lax.ppermute(value, ("row", "col"), pairs), value)
        stages.append(value)
        holders = [moved(h, dim, k) for h in holders for k in range(4)]
    return stages


def after(value, token):
    return lax.optimization_barrier((value, token))[0]


def shards(covariance, check_weights):
    row = lax.axis_index("row")
    col = lax.axis_index("col")
    core = col % 2
    x = col // 2
    here = [row // 4, row % 4, x]
    flat = covariance.reshape(1024, 16, 128)
    tiles = jnp.arange(4, dtype=jnp.int32) * 16 + row
    weights = jnp.where((tiles >= 2)[:, None], check_weights.reshape(4, NB), 0.0).reshape(1024)
    place = jnp.stack([row, col]).astype(jnp.int32)
    swap_cores = [(c, c ^ 1) for c in range(8)]

    pieces = corner_call(flat)
    tree0 = spread(pieces[0], [device_at(0, 0, 0, 0)], (2, 1, 0), (0, 0, 0), here)
    c00 = jnp.where(core == 1, lax.ppermute(tree0[-1], "col", [(c, c + 1) for c in (0, 2, 4, 6)]), tree0[-1])
    tree1 = spread(pieces[0], [device_at(0, 1, 0, 0), device_at(0, 1, 0, 1)], (1, 0, 2), (0, 1, 0), here)
    below = tree1[-1]
    other = lax.ppermute(below, "col", swap_cores)
    c10 = jnp.where(core == 0, below, other)
    c11 = jnp.where(core == 0, other, below)

    piece = pieces[0]
    for j in range(1, 8):
        piece = jnp.where(row // 2 == j, lax.ppermute(pieces[j], "row", [(0, 2 * j), (1, 2 * j + 1)]), piece)
    across = lax.all_gather(piece, "row", axis=0)

    column, sums = column_call(weights, after(flat, tree0[0]))
    from_left = lax.ppermute(column, "col", [(0, 2), (1, 3)])
    from_right = lax.ppermute(column, "col", [(0, 6), (1, 7)])
    mine = jnp.where(x == 1, from_left, jnp.where(x == 3, from_right, column))
    upper = jnp.where(x == 2, lax.ppermute(mine[0:512], "col", [(2, 4), (3, 5)]), mine[0:512])
    lower = jnp.where(x == 2, lax.ppermute(mine[512:1032], "col", [(6, 4), (7, 5)]), mine[512:1032])
    mine = jnp.concatenate([upper, lower], axis=0)
    theirs = lax.ppermute(mine, "col", swap_cores)
    first_sums = jnp.where(core == 0, mine[1024:1025], theirs[1024:1025])
    second_sums = jnp.where(core == 0, theirs[1024:1025], mine[1024:1025])
    total = jnp.concatenate([sums, first_sums.reshape(2, 128), second_sums.reshape(2, 128), jnp.zeros((4, 128), F32)], axis=0)
    for d in (1, 3, 4, 12):
        total = total + lax.ppermute(total, "row", [(r, r ^ d) for r in range(16)])

    w00 = first_factor(c00)
    l10, w11 = second_factor(w00, c10, c11)
    panels, high, low, taken = panel_call(place, mine, theirs, total, w00, l10, w11)
    trailing, checksum = update_call(place, flat, across, high, low, total, taken)
    return (
        trailing.reshape(4, 1, NB, 8, 1, NB),
        panels.reshape(4, 1, NB, 512),
        checksum.reshape(8, 1, NB),
    )


def solution(mesh):
    in_specs = (P(None, "row", None, None, "col", None), P(None, "row", None))
    out_specs = (
        P(None, "row", None, None, "col", None),
        P(None, "row", None, None),
        P(None, "col", None),
    )
    return jax.shard_map(shards, mesh=mesh, in_specs=in_specs, out_specs=out_specs, check_vma=False)
```

time: 186 us -> 186 us (level)
  the two profiles are of different devices: /device:TPU:1 before, /device:TPU:2 now
where the time goes in v2:
time: 186 us; the launch traced here: 185 us
  Pallas kernels  61.9 us (33%)
  starting transfers between devices  55 us (30%)
  waiting for transfers between devices  44.6 us (24%)
  between operations  14.6 us (8%)
  other arithmetic  8.12 us (4%)
    ppermute x12, starting transfers between devices, spread(): lax.ppermute(value, ('row', 'col'), pairs)  21.8 us
    pallas_call x1, Pallas kernels, update_call(): pl.pallas_call(update_kernel, grid=(2, 1024 // rows), out_shape=(jax.Shap...  20.8 us
    ppermute x7, starting transfers between devices, shards(): lax.ppermute(pieces[j], 'row', [(0, 2 * j), (1, 2 * j + 1)])  16.4 us
    ppermute x1, waiting for transfers between devices, shards(): from_left = lax.ppermute(column, 'col', [(0, 2), (1, 3)])  15.8 us
    ppermute x12, waiting for transfers between devices, spread(): lax.ppermute(value, ('row', 'col'), pairs)  12.7 us
    ppermute x7, waiting for transfers between devices, shards(): lax.ppermute(pieces[j], 'row', [(0, 2 * j), (1, 2 * j + 1)])  12.1 us
    pallas_call x1, Pallas kernels, second_factor(): pl.pallas_call(second_kernel, out_shape=(TILE, TILE), in_specs=[VMEM] * 3...  10.6 us
    pallas_call x1, Pallas kernels, panel_call(): pl.pallas_call(panel_kernel, grid=(2,), out_shape=(jax.ShapeDtypeStruct((...  9.88 us
  transfers between devices with their start and end apart: 31, of which 12 were waited for; matrix products, arithmetic and copies ran while one was open for 4% of the time, Pallas kernels for 16%

profile of v2, /device:TPU:2, one launch (start us, length us, event | category | flops | bytes accessed | tf_op | source)
XLA Modules:
  0.0 185.3 jit_solution(15688227660810481774)
XLA Ops:
  7.2 3.3 %corner_tiles.1 = (f32[256,256]{1,0:T(8,128)}, f32[256,256]{1,0:T(8,128)}, f32[256,256]{1,0:T(8,128)}, f32[256,256]{1,0:T(8,128)}, f32[256,256]{1,0:T(8,128)}, /...) custom-call(f32[1024,16,128]{2,1,0:T(8,128)} %bitcast.12), custom_call_target="tpu_custom_call" | custom-call | tf_op jit(solution)/shard_map/corner_tiles/pallas_call | solution.py:154
  10.5 8.6 %collective-permute-start = (f32[256,256]{1,0:T(8,128)}, f32[256,256]{1,0:T(8,128)S(1)}, u32[]{:S(2)}, u32[]{:S(2)}) collective-permute-start(f32[256,256]{1,0:T(8,128)} %get-tuple-element.22), channel_id=1, source_target_pairs={{0,112},{8,120},{1,113},{9,121},{2,114},{10,122},{3,115},{11,123},... | collective-permute-start | bytes 786440 | tf_op jit(solution)/shard_map/ppermute | solution.py:357
  19.1 1.3 collective-permute-start.1
  20.4 1.3 collective-permute-start.2
  21.8 1.3 collective-permute-start.3
  23.1 1.3 collective-permute-start.7
  24.4 1.7 collective-permute-done
  26.8 1.3 collective-permute-start.4
  28.1 3.6 %collective-permute-done.2 = f32[256,256]{1,0:T(8,128)S(1)} collective-permute-done((f32[256,256]{1,0:T(8,128)}, f32[256,256]{1,0:T(8,128)S(1)}, u32[]{:S(2)}, u32[]{:S(2)}) %collective-permute-start.2) | collective-permute-done | bytes 262176 | tf_op jit(solution)/shard_map/ppermute | solution.py:357
  31.7 1.3 collective-permute-start.5
  33.0 1.3 collective-permute-start.6
  35.1 2.2 %collective-permute-done.4 = f32[256,256]{1,0:T(8,128)S(1)} collective-permute-done((f32[256,256]{1,0:T(8,128)}, f32[256,256]{1,0:T(8,128)S(1)}, u32[]{:S(2)}, u32[]{:S(2)}) %collective-permute-start.4) | collective-permute-done | bytes 262176 | tf_op jit(solution)/shard_map/ppermute | solution.py:357
  37.4 4.5 %collective-permute-done.6 = f32[256,256]{1,0:T(8,128)S(1)} collective-permute-done((f32[256,256]{1,0:T(8,128)}, f32[256,256]{1,0:T(8,128)S(1)}, u32[]{:S(2)}, u32[]{:S(2)}) %collective-permute-start.6) | collective-permute-done | bytes 262176 | tf_op jit(solution)/shard_map/ppermute | solution.py:357
  41.8 1.8 broadcast_select_fusion.2
  43.7 8.0 %first_column.1 = (f32[1032,256]{1,0:T(8,128)}, f32[16,128]{1,0:T(8,128)}) custom-call(f32[1024]{0:T(1024)} %broadcast_select_fusion.17.weights, f32[1024,16,128]{2,1,0:T(8,128)} %bitcast.13), custom_call_target="tpu_custom_call" | custom-call | tf_op jit(solution)/shard_map/first_column/pallas_call | solution.py:191
  51.6 0.7 collective-permute-start.9
  52.3 1.3 collective-permute-start.8
  53.6 0.7 collective-permute-start.24
  54.3 3.9 %collective-permute-start.17 = (f32[256,256]{1,0:T(8,128)S(1)}, f32[256,256]{1,0:T(8,128)S(1)}, u32[]{:S(2)}, u32[]{:S(2)}) collective-permute-start(f32[256,256]{1,0:T(8,128)S(1)} %get-tuple-element.49), channel_id=1, source_target_pairs={{0,6},{2,4}} | collective-permute-start | bytes 786440 | tf_op jit(solution)/shard_map/ppermute | solution.py:324
  59.0 3.1 %collective-permute-done.17 = f32[256,256]{1,0:T(8,128)S(1)} collective-permute-done((f32[256,256]{1,0:T(8,128)S(1)}, f32[256,256]{1,0:T(8,128)S(1)}, u32[]{:S(2)}, u32[]{:S(2)}) %collective-permute-start.17) | collective-permute-done | bytes 262176 | tf_op jit(solution)/shard_map/ppermute | solution.py:324
  62.1 1.3 collective-permute-start.18
  63.5 1.4 collective-permute-start.26
  64.9 15.8 %collective-permute-done.8 = f32[1032,256]{1,0:T(8,128)} collective-permute-done((f32[1032,256]{1,0:T(8,128)}, f32[1032,256]{1,0:T(8,128)}, u32[]{:S(2)}, u32[]{:S(2)}) %collective-permute-start.8) | collective-permute-done | bytes 1056800 | tf_op jit(solution)/shard_map/ppermute | solution.py:361
  80.6 1.5 select_select_fusion
  82.1 0.8 slice.20
  83.0 2.1 %collective-permute-start.10 = (f32[512,256]{1,0:T(8,128)}, f32[512,256]{1,0:T(8,128)}, u32[]{:S(2)}, u32[]{:S(2)}) collective-permute-start(f32[512,256]{1,0:T(8,128)} %slice.20), channel_id=1, source_target_pairs={{2,4},{3,5},{10,12},{11,13},{18,20},{19,21},{26,28},{27,29},{34,36... | collective-permute-start | bytes 1572872 | tf_op jit(solution)/shard_map/ppermute | solution.py:364
  85.1 5.6 %collective-permute-start.19 = (f32[256,256]{1,0:T(8,128)S(1)}, f32[256,256]{1,0:T(8,128)S(1)}, u32[]{:S(2)}, u32[]{:S(2)}) collective-permute-start(f32[256,256]{1,0:T(8,128)S(1)} %broadcast_select_fusion.8), channel_id=1, source_target_pairs={{0,24},{2,26},{4,28},{6,30},{8,16},{10,18},{12,20},{14,22}} | collective-permute-start | bytes 786440 | tf_op jit(solution)/shard_map/ppermute | solution.py:324
  90.8 0.7 collective-permute-start.11
  91.6 1.3 collective-permute-start.27
  92.9 1.7 collective-permute-done.19
  94.6 1.3 collective-permute-start.20
  96.3 3.5 %collective-permute-done.27 = f32[256,256]{1,0:T(8,128)S(1)} collective-permute-done((f32[256,256]{1,0:T(8,128)S(1)}, f32[256,256]{1,0:T(8,128)S(1)}, u32[]{:S(2)}, u32[]{:S(2)}) %collective-permute-start.27) | collective-permute-done | bytes 262176 | tf_op jit(solution)/shard_map/ppermute | solution.py:321
  99.9 2.4 %collective-permute-start.28 = (f32[256,256]{1,0:T(8,128)S(1)}, f32[256,256]{1,0:T(8,128)S(1)}, u32[]{:S(2)}, u32[]{:S(2)}) collective-permute-start(f32[256,256]{1,0:T(8,128)S(1)} %broadcast_select_fusion.15), channel_id=1, source_target_pairs={{8,14},{40,46},{72,78},{104,110},{16,22},{48,54},{80,86},{112,118}... | collective-permute-start | bytes 786440 | tf_op jit(solution)/shard_map/ppermute | solution.py:324
  102.4 1.3 collective-permute-start.21
  104.4 4.0 %collective-permute-done.28 = f32[256,256]{1,0:T(8,128)S(1)} collective-permute-done((f32[256,256]{1,0:T(8,128)S(1)}, f32[256,256]{1,0:T(8,128)S(1)}, u32[]{:S(2)}, u32[]{:S(2)}) %collective-permute-start.28) | collective-permute-done | bytes 262176 | tf_op jit(solution)/shard_map/ppermute | solution.py:324
  108.9 2.0 %collective-permute-start.22 = (f32[256,256]{1,0:T(8,128)S(1)}, f32[256,256]{1,0:T(8,128)S(1)}, u32[]{:S(2)}, u32[]{:S(2)}) collective-permute-start(f32[256,256]{1,0:T(8,128)S(1)} %broadcast_select_fusion.13), channel_id=1, source_target_pairs={{0,1},{2,3},{4,5},{6,7},{8,9},{10,11},{12,13},{14,15},{16,17},{18,... | collective-permute-start | bytes 786440 | tf_op jit(solution)/shard_map/ppermute | solution.py:348
  111.0 0.7 broadcast_select_fusion.19
  111.8 4.4 %collective-permute-start.13 = (f32[24,128]{1,0:T(8,128)S(1)}, f32[24,128]{1,0:T(8,128)S(1)}, u32[]{:S(2)}, u32[]{:S(2)}) collective-permute-start(f32[24,128]{1,0:T(8,128)S(1)} %maximum_maximum_fusion), channel_id=1, source_target_pairs={{0,8},{8,0},{16,24},{24,16},{32,40},{40,32},{48,56},{56,48},{64,72... | collective-permute-start | bytes 36872 | tf_op jit(solution)/shard_map/ppermute | solution.py:372
  116.2 0.7 broadcast_select_fusion.14.c00
  116.9 0.9 collective-permute-done.13
  117.9 3.0 %collective-permute-start.14 = (f32[24,128]{1,0:T(8,128)S(1)}, f32[24,128]{1,0:T(8,128)S(1)}, u32[]{:S(2)}, u32[]{:S(2)}) collective-permute-start(f32[24,128]{1,0:T(8,128)S(1)} %fusion), channel_id=1, source_target_pairs={{0,24},{8,16},{16,8},{24,0},{32,56},{40,48},{48,40},{56,32},{64,88... | collective-permute-start | bytes 36872 | tf_op jit(solution)/shard_map/ppermute | solution.py:372
  120.9 9.3 %first_factor.1.w00 = f32[256,256]{1,0:T(8,128)} custom-call(f32[256,256]{1,0:T(8,128)} %broadcast_select_fusion.14.c00), custom_call_target="tpu_custom_call" | custom-call | flops 20000000000 | bytes 1000000 | tf_op jit(solution)/shard_map/first_factor/pallas_call | solution.py:134
  130.3 0.8 broadcast_select_fusion.4
  131.1 3.1 %collective-permute-done.15 = f32[24,128]{1,0:T(8,128)S(1)} collective-permute-done((f32[24,128]{1,0:T(8,128)S(1)}, f32[24,128]{1,0:T(8,128)S(1)}, u32[]{:S(2)}, u32[]{:S(2)}) %collective-permute-start.15) | collective-permute-done | bytes 12320 | tf_op jit(solution)/shard_map/ppermute | solution.py:372
  134.2 2.3 %collective-permute-start.16 = (f32[24,128]{1,0:T(8,128)S(1)}, f32[24,128]{1,0:T(8,128)S(1)}, u32[]{:S(2)}, u32[]{:S(2)}) collective-permute-start(f32[24,128]{1,0:T(8,128)S(1)} %add.53), channel_id=1, source_target_pairs={{0,96},{8,104},{16,112},{24,120},{32,64},{40,72},{48,80},{56,88},{... | collective-permute-start | bytes 36872 | tf_op jit(solution)/shard_map/ppermute | solution.py:372
  136.5 10.6 %second_factor.1 = (f32[256,256]{1,0:T(8,128)}, f32[256,256]{1,0:T(8,128)}) custom-call(f32[256,256]{1,0:T(8,128)} %first_factor.1.w00, f32[256,256]{1,0:T(8,128)} %get-tuple-element.47.c10, f32[256,256]{1,0:T(8,128)} %get-tuple-element.46.c11), custom_call_target="tpu_custom_call" | custom-call | flops 20000000000 | bytes 1000000 | tf_op jit(solution)/shard_map/second_factor/pallas_call | solution.py:141
  147.7 9.9 %panel_solve.1 = (f32[1024,512]{1,0:T(8,128)}, bf16[1024,512]{1,0:T(8,128)(2,1)}, bf16[1024,512]{1,0:T(8,128)(2,1)}, f32[8,512]{1,0:T(8,128)}) custom-call(s32[2]{0:T(128)} %pad_add_fusion.place, f32[1032,256]{1,0:T(8,128)} %copy-done, f32[1032,256]{1,0:T(8,128)} %collective-permute-done.12.theirs, f32[24,128]{1,0:T(8,128)} %add.54.sums, ...), custom_call_target="tpu_custom_call" | custom-call | flops 8000000000 | bytes 8000000 | tf_op jit(solution)/shard_map/panel_solve/pallas_call | solution.py:233
  157.6 20.8 %trailing_update.1 = (f32[1024,16,128]{2,1,0:T(8,128)}, f32[16,128]{1,0:T(8,128)}) custom-call(s32[2]{0:T(128)} %pad_add_fusion.place, f32[1024,16,128]{2,1,0:T(8,128)} %bitcast.14, f32[16,256,256]{2,1,0:T(8,128)} %bitcast.15, bf16[1024,512]{1,0:T(8,128)(2,1)} %get-tuple-element.35.high, bf16[1024,512]{1,0:T(8,128)(2,1)} %get-tuple-element.36.low, ...), custom_call_target="tpu_custom_call" | custom-call | tf_op jit(solution)/shard_map/trailing_update/pallas_call | solution.py:282
  (61 shorter events, 4.8 us)
Async XLA Ops:
  7.2 150.4 %all-gather.3.cloned.1.call-start = ((), (), s32[]{:S(2)}) async-start(), calls=%async_computation | async-start | bytes 4456448 | tf_op jit(solution)/shard_map/all_gather | solution.py:358
  7.2 27.3 %copy-start.3 = (f32[4,1,256]{2,1,0:T(1,128)S(1)}, f32[4,1,256]{2,1,0:T(1,128)}, u32[]{:S(2)}) copy-start(f32[4,1,256]{2,1,0:T(1,128)} %param.3) | copy-start | bytes 12292
  10.5 15.6 %collective-permute-start = (f32[256,256]{1,0:T(8,128)}, f32[256,256]{1,0:T(8,128)S(1)}, u32[]{:S(2)}, u32[]{:S(2)}) collective-permute-start(f32[256,256]{1,0:T(8,128)} %get-tuple-element.22), channel_id=1, source_target_pairs={{0,112},{8,120},{1,113},{9,121},{2,114},{10,122},{3,115},{11,123},... | collective-permute-start | bytes 786440 | tf_op jit(solution)/shard_map/ppermute | solution.py:357
  19.1 7.7 %collective-permute-start.1 = (f32[256,256]{1,0:T(8,128)}, f32[256,256]{1,0:T(8,128)S(1)}, u32[]{:S(2)}, u32[]{:S(2)}) collective-permute-start(f32[256,256]{1,0:T(8,128)} %get-tuple-element.23), channel_id=1, source_target_pairs={{0,96},{8,104},{1,97},{9,105},{2,98},{10,106},{3,99},{11,107},{4,1... | collective-permute-start | bytes 786440 | tf_op jit(solution)/shard_map/ppermute | solution.py:357
  20.4 11.3 %collective-permute-start.2 = (f32[256,256]{1,0:T(8,128)}, f32[256,256]{1,0:T(8,128)S(1)}, u32[]{:S(2)}, u32[]{:S(2)}) collective-permute-start(f32[256,256]{1,0:T(8,128)} %get-tuple-element.24), channel_id=1, source_target_pairs={{0,80},{8,88},{1,81},{9,89},{2,82},{10,90},{3,83},{11,91},{4,84},{... | collective-permute-start | bytes 786440 | tf_op jit(solution)/shard_map/ppermute | solution.py:357
  21.8 11.3 %collective-permute-start.3 = (f32[256,256]{1,0:T(8,128)}, f32[256,256]{1,0:T(8,128)S(1)}, u32[]{:S(2)}, u32[]{:S(2)}) collective-permute-start(f32[256,256]{1,0:T(8,128)} %get-tuple-element.25), channel_id=1, source_target_pairs={{0,64},{8,72},{1,65},{9,73},{2,66},{10,74},{3,67},{11,75},{4,68},{... | collective-permute-start | bytes 786440 | tf_op jit(solution)/shard_map/ppermute | solution.py:357
  23.1 18.8 %collective-permute-start.7 = (f32[256,256]{1,0:T(8,128)}, f32[256,256]{1,0:T(8,128)S(1)}, u32[]{:S(2)}, u32[]{:S(2)}) collective-permute-start(f32[256,256]{1,0:T(8,128)} %get-tuple-element.29), channel_id=1, source_target_pairs={{0,2}} | collective-permute-start | bytes 786440 | tf_op jit(solution)/shard_map/ppermute | solution.py:321
  26.1 15.7 %collective-permute-start.23 = (f32[256,256]{1,0:T(8,128)}, f32[256,256]{1,0:T(8,128)S(1)}, u32[]{:S(2)}, u32[]{:S(2)}) collective-permute-start(f32[256,256]{1,0:T(8,128)} %get-tuple-element.29), channel_id=1, source_target_pairs={{8,16},{9,17}} | collective-permute-start | bytes 786440 | tf_op jit(solution)/shard_map/ppermute | solution.py:321
  26.8 10.6 %collective-permute-start.4 = (f32[256,256]{1,0:T(8,128)}, f32[256,256]{1,0:T(8,128)S(1)}, u32[]{:S(2)}, u32[]{:S(2)}) collective-permute-start(f32[256,256]{1,0:T(8,128)} %get-tuple-element.26), channel_id=1, source_target_pairs={{0,48},{8,56},{1,49},{9,57},{2,50},{10,58},{3,51},{11,59},{4,52},{... | collective-permute-start | bytes 786440 | tf_op jit(solution)/shard_map/ppermute | solution.py:357
  31.7 5.6 %collective-permute-start.5 = (f32[256,256]{1,0:T(8,128)}, f32[256,256]{1,0:T(8,128)S(1)}, u32[]{:S(2)}, u32[]{:S(2)}) collective-permute-start(f32[256,256]{1,0:T(8,128)} %get-tuple-element.27), channel_id=1, source_target_pairs={{0,32},{8,40},{1,33},{9,41},{2,34},{10,42},{3,35},{11,43},{4,36},{... | collective-permute-start | bytes 786440 | tf_op jit(solution)/shard_map/ppermute | solution.py:357
  33.0 8.8 %collective-permute-start.6 = (f32[256,256]{1,0:T(8,128)}, f32[256,256]{1,0:T(8,128)S(1)}, u32[]{:S(2)}, u32[]{:S(2)}) collective-permute-start(f32[256,256]{1,0:T(8,128)} %get-tuple-element.28), channel_id=1, source_target_pairs={{0,16},{8,24},{1,17},{9,25},{2,18},{10,26},{3,19},{11,27},{4,20},{... | collective-permute-start | bytes 786440 | tf_op jit(solution)/shard_map/ppermute | solution.py:357
  51.6 13.3 %collective-permute-start.9 = (f32[1032,256]{1,0:T(8,128)}, f32[1032,256]{1,0:T(8,128)S(1)}, u32[]{:S(2)}, u32[]{:S(2)}) collective-permute-start(f32[1032,256]{1,0:T(8,128)} %get-tuple-element.31), channel_id=1, source_target_pairs={{0,6},{1,7},{8,14},{9,15},{16,22},{17,23},{24,30},{25,31},{32,38},... | collective-permute-start | bytes 3170312 | tf_op jit(solution)/shard_map/ppermute | solution.py:362
  52.3 28.3 %collective-permute-start.8 = (f32[1032,256]{1,0:T(8,128)}, f32[1032,256]{1,0:T(8,128)}, u32[]{:S(2)}, u32[]{:S(2)}) collective-permute-start(f32[1032,256]{1,0:T(8,128)} %get-tuple-element.31), channel_id=1, source_target_pairs={{0,2},{1,3},{8,10},{9,11},{16,18},{17,19},{24,26},{25,27},{32,34},... | collective-permute-start | bytes 3170312 | tf_op jit(solution)/shard_map/ppermute | solution.py:361
  53.6 4.6 %collective-permute-start.24 = (f32[256,256]{1,0:T(8,128)S(1)}, f32[256,256]{1,0:T(8,128)S(1)}, u32[]{:S(2)}, u32[]{:S(2)}) collective-permute-start(f32[256,256]{1,0:T(8,128)S(1)} %get-tuple-element.48), channel_id=1, source_target_pairs={{8,0},{9,1},{16,24},{17,25}} | collective-permute-start | bytes 786440 | tf_op jit(solution)/shard_map/ppermute | solution.py:324
  54.3 26.3 %copy-start.1 = (f32[1032,256]{1,0:T(8,128)S(1)}, f32[1032,256]{1,0:T(8,128)}, u32[]{:S(2)}) copy-start(f32[1032,256]{1,0:T(8,128)} %get-tuple-element.31) | copy-start | bytes 3170308
  54.3 7.8 %collective-permute-start.17 = (f32[256,256]{1,0:T(8,128)S(1)}, f32[256,256]{1,0:T(8,128)S(1)}, u32[]{:S(2)}, u32[]{:S(2)}) collective-permute-start(f32[256,256]{1,0:T(8,128)S(1)} %get-tuple-element.49), channel_id=1, source_target_pairs={{0,6},{2,4}} | collective-permute-start | bytes 786440 | tf_op jit(solution)/shard_map/ppermute | solution.py:324
  58.3 5.2 %collective-permute-start.25 = (f32[256,256]{1,0:T(8,128)S(1)}, f32[256,256]{1,0:T(8,128)S(1)}, u32[]{:S(2)}, u32[]{:S(2)}) collective-permute-start(f32[256,256]{1,0:T(8,128)S(1)} %broadcast_select_fusion.3), channel_id=1, source_target_pairs={{8,40},{16,48},{24,56},{0,32},{9,41},{17,49},{25,57},{1,33}} | collective-permute-start | bytes 786440 | tf_op jit(solution)/shard_map/ppermute | solution.py:321
  62.1 22.9 %collective-permute-start.18 = (f32[256,256]{1,0:T(8,128)S(1)}, f32[256,256]{1,0:T(8,128)S(1)}, u32[]{:S(2)}, u32[]{:S(2)}) collective-permute-start(f32[256,256]{1,0:T(8,128)S(1)} %broadcast_select_fusion.7), channel_id=1, source_target_pairs={{0,8},{2,10},{4,12},{6,14}} | collective-permute-start | bytes 786440 | tf_op jit(solution)/shard_map/ppermute | solution.py:321
  63.5 28.0 %collective-permute-start.26 = (f32[256,256]{1,0:T(8,128)S(1)}, f32[256,256]{1,0:T(8,128)}, u32[]{:S(2)}, u32[]{:S(2)}) collective-permute-start(f32[256,256]{1,0:T(8,128)S(1)} %broadcast_select_fusion.10), channel_id=1, source_target_pairs={{8,104},{16,112},{24,120},{0,96},{9,105},{17,113},{25,121},{1,97},... | collective-permute-start | bytes 786440 | tf_op jit(solution)/shard_map/ppermute | solution.py:324
  83.0 13.0 %collective-permute-start.10 = (f32[512,256]{1,0:T(8,128)}, f32[512,256]{1,0:T(8,128)}, u32[]{:S(2)}, u32[]{:S(2)}) collective-permute-start(f32[512,256]{1,0:T(8,128)} %slice.20), channel_id=1, source_target_pairs={{2,4},{3,5},{10,12},{11,13},{18,20},{19,21},{26,28},{27,29},{34,36... | collective-permute-start | bytes 1572872 | tf_op jit(solution)/shard_map/ppermute | solution.py:364
  85.1 9.5 %collective-permute-start.19 = (f32[256,256]{1,0:T(8,128)S(1)}, f32[256,256]{1,0:T(8,128)S(1)}, u32[]{:S(2)}, u32[]{:S(2)}) collective-permute-start(f32[256,256]{1,0:T(8,128)S(1)} %broadcast_select_fusion.8), channel_id=1, source_target_pairs={{0,24},{2,26},{4,28},{6,30},{8,16},{10,18},{12,20},{14,22}} | collective-permute-start | bytes 786440 | tf_op jit(solution)/shard_map/ppermute | solution.py:324
  90.8 5.2 %collective-permute-start.11 = (f32[520,256]{1,0:T(8,128)S(1)}, f32[520,256]{1,0:T(8,128)S(1)}, u32[]{:S(2)}, u32[]{:S(2)}) collective-permute-start(f32[520,256]{1,0:T(8,128)S(1)} %slice.21), channel_id=1, source_target_pairs={{6,4},{7,5},{14,12},{15,13},{22,20},{23,21},{30,28},{31,29},{38,36... | collective-permute-start | bytes 1597448 | tf_op jit(solution)/shard_map/ppermute | solution.py:365
  91.6 8.3 %collective-permute-start.27 = (f32[256,256]{1,0:T(8,128)S(1)}, f32[256,256]{1,0:T(8,128)S(1)}, u32[]{:S(2)}, u32[]{:S(2)}) collective-permute-start(f32[256,256]{1,0:T(8,128)S(1)} %broadcast_select_fusion.12), channel_id=1, source_target_pairs={{8,10},{40,42},{72,74},{104,106},{16,18},{48,50},{80,82},{112,114}... | collective-permute-start | bytes 786440 | tf_op jit(solution)/shard_map/ppermute | solution.py:321
  94.6 7.7 %collective-permute-start.20 = (f32[256,256]{1,0:T(8,128)S(1)}, f32[256,256]{1,0:T(8,128)S(1)}, u32[]{:S(2)}, u32[]{:S(2)}) collective-permute-start(f32[256,256]{1,0:T(8,128)S(1)} %broadcast_select_fusion.9), channel_id=1, source_target_pairs={{0,32},{8,40},{16,48},{24,56},{2,34},{10,42},{18,50},{26,58},{4,36... | collective-permute-start | bytes 786440 | tf_op jit(solution)/shard_map/ppermute | solution.py:321
  96.2 12.2 %copy-start = (f32[1032,256]{1,0:T(8,128)}, f32[1032,256]{1,0:T(8,128)S(1)}, u32[]{:S(2)}) copy-start(f32[1032,256]{1,0:T(8,128)S(1)} %pad_maximum_fusion.mine) | copy-start | bytes 3170308
  96.2 14.8 %collective-permute-start.12 = (f32[1032,256]{1,0:T(8,128)S(1)}, f32[1032,256]{1,0:T(8,128)}, u32[]{:S(2)}, u32[]{:S(2)}) collective-permute-start(f32[1032,256]{1,0:T(8,128)S(1)} %pad_maximum_fusion.mine), channel_id=1, source_target_pairs={{0,1},{1,0},{2,3},{3,2},{4,5},{5,4},{6,7},{7,6},{8,9},{9,8},{10,11... | collective-permute-start | bytes 3170312 | tf_op jit(solution)/shard_map/ppermute | solution.py:367
  99.9 11.8 %copy-start.2 = (f32[16,128]{1,0:T(8,128)S(1)}, f32[16,128]{1,0:T(8,128)}, u32[]{:S(2)}) copy-start(f32[16,128]{1,0:T(8,128)} %get-tuple-element.32) | copy-start | bytes 24580
  99.9 8.5 %collective-permute-start.28 = (f32[256,256]{1,0:T(8,128)S(1)}, f32[256,256]{1,0:T(8,128)S(1)}, u32[]{:S(2)}, u32[]{:S(2)}) collective-permute-start(f32[256,256]{1,0:T(8,128)S(1)} %broadcast_select_fusion.15), channel_id=1, source_target_pairs={{8,14},{40,46},{72,78},{104,110},{16,22},{48,54},{80,86},{112,118}... | collective-permute-start | bytes 786440 | tf_op jit(solution)/shard_map/ppermute | solution.py:324
  102.4 6.5 %collective-permute-start.21 = (f32[256,256]{1,0:T(8,128)S(1)}, f32[256,256]{1,0:T(8,128)S(1)}, u32[]{:S(2)}, u32[]{:S(2)}) collective-permute-start(f32[256,256]{1,0:T(8,128)S(1)} %broadcast_select_fusion.11), channel_id=1, source_target_pairs={{0,96},{8,104},{16,112},{24,120},{2,98},{10,106},{18,114},{26,122}... | collective-permute-start | bytes 786440 | tf_op jit(solution)/shard_map/ppermute | solution.py:324
  108.4 21.8 %collective-permute-start.29 = (f32[256,256]{1,0:T(8,128)S(1)}, f32[256,256]{1,0:T(8,128)S(1)}, u32[]{:S(2)}, u32[]{:S(2)}) collective-permute-start(f32[256,256]{1,0:T(8,128)S(1)} %broadcast_select_fusion.6), channel_id=1, source_target_pairs={{0,1},{1,0},{2,3},{3,2},{4,5},{5,4},{6,7},{7,6},{8,9},{9,8},{10,11... | collective-permute-start | bytes 786440 | tf_op jit(solution)/shard_map/ppermute | solution.py:351
  108.9 7.2 %collective-permute-start.22 = (f32[256,256]{1,0:T(8,128)S(1)}, f32[256,256]{1,0:T(8,128)S(1)}, u32[]{:S(2)}, u32[]{:S(2)}) collective-permute-start(f32[256,256]{1,0:T(8,128)S(1)} %broadcast_select_fusion.13), channel_id=1, source_target_pairs={{0,1},{2,3},{4,5},{6,7},{8,9},{10,11},{12,13},{14,15},{16,17},{18,... | collective-permute-start | bytes 786440 | tf_op jit(solution)/shard_map/ppermute | solution.py:348
  111.8 6.1 %collective-permute-start.13 = (f32[24,128]{1,0:T(8,128)S(1)}, f32[24,128]{1,0:T(8,128)S(1)}, u32[]{:S(2)}, u32[]{:S(2)}) collective-permute-start(f32[24,128]{1,0:T(8,128)S(1)} %maximum_maximum_fusion), channel_id=1, source_target_pairs={{0,8},{8,0},{16,24},{24,16},{32,40},{40,32},{48,56},{56,48},{64,72... | collective-permute-start | bytes 36872 | tf_op jit(solution)/shard_map/ppermute | solution.py:372
  117.9 12.3 %collective-permute-start.14 = (f32[24,128]{1,0:T(8,128)S(1)}, f32[24,128]{1,0:T(8,128)S(1)}, u32[]{:S(2)}, u32[]{:S(2)}) collective-permute-start(f32[24,128]{1,0:T(8,128)S(1)} %fusion), channel_id=1, source_target_pairs={{0,24},{8,16},{16,8},{24,0},{32,56},{40,48},{48,40},{56,32},{64,88... | collective-permute-start | bytes 36872 | tf_op jit(solution)/shard_map/ppermute | solution.py:372
  130.2 3.9 %collective-permute-start.15 = (f32[24,128]{1,0:T(8,128)S(1)}, f32[24,128]{1,0:T(8,128)S(1)}, u32[]{:S(2)}, u32[]{:S(2)}) collective-permute-start(f32[24,128]{1,0:T(8,128)S(1)} %add.52), channel_id=1, source_target_pairs={{0,32},{8,40},{16,48},{24,56},{32,0},{40,8},{48,16},{56,24},{64,96... | collective-permute-start | bytes 36872 | tf_op jit(solution)/shard_map/ppermute | solution.py:372
  134.2 12.9 %collective-permute-start.16 = (f32[24,128]{1,0:T(8,128)S(1)}, f32[24,128]{1,0:T(8,128)S(1)}, u32[]{:S(2)}, u32[]{:S(2)}) collective-permute-start(f32[24,128]{1,0:T(8,128)S(1)} %add.53), channel_id=1, source_target_pairs={{0,96},{8,104},{16,112},{24,120},{32,64},{40,72},{48,80},{56,88},{... | collective-permute-start | bytes 36872 | tf_op jit(solution)/shard_map/ppermute | solution.py:372
Sparse Core Ops, SparseCore 0:
  90.9 50.0 all-gather.2

commit v3 on v2

--- a/solution.py
+++ b/solution.py
@@ -133,7 +133,7 @@
 def first_factor(c00):
     return pl.pallas_call(
         first_kernel, out_shape=TILE, in_specs=[VMEM], out_specs=VMEM, scratch_shapes=WORK, name="first_factor",
-        cost_estimate=pl.CostEstimate(flops=20_000_000_000, bytes_accessed=1_000_000, transcendentals=0),
+        cost_estimate=pl.CostEstimate(flops=100_000_000, bytes_accessed=100_000, transcendentals=0),
     )(c00)
 
 
@@ -141,63 +141,89 @@
     return pl.pallas_call(
         second_kernel, out_shape=(TILE, TILE), in_specs=[VMEM] * 3, out_specs=(VMEM, VMEM),
         scratch_shapes=[pltpu.VMEM((NB, NB), F32)] + WORK, name="second_factor",
-        cost_estimate=pl.CostEstimate(flops=20_000_000_000, bytes_accessed=1_000_000, transcendentals=0),
+        cost_estimate=pl.CostEstimate(flops=100_000_000, bytes_accessed=100_000, transcendentals=0),
     )(w00, c10, c11)
 
 
 def corner_kernel(a, *pieces):
     for q in range(16):
-        pieces[q // 2][:, 128 * (q % 2) : 128 * (q % 2) + 128] = a[:, q, :]
+        value = a[:, q, :]
+        for ref in pieces[q // 2 :: 8]:
+            ref[:, 128 * (q % 2) : 128 * (q % 2) + 128] = value
 
 
 def corner_call(flat):
     return pl.pallas_call(
-        corner_kernel, grid=(2,), out_shape=(TILE,) * 8,
+        corner_kernel, grid=(2,), out_shape=(TILE,) * 9,
         in_specs=[pl.BlockSpec((128, 16, 128), lambda i: (i, 0, 0))],
-        out_specs=(pl.BlockSpec((128, NB), lambda i: (i, 0)),) * 8,
+        out_specs=(pl.BlockSpec((128, NB), lambda i: (i, 0)),) * 9,
         name="corner_tiles",
     )(flat)
 
 
-def column_kernel(weights, a, column, sums):
+def column_kernel(a, column, again):
+    for q in range(2):
+        value = a[:, q, :]
+        column[:, 128 * q : 128 * q + 128] = value
+
+        @pl.when(pl.program_id(0) == 0)
+        def _():
+            again[:, 128 * q : 128 * q + 128] = value[0:NB]
+
+
+def column_call(flat):
+    return pl.pallas_call(
+        column_kernel, grid=(4,), out_shape=(jax.ShapeDtypeStruct((1024, NB), F32), TILE),
+        in_specs=[pl.BlockSpec((256, 8, 128), lambda i: (i, 0, 0))],
+        out_specs=(pl.BlockSpec((256, NB), lambda i: (i, 0)), pl.BlockSpec((NB, NB), lambda i: (0, 0))),
+        name="first_column",
+    )(flat)
+
+
+def sums_kernel(weights, a, sums):
     step = pl.program_id(0)
-
-    @pl.when(step < 8)
-    def _():
-        for q in range(2):
-            column[:, 128 * q : 128 * q + 128] = a[:, q, :]
 
     @pl.when(step == 0)
     def _():
         sums[...] = jnp.zeros_like(sums)
 
-    @pl.when(step < 8)
-    def _():
-        def body(i, total):
-            for j in range(8):
-                row = 8 * i + j
-                total = total + weights[step * 128 + row] * a[row]
-            return total
-
-        sums[...] += lax.fori_loop(0, 16, body, jnp.zeros((16, 128), F32))
-
-    @pl.when(step == 8)
-    def _():
-        for q in range(2):
-            column[0:8, 128 * q : 128 * q + 128] = jnp.broadcast_to(sums[q : q + 1, :], (8, 128))
-
-
-def column_call(weights, flat):
-    return pl.pallas_call(
-        column_kernel, grid=(9,),
-        out_shape=(jax.ShapeDtypeStruct((1032, NB), F32), jax.ShapeDtypeStruct((16, 128), F32)),
-        in_specs=[SMEM, pl.BlockSpec((128, 16, 128), lambda i: (jnp.minimum(i, 7), 0, 0))],
-        out_specs=(pl.BlockSpec((128, NB), lambda i: (i, 0)), pl.BlockSpec((16, 128), lambda i: (0, 0))),
-        name="first_column",
+    def body(i, total):
+        for j in range(8):
+            row = 8 * i + j
+            total = total + weights[step * 128 + row] * a[row]
+        return total
+
+    sums[...] += lax.fori_loop(0, 16, body, jnp.zeros((16, 128), F32))
+
+
+def sums_call(weights, flat):
+    return pl.pallas_call(
+        sums_kernel, grid=(8,), out_shape=jax.ShapeDtypeStruct((16, 128), F32),
+        in_specs=[SMEM, pl.BlockSpec((128, 16, 128), lambda i: (i, 0, 0))],
+        out_specs=pl.BlockSpec((16, 128), lambda i: (0, 0)),
+        name="column_sums",
+        cost_estimate=pl.CostEstimate(flops=100_000_000, bytes_accessed=100_000, transcendentals=0),
     )(weights, flat)
 
 
-def panel_kernel(place, mine, theirs, sums, w00, l10, w11, panels, high, low, taken, factors):
+def taken_kernel(sums, w00, l10, w11, taken):
+    v0 = jnp.broadcast_to(jnp.concatenate([sums[16:17], sums[17:18]], axis=1), (8, NB))
+    v1 = jnp.broadcast_to(jnp.concatenate([sums[18:19], sums[19:20]], axis=1), (8, NB))
+    y0 = dot6(v0, w00[...], NT)
+    y1 = dot6(v1 - dot6(y0, l10[...], NT), w11[...], NT)
+    z1 = dot6(y1, w11[...], NN)
+    taken[:, 256:512] = z1
+    taken[:, 0:256] = dot6(y0 - dot6(z1, l10[...], NN), w00[...], NN)
+
+
+def taken_call(sums, w00, l10, w11):
+    return pl.pallas_call(
+        taken_kernel, out_shape=jax.ShapeDtypeStruct((8, 512), F32), in_specs=[VMEM] * 4, out_specs=VMEM, name="taken_sums",
+        cost_estimate=pl.CostEstimate(flops=100_000_000, bytes_accessed=100_000, transcendentals=0),
+    )(sums, w00, l10, w11)
+
+
+def panel_kernel(place, mine, theirs, w00, l10, w11, panels, high, low, factors):
     step = pl.program_id(0)
     even = place[1] % 2 == 0
 
@@ -205,13 +231,6 @@
     def _():
         for k, ref in enumerate((w00, l10, w11)):
             factors[0, k], factors[1, k] = halves(ref[...])
-        v0 = jnp.broadcast_to(jnp.concatenate([sums[16:17], sums[17:18]], axis=1), (8, NB))
-        v1 = jnp.broadcast_to(jnp.concatenate([sums[18:19], sums[19:20]], axis=1), (8, NB))
-        y0 = dot6(v0, w00[...], NT)
-        y1 = dot6(v1 - dot6(y0, l10[...], NT), w11[...], NT)
-        z1 = dot6(y1, w11[...], NN)
-        taken[:, 256:512] = z1
-        taken[:, 0:256] = dot6(y0 - dot6(z1, l10[...], NN), w00[...], NN)
 
     f00, f10, f11 = [(factors[0, k], factors[1, k]) for k in range(3)]
     own, other = mine[...], theirs[...]
@@ -227,7 +246,7 @@
     high[:, 0:256], low[:, 0:256] = halves(dot3(halves(left - dot3(last_halves, f10, NN)), f00, NN))
 
 
-def panel_call(place, mine, theirs, sums, w00, l10, w11):
+def panel_call(place, mine, theirs, w00, l10, w11):
     full = lambda *shape: pl.BlockSpec(shape, lambda i: (0,) * len(shape))
     part = lambda n: pl.BlockSpec((512, n), lambda i: (i, 0))
     return pl.pallas_call(
@@ -236,14 +255,13 @@
             jax.ShapeDtypeStruct((1024, 512), F32),
             jax.ShapeDtypeStruct((1024, 512), BF16),
             jax.ShapeDtypeStruct((1024, 512), BF16),
-            jax.ShapeDtypeStruct((8, 512), F32),
         ),
-        in_specs=[SMEM, part(NB), part(NB), full(24, 128), full(NB, NB), full(NB, NB), full(NB, NB)],
-        out_specs=(part(512), part(512), part(512), full(8, 512)),
+        in_specs=[SMEM, part(NB), part(NB), full(NB, NB), full(NB, NB), full(NB, NB)],
+        out_specs=(part(512), part(512), part(512)),
         scratch_shapes=[pltpu.VMEM((2, 3, NB, NB), BF16)],
         name="panel_solve",
-        cost_estimate=pl.CostEstimate(flops=8_000_000_000, bytes_accessed=8_000_000, transcendentals=0),
-    )(place, mine, theirs, sums, w00, l10, w11)
+        cost_estimate=pl.CostEstimate(flops=100_000_000, bytes_accessed=100_000, transcendentals=0),
+    )(place, mine, theirs, w00, l10, w11)
 
 
 def update_kernel(place, flat, across, high, low, sums, taken, out, checksum, right_high, right_low):
@@ -277,7 +295,7 @@
 
 
 def update_call(place, flat, across, high, low, sums, taken):
-    rows = 256
+    rows = 512
     full = lambda *shape: pl.BlockSpec(shape, lambda g, i: (0,) * len(shape))
     return pl.pallas_call(
         update_kernel, grid=(2, 1024 // rows),
@@ -344,36 +362,44 @@
     swap_cores = [(c, c ^ 1) for c in range(8)]
 
     pieces = corner_call(flat)
+    column, corner = column_call(after(flat, pieces[7]))
     tree0 = spread(pieces[0], [device_at(0, 0, 0, 0)], (2, 1, 0), (0, 0, 0), here)
     c00 = jnp.where(core == 1, lax.ppermute(tree0[-1], "col", [(c, c + 1) for c in (0, 2, 4, 6)]), tree0[-1])
-    tree1 = spread(pieces[0], [device_at(0, 1, 0, 0), device_at(0, 1, 0, 1)], (1, 0, 2), (0, 1, 0), here)
+    tree1 = spread(pieces[8], [device_at(0, 1, 0, 0), device_at(0, 1, 0, 1)], (1, 0, 2), (0, 1, 0), here)
     below = tree1[-1]
     other = lax.ppermute(below, "col", swap_cores)
     c10 = jnp.where(core == 0, below, other)
     c11 = jnp.where(core == 0, other, below)
 
-    piece = pieces[0]
+    piece = corner
     for j in range(1, 8):
         piece = jnp.where(row // 2 == j, lax.ppermute(pieces[j], "row", [(0, 2 * j), (1, 2 * j + 1)]), piece)
-    across = lax.all_gather(piece, "row", axis=0)
-
-    column, sums = column_call(weights, after(flat, tree0[0]))
+    sums = sums_call(weights, after(flat, (tree0[0], column)))
+    across = lax.all_gather(after(piece, (tree0[2], tree1[0], sums)), "row", axis=0)
+
+    w00 = first_factor(c00)
+    l10, w11 = second_factor(w00, c10, c11)
     from_left = lax.ppermute(column, "col", [(0, 2), (1, 3)])
     from_right = lax.ppermute(column, "col", [(0, 6), (1, 7)])
+    from_left, from_right = after((from_left, from_right), (tree0[4], tree1[3]))
     mine = jnp.where(x == 1, from_left, jnp.where(x == 3, from_right, column))
-    upper = jnp.where(x == 2, lax.ppermute(mine[0:512], "col", [(2, 4), (3, 5)]), mine[0:512])
-    lower = jnp.where(x == 2, lax.ppermute(mine[512:1032], "col", [(6, 4), (7, 5)]), mine[512:1032])
+    upper = lax.ppermute(mine[0:512], "col", [(2, 4), (3, 5)])
+    lower = lax.ppermute(mine[512:1024], "col", [(6, 4), (7, 5)])
+    upper, lower = after((upper, lower), (w00, tree1[-1]))
+    upper = jnp.where(x == 2, upper, mine[0:512])
+    lower = jnp.where(x == 2, lower, mine[512:1024])
     mine = jnp.concatenate([upper, lower], axis=0)
-    theirs = lax.ppermute(mine, "col", swap_cores)
-    first_sums = jnp.where(core == 0, mine[1024:1025], theirs[1024:1025])
-    second_sums = jnp.where(core == 0, theirs[1024:1025], mine[1024:1025])
+    theirs = after(lax.ppermute(mine, "col", swap_cores), w11)
+    own_sums = jnp.dot(weights[None], mine, precision=HIGHEST)
+    other_sums = jnp.dot(weights[None], theirs, precision=HIGHEST)
+    first_sums = jnp.where(core == 0, own_sums, other_sums)
+    second_sums = jnp.where(core == 0, other_sums, own_sums)
     total = jnp.concatenate([sums, first_sums.reshape(2, 128), second_sums.reshape(2, 128), jnp.zeros((4, 128), F32)], axis=0)
     for d in (1, 3, 4, 12):
         total = total + lax.ppermute(total, "row", [(r, r ^ d) for r in range(16)])
 
-    w00 = first_factor(c00)
-    l10, w11 = second_factor(w00, c10, c11)
-    panels, high, low, taken = panel_call(place, mine, theirs, total, w00, l10, w11)
+    panels, high, low = panel_call(place, mine, theirs, w00, l10, w11)
+    taken = taken_call(total, w00, l10, w11)
     trailing, checksum = update_call(place, flat, across, high, low, total, taken)
     return (
         trailing.reshape(4, 1, NB, 8, 1, NB),

time: 186 us -> 183 us (0.984)
  the two profiles are of different devices: /device:TPU:2 before, /device:TPU:4 now
where the time goes in v3:
time: 183 us; the launch traced here: 182 us
  Pallas kernels  67.3 us (37%)
  waiting for transfers between devices  48.9 us (27%)
  starting transfers between devices  39.3 us (21%)
  between operations  14.6 us (8%)
  other arithmetic  10.8 us (6%)
    ppermute x12, waiting for transfers between devices, spread(): lax.ppermute(value, ('row', 'col'), pairs)  32.2 us
    pallas_call x1, Pallas kernels, update_call(): pl.pallas_call(update_kernel, grid=(2, 1024 // rows), out_shape=(jax.Shap...  20.9 us
    ppermute x7, starting transfers between devices, shards(): lax.ppermute(pieces[j], 'row', [(0, 2 * j), (1, 2 * j + 1)])  17.8 us
    ppermute x12, starting transfers between devices, spread(): lax.ppermute(value, ('row', 'col'), pairs)  13.1 us
    ppermute x4, waiting for transfers between devices, shards(): total = total + lax.ppermute(total, 'row', [(r, r ^ d) for r in range(16)])  10.8 us
    pallas_call x1, Pallas kernels, second_factor(): pl.pallas_call(second_kernel, out_shape=(TILE, TILE), in_specs=[VMEM] * 3...  10.6 us
    pallas_call x1, Pallas kernels, first_factor(): pl.pallas_call(first_kernel, out_shape=TILE, in_specs=[VMEM], out_specs=V...  9.37 us
    pallas_call x1, Pallas kernels, panel_call(): pl.pallas_call(panel_kernel, grid=(2,), out_shape=(jax.ShapeDtypeStruct((...  7.71 us
  transfers between devices with their start and end apart: 31, of which 10 were waited for; matrix products, arithmetic and copies ran while one was open for 7% of the time, Pallas kernels for 24%

profile of v3, /device:TPU:4, one launch (start us, length us, event | category | flops | bytes accessed | tf_op | source)
XLA Modules:
  0.0 182.3 jit_solution(6414217818849041335)
XLA Ops:
  7.2 3.4 %corner_tiles.1 = (f32[256,256]{1,0:T(8,128)}, f32[256,256]{1,0:T(8,128)}, f32[256,256]{1,0:T(8,128)}, f32[256,256]{1,0:T(8,128)}, f32[256,256]{1,0:T(8,128)}, /...) custom-call(f32[1024,16,128]{2,1,0:T(8,128)} %bitcast.21), custom_call_target="tpu_custom_call" | custom-call | tf_op jit(solution)/shard_map/corner_tiles/pallas_call | solution.py:156
  10.6 0.8 collective-permute-start.7
  11.4 6.0 %collective-permute-start.1 = (f32[256,256]{1,0:T(8,128)}, f32[256,256]{1,0:T(8,128)S(1)}, u32[]{:S(2)}, u32[]{:S(2)}) collective-permute-start(f32[256,256]{1,0:T(8,128)} %get-tuple-element.30), channel_id=1, source_target_pairs={{0,96},{8,104},{1,97},{9,105},{2,98},{10,106},{3,99},{11,107},{4,1... | collective-permute-start | bytes 786440 | tf_op jit(solution)/shard_map/ppermute | solution.py:376
  17.4 3.1 %collective-permute-start.2 = (f32[256,256]{1,0:T(8,128)}, f32[256,256]{1,0:T(8,128)S(1)}, u32[]{:S(2)}, u32[]{:S(2)}) collective-permute-start(f32[256,256]{1,0:T(8,128)} %get-tuple-element.31), channel_id=1, source_target_pairs={{0,80},{8,88},{1,81},{9,89},{2,82},{10,90},{3,83},{11,91},{4,84},{... | collective-permute-start | bytes 786440 | tf_op jit(solution)/shard_map/ppermute | solution.py:376
  20.6 1.0 broadcast_select_fusion.13
  21.6 1.3 collective-permute-start.8
  22.9 1.3 collective-permute-start.3
  24.2 1.3 collective-permute-start.4
  25.6 2.0 %collective-permute-start.5 = (f32[256,256]{1,0:T(8,128)}, f32[256,256]{1,0:T(8,128)}, u32[]{:S(2)}, u32[]{:S(2)}) collective-permute-start(f32[256,256]{1,0:T(8,128)} %get-tuple-element.34), channel_id=1, source_target_pairs={{0,32},{8,40},{1,33},{9,41},{2,34},{10,42},{3,35},{11,43},{4,36},{... | collective-permute-start | bytes 786440 | tf_op jit(solution)/shard_map/ppermute | solution.py:376
  27.7 2.0 %collective-permute-start.6 = (f32[256,256]{1,0:T(8,128)}, f32[256,256]{1,0:T(8,128)}, u32[]{:S(2)}, u32[]{:S(2)}) collective-permute-start(f32[256,256]{1,0:T(8,128)} %get-tuple-element.35), channel_id=1, source_target_pairs={{0,16},{8,24},{1,17},{9,25},{2,18},{10,26},{3,19},{11,27},{4,20},{... | collective-permute-start | bytes 786440 | tf_op jit(solution)/shard_map/ppermute | solution.py:376
  29.9 2.0 %collective-permute-start = (f32[256,256]{1,0:T(8,128)}, f32[256,256]{1,0:T(8,128)}, u32[]{:S(2)}, u32[]{:S(2)}) collective-permute-start(f32[256,256]{1,0:T(8,128)} %get-tuple-element.29), channel_id=1, source_target_pairs={{0,112},{8,120},{1,113},{9,121},{2,114},{10,122},{3,115},{11,123},... | collective-permute-start | bytes 786440 | tf_op jit(solution)/shard_map/ppermute | solution.py:376
  32.4 4.3 %first_column.1 = (f32[1024,256]{1,0:T(8,128)}, f32[256,256]{1,0:T(8,128)}) custom-call(f32[1024,16,128]{2,1,0:T(8,128)} %bitcast.22), custom_call_target="tpu_custom_call" | custom-call | tf_op jit(solution)/shard_map/first_column/pallas_call | solution.py:175
  36.9 0.8 collective-permute-start.10
  37.7 2.3 %collective-permute-start.9 = (f32[256,256]{1,0:T(8,128)S(1)}, f32[256,256]{1,0:T(8,128)S(1)}, u32[]{:S(2)}, u32[]{:S(2)}) collective-permute-start(f32[256,256]{1,0:T(8,128)S(1)} %broadcast_select_fusion.15), channel_id=1, source_target_pairs={{0,8},{2,10},{4,12},{6,14}} | collective-permute-start | bytes 786440 | tf_op jit(solution)/shard_map/ppermute | solution.py:339
  40.0 3.2 %collective-permute-done = f32[256,256]{1,0:T(8,128)} collective-permute-done((f32[256,256]{1,0:T(8,128)}, f32[256,256]{1,0:T(8,128)}, u32[]{:S(2)}, u32[]{:S(2)}) %collective-permute-start) | collective-permute-done | bytes 262176 | tf_op jit(solution)/shard_map/ppermute | solution.py:376
  43.2 1.8 select_select_fusion.1
  45.1 7.1 %column_sums.1 = f32[16,128]{1,0:T(8,128)} custom-call(f32[1024]{0:T(1024)} %broadcast_select_fusion.17.weights, f32[1024,16,128]{2,1,0:T(8,128)} %bitcast.23), custom_call_target="tpu_custom_call" | custom-call | flops 100000000 | bytes 100000 | tf_op jit(solution)/shard_map/column_sums/pallas_call | solution.py:200
  52.3 0.7 collective-permute-start.15
  53.1 0.7 collective-permute-start.16
  53.8 0.7 collective-permute-start.12
  54.5 1.7 collective-permute-start.11
  56.2 1.3 collective-permute-start.13
  57.5 0.7 collective-permute-start.17
  58.2 3.1 %collective-permute-done.13 = f32[256,256]{1,0:T(8,128)S(1)} collective-permute-done((f32[256,256]{1,0:T(8,128)S(1)}, f32[256,256]{1,0:T(8,128)S(1)}, u32[]{:S(2)}, u32[]{:S(2)}) %collective-permute-start.13) | collective-permute-done | bytes 262176 | tf_op jit(solution)/shard_map/ppermute | solution.py:342
  61.4 1.3 collective-permute-start.14
  62.7 0.7 collective-permute-start.22
  63.4 4.5 %collective-permute-done.14 = f32[256,256]{1,0:T(8,128)S(1)} collective-permute-done((f32[256,256]{1,0:T(8,128)S(1)}, f32[256,256]{1,0:T(8,128)S(1)}, u32[]{:S(2)}, u32[]{:S(2)}) %collective-permute-start.14) | collective-permute-done | bytes 262176 | tf_op jit(solution)/shard_map/ppermute | solution.py:339
  68.0 1.3 collective-permute-start.20
  69.4 1.3 collective-permute-start.23
  71.0 1.3 collective-permute-start.19
  72.3 1.3 collective-permute-start.18
  73.6 0.9 collective-permute-done.20
  74.5 1.3 collective-permute-start.21
  75.8 23.5 %collective-permute-done.23 = f32[256,256]{1,0:T(8,128)} collective-permute-done((f32[256,256]{1,0:T(8,128)S(1)}, f32[256,256]{1,0:T(8,128)}, u32[]{:S(2)}, u32[]{:S(2)}) %collective-permute-start.23) | collective-permute-done | bytes 262176 | tf_op jit(solution)/shard_map/ppermute | solution.py:342
  99.3 1.7 broadcast_select_fusion.14
  101.0 0.7 broadcast_select_fusion.4.c00
  101.7 9.4 %first_factor.1.w00 = f32[256,256]{1,0:T(8,128)} custom-call(f32[256,256]{1,0:T(8,128)} %broadcast_select_fusion.4.c00), custom_call_target="tpu_custom_call" | custom-call | flops 100000000 | bytes 100000 | tf_op jit(solution)/shard_map/first_factor/pallas_call | solution.py:134
  111.1 1.2 broadcast_select_fusion.1
  113.0 2.7 %collective-permute-done.25 = f32[256,256]{1,0:T(8,128)S(1)} collective-permute-done((f32[256,256]{1,0:T(8,128)}, f32[256,256]{1,0:T(8,128)S(1)}, u32[]{:S(2)}, u32[]{:S(2)}) %collective-permute-start.25) | collective-permute-done | bytes 262176 | tf_op jit(solution)/shard_map/ppermute | solution.py:370
  115.7 1.8 broadcast_select_fusion.2
  117.5 10.6 %second_factor.1 = (f32[256,256]{1,0:T(8,128)}, f32[256,256]{1,0:T(8,128)}) custom-call(f32[256,256]{1,0:T(8,128)} %first_factor.1.w00, f32[256,256]{1,0:T(8,128)} %get-tuple-element.63.c10, f32[256,256]{1,0:T(8,128)} %get-tuple-element.62.c11), custom_call_target="tpu_custom_call" | custom-call | flops 100000000 | bytes 100000 | tf_op jit(solution)/shard_map/second_factor/pallas_call | solution.py:141
  129.3 3.7 %collective-permute-done.26 = f32[24,128]{1,0:T(8,128)S(1)} collective-permute-done((f32[24,128]{1,0:T(8,128)S(1)}, f32[24,128]{1,0:T(8,128)S(1)}, u32[]{:S(2)}, u32[]{:S(2)}) %collective-permute-start.26) | collective-permute-done | bytes 12320 | tf_op jit(solution)/shard_map/ppermute | solution.py:399
  133.0 1.5 collective-permute-start.27
  134.6 3.4 %collective-permute-done.27 = f32[24,128]{1,0:T(8,128)S(1)} collective-permute-done((f32[24,128]{1,0:T(8,128)S(1)}, f32[24,128]{1,0:T(8,128)S(1)}, u32[]{:S(2)}, u32[]{:S(2)}) %collective-permute-start.27) | collective-permute-done | bytes 12320 | tf_op jit(solution)/shard_map/ppermute | solution.py:399
  138.0 3.7 %collective-permute-done.28 = f32[24,128]{1,0:T(8,128)S(1)} collective-permute-done((f32[24,128]{1,0:T(8,128)S(1)}, f32[24,128]{1,0:T(8,128)S(1)}, u32[]{:S(2)}, u32[]{:S(2)}) %collective-permute-start.28) | collective-permute-done | bytes 12320 | tf_op jit(solution)/shard_map/ppermute | solution.py:399
  142.3 7.7 %panel_solve.1 = (f32[1024,512]{1,0:T(8,128)}, bf16[1024,512]{1,0:T(8,128)(2,1)}, bf16[1024,512]{1,0:T(8,128)(2,1)}) custom-call(s32[2]{0:T(128)} %pad_add_fusion.place, f32[1024,256]{1,0:T(8,128)} %copy-done, f32[1024,256]{1,0:T(8,128)} %copy-done.1, f32[256,256]{1,0:T(8,128)} %first_factor.1.w00, f32[256,256]{1,0:T(8,128)} %get-tuple-element.49.l10, ...), custom_call_target="tpu_custom_call" | custom-call | flops 100000000 | bytes 100000 | tf_op jit(solution)/shard_map/panel_solve/pallas_call | solution.py:252
  150.6 3.9 %taken_sums.1.taken = f32[8,512]{1,0:T(8,128)} custom-call(f32[24,128]{1,0:T(8,128)} %add.58.sums, f32[256,256]{1,0:T(8,128)} %first_factor.1.w00, f32[256,256]{1,0:T(8,128)} %get-tuple-element.49.l10, f32[256,256]{1,0:T(8,128)} %get-tuple-element.47.w11), custom_call_target="tpu_custom_call" | custom-call | flops 100000000 | bytes 100000 | tf_op jit(solution)/shard_map/taken_sums/pallas_call | solution.py:220
  154.5 20.9 %trailing_update.1 = (f32[1024,16,128]{2,1,0:T(8,128)}, f32[16,128]{1,0:T(8,128)}) custom-call(s32[2]{0:T(128)} %pad_add_fusion.place, f32[1024,16,128]{2,1,0:T(8,128)} %bitcast.24, f32[16,256,256]{2,1,0:T(8,128)} %bitcast.25, bf16[1024,512]{1,0:T(8,128)(2,1)} %get-tuple-element.50.high, bf16[1024,512]{1,0:T(8,128)(2,1)} %get-tuple-element.51.low, ...), custom_call_target="tpu_custom_call" | custom-call | tf_op jit(solution)/shard_map/trailing_update/pallas_call | solution.py:300
  (71 shorter events, 4.8 us)
Async XLA Ops:
  7.2 24.7 %copy-start.6 = (f32[4,1,256]{2,1,0:T(1,128)S(1)}, f32[4,1,256]{2,1,0:T(1,128)}, u32[]{:S(2)}) copy-start(f32[4,1,256]{2,1,0:T(1,128)} %param.3) | copy-start | bytes 12292
  7.2 147.4 %all-gather.3.cloned.1.call-start = ((), (), s32[]{:S(2)}) async-start(), calls=%async_computation | async-start | bytes 4456448 | tf_op jit(solution)/shard_map/all_gather | solution.py:378
  10.6 26.2 %copy-start.3 = (f32[256,256]{1,0:T(8,128)S(1)}, f32[256,256]{1,0:T(8,128)}, u32[]{:S(2)}) copy-start(f32[256,256]{1,0:T(8,128)} %get-tuple-element.39) | copy-start | bytes 786436
  10.6 10.0 %collective-permute-start.7 = (f32[256,256]{1,0:T(8,128)}, f32[256,256]{1,0:T(8,128)S(1)}, u32[]{:S(2)}, u32[]{:S(2)}) collective-permute-start(f32[256,256]{1,0:T(8,128)} %get-tuple-element.38), channel_id=1, source_target_pairs={{0,2}} | collective-permute-start | bytes 786440 | tf_op jit(solution)/shard_map/ppermute | solution.py:339
  11.4 14.2 %collective-permute-start.1 = (f32[256,256]{1,0:T(8,128)}, f32[256,256]{1,0:T(8,128)S(1)}, u32[]{:S(2)}, u32[]{:S(2)}) collective-permute-start(f32[256,256]{1,0:T(8,128)} %get-tuple-element.30), channel_id=1, source_target_pairs={{0,96},{8,104},{1,97},{9,105},{2,98},{10,106},{3,99},{11,107},{4,1... | collective-permute-start | bytes 786440 | tf_op jit(solution)/shard_map/ppermute | solution.py:376
  17.4 10.3 %collective-permute-start.2 = (f32[256,256]{1,0:T(8,128)}, f32[256,256]{1,0:T(8,128)S(1)}, u32[]{:S(2)}, u32[]{:S(2)}) collective-permute-start(f32[256,256]{1,0:T(8,128)} %get-tuple-element.31), channel_id=1, source_target_pairs={{0,80},{8,88},{1,81},{9,89},{2,82},{10,90},{3,83},{11,91},{4,84},{... | collective-permute-start | bytes 786440 | tf_op jit(solution)/shard_map/ppermute | solution.py:376
  21.6 8.3 %collective-permute-start.8 = (f32[256,256]{1,0:T(8,128)S(1)}, f32[256,256]{1,0:T(8,128)S(1)}, u32[]{:S(2)}, u32[]{:S(2)}) collective-permute-start(f32[256,256]{1,0:T(8,128)S(1)} %broadcast_select_fusion.13), channel_id=1, source_target_pairs={{0,6},{2,4}} | collective-permute-start | bytes 786440 | tf_op jit(solution)/shard_map/ppermute | solution.py:342
  22.9 13.9 %collective-permute-start.3 = (f32[256,256]{1,0:T(8,128)}, f32[256,256]{1,0:T(8,128)S(1)}, u32[]{:S(2)}, u32[]{:S(2)}) collective-permute-start(f32[256,256]{1,0:T(8,128)} %get-tuple-element.32), channel_id=1, source_target_pairs={{0,64},{8,72},{1,65},{9,73},{2,66},{10,74},{3,67},{11,75},{4,68},{... | collective-permute-start | bytes 786440 | tf_op jit(solution)/shard_map/ppermute | solution.py:376
  24.2 13.5 %collective-permute-start.4 = (f32[256,256]{1,0:T(8,128)}, f32[256,256]{1,0:T(8,128)S(1)}, u32[]{:S(2)}, u32[]{:S(2)}) collective-permute-start(f32[256,256]{1,0:T(8,128)} %get-tuple-element.33), channel_id=1, source_target_pairs={{0,48},{8,56},{1,49},{9,57},{2,50},{10,58},{3,51},{11,59},{4,52},{... | collective-permute-start | bytes 786440 | tf_op jit(solution)/shard_map/ppermute | solution.py:376
  25.6 14.4 %collective-permute-start.5 = (f32[256,256]{1,0:T(8,128)}, f32[256,256]{1,0:T(8,128)}, u32[]{:S(2)}, u32[]{:S(2)}) collective-permute-start(f32[256,256]{1,0:T(8,128)} %get-tuple-element.34), channel_id=1, source_target_pairs={{0,32},{8,40},{1,33},{9,41},{2,34},{10,42},{3,35},{11,43},{4,36},{... | collective-permute-start | bytes 786440 | tf_op jit(solution)/shard_map/ppermute | solution.py:376
  27.7 12.3 %collective-permute-start.6 = (f32[256,256]{1,0:T(8,128)}, f32[256,256]{1,0:T(8,128)}, u32[]{:S(2)}, u32[]{:S(2)}) collective-permute-start(f32[256,256]{1,0:T(8,128)} %get-tuple-element.35), channel_id=1, source_target_pairs={{0,16},{8,24},{1,17},{9,25},{2,18},{10,26},{3,19},{11,27},{4,20},{... | collective-permute-start | bytes 786440 | tf_op jit(solution)/shard_map/ppermute | solution.py:376
  29.9 13.4 %collective-permute-start = (f32[256,256]{1,0:T(8,128)}, f32[256,256]{1,0:T(8,128)}, u32[]{:S(2)}, u32[]{:S(2)}) collective-permute-start(f32[256,256]{1,0:T(8,128)} %get-tuple-element.29), channel_id=1, source_target_pairs={{0,112},{8,120},{1,113},{9,121},{2,114},{10,122},{3,115},{11,123},... | collective-permute-start | bytes 786440 | tf_op jit(solution)/shard_map/ppermute | solution.py:376
  36.8 17.0 %copy-start.2 = (f32[1024,256]{1,0:T(8,128)S(1)}, f32[1024,256]{1,0:T(8,128)}, u32[]{:S(2)}) copy-start(f32[1024,256]{1,0:T(8,128)} %get-tuple-element.40) | copy-start | bytes 3145732
  36.9 15.4 %collective-permute-start.10 = (f32[256,256]{1,0:T(8,128)S(1)}, f32[256,256]{1,0:T(8,128)S(1)}, u32[]{:S(2)}, u32[]{:S(2)}) collective-permute-start(f32[256,256]{1,0:T(8,128)S(1)} %copy-done.3), channel_id=1, source_target_pairs={{8,16},{9,17}} | collective-permute-start | bytes 786440 | tf_op jit(solution)/shard_map/ppermute | solution.py:339
  37.7 14.6 %collective-permute-start.9 = (f32[256,256]{1,0:T(8,128)S(1)}, f32[256,256]{1,0:T(8,128)S(1)}, u32[]{:S(2)}, u32[]{:S(2)}) collective-permute-start(f32[256,256]{1,0:T(8,128)S(1)} %broadcast_select_fusion.15), channel_id=1, source_target_pairs={{0,8},{2,10},{4,12},{6,14}} | collective-permute-start | bytes 786440 | tf_op jit(solution)/shard_map/ppermute | solution.py:339
  52.3 0.7 collective-permute-start.15
  53.1 4.4 %collective-permute-start.16 = (f32[256,256]{1,0:T(8,128)S(1)}, f32[256,256]{1,0:T(8,128)S(1)}, u32[]{:S(2)}, u32[]{:S(2)}) collective-permute-start(f32[256,256]{1,0:T(8,128)S(1)} %broadcast_select_fusion.5), channel_id=1, source_target_pairs={{8,40},{16,48},{24,56},{0,32},{9,41},{17,49},{25,57},{1,33}} | collective-permute-start | bytes 786440 | tf_op jit(solution)/shard_map/ppermute | solution.py:339
  53.8 16.9 %collective-permute-start.12 = (f32[1024,256]{1,0:T(8,128)S(1)}, f32[1024,256]{1,0:T(8,128)S(1)}, u32[]{:S(2)}, u32[]{:S(2)}) collective-permute-start(f32[1024,256]{1,0:T(8,128)S(1)} %copy-done.2), channel_id=1, source_target_pairs={{0,6},{1,7},{8,14},{9,15},{16,22},{17,23},{24,30},{25,31},{32,38},... | collective-permute-start | bytes 3145736 | tf_op jit(solution)/shard_map/ppermute | solution.py:383
  54.5 16.2 %collective-permute-start.11 = (f32[1024,256]{1,0:T(8,128)S(1)}, f32[1024,256]{1,0:T(8,128)}, u32[]{:S(2)}, u32[]{:S(2)}) collective-permute-start(f32[1024,256]{1,0:T(8,128)S(1)} %copy-done.2), channel_id=1, source_target_pairs={{0,2},{1,3},{8,10},{9,11},{16,18},{17,19},{24,26},{25,27},{32,34},... | collective-permute-start | bytes 3145736 | tf_op jit(solution)/shard_map/ppermute | solution.py:382
  56.2 5.2 %collective-permute-start.13 = (f32[256,256]{1,0:T(8,128)S(1)}, f32[256,256]{1,0:T(8,128)S(1)}, u32[]{:S(2)}, u32[]{:S(2)}) collective-permute-start(f32[256,256]{1,0:T(8,128)S(1)} %broadcast_select_fusion.16), channel_id=1, source_target_pairs={{0,24},{2,26},{4,28},{6,30},{8,16},{10,18},{12,20},{14,22}} | collective-permute-start | bytes 786440 | tf_op jit(solution)/shard_map/ppermute | solution.py:342
  57.5 5.2 %collective-permute-start.17 = (f32[256,256]{1,0:T(8,128)S(1)}, f32[256,256]{1,0:T(8,128)S(1)}, u32[]{:S(2)}, u32[]{:S(2)}) collective-permute-start(f32[256,256]{1,0:T(8,128)S(1)} %broadcast_select_fusion.9), channel_id=1, source_target_pairs={{8,104},{16,112},{24,120},{0,96},{9,105},{17,113},{25,121},{1,97},... | collective-permute-start | bytes 786440 | tf_op jit(solution)/shard_map/ppermute | solution.py:342
  61.4 6.6 %collective-permute-start.14 = (f32[256,256]{1,0:T(8,128)S(1)}, f32[256,256]{1,0:T(8,128)S(1)}, u32[]{:S(2)}, u32[]{:S(2)}) collective-permute-start(f32[256,256]{1,0:T(8,128)S(1)} %broadcast_select_fusion.8), channel_id=1, source_target_pairs={{0,32},{8,40},{16,48},{24,56},{2,34},{10,42},{18,50},{26,58},{4,36... | collective-permute-start | bytes 786440 | tf_op jit(solution)/shard_map/ppermute | solution.py:339
  62.7 6.6 %collective-permute-start.22 = (f32[256,256]{1,0:T(8,128)S(1)}, f32[256,256]{1,0:T(8,128)S(1)}, u32[]{:S(2)}, u32[]{:S(2)}) collective-permute-start(f32[256,256]{1,0:T(8,128)S(1)} %broadcast_select_fusion.7), channel_id=1, source_target_pairs={{8,10},{40,42},{72,74},{104,106},{16,18},{48,50},{80,82},{112,114}... | collective-permute-start | bytes 786440 | tf_op jit(solution)/shard_map/ppermute | solution.py:339
  68.0 60.1 %copy-start.5 = (f32[1024]{0:T(1024)S(1)}, f32[1024]{0:T(1024)}, u32[]{:S(2)}) copy-start(f32[1024]{0:T(1024)} %broadcast_select_fusion.17.weights) | copy-start | bytes 12292
  68.0 6.5 %collective-permute-start.20 = (f32[256,256]{1,0:T(8,128)S(1)}, f32[256,256]{1,0:T(8,128)S(1)}, u32[]{:S(2)}, u32[]{:S(2)}) collective-permute-start(f32[256,256]{1,0:T(8,128)S(1)} %broadcast_select_fusion.10), channel_id=1, source_target_pairs={{0,96},{8,104},{16,112},{24,120},{2,98},{10,106},{18,114},{26,122}... | collective-permute-start | bytes 786440 | tf_op jit(solution)/shard_map/ppermute | solution.py:342
  69.3 59.8 %copy-start.4 = (f32[16,128]{1,0:T(8,128)S(1)}, f32[16,128]{1,0:T(8,128)}, u32[]{:S(2)}) copy-start(f32[16,128]{1,0:T(8,128)} %column_sums.1) | copy-start | bytes 24580
  69.4 29.9 %collective-permute-start.23 = (f32[256,256]{1,0:T(8,128)S(1)}, f32[256,256]{1,0:T(8,128)}, u32[]{:S(2)}, u32[]{:S(2)}) collective-permute-start(f32[256,256]{1,0:T(8,128)S(1)} %broadcast_select_fusion.12), channel_id=1, source_target_pairs={{8,14},{40,46},{72,78},{104,110},{16,22},{48,54},{80,86},{112,118}... | collective-permute-start | bytes 786440 | tf_op jit(solution)/shard_map/ppermute | solution.py:342
  71.0 40.1 %collective-permute-start.19 = (f32[512,256]{1,0:T(8,128)S(1)}, f32[512,256]{1,0:T(8,128)S(1)}, u32[]{:S(2)}, u32[]{:S(2)}) collective-permute-start(f32[512,256]{1,0:T(8,128)S(1)} %get-tuple-element.60), channel_id=1, source_target_pairs={{6,4},{7,5},{14,12},{15,13},{22,20},{23,21},{30,28},{31,29},{38,36... | collective-permute-start | bytes 1572872 | tf_op jit(solution)/shard_map/ppermute | solution.py:387
  72.3 38.8 %collective-permute-start.18 = (f32[512,256]{1,0:T(8,128)S(1)}, f32[512,256]{1,0:T(8,128)}, u32[]{:S(2)}, u32[]{:S(2)}) collective-permute-start(f32[512,256]{1,0:T(8,128)S(1)} %get-tuple-element.61), channel_id=1, source_target_pairs={{2,4},{3,5},{10,12},{11,13},{18,20},{19,21},{26,28},{27,29},{34,36... | collective-permute-start | bytes 1572872 | tf_op jit(solution)/shard_map/ppermute | solution.py:386
  74.5 26.5 %collective-permute-start.21 = (f32[256,256]{1,0:T(8,128)S(1)}, f32[256,256]{1,0:T(8,128)S(1)}, u32[]{:S(2)}, u32[]{:S(2)}) collective-permute-start(f32[256,256]{1,0:T(8,128)S(1)} %broadcast_select_fusion.6), channel_id=1, source_target_pairs={{0,1},{2,3},{4,5},{6,7},{8,9},{10,11},{12,13},{14,15},{16,17},{18,... | collective-permute-start | bytes 786440 | tf_op jit(solution)/shard_map/ppermute | solution.py:367
  112.4 29.9 %copy-start = (f32[1024,256]{1,0:T(8,128)}, f32[1024,256]{1,0:T(8,128)S(1)}, u32[]{:S(2)}) copy-start(f32[1024,256]{1,0:T(8,128)S(1)} %pad_maximum_fusion.mine) | copy-start | bytes 3145732
  112.4 16.2 %collective-permute-start.24 = (f32[1024,256]{1,0:T(8,128)S(1)}, f32[1024,256]{1,0:T(8,128)S(1)}, u32[]{:S(2)}, u32[]{:S(2)}) collective-permute-start(f32[1024,256]{1,0:T(8,128)S(1)} %pad_maximum_fusion.mine), channel_id=1, source_target_pairs={{0,1},{1,0},{2,3},{3,2},{4,5},{5,4},{6,7},{7,6},{8,9},{9,8},{10,11... | collective-permute-start | bytes 3145736 | tf_op jit(solution)/shard_map/ppermute | solution.py:392
  112.5 3.2 %collective-permute-start.25 = (f32[256,256]{1,0:T(8,128)}, f32[256,256]{1,0:T(8,128)S(1)}, u32[]{:S(2)}, u32[]{:S(2)}) collective-permute-start(f32[256,256]{1,0:T(8,128)} %broadcast_select_fusion.14), channel_id=1, source_target_pairs={{0,1},{1,0},{2,3},{3,2},{4,5},{5,4},{6,7},{7,6},{8,9},{9,8},{10,11... | collective-permute-start | bytes 786440 | tf_op jit(solution)/shard_map/ppermute | solution.py:370
  128.6 13.7 %copy-start.1 = (f32[1024,256]{1,0:T(8,128)}, f32[1024,256]{1,0:T(8,128)S(1)}, u32[]{:S(2)}) copy-start(f32[1024,256]{1,0:T(8,128)S(1)} %collective-permute-done.24.theirs) | copy-start | bytes 3145732
  129.2 3.7 %collective-permute-start.26 = (f32[24,128]{1,0:T(8,128)S(1)}, f32[24,128]{1,0:T(8,128)S(1)}, u32[]{:S(2)}, u32[]{:S(2)}) collective-permute-start(f32[24,128]{1,0:T(8,128)S(1)} %maximum_maximum_fusion), channel_id=1, source_target_pairs={{0,8},{8,0},{16,24},{24,16},{32,40},{40,32},{48,56},{56,48},{64,72... | collective-permute-start | bytes 36872 | tf_op jit(solution)/shard_map/ppermute | solution.py:399
  133.0 4.9 %collective-permute-start.27 = (f32[24,128]{1,0:T(8,128)S(1)}, f32[24,128]{1,0:T(8,128)S(1)}, u32[]{:S(2)}, u32[]{:S(2)}) collective-permute-start(f32[24,128]{1,0:T(8,128)S(1)} %fusion), channel_id=1, source_target_pairs={{0,24},{8,16},{16,8},{24,0},{32,56},{40,48},{48,40},{56,32},{64,88... | collective-permute-start | bytes 36872 | tf_op jit(solution)/shard_map/ppermute | solution.py:399
  138.0 3.7 %collective-permute-start.28 = (f32[24,128]{1,0:T(8,128)S(1)}, f32[24,128]{1,0:T(8,128)S(1)}, u32[]{:S(2)}, u32[]{:S(2)}) collective-permute-start(f32[24,128]{1,0:T(8,128)S(1)} %add.56), channel_id=1, source_target_pairs={{0,32},{8,40},{16,48},{24,56},{32,0},{40,8},{48,16},{56,24},{64,96... | collective-permute-start | bytes 36872 | tf_op jit(solution)/shard_map/ppermute | solution.py:399
  141.7 8.3 %collective-permute-start.29 = (f32[24,128]{1,0:T(8,128)S(1)}, f32[24,128]{1,0:T(8,128)S(1)}, u32[]{:S(2)}, u32[]{:S(2)}) collective-permute-start(f32[24,128]{1,0:T(8,128)S(1)} %add.57), channel_id=1, source_target_pairs={{0,96},{8,104},{16,112},{24,120},{32,64},{40,72},{48,80},{56,88},{... | collective-permute-start | bytes 36872 | tf_op jit(solution)/shard_map/ppermute | solution.py:399
Sparse Core Ops, SparseCore 0:
  52.4 54.2 all-gather.2

commit v4 on v3

--- a/solution.py
+++ b/solution.py
@@ -113,14 +113,16 @@
     out[128:256, 0:128] = -dot6(part[1], dot6(part[2], part[0], NN), NN)
 
 
-def first_kernel(c00, w00, m, part):
-    factor_tile(c00, w00, m, part)
-
-
-def second_kernel(w00, c10, c11, l10, w11, schur, m, part):
-    low = dot6(c10[...], w00[...], NT)
+def first_kernel(place, own, other, w00, tile, m, part):
+    tile[...] = jnp.where(place[1] % 2 == 0, own[...], other[...])
+    factor_tile(tile, w00, m, part)
+
+
+def second_kernel(place, w00, own, other, l10, w11, schur, m, part):
+    even = place[1] % 2 == 0
+    low = dot6(jnp.where(even, own[0:NB], other[0:NB]), w00[...], NT)
     l10[...] = low
-    schur[...] = c11[...] - dot6(low, low, NT)
+    schur[...] = jnp.where(even, other[0:NB], own[0:NB]) - dot6(low, low, NT)
     factor_tile(schur, w11, m, part)
 
 
@@ -130,19 +132,24 @@
 SMEM = pl.BlockSpec(memory_space=pltpu.SMEM)
 
 
-def first_factor(c00):
-    return pl.pallas_call(
-        first_kernel, out_shape=TILE, in_specs=[VMEM], out_specs=VMEM, scratch_shapes=WORK, name="first_factor",
-        cost_estimate=pl.CostEstimate(flops=100_000_000, bytes_accessed=100_000, transcendentals=0),
-    )(c00)
-
-
-def second_factor(w00, c10, c11):
-    return pl.pallas_call(
-        second_kernel, out_shape=(TILE, TILE), in_specs=[VMEM] * 3, out_specs=(VMEM, VMEM),
-        scratch_shapes=[pltpu.VMEM((NB, NB), F32)] + WORK, name="second_factor",
-        cost_estimate=pl.CostEstimate(flops=100_000_000, bytes_accessed=100_000, transcendentals=0),
-    )(w00, c10, c11)
+LIMIT = 24 * 1024 * 1024
+SMALL = pl.CostEstimate(flops=100_000_000, bytes_accessed=100_000, transcendentals=0)
+FACTOR = dict(compiler_params=pltpu.CompilerParams(vmem_limit_bytes=LIMIT), cost_estimate=SMALL)
+TILE_WORK = [pltpu.VMEM((NB, NB), F32)] + WORK
+
+
+def first_factor(place, own, other):
+    return pl.pallas_call(
+        first_kernel, out_shape=TILE, in_specs=[SMEM, VMEM, VMEM], out_specs=VMEM,
+        scratch_shapes=TILE_WORK, name="first_factor", **FACTOR,
+    )(place, own, other)
+
+
+def second_factor(place, w00, own, other):
+    return pl.pallas_call(
+        second_kernel, out_shape=(TILE, TILE), in_specs=[SMEM, VMEM, VMEM, VMEM], out_specs=(VMEM, VMEM),
+        scratch_shapes=TILE_WORK, name="second_factor", **FACTOR,
+    )(place, w00, own, other)
 
 
 def corner_kernel(a, *pieces):
@@ -161,27 +168,15 @@
     )(flat)
 
 
-def column_kernel(a, column, again):
+def column_kernel(weights, a, column, again, sums):
+    step = pl.program_id(0)
     for q in range(2):
         value = a[:, q, :]
         column[:, 128 * q : 128 * q + 128] = value
 
-        @pl.when(pl.program_id(0) == 0)
+        @pl.when(step < 2)
         def _():
-            again[:, 128 * q : 128 * q + 128] = value[0:NB]
-
-
-def column_call(flat):
-    return pl.pallas_call(
-        column_kernel, grid=(4,), out_shape=(jax.ShapeDtypeStruct((1024, NB), F32), TILE),
-        in_specs=[pl.BlockSpec((256, 8, 128), lambda i: (i, 0, 0))],
-        out_specs=(pl.BlockSpec((256, NB), lambda i: (i, 0)), pl.BlockSpec((NB, NB), lambda i: (0, 0))),
-        name="first_column",
-    )(flat)
-
-
-def sums_kernel(weights, a, sums):
-    step = pl.program_id(0)
+            again[:, 128 * q : 128 * q + 128] = value
 
     @pl.when(step == 0)
     def _():
@@ -196,34 +191,21 @@
     sums[...] += lax.fori_loop(0, 16, body, jnp.zeros((16, 128), F32))
 
 
-def sums_call(weights, flat):
-    return pl.pallas_call(
-        sums_kernel, grid=(8,), out_shape=jax.ShapeDtypeStruct((16, 128), F32),
+def column_call(weights, flat):
+    return pl.pallas_call(
+        column_kernel, grid=(8,),
+        out_shape=(jax.ShapeDtypeStruct((1024, NB), F32), TILE, jax.ShapeDtypeStruct((16, 128), F32)),
         in_specs=[SMEM, pl.BlockSpec((128, 16, 128), lambda i: (i, 0, 0))],
-        out_specs=pl.BlockSpec((16, 128), lambda i: (0, 0)),
-        name="column_sums",
-        cost_estimate=pl.CostEstimate(flops=100_000_000, bytes_accessed=100_000, transcendentals=0),
+        out_specs=(
+            pl.BlockSpec((128, NB), lambda i: (i, 0)),
+            pl.BlockSpec((128, NB), lambda i: (jnp.minimum(i, 1), 0)),
+            pl.BlockSpec((16, 128), lambda i: (0, 0)),
+        ),
+        name="first_column", **FACTOR,
     )(weights, flat)
 
 
-def taken_kernel(sums, w00, l10, w11, taken):
-    v0 = jnp.broadcast_to(jnp.concatenate([sums[16:17], sums[17:18]], axis=1), (8, NB))
-    v1 = jnp.broadcast_to(jnp.concatenate([sums[18:19], sums[19:20]], axis=1), (8, NB))
-    y0 = dot6(v0, w00[...], NT)
-    y1 = dot6(v1 - dot6(y0, l10[...], NT), w11[...], NT)
-    z1 = dot6(y1, w11[...], NN)
-    taken[:, 256:512] = z1
-    taken[:, 0:256] = dot6(y0 - dot6(z1, l10[...], NN), w00[...], NN)
-
-
-def taken_call(sums, w00, l10, w11):
-    return pl.pallas_call(
-        taken_kernel, out_shape=jax.ShapeDtypeStruct((8, 512), F32), in_specs=[VMEM] * 4, out_specs=VMEM, name="taken_sums",
-        cost_estimate=pl.CostEstimate(flops=100_000_000, bytes_accessed=100_000, transcendentals=0),
-    )(sums, w00, l10, w11)
-
-
-def panel_kernel(place, mine, theirs, w00, l10, w11, panels, high, low, factors):
+def panel_kernel(place, mine, theirs, own_sums, other_sums, w00, l10, w11, panels, high, low, taken, factors):
     step = pl.program_id(0)
     even = place[1] % 2 == 0
 
@@ -233,35 +215,42 @@
             factors[0, k], factors[1, k] = halves(ref[...])
 
     f00, f10, f11 = [(factors[0, k], factors[1, k]) for k in range(3)]
-    own, other = mine[...], theirs[...]
+    own = jnp.concatenate([mine[...], own_sums[...]], axis=0)
+    other = jnp.concatenate([theirs[...], other_sums[...]], axis=0)
     first = jnp.where(even, own, other)
     second = jnp.where(even, other, own)
     left = dot3(halves(first), f00, NT)
     right = dot3(halves(second - dot3(halves(left), f10, NT)), f11, NT)
-    panels[:, 0:256] = left
-    panels[:, 256:512] = jnp.where((step * 512 < 256) & (place[0] == 0) & (lax.broadcasted_iota(jnp.int32, (512, 1), 0) < 256), 0.0, right)
+    panels[:, 0:256] = left[0:512]
+    top = (step == 0) & (place[0] == 0) & (lax.broadcasted_iota(jnp.int32, (512, 1), 0) < NB)
+    panels[:, 256:512] = jnp.where(top, 0.0, right[0:512])
     last = dot3(halves(right), f11, NN)
-    last_halves = halves(last)
-    high[:, 256:512], low[:, 256:512] = last_halves
-    high[:, 0:256], low[:, 0:256] = halves(dot3(halves(left - dot3(last_halves, f10, NN)), f00, NN))
-
-
-def panel_call(place, mine, theirs, w00, l10, w11):
+    last_high, last_low = halves(last)
+    rest = dot3(halves(left - dot3((last_high, last_low), f10, NN)), f00, NN)
+    high[:, 256:512] = last_high[0:512]
+    low[:, 256:512] = last_low[0:512]
+    high[:, 0:256], low[:, 0:256] = halves(rest[0:512])
+    taken[:, 0:256] = rest[512:520]
+    taken[:, 256:512] = last[512:520]
+
+
+def panel_call(place, mine, theirs, below, other, w00, l10, w11):
     full = lambda *shape: pl.BlockSpec(shape, lambda i: (0,) * len(shape))
     part = lambda n: pl.BlockSpec((512, n), lambda i: (i, 0))
+    tail = pl.BlockSpec((8, NB), lambda i: (NB // 8, 0))
     return pl.pallas_call(
         panel_kernel, grid=(2,),
         out_shape=(
             jax.ShapeDtypeStruct((1024, 512), F32),
             jax.ShapeDtypeStruct((1024, 512), BF16),
             jax.ShapeDtypeStruct((1024, 512), BF16),
+            jax.ShapeDtypeStruct((8, 512), F32),
         ),
-        in_specs=[SMEM, part(NB), part(NB), full(NB, NB), full(NB, NB), full(NB, NB)],
-        out_specs=(part(512), part(512), part(512)),
+        in_specs=[SMEM, part(NB), part(NB), tail, tail, full(NB, NB), full(NB, NB), full(NB, NB)],
+        out_specs=(part(512), part(512), part(512), full(8, 512)),
         scratch_shapes=[pltpu.VMEM((2, 3, NB, NB), BF16)],
-        name="panel_solve",
-        cost_estimate=pl.CostEstimate(flops=100_000_000, bytes_accessed=100_000, transcendentals=0),
-    )(place, mine, theirs, w00, l10, w11)
+        name="panel_solve", **FACTOR,
+    )(place, mine, theirs, below, other, w00, l10, w11)
 
 
 def update_kernel(place, flat, across, high, low, sums, taken, out, checksum, right_high, right_low):
@@ -283,10 +272,12 @@
                     kept = jnp.where((group == 0) & (col_index < 2), 0.0, kept)
                 checksum[pl.ds(8 * group + q, 1), :] = kept
 
-    rows = flat.shape[0]
+    rows = out.shape[0]
+    base = pl.multiple_of(step * rows, rows)
     top = (step * rows + lax.broadcasted_iota(jnp.int32, (rows, 1), 0) < NB) & (row_index < 2)
+    mine = high[pl.ds(base, rows), :], low[pl.ds(base, rows), :]
     for u in range(4):
-        product = dot3((high[...], low[...]), (right_high[u], right_low[u]), NN)
+        product = dot3(mine, (right_high[u], right_low[u]), NN)
         gone = top | ((group == 0) & (col_index < 2)) if u == 0 else top
         for h in range(2):
             q = 2 * u + h
@@ -295,7 +286,7 @@
 
 
 def update_call(place, flat, across, high, low, sums, taken):
-    rows = 512
+    rows = 256
     full = lambda *shape: pl.BlockSpec(shape, lambda g, i: (0,) * len(shape))
     return pl.pallas_call(
         update_kernel, grid=(2, 1024 // rows),
@@ -304,14 +295,14 @@
             SMEM,
             pl.BlockSpec((rows, 8, 128), lambda g, i: (i, g, 0)),
             pl.BlockSpec((8, NB, NB), lambda g, i: (g, 0, 0)),
-            pl.BlockSpec((rows, 512), lambda g, i: (i, 0)),
-            pl.BlockSpec((rows, 512), lambda g, i: (i, 0)),
-            full(24, 128),
+            full(1024, 512),
+            full(1024, 512),
+            full(16, 128),
             full(8, 512),
         ],
         out_specs=(pl.BlockSpec((rows, 8, 128), lambda g, i: (i, g, 0)), full(16, 128)),
         scratch_shapes=[pltpu.VMEM((4, 512, NB), BF16), pltpu.VMEM((4, 512, NB), BF16)],
-        name="trailing_update",
+        name="trailing_update", **FACTOR,
     )(place, flat, across, high, low, sums, taken)
 
 
@@ -330,18 +321,31 @@
     return device_at(*at)
 
 
-def spread(value, sources, dims, start, here):
-    holders = list(sources)
+def spread(value, trees, here, gates=None, cargo=None):
+    core = here[3]
+    holders = [[device_at(z, y, 0, c)] for (z, y), c, _ in trees]
     stages = []
-    for dim in dims:
-        away = (here[dim] - start[dim]) % 4
-        pairs = [(h, moved(h, dim, 1)) for h in holders]
-        value = jnp.where(away == 1, lax.ppermute(value, ("row", "col"), pairs), value)
-        stages.append(value)
-        pairs = [(h, moved(h, dim, -1)) for h in holders] + [(moved(h, dim, 1), moved(h, dim, 2)) for h in holders]
-        value = jnp.where(away >= 2, lax.ppermute(value, ("row", "col"), pairs), value)
-        stages.append(value)
-        holders = [moved(h, dim, k) for h in holders for k in range(4)]
+    for at in range(3):
+        if at == 2 and cargo is not None:
+            value = jnp.concatenate([value, cargo], axis=0)
+        aways = []
+        for (z, y), c, dims in trees:
+            start = (z, y, 0)
+            aways.append((c, (here[dims[at]] - start[dims[at]]) % 4))
+        away = aways[0][1] if len(trees) == 1 else jnp.where(core == aways[0][0], aways[0][1], aways[1][1])
+        for half in range(2):
+            pairs = []
+            for held, (_, _, dims) in zip(holders, trees):
+                dim = dims[at]
+                if half == 0:
+                    pairs += [(h, moved(h, dim, 1)) for h in held]
+                else:
+                    pairs += [(h, moved(h, dim, -1)) for h in held] + [(moved(h, dim, 1), moved(h, dim, 2)) for h in held]
+            sent = value if gates is None else after(value, gates[2 * at + half])
+            arrived = lax.ppermute(sent, ("row", "col"), pairs)
+            value = jnp.where((away == 1) if half == 0 else (away >= 2), arrived, sent)
+            stages.append(value)
+        holders = [[moved(h, dims[at], k) for h in held for k in range(4)] for held, (_, _, dims) in zip(holders, trees)]
     return stages
 
 
@@ -354,31 +358,32 @@
     col = lax.axis_index("col")
     core = col % 2
     x = col // 2
-    here = [row // 4, row % 4, x]
-    flat = covariance.reshape(1024, 16, 128)
+    here = [row // 4, row % 4, x, core]
+    flat = pltpu.with_memory_space_constraint(covariance.reshape(1024, 16, 128), pltpu.HBM)
     tiles = jnp.arange(4, dtype=jnp.int32) * 16 + row
     weights = jnp.where((tiles >= 2)[:, None], check_weights.reshape(4, NB), 0.0).reshape(1024)
     place = jnp.stack([row, col]).astype(jnp.int32)
     swap_cores = [(c, c ^ 1) for c in range(8)]
 
     pieces = corner_call(flat)
-    column, corner = column_call(after(flat, pieces[7]))
-    tree0 = spread(pieces[0], [device_at(0, 0, 0, 0)], (2, 1, 0), (0, 0, 0), here)
-    c00 = jnp.where(core == 1, lax.ppermute(tree0[-1], "col", [(c, c + 1) for c in (0, 2, 4, 6)]), tree0[-1])
-    tree1 = spread(pieces[8], [device_at(0, 1, 0, 0), device_at(0, 1, 0, 1)], (1, 0, 2), (0, 1, 0), here)
+    tree0 = spread(pieces[0], [((0, 0), 0, (2, 1, 0))], here)
+    c00_other = lax.ppermute(tree0[-1], "col", [(c, c + 1) for c in (0, 2, 4, 6)])
+    column, corner, sums = column_call(weights, after(flat, tree0[1]))
+    for d in (1, 3, 4, 12):
+        sums = sums + lax.ppermute(sums, "row", [(r, r ^ d) for r in range(16)])
+    panel_sums = jnp.broadcast_to(sums[0:2].reshape(1, NB), (8, NB))
+    tree1 = spread(pieces[8], [((0, 1), 0, (0, 1, 2)), ((0, 1), 1, (1, 0, 2))], here, tree0, panel_sums)
     below = tree1[-1]
-    other = lax.ppermute(below, "col", swap_cores)
-    c10 = jnp.where(core == 0, below, other)
-    c11 = jnp.where(core == 0, other, below)
+    below_other = lax.ppermute(below, "col", swap_cores)
 
     piece = corner
     for j in range(1, 8):
         piece = jnp.where(row // 2 == j, lax.ppermute(pieces[j], "row", [(0, 2 * j), (1, 2 * j + 1)]), piece)
-    sums = sums_call(weights, after(flat, (tree0[0], column)))
-    across = lax.all_gather(after(piece, (tree0[2], tree1[0], sums)), "row", axis=0)
-
-    w00 = first_factor(c00)
-    l10, w11 = second_factor(w00, c10, c11)
+    across = lax.all_gather(after(piece, tree0[1]), "row", axis=0)
+    across = pltpu.with_memory_space_constraint(across, pltpu.HBM)
+
+    w00 = first_factor(place, tree0[-1], c00_other)
+    l10, w11 = second_factor(place, w00, below, below_other)
     from_left = lax.ppermute(column, "col", [(0, 2), (1, 3)])
     from_right = lax.ppermute(column, "col", [(0, 6), (1, 7)])
     from_left, from_right = after((from_left, from_right), (tree0[4], tree1[3]))
@@ -390,17 +395,9 @@
     lower = jnp.where(x == 2, lower, mine[512:1024])
     mine = jnp.concatenate([upper, lower], axis=0)
     theirs = after(lax.ppermute(mine, "col", swap_cores), w11)
-    own_sums = jnp.dot(weights[None], mine, precision=HIGHEST)
-    other_sums = jnp.dot(weights[None], theirs, precision=HIGHEST)
-    first_sums = jnp.where(core == 0, own_sums, other_sums)
-    second_sums = jnp.where(core == 0, other_sums, own_sums)
-    total = jnp.concatenate([sums, first_sums.reshape(2, 128), second_sums.reshape(2, 128), jnp.zeros((4, 128), F32)], axis=0)
-    for d in (1, 3, 4, 12):
-        total = total + lax.ppermute(total, "row", [(r, r ^ d) for r in range(16)])
-
-    panels, high, low = panel_call(place, mine, theirs, w00, l10, w11)
-    taken = taken_call(total, w00, l10, w11)
-    trailing, checksum = update_call(place, flat, across, high, low, total, taken)
+
+    panels, high, low, taken = panel_call(place, mine, theirs, below, below_other, w00, l10, w11)
+    trailing, checksum = update_call(place, flat, across, high, low, sums, taken)
     return (
         trailing.reshape(4, 1, NB, 8, 1, NB),
         panels.reshape(4, 1, NB, 512),

time: 183 us -> 160 us (0.87)
  the two profiles are of different devices: /device:TPU:4 before, /device:TPU:37 now
where the time goes in v4:
time: 160 us; the launch traced here: 159 us
  Pallas kernels  54.9 us (34%)
  waiting for transfers between devices  53.8 us (34%)
  starting transfers between devices  31.1 us (19%)
  between operations  14.7 us (9%)
  other arithmetic  3.84 us (2%)
    pallas_call x1, Pallas kernels, update_call(): pl.pallas_call(update_kernel, grid=(2, 1024 // rows), out_shape=(jax.Shap...  20.6 us
    ppermute x1, waiting for transfers between devices, shards(): lax.ppermute(tree0[-1], 'col', [(c, c + 1) for c in (0, 2, 4, 6)])  19.7 us
    ppermute x12, waiting for transfers between devices, spread(): arrived = lax.ppermute(sent, ('row', 'col'), pairs)  17.3 us
    ppermute x7, waiting for transfers between devices, shards(): lax.ppermute(pieces[j], 'row', [(0, 2 * j), (1, 2 * j + 1)])  10.4 us
    ppermute x4, starting transfers between devices, shards(): sums = sums + lax.ppermute(sums, 'row', [(r, r ^ d) for r in range(16)])  10.2 us
    pallas_call x1, Pallas kernels, second_factor(): pl.pallas_call(second_kernel, out_shape=(TILE, TILE), in_specs=[SMEM, VME...  9.32 us
    ppermute x12, starting transfers between devices, spread(): arrived = lax.ppermute(sent, ('row', 'col'), pairs)  8.88 us
    pallas_call x1, Pallas kernels, first_factor(): pl.pallas_call(first_kernel, out_shape=TILE, in_specs=[SMEM, VMEM, VMEM],...  8.22 us
  transfers between devices with their start and end apart: 31, of which 7 were waited for; matrix products, arithmetic and copies ran while one was open for 2% of the time, Pallas kernels for 19%

profile of v4, /device:TPU:37, one launch (start us, length us, event | category | flops | bytes accessed | tf_op | source)
XLA Modules:
  0.0 159.4 jit_solution(12850756513469924380)
XLA Ops:
  7.2 3.4 %corner_tiles.1 = (f32[256,256]{1,0:T(8,128)}, f32[256,256]{1,0:T(8,128)}, f32[256,256]{1,0:T(8,128)}, f32[256,256]{1,0:T(8,128)}, f32[256,256]{1,0:T(8,128)}, /...) custom-call(f32[1024,16,128]{2,1,0:T(8,128)} %bitcast.12), custom_call_target="tpu_custom_call" | custom-call | tf_op jit(solution)/shard_map/corner_tiles/pallas_call | solution.py:163
  10.6 0.8 collective-permute-start.7
  11.4 0.7 collective-permute-start
  12.1 0.7 collective-permute-start.1
  12.8 1.0 broadcast_select_fusion.12
  13.8 0.7 collective-permute-start.8
  14.5 0.7 collective-permute-start.2
  15.2 0.7 collective-permute-start.3
  16.0 0.7 collective-permute-start.4
  16.7 1.3 collective-permute-start.5
  18.0 0.7 collective-permute-start.6
  18.8 6.9 %first_column.1 = (f32[1024,256]{1,0:T(8,128)S(1)}, f32[256,256]{1,0:T(8,128)S(1)}, f32[16,128]{1,0:T(8,128)S(1)}) custom-call(f32[1024]{0:T(1024)S(1)} %broadcast_select_fusion.14.weights, f32[1024,16,128]{2,1,0:T(8,128)} %bitcast.13), custom_call_target="tpu_custom_call" | custom-call | flops 100000000 | bytes 100000 | tf_op jit(solution)/shard_map/first_column/pallas_call | solution.py:195
  25.7 10.4 %collective-permute-done.5 = f32[256,256]{1,0:T(8,128)S(1)} collective-permute-done((f32[256,256]{1,0:T(8,128)}, f32[256,256]{1,0:T(8,128)S(1)}, u32[]{:S(2)}, u32[]{:S(2)}) %collective-permute-start.5) | collective-permute-done | bytes 262176 | tf_op jit(solution)/shard_map/ppermute | solution.py:381
  36.1 0.9 select_select_fusion.1
  37.0 0.7 collective-permute-start.14
  37.7 0.7 collective-permute-start.11
  38.5 0.7 collective-permute-start.15
  39.2 1.1 collective-permute-start.22
  40.3 1.4 collective-permute-done.22
  41.7 3.1 %collective-permute-start.23 = (f32[16,128]{1,0:T(8,128)S(1)}, f32[16,128]{1,0:T(8,128)S(1)}, u32[]{:S(2)}, u32[]{:S(2)}) collective-permute-start(f32[16,128]{1,0:T(8,128)S(1)} %add.58), channel_id=1, source_target_pairs={{0,24},{8,16},{16,8},{24,0},{32,56},{40,48},{48,40},{56,32},{64,88... | collective-permute-start | bytes 24584 | tf_op jit(solution)/shard_map/ppermute | solution.py:373
  44.9 0.7 collective-permute-start.12
  45.6 0.7 collective-permute-start.16
  46.4 6.0 %collective-permute-start.24 = (f32[16,128]{1,0:T(8,128)S(1)}, f32[16,128]{1,0:T(8,128)S(1)}, u32[]{:S(2)}, u32[]{:S(2)}) collective-permute-start(f32[16,128]{1,0:T(8,128)S(1)} %add.59), channel_id=1, source_target_pairs={{0,32},{8,40},{16,48},{24,56},{32,0},{40,8},{48,16},{56,24},{64,96... | collective-permute-start | bytes 24584 | tf_op jit(solution)/shard_map/ppermute | solution.py:373
  52.3 1.0 collective-permute-done.24
  53.4 0.7 collective-permute-start.10
  54.1 0.7 collective-permute-start.9
  54.8 1.5 collective-permute-done.25
  56.4 0.7 collective-permute-start.13
  57.1 0.7 collective-permute-start.17
  57.9 0.7 collective-permute-start.20
  58.6 0.7 collective-permute-start.26
  59.4 0.2 select_select_fusion
  59.6 0.9 fusion
  60.4 1.3 collective-permute-start.19
  61.7 1.3 collective-permute-start.18
  63.1 1.3 collective-permute-start.21
  64.4 1.3 collective-permute-start.27
  65.7 0.1 pad_add_fusion.place
  65.8 19.7 %collective-permute-done.21.other = f32[256,256]{1,0:T(8,128)S(1)} collective-permute-done((f32[256,256]{1,0:T(8,128)S(1)}, f32[256,256]{1,0:T(8,128)S(1)}, u32[]{:S(2)}, u32[]{:S(2)}) %collective-permute-start.21) | collective-permute-done | bytes 262176 | tf_op jit(solution)/shard_map/ppermute | solution.py:370
  85.5 8.2 %first_factor.1.w00 = f32[256,256]{1,0:T(8,128)S(1)} custom-call(s32[2]{0:T(128)S(1)} %pad_add_fusion.place, f32[256,256]{1,0:T(8,128)S(1)} %broadcast_select_fusion.4.own, f32[256,256]{1,0:T(8,128)S(1)} %collective-permute-done.21.other), custom_call_target="tpu_custom_call" | custom-call | flops 100000000 | bytes 100000 | tf_op jit(solution)/shard_map/first_factor/pallas_call | solution.py:142
  93.7 17.3 %collective-permute-done.27 = f32[264,256]{1,0:T(8,128)S(1)} collective-permute-done((f32[264,256]{1,0:T(8,128)S(1)}, f32[264,256]{1,0:T(8,128)S(1)}, u32[]{:S(2)}, u32[]{:S(2)}) %collective-permute-start.27) | collective-permute-done | bytes 270368 | tf_op jit(solution)/shard_map/ppermute | solution.py:345
  111.1 1.2 broadcast_select_fusion.1
  112.3 1.1 collective-permute-start.28
  113.4 0.3 collective-permute-start.29
  113.7 2.4 %collective-permute-done.29.other.other_sums = f32[264,256]{1,0:T(8,128)S(1)} collective-permute-done((f32[264,256]{1,0:T(8,128)S(1)}, f32[264,256]{1,0:T(8,128)S(1)}, u32[]{:S(2)}, u32[]{:S(2)}) %collective-permute-start.29) | collective-permute-done | bytes 270368 | tf_op jit(solution)/shard_map/ppermute | solution.py:377
  116.1 9.3 %second_factor.1 = (f32[256,256]{1,0:T(8,128)S(1)}, f32[256,256]{1,0:T(8,128)S(1)}) custom-call(s32[2]{0:T(128)S(1)} %pad_add_fusion.place, f32[256,256]{1,0:T(8,128)S(1)} %first_factor.1.w00, f32[264,256]{1,0:T(8,128)S(1)} %broadcast_select_fusion.3.own.own_sums, f32[264,256]{1,0:T(8,128)S(1)} %collective-permute-done.29.other.other_sums), custom_call_target="tpu_custom_call" | custom-call | flops 100000000 | bytes 100000 | tf_op jit(solution)/shard_map/second_factor/pallas_call | solution.py:149
  125.4 6.5 %panel_solve.1 = (f32[1024,512]{1,0:T(8,128)}, bf16[1024,512]{1,0:T(8,128)(2,1)S(1)}, bf16[1024,512]{1,0:T(8,128)(2,1)S(1)}, f32[8,512]{1,0:T(8,128)S(1)}) custom-call(s32[2]{0:T(128)S(1)} %pad_add_fusion.place, f32[1024,256]{1,0:T(8,128)S(1)} %pad_maximum_fusion.mine, f32[1024,256]{1,0:T(8,128)S(1)} %collective-permute-done.28.theirs, ...), custom_call_target="tpu_custom_call" | custom-call | flops 100000000 | bytes 100000 | tf_op jit(solution)/shard_map/panel_solve/pallas_call | solution.py:241
  131.9 20.6 %trailing_update.1 = (f32[1024,16,128]{2,1,0:T(8,128)}, f32[16,128]{1,0:T(8,128)}) custom-call(s32[2]{0:T(128)S(1)} %pad_add_fusion.place, f32[1024,16,128]{2,1,0:T(8,128)} %bitcast.14, f32[16,256,256]{2,1,0:T(8,128)} %bitcast.15, bf16[1024,512]{1,0:T(8,128)(2,1)S(1)} %get-tuple-element.63.high, bf16[1024,512]{1,0:T(8,128)(2,1)S(1)} %get-tuple-element.64.low, ...), custom_call_target="tpu_custom_call" | custom-call | flops 100000000 | bytes 100000 | tf_op jit(solution)/shard_map/trailing_update/pallas_call | solution.py:291
  (54 shorter events, 0.7 us)
Async XLA Ops:
  7.2 11.5 %copy-start.1 = (f32[4,1,256]{2,1,0:T(1,128)S(1)}, f32[4,1,256]{2,1,0:T(1,128)}, u32[]{:S(2)}) copy-start(f32[4,1,256]{2,1,0:T(1,128)} %param.3) | copy-start | bytes 12292
  7.2 124.8 %all-gather.3.cloned.1.call-start = ((), (), s32[]{:S(2)}) async-start(), calls=%async_computation | async-start | bytes 4456448 | tf_op jit(solution)/shard_map/all_gather | solution.py:382
  10.6 26.4 %copy-start = (f32[256,256]{1,0:T(8,128)S(1)}, f32[256,256]{1,0:T(8,128)}, u32[]{:S(2)}) copy-start(f32[256,256]{1,0:T(8,128)} %get-tuple-element.49) | copy-start | bytes 786436
  10.6 2.2 %collective-permute-start.7 = (f32[256,256]{1,0:T(8,128)}, f32[256,256]{1,0:T(8,128)S(1)}, u32[]{:S(2)}, u32[]{:S(2)}) collective-permute-start(f32[256,256]{1,0:T(8,128)} %get-tuple-element.43), channel_id=1, source_target_pairs={{0,2}} | collective-permute-start | bytes 786440 | tf_op jit(solution)/shard_map/ppermute | solution.py:345
  11.4 4.6 %collective-permute-start = (f32[256,256]{1,0:T(8,128)}, f32[256,256]{1,0:T(8,128)S(1)}, u32[]{:S(2)}, u32[]{:S(2)}) collective-permute-start(f32[256,256]{1,0:T(8,128)} %get-tuple-element.36), channel_id=1, source_target_pairs={{0,112},{8,120},{1,113},{9,121},{2,114},{10,122},{3,115},{11,123},... | collective-permute-start | bytes 786440 | tf_op jit(solution)/shard_map/ppermute | solution.py:381
  12.1 4.6 %collective-permute-start.1 = (f32[256,256]{1,0:T(8,128)}, f32[256,256]{1,0:T(8,128)S(1)}, u32[]{:S(2)}, u32[]{:S(2)}) collective-permute-start(f32[256,256]{1,0:T(8,128)} %get-tuple-element.37), channel_id=1, source_target_pairs={{0,96},{8,104},{1,97},{9,105},{2,98},{10,106},{3,99},{11,107},{4,1... | collective-permute-start | bytes 786440 | tf_op jit(solution)/shard_map/ppermute | solution.py:381
  13.8 4.2 %collective-permute-start.8 = (f32[256,256]{1,0:T(8,128)S(1)}, f32[256,256]{1,0:T(8,128)S(1)}, u32[]{:S(2)}, u32[]{:S(2)}) collective-permute-start(f32[256,256]{1,0:T(8,128)S(1)} %broadcast_select_fusion.12), channel_id=1, source_target_pairs={{0,6},{2,4}} | collective-permute-start | bytes 786440 | tf_op jit(solution)/shard_map/ppermute | solution.py:345
  14.5 11.2 %collective-permute-start.2 = (f32[256,256]{1,0:T(8,128)}, f32[256,256]{1,0:T(8,128)S(1)}, u32[]{:S(2)}, u32[]{:S(2)}) collective-permute-start(f32[256,256]{1,0:T(8,128)} %get-tuple-element.38), channel_id=1, source_target_pairs={{0,80},{8,88},{1,81},{9,89},{2,82},{10,90},{3,83},{11,91},{4,84},{... | collective-permute-start | bytes 786440 | tf_op jit(solution)/shard_map/ppermute | solution.py:381
  15.2 10.5 %collective-permute-start.3 = (f32[256,256]{1,0:T(8,128)}, f32[256,256]{1,0:T(8,128)S(1)}, u32[]{:S(2)}, u32[]{:S(2)}) collective-permute-start(f32[256,256]{1,0:T(8,128)} %get-tuple-element.39), channel_id=1, source_target_pairs={{0,64},{8,72},{1,65},{9,73},{2,66},{10,74},{3,67},{11,75},{4,68},{... | collective-permute-start | bytes 786440 | tf_op jit(solution)/shard_map/ppermute | solution.py:381
  16.0 9.7 %collective-permute-start.4 = (f32[256,256]{1,0:T(8,128)}, f32[256,256]{1,0:T(8,128)S(1)}, u32[]{:S(2)}, u32[]{:S(2)}) collective-permute-start(f32[256,256]{1,0:T(8,128)} %get-tuple-element.40), channel_id=1, source_target_pairs={{0,48},{8,56},{1,49},{9,57},{2,50},{10,58},{3,51},{11,59},{4,52},{... | collective-permute-start | bytes 786440 | tf_op jit(solution)/shard_map/ppermute | solution.py:381
  16.7 19.4 %collective-permute-start.5 = (f32[256,256]{1,0:T(8,128)}, f32[256,256]{1,0:T(8,128)S(1)}, u32[]{:S(2)}, u32[]{:S(2)}) collective-permute-start(f32[256,256]{1,0:T(8,128)} %get-tuple-element.41), channel_id=1, source_target_pairs={{0,32},{8,40},{1,33},{9,41},{2,34},{10,42},{3,35},{11,43},{4,36},{... | collective-permute-start | bytes 786440 | tf_op jit(solution)/shard_map/ppermute | solution.py:381
  18.0 18.1 %collective-permute-start.6 = (f32[256,256]{1,0:T(8,128)}, f32[256,256]{1,0:T(8,128)S(1)}, u32[]{:S(2)}, u32[]{:S(2)}) collective-permute-start(f32[256,256]{1,0:T(8,128)} %get-tuple-element.42), channel_id=1, source_target_pairs={{0,16},{8,24},{1,17},{9,25},{2,18},{10,26},{3,19},{11,27},{4,20},{... | collective-permute-start | bytes 786440 | tf_op jit(solution)/shard_map/ppermute | solution.py:381
  37.0 1.4 collective-permute-start.14
  37.7 7.1 %collective-permute-start.11 = (f32[256,256]{1,0:T(8,128)S(1)}, f32[256,256]{1,0:T(8,128)S(1)}, u32[]{:S(2)}, u32[]{:S(2)}) collective-permute-start(f32[256,256]{1,0:T(8,128)S(1)} %broadcast_select_fusion.13), channel_id=1, source_target_pairs={{0,8},{2,10},{4,12},{6,14}} | collective-permute-start | bytes 786440 | tf_op jit(solution)/shard_map/ppermute | solution.py:345
  38.5 7.1 %collective-permute-start.15 = (f32[256,256]{1,0:T(8,128)S(1)}, f32[256,256]{1,0:T(8,128)S(1)}, u32[]{:S(2)}, u32[]{:S(2)}) collective-permute-start(f32[256,256]{1,0:T(8,128)S(1)} %broadcast_select_fusion.5), channel_id=1, source_target_pairs={{8,104},{40,72},{9,1},{17,25}} | collective-permute-start | bytes 786440 | tf_op jit(solution)/shard_map/ppermute | solution.py:345
  39.2 2.6 %collective-permute-start.22 = (f32[16,128]{1,0:T(8,128)S(1)}, f32[16,128]{1,0:T(8,128)S(1)}, u32[]{:S(2)}, u32[]{:S(2)}) collective-permute-start(f32[16,128]{1,0:T(8,128)S(1)} %get-tuple-element.55), channel_id=1, source_target_pairs={{0,8},{8,0},{16,24},{24,16},{32,40},{40,32},{48,56},{56,48},{64,72... | collective-permute-start | bytes 24584 | tf_op jit(solution)/shard_map/ppermute | solution.py:373
  41.7 4.6 %collective-permute-start.23 = (f32[16,128]{1,0:T(8,128)S(1)}, f32[16,128]{1,0:T(8,128)S(1)}, u32[]{:S(2)}, u32[]{:S(2)}) collective-permute-start(f32[16,128]{1,0:T(8,128)S(1)} %add.58), channel_id=1, source_target_pairs={{0,24},{8,16},{16,8},{24,0},{32,56},{40,48},{48,40},{56,32},{64,88... | collective-permute-start | bytes 24584 | tf_op jit(solution)/shard_map/ppermute | solution.py:373
  44.9 11.4 %collective-permute-start.12 = (f32[256,256]{1,0:T(8,128)S(1)}, f32[256,256]{1,0:T(8,128)S(1)}, u32[]{:S(2)}, u32[]{:S(2)}) collective-permute-start(f32[256,256]{1,0:T(8,128)S(1)} %broadcast_select_fusion.9), channel_id=1, source_target_pairs={{0,24},{2,26},{4,28},{6,30},{8,16},{10,18},{12,20},{14,22}} | collective-permute-start | bytes 786440 | tf_op jit(solution)/shard_map/ppermute | solution.py:345
  45.6 11.4 %collective-permute-start.16 = (f32[256,256]{1,0:T(8,128)S(1)}, f32[256,256]{1,0:T(8,128)S(1)}, u32[]{:S(2)}, u32[]{:S(2)}) collective-permute-start(f32[256,256]{1,0:T(8,128)S(1)} %broadcast_select_fusion.6), channel_id=1, source_target_pairs={{8,16},{40,48},{72,80},{104,112},{9,41},{17,49},{25,57},{1,33}} | collective-permute-start | bytes 786440 | tf_op jit(solution)/shard_map/ppermute | solution.py:345
  46.4 7.0 %collective-permute-start.24 = (f32[16,128]{1,0:T(8,128)S(1)}, f32[16,128]{1,0:T(8,128)S(1)}, u32[]{:S(2)}, u32[]{:S(2)}) collective-permute-start(f32[16,128]{1,0:T(8,128)S(1)} %add.59), channel_id=1, source_target_pairs={{0,32},{8,40},{16,48},{24,56},{32,0},{40,8},{48,16},{56,24},{64,96... | collective-permute-start | bytes 24584 | tf_op jit(solution)/shard_map/ppermute | solution.py:373
  53.4 3.0 %collective-permute-start.25 = (f32[16,128]{1,0:T(8,128)S(1)}, f32[16,128]{1,0:T(8,128)S(1)}, u32[]{:S(2)}, u32[]{:S(2)}) collective-permute-start(f32[16,128]{1,0:T(8,128)S(1)} %add.60), channel_id=1, source_target_pairs={{0,96},{8,104},{16,112},{24,120},{32,64},{40,72},{48,80},{56,88},{... | collective-permute-start | bytes 24584 | tf_op jit(solution)/shard_map/ppermute | solution.py:373
  53.4 6.0 %collective-permute-start.10 = (f32[1024,256]{1,0:T(8,128)S(1)}, f32[1024,256]{1,0:T(8,128)S(1)}, u32[]{:S(2)}, u32[]{:S(2)}) collective-permute-start(f32[1024,256]{1,0:T(8,128)S(1)} %get-tuple-element.47), channel_id=1, source_target_pairs={{0,6},{1,7},{8,14},{9,15},{16,22},{17,23},{24,30},{25,31},{32,38},... | collective-permute-start | bytes 3145736 | tf_op jit(solution)/shard_map/ppermute | solution.py:388
  54.1 5.2 %collective-permute-start.9 = (f32[1024,256]{1,0:T(8,128)S(1)}, f32[1024,256]{1,0:T(8,128)S(1)}, u32[]{:S(2)}, u32[]{:S(2)}) collective-permute-start(f32[1024,256]{1,0:T(8,128)S(1)} %get-tuple-element.47), channel_id=1, source_target_pairs={{0,2},{1,3},{8,10},{9,11},{16,18},{17,19},{24,26},{25,27},{32,34},... | collective-permute-start | bytes 3145736 | tf_op jit(solution)/shard_map/ppermute | solution.py:387
  56.4 1.4 collective-permute-start.13
  57.1 1.4 collective-permute-start.17
  57.9 5.1 %collective-permute-start.20 = (f32[256,256]{1,0:T(8,128)S(1)}, f32[256,256]{1,0:T(8,128)S(1)}, u32[]{:S(2)}, u32[]{:S(2)}) collective-permute-start(f32[256,256]{1,0:T(8,128)S(1)} %broadcast_select_fusion.11), channel_id=1, source_target_pairs={{0,96},{8,104},{16,112},{24,120},{2,98},{10,106},{18,114},{26,122}... | collective-permute-start | bytes 786440 | tf_op jit(solution)/shard_map/ppermute | solution.py:345
  58.6 5.7 %collective-permute-start.26 = (f32[264,256]{1,0:T(8,128)S(1)}, f32[264,256]{1,0:T(8,128)S(1)}, u32[]{:S(2)}, u32[]{:S(2)}) collective-permute-start(f32[264,256]{1,0:T(8,128)S(1)} %pad_maximum_fusion.1), channel_id=1, source_target_pairs={{8,10},{16,18},{24,26},{0,2},{40,42},{48,50},{56,58},{32,34},{72,7... | collective-permute-start | bytes 811016 | tf_op jit(solution)/shard_map/ppermute | solution.py:345
  60.4 50.6 %collective-permute-start.19 = (f32[512,256]{1,0:T(8,128)}, f32[512,256]{1,0:T(8,128)S(1)}, u32[]{:S(2)}, u32[]{:S(2)}) collective-permute-start(f32[512,256]{1,0:T(8,128)} %get-tuple-element.74), channel_id=1, source_target_pairs={{6,4},{7,5},{14,12},{15,13},{22,20},{23,21},{30,28},{31,29},{38,36... | collective-permute-start | bytes 1572872 | tf_op jit(solution)/shard_map/ppermute | solution.py:392
  61.7 49.4 %collective-permute-start.18 = (f32[512,256]{1,0:T(8,128)S(1)}, f32[512,256]{1,0:T(8,128)}, u32[]{:S(2)}, u32[]{:S(2)}) collective-permute-start(f32[512,256]{1,0:T(8,128)S(1)} %get-tuple-element.75), channel_id=1, source_target_pairs={{2,4},{3,5},{10,12},{11,13},{18,20},{19,21},{26,28},{27,29},{34,36... | collective-permute-start | bytes 1572872 | tf_op jit(solution)/shard_map/ppermute | solution.py:391
  63.1 22.4 %collective-permute-start.21 = (f32[256,256]{1,0:T(8,128)S(1)}, f32[256,256]{1,0:T(8,128)S(1)}, u32[]{:S(2)}, u32[]{:S(2)}) collective-permute-start(f32[256,256]{1,0:T(8,128)S(1)} %broadcast_select_fusion.4.own), channel_id=1, source_target_pairs={{0,1},{2,3},{4,5},{6,7},{8,9},{10,11},{12,13},{14,15},{16,17},{18,... | collective-permute-start | bytes 786440 | tf_op jit(solution)/shard_map/ppermute | solution.py:370
  64.4 46.6 %collective-permute-start.27 = (f32[264,256]{1,0:T(8,128)S(1)}, f32[264,256]{1,0:T(8,128)S(1)}, u32[]{:S(2)}, u32[]{:S(2)}) collective-permute-start(f32[264,256]{1,0:T(8,128)S(1)} %broadcast_select_fusion.2), channel_id=1, source_target_pairs={{8,14},{16,22},{24,30},{0,6},{40,46},{48,54},{56,62},{32,38},{72,7... | collective-permute-start | bytes 811016 | tf_op jit(solution)/shard_map/ppermute | solution.py:345
  112.3 13.1 %collective-permute-start.28 = (f32[1024,256]{1,0:T(8,128)S(1)}, f32[1024,256]{1,0:T(8,128)S(1)}, u32[]{:S(2)}, u32[]{:S(2)}) collective-permute-start(f32[1024,256]{1,0:T(8,128)S(1)} %pad_maximum_fusion.mine), channel_id=1, source_target_pairs={{0,1},{1,0},{2,3},{3,2},{4,5},{5,4},{6,7},{7,6},{8,9},{9,8},{10,11... | collective-permute-start | bytes 3145736 | tf_op jit(solution)/shard_map/ppermute | solution.py:397
  113.4 2.7 %collective-permute-start.29 = (f32[264,256]{1,0:T(8,128)S(1)}, f32[264,256]{1,0:T(8,128)S(1)}, u32[]{:S(2)}, u32[]{:S(2)}) collective-permute-start(f32[264,256]{1,0:T(8,128)S(1)} %broadcast_select_fusion.3.own.own_sums), channel_id=1, source_target_pairs={{0,1},{1,0},{2,3},{3,2},{4,5},{5,4},{6,7},{7,6},{8,9},{9,8},{10,11... | collective-permute-start | bytes 811016 | tf_op jit(solution)/shard_map/ppermute | solution.py:377
Sparse Core Ops, SparseCore 0:
  37.1 57.2 all-gather.2

commit v5 on v4

--- a/solution.py
+++ b/solution.py
@@ -114,13 +114,15 @@
 
 
 def first_kernel(place, own, other, w00, tile, m, part):
-    tile[...] = jnp.where(place[1] % 2 == 0, own[...], other[...])
+    tile[...] = jnp.where(place[1] % 2 == 0, own[0:NB], other[0:NB])
     factor_tile(tile, w00, m, part)
 
 
 def second_kernel(place, w00, own, other, l10, w11, schur, m, part):
     even = place[1] % 2 == 0
-    low = dot6(jnp.where(even, own[0:NB], other[0:NB]), w00[...], NT)
+    top, bottom = own[NB : NB + 128], other[NB : NB + 128]
+    c10 = jnp.concatenate([jnp.where(even, top, bottom), jnp.where(even, bottom, top)], axis=0)
+    low = dot6(c10, w00[...], NT)
     l10[...] = low
     schur[...] = jnp.where(even, other[0:NB], own[0:NB]) - dot6(low, low, NT)
     factor_tile(schur, w11, m, part)
@@ -153,6 +155,8 @@
 
 
 def corner_kernel(a, *pieces):
+    *pieces, flipped = pieces
+    flipped[...] = a[:, 1, :].T
     for q in range(16):
         value = a[:, q, :]
         for ref in pieces[q // 2 :: 8]:
@@ -161,22 +165,17 @@
 
 def corner_call(flat):
     return pl.pallas_call(
-        corner_kernel, grid=(2,), out_shape=(TILE,) * 9,
+        corner_kernel, grid=(2,), out_shape=(TILE,) * 9 + (jax.ShapeDtypeStruct((128, NB), F32),),
         in_specs=[pl.BlockSpec((128, 16, 128), lambda i: (i, 0, 0))],
-        out_specs=(pl.BlockSpec((128, NB), lambda i: (i, 0)),) * 9,
+        out_specs=(pl.BlockSpec((128, NB), lambda i: (i, 0)),) * 9 + (pl.BlockSpec((128, 128), lambda i: (0, i)),),
         name="corner_tiles",
     )(flat)
 
 
-def column_kernel(weights, a, column, again, sums):
+def column_kernel(weights, a, column, sums):
     step = pl.program_id(0)
     for q in range(2):
-        value = a[:, q, :]
-        column[:, 128 * q : 128 * q + 128] = value
-
-        @pl.when(step < 2)
-        def _():
-            again[:, 128 * q : 128 * q + 128] = value
+        column[:, 128 * q : 128 * q + 128] = a[:, q, :]
 
     @pl.when(step == 0)
     def _():
@@ -194,11 +193,10 @@
 def column_call(weights, flat):
     return pl.pallas_call(
         column_kernel, grid=(8,),
-        out_shape=(jax.ShapeDtypeStruct((1024, NB), F32), TILE, jax.ShapeDtypeStruct((16, 128), F32)),
+        out_shape=(jax.ShapeDtypeStruct((1024, NB), F32), jax.ShapeDtypeStruct((16, 128), F32)),
         in_specs=[SMEM, pl.BlockSpec((128, 16, 128), lambda i: (i, 0, 0))],
         out_specs=(
             pl.BlockSpec((128, NB), lambda i: (i, 0)),
-            pl.BlockSpec((128, NB), lambda i: (jnp.minimum(i, 1), 0)),
             pl.BlockSpec((16, 128), lambda i: (0, 0)),
         ),
         name="first_column", **FACTOR,
@@ -230,27 +228,27 @@
     high[:, 256:512] = last_high[0:512]
     low[:, 256:512] = last_low[0:512]
     high[:, 0:256], low[:, 0:256] = halves(rest[0:512])
-    taken[:, 0:256] = rest[512:520]
-    taken[:, 256:512] = last[512:520]
-
-
-def panel_call(place, mine, theirs, below, other, w00, l10, w11):
+    taken[:, 0:256] = rest[512:528]
+    taken[:, 256:512] = last[512:528]
+
+
+def panel_call(place, mine, theirs, w00, l10, w11):
     full = lambda *shape: pl.BlockSpec(shape, lambda i: (0,) * len(shape))
     part = lambda n: pl.BlockSpec((512, n), lambda i: (i, 0))
-    tail = pl.BlockSpec((8, NB), lambda i: (NB // 8, 0))
+    tail = pl.BlockSpec((16, NB), lambda i: (1024 // 16, 0))
     return pl.pallas_call(
         panel_kernel, grid=(2,),
         out_shape=(
             jax.ShapeDtypeStruct((1024, 512), F32),
             jax.ShapeDtypeStruct((1024, 512), BF16),
             jax.ShapeDtypeStruct((1024, 512), BF16),
-            jax.ShapeDtypeStruct((8, 512), F32),
+            jax.ShapeDtypeStruct((16, 512), F32),
         ),
         in_specs=[SMEM, part(NB), part(NB), tail, tail, full(NB, NB), full(NB, NB), full(NB, NB)],
-        out_specs=(part(512), part(512), part(512), full(8, 512)),
+        out_specs=(part(512), part(512), part(512), full(16, 512)),
         scratch_shapes=[pltpu.VMEM((2, 3, NB, NB), BF16)],
         name="panel_solve", **FACTOR,
-    )(place, mine, theirs, below, other, w00, l10, w11)
+    )(place, mine, theirs, mine, theirs, w00, l10, w11)
 
 
 def update_kernel(place, flat, across, high, low, sums, taken, out, checksum, right_high, right_low):
@@ -259,30 +257,33 @@
 
     @pl.when(step == 0)
     def _():
-        y = halves(taken[...])
         for u in range(4):
             for h in range(2):
                 span = slice(NB * h, NB * h + NB)
                 right_high[u, span], right_low[u, span] = halves(across[2 * u + h])
-            part = dot3(y, (right_high[u], right_low[u]), NN)[0:1]
-            for h in range(2):
-                q = 2 * u + h
-                kept = sums[pl.ds(8 * group + q, 1), :] - part[:, 128 * h : 128 * h + 128]
-                if u == 0:
-                    kept = jnp.where((group == 0) & (col_index < 2), 0.0, kept)
-                checksum[pl.ds(8 * group + q, 1), :] = kept
 
     rows = out.shape[0]
     base = pl.multiple_of(step * rows, rows)
     top = (step * rows + lax.broadcasted_iota(jnp.int32, (rows, 1), 0) < NB) & (row_index < 2)
-    mine = high[pl.ds(base, rows), :], low[pl.ds(base, rows), :]
+    y_high, y_low = halves(taken[...])
+    mine = (
+        jnp.concatenate([high[pl.ds(base, rows), :], y_high], axis=0),
+        jnp.concatenate([low[pl.ds(base, rows), :], y_low], axis=0),
+    )
     for u in range(4):
         product = dot3(mine, (right_high[u], right_low[u]), NN)
         gone = top | ((group == 0) & (col_index < 2)) if u == 0 else top
         for h in range(2):
             q = 2 * u + h
-            value = flat[:, q, :] - product[:, 128 * h : 128 * h + 128]
+            value = flat[:, q, :] - product[0:rows, 128 * h : 128 * h + 128]
             out[:, q, :] = jnp.where(gone, 0.0, value)
+
+            @pl.when(step == 0)
+            def _():
+                kept = sums[pl.ds(8 * group + q, 1), :] - product[rows : rows + 1, 128 * h : 128 * h + 128]
+                if u == 0:
+                    kept = jnp.where((group == 0) & (col_index < 2), 0.0, kept)
+                checksum[pl.ds(8 * group + q, 1), :] = kept
 
 
 def update_call(place, flat, across, high, low, sums, taken):
@@ -298,7 +299,7 @@
             full(1024, 512),
             full(1024, 512),
             full(16, 128),
-            full(8, 512),
+            full(16, 512),
         ],
         out_specs=(pl.BlockSpec((rows, 8, 128), lambda g, i: (i, g, 0)), full(16, 128)),
         scratch_shapes=[pltpu.VMEM((4, 512, NB), BF16), pltpu.VMEM((4, 512, NB), BF16)],
@@ -321,18 +322,12 @@
     return device_at(*at)
 
 
-def spread(value, trees, here, gates=None, cargo=None):
-    core = here[3]
+def spread(value, trees, here):
     holders = [[device_at(z, y, 0, c)] for (z, y), c, _ in trees]
     stages = []
     for at in range(3):
-        if at == 2 and cargo is not None:
-            value = jnp.concatenate([value, cargo], axis=0)
-        aways = []
-        for (z, y), c, dims in trees:
-            start = (z, y, 0)
-            aways.append((c, (here[dims[at]] - start[dims[at]]) % 4))
-        away = aways[0][1] if len(trees) == 1 else jnp.where(core == aways[0][0], aways[0][1], aways[1][1])
+        aways = [(here[dims[at]] - (z, y, 0)[dims[at]]) % 4 for (z, y), _, dims in trees]
+        away = jnp.where(here[3] == trees[0][1], aways[0], aways[1])
         for half in range(2):
             pairs = []
             for held, (_, _, dims) in zip(holders, trees):
@@ -341,9 +336,8 @@
                     pairs += [(h, moved(h, dim, 1)) for h in held]
                 else:
                     pairs += [(h, moved(h, dim, -1)) for h in held] + [(moved(h, dim, 1), moved(h, dim, 2)) for h in held]
-            sent = value if gates is None else after(value, gates[2 * at + half])
-            arrived = lax.ppermute(sent, ("row", "col"), pairs)
-            value = jnp.where((away == 1) if half == 0 else (away >= 2), arrived, sent)
+            arrived = lax.ppermute(value, ("row", "col"), pairs)
+            value = jnp.where((away == 1) if half == 0 else (away >= 2), arrived, value)
             stages.append(value)
         holders = [[moved(h, dims[at], k) for h in held for k in range(4)] for held, (_, _, dims) in zip(holders, trees)]
     return stages
@@ -366,37 +360,46 @@
     swap_cores = [(c, c ^ 1) for c in range(8)]
 
     pieces = corner_call(flat)
-    tree0 = spread(pieces[0], [((0, 0), 0, (2, 1, 0))], here)
-    c00_other = lax.ppermute(tree0[-1], "col", [(c, c + 1) for c in (0, 2, 4, 6)])
-    column, corner, sums = column_call(weights, after(flat, tree0[1]))
-    for d in (1, 3, 4, 12):
-        sums = sums + lax.ppermute(sums, "row", [(r, r ^ d) for r in range(16)])
-    panel_sums = jnp.broadcast_to(sums[0:2].reshape(1, NB), (8, NB))
-    tree1 = spread(pieces[8], [((0, 1), 0, (0, 1, 2)), ((0, 1), 1, (1, 0, 2))], here, tree0, panel_sums)
-    below = tree1[-1]
-    below_other = lax.ppermute(below, "col", swap_cores)
-
-    piece = corner
+    fetched = lax.ppermute(pieces[0], ("row", "col"), [(8, 0), (9, 1)])
+    corner = jnp.where(
+        core == 0,
+        jnp.concatenate([pieces[0], fetched[0:128]], axis=0),
+        jnp.concatenate([fetched, pieces[9]], axis=0),
+    )
+    tree = spread(corner, [((0, 0), 0, (2, 1, 0)), ((0, 0), 1, (1, 0, 2))], here)
+    own = tree[-1]
+    other = lax.ppermute(own, "col", swap_cores)
+
+    piece = pieces[8]
     for j in range(1, 8):
         piece = jnp.where(row // 2 == j, lax.ppermute(pieces[j], "row", [(0, 2 * j), (1, 2 * j + 1)]), piece)
-    across = lax.all_gather(after(piece, tree0[1]), "row", axis=0)
+    across = lax.all_gather(after(piece, tree[0]), "row", axis=0)
     across = pltpu.with_memory_space_constraint(across, pltpu.HBM)
 
-    w00 = first_factor(place, tree0[-1], c00_other)
-    l10, w11 = second_factor(place, w00, below, below_other)
+    column, sums = column_call(weights, after(flat, corner))
+    for d, stage in ((1, 1), (3, 2), (4, 3), (12, 4)):
+        sums = sums + lax.ppermute(after(sums, tree[stage]), "row", [(r, r ^ d) for r in range(16)])
+    near_sums = jnp.broadcast_to(sums[0:2].reshape(1, NB), (16, NB))
+    panel_sums = near_sums
+    for k in (1, 2, 3):
+        arrived = lax.ppermute(near_sums, "col", [(0, 2 * k), (1, 2 * k + 1)])
+        panel_sums = jnp.where(x == k, arrived, panel_sums)
+
+    w00 = first_factor(place, own, other)
+    l10, w11 = second_factor(place, w00, own, other)
     from_left = lax.ppermute(column, "col", [(0, 2), (1, 3)])
     from_right = lax.ppermute(column, "col", [(0, 6), (1, 7)])
-    from_left, from_right = after((from_left, from_right), (tree0[4], tree1[3]))
+    from_left, from_right = after((from_left, from_right), tree[5])
     mine = jnp.where(x == 1, from_left, jnp.where(x == 3, from_right, column))
     upper = lax.ppermute(mine[0:512], "col", [(2, 4), (3, 5)])
     lower = lax.ppermute(mine[512:1024], "col", [(6, 4), (7, 5)])
-    upper, lower = after((upper, lower), (w00, tree1[-1]))
+    upper, lower = after((upper, lower), w00)
     upper = jnp.where(x == 2, upper, mine[0:512])
     lower = jnp.where(x == 2, lower, mine[512:1024])
-    mine = jnp.concatenate([upper, lower], axis=0)
+    mine = jnp.concatenate([upper, lower, panel_sums], axis=0)
     theirs = after(lax.ppermute(mine, "col", swap_cores), w11)
 
-    panels, high, low, taken = panel_call(place, mine, theirs, below, below_other, w00, l10, w11)
+    panels, high, low, taken = panel_call(place, mine, theirs, w00, l10, w11)
     trailing, checksum = update_call(place, flat, across, high, low, sums, taken)
     return (
         trailing.reshape(4, 1, NB, 8, 1, NB),

time: 160 us -> 187 us (1.17)
  the two profiles are of different devices: /device:TPU:37 before, /device:TPU:1 now
where the time goes in v5:
time: 187 us; the launch traced here: 186 us
  Pallas kernels  62.7 us (34%)
  starting transfers between devices  59 us (32%)
  waiting for transfers between devices  45.2 us (24%)
  between operations  14.5 us (8%)
  other arithmetic  2.74 us (1%)
  local copies, waits for them, and re-layouts  1.94 us (1%)
    ppermute x6, waiting for transfers between devices, spread(): arrived = lax.ppermute(value, ('row', 'col'), pairs)  30.7 us
    pallas_call x1, Pallas kernels, update_call(): pl.pallas_call(update_kernel, grid=(2, 1024 // rows), out_shape=(jax.Shap...  28.5 us
    ppermute x7, starting transfers between devices, shards(): lax.ppermute(pieces[j], 'row', [(0, 2 * j), (1, 2 * j + 1)])  17.1 us
    ppermute x6, starting transfers between devices, spread(): arrived = lax.ppermute(value, ('row', 'col'), pairs)  16.3 us
    pallas_call x1, Pallas kernels, second_factor(): pl.pallas_call(second_kernel, out_shape=(TILE, TILE), in_specs=[SMEM, VME...  9.31 us
    ppermute x4, starting transfers between devices, shards(): lax.ppermute(after(sums, tree[stage]), 'row', [(r, r ^ d) for r in range(...  8.63 us
    pallas_call x1, Pallas kernels, first_factor(): pl.pallas_call(first_kernel, out_shape=TILE, in_specs=[SMEM, VMEM, VMEM],...  8.22 us
    ppermute x3, starting transfers between devices, shards(): arrived = lax.ppermute(near_sums, 'col', [(0, 2 * k), (1, 2 * k + 1)])  8.18 us
  transfers between devices with their start and end apart: 28, of which 12 were waited for; matrix products, arithmetic and copies ran while one was open for 2% of the time, Pallas kernels for 17%

profile of v5, /device:TPU:1, one launch (start us, length us, event | category | flops | bytes accessed | tf_op | source)
XLA Modules:
  0.0 186.1 jit_solution(15829059744361108094)
XLA Ops:
  7.2 3.3 %corner_tiles.1 = (f32[256,256]{1,0:T(8,128)}, f32[256,256]{1,0:T(8,128)}, f32[256,256]{1,0:T(8,128)}, f32[256,256]{1,0:T(8,128)}, f32[256,256]{1,0:T(8,128)}, /...) custom-call(f32[1024,16,128]{2,1,0:T(8,128)} %bitcast.12), custom_call_target="tpu_custom_call" | custom-call | tf_op jit(solution)/shard_map/corner_tiles/pallas_call | solution.py:167
  10.5 9.3 %collective-permute-start = (f32[256,256]{1,0:T(8,128)}, f32[256,256]{1,0:T(8,128)S(1)}, u32[]{:S(2)}, u32[]{:S(2)}) collective-permute-start(f32[256,256]{1,0:T(8,128)} %get-tuple-element.34), channel_id=1, source_target_pairs={{0,112},{8,120},{1,113},{9,121},{2,114},{10,122},{3,115},{11,123},... | collective-permute-start | bytes 786440 | tf_op jit(solution)/shard_map/ppermute | solution.py:375
  19.8 1.3 collective-permute-start.1
  21.1 1.3 collective-permute-start.7
  22.4 1.3 collective-permute-start.2
  23.7 1.3 collective-permute-start.3
  25.0 1.3 collective-permute-start.4
  26.4 1.3 collective-permute-start.5
  27.7 4.0 %collective-permute-done.7 = f32[256,256]{1,0:T(8,128)S(1)} collective-permute-done((f32[256,256]{1,0:T(8,128)}, f32[256,256]{1,0:T(8,128)S(1)}, u32[]{:S(2)}, u32[]{:S(2)}) %collective-permute-start.7) | collective-permute-done | bytes 262176 | tf_op jit(solution)/shard_map/ppermute | solution.py:363
  31.7 1.3 collective-permute-start.6
  33.0 1.0 maximum_select_fusion
  34.1 4.5 %collective-permute-start.8 = (f32[384,256]{1,0:T(8,128)S(1)}, f32[384,256]{1,0:T(8,128)S(1)}, u32[]{:S(2)}, u32[]{:S(2)}) collective-permute-start(f32[384,256]{1,0:T(8,128)S(1)} %maximum_select_fusion), channel_id=1, source_target_pairs={{0,2},{1,9}} | collective-permute-start | bytes 1179656 | tf_op jit(solution)/shard_map/ppermute | solution.py:339
  38.7 3.2 %collective-permute-done.6 = f32[256,256]{1,0:T(8,128)S(1)} collective-permute-done((f32[256,256]{1,0:T(8,128)}, f32[256,256]{1,0:T(8,128)S(1)}, u32[]{:S(2)}, u32[]{:S(2)}) %collective-permute-start.6) | collective-permute-done | bytes 262176 | tf_op jit(solution)/shard_map/ppermute | solution.py:375
  41.9 0.8 select_select_fusion.1
  42.7 4.4 %collective-permute-done.8 = f32[384,256]{1,0:T(8,128)S(1)} collective-permute-done((f32[384,256]{1,0:T(8,128)S(1)}, f32[384,256]{1,0:T(8,128)S(1)}, u32[]{:S(2)}, u32[]{:S(2)}) %collective-permute-start.8) | collective-permute-done | bytes 393248 | tf_op jit(solution)/shard_map/ppermute | solution.py:339
  47.2 6.5 %collective-permute-start.11 = (f32[384,256]{1,0:T(8,128)S(1)}, f32[384,256]{1,0:T(8,128)S(1)}, u32[]{:S(2)}, u32[]{:S(2)}) collective-permute-start(f32[384,256]{1,0:T(8,128)S(1)} %broadcast_select_fusion.7), channel_id=1, source_target_pairs={{0,6},{2,4},{1,25},{9,17}} | collective-permute-start | bytes 1179656 | tf_op jit(solution)/shard_map/ppermute | solution.py:339
  53.8 6.1 %collective-permute-done.11 = f32[384,256]{1,0:T(8,128)S(1)} collective-permute-done((f32[384,256]{1,0:T(8,128)S(1)}, f32[384,256]{1,0:T(8,128)S(1)}, u32[]{:S(2)}, u32[]{:S(2)}) %collective-permute-start.11) | collective-permute-done | bytes 393248 | tf_op jit(solution)/shard_map/ppermute | solution.py:339
  59.9 1.3 collective-permute-start.12
  61.3 7.2 %collective-permute-done.12 = f32[384,256]{1,0:T(8,128)S(1)} collective-permute-done((f32[384,256]{1,0:T(8,128)S(1)}, f32[384,256]{1,0:T(8,128)S(1)}, u32[]{:S(2)}, u32[]{:S(2)}) %collective-permute-start.12) | collective-permute-done | bytes 393248 | tf_op jit(solution)/shard_map/ppermute | solution.py:339
  68.6 1.3 collective-permute-start.13
  69.9 4.7 %collective-permute-done.13 = f32[384,256]{1,0:T(8,128)S(1)} collective-permute-done((f32[384,256]{1,0:T(8,128)S(1)}, f32[384,256]{1,0:T(8,128)S(1)}, u32[]{:S(2)}, u32[]{:S(2)}) %collective-permute-start.13) | collective-permute-done | bytes 393248 | tf_op jit(solution)/shard_map/ppermute | solution.py:339
  74.6 1.3 collective-permute-start.14
  76.1 6.9 %first_column.1 = (f32[1024,256]{1,0:T(8,128)S(1)}, f32[16,128]{1,0:T(8,128)S(1)}) custom-call(f32[1024]{0:T(1024)S(1)} %broadcast_select_fusion.8.weights, f32[1024,16,128]{2,1,0:T(8,128)} %bitcast.13), custom_call_target="tpu_custom_call" | custom-call | flops 100000000 | bytes 100000 | tf_op jit(solution)/shard_map/first_column/pallas_call | solution.py:194
  82.9 1.4 collective-permute-start.10
  84.3 2.3 %collective-permute-start.9 = (f32[1024,256]{1,0:T(8,128)S(1)}, f32[1024,256]{1,0:T(8,128)}, u32[]{:S(2)}, u32[]{:S(2)}) collective-permute-start(f32[1024,256]{1,0:T(8,128)S(1)} %get-tuple-element.46), channel_id=1, source_target_pairs={{0,2},{1,3},{8,10},{9,11},{16,18},{17,19},{24,26},{25,27},{32,34},... | collective-permute-start | bytes 3145736 | tf_op jit(solution)/shard_map/ppermute | solution.py:390
  86.7 1.3 collective-permute-start.15
  88.1 2.9 %collective-permute-done.19 = f32[16,128]{1,0:T(8,128)S(1)} collective-permute-done((f32[16,128]{1,0:T(8,128)S(1)}, f32[16,128]{1,0:T(8,128)S(1)}, u32[]{:S(2)}, u32[]{:S(2)}) %collective-permute-start.19) | collective-permute-done | bytes 8224 | tf_op jit(solution)/shard_map/ppermute | solution.py:381
  91.0 3.2 %collective-permute-start.20 = (f32[16,128]{1,0:T(8,128)S(1)}, f32[16,128]{1,0:T(8,128)S(1)}, u32[]{:S(2)}, u32[]{:S(2)}) collective-permute-start(f32[16,128]{1,0:T(8,128)S(1)} %add.51), channel_id=1, source_target_pairs={{0,24},{8,16},{16,8},{24,0},{32,56},{40,48},{48,40},{56,32},{64,88... | collective-permute-start | bytes 24584 | tf_op jit(solution)/shard_map/ppermute | solution.py:381
  94.2 1.4 collective-permute-done.20
  95.6 2.4 %collective-permute-start.21 = (f32[16,128]{1,0:T(8,128)S(1)}, f32[16,128]{1,0:T(8,128)S(1)}, u32[]{:S(2)}, u32[]{:S(2)}) collective-permute-start(f32[16,128]{1,0:T(8,128)S(1)} %add.52), channel_id=1, source_target_pairs={{0,32},{8,40},{16,48},{24,56},{32,0},{40,8},{48,16},{56,24},{64,96... | collective-permute-start | bytes 24584 | tf_op jit(solution)/shard_map/ppermute | solution.py:381
  98.0 1.0 collective-permute-done.21
  99.1 2.9 %collective-permute-start.22 = (f32[16,128]{1,0:T(8,128)S(1)}, f32[16,128]{1,0:T(8,128)S(1)}, u32[]{:S(2)}, u32[]{:S(2)}) collective-permute-start(f32[16,128]{1,0:T(8,128)S(1)} %add.53), channel_id=1, source_target_pairs={{0,96},{8,104},{16,112},{24,120},{32,64},{40,72},{48,80},{56,88},{... | collective-permute-start | bytes 24584 | tf_op jit(solution)/shard_map/ppermute | solution.py:381
  102.0 1.0 collective-permute-done.22
  103.0 8.4 %collective-permute-done.15 = f32[384,256]{1,0:T(8,128)S(1)} collective-permute-done((f32[384,256]{1,0:T(8,128)S(1)}, f32[384,256]{1,0:T(8,128)S(1)}, u32[]{:S(2)}, u32[]{:S(2)}) %collective-permute-start.15) | collective-permute-done | bytes 393248 | tf_op jit(solution)/shard_map/ppermute | solution.py:339
  111.6 1.0 copy-done
  112.5 0.2 select_select_fusion
  112.7 0.9 fusion
  113.6 0.7 collective-permute-start.17
  114.3 1.5 collective-permute-start.16
  115.8 1.3 collective-permute-start.25
  117.0 1.3 collective-permute-start.24
  118.4 5.6 %collective-permute-start.23 = (f32[16,256]{1,0:T(8,128)S(1)}, f32[16,256]{1,0:T(8,128)S(1)}, u32[]{:S(2)}, u32[]{:S(2)}) collective-permute-start(f32[16,256]{1,0:T(8,128)S(1)} %broadcast_in_dim.26), channel_id=1, source_target_pairs={{0,6},{1,7},{8,14},{9,15},{16,22},{17,23},{24,30},{25,31},{32,38},... | collective-permute-start | bytes 49160 | tf_op jit(solution)/shard_map/ppermute | solution.py:385
  124.1 0.8 collective-permute-done.23
  124.8 8.2 %first_factor.1.w00 = f32[256,256]{1,0:T(8,128)S(1)} custom-call(s32[2]{0:T(128)S(1)} %pad_add_fusion.place, f32[384,256]{1,0:T(8,128)S(1)} %broadcast_select_fusion.6.own, f32[384,256]{1,0:T(8,128)S(1)} %collective-permute-done.18.other), custom_call_target="tpu_custom_call" | custom-call | flops 100000000 | bytes 100000 | tf_op jit(solution)/shard_map/first_factor/pallas_call | solution.py:144
  133.3 1.6 collective-permute-start.26
  134.9 9.3 %second_factor.1 = (f32[256,256]{1,0:T(8,128)S(1)}, f32[256,256]{1,0:T(8,128)S(1)}) custom-call(s32[2]{0:T(128)S(1)} %pad_add_fusion.place, f32[256,256]{1,0:T(8,128)S(1)} %first_factor.1.w00, f32[384,256]{1,0:T(8,128)S(1)} %broadcast_select_fusion.6.own, f32[384,256]{1,0:T(8,128)S(1)} %collective-permute-done.18.other), custom_call_target="tpu_custom_call" | custom-call | flops 100000000 | bytes 100000 | tf_op jit(solution)/shard_map/second_factor/pallas_call | solution.py:151
  144.3 6.5 %panel_solve.1 = (f32[1024,512]{1,0:T(8,128)}, bf16[1024,512]{1,0:T(8,128)(2,1)S(1)}, bf16[1024,512]{1,0:T(8,128)(2,1)S(1)}, f32[16,512]{1,0:T(8,128)S(1)}) custom-call(s32[2]{0:T(128)S(1)} %pad_add_fusion.place, f32[1040,256]{1,0:T(8,128)S(1)} %pad_maximum_fusion.mine.own_sums, f32[1040,256]{1,0:T(8,128)S(1)} %collective-permute-done.26.theirs.other_sums, ...), custom_call_target="tpu_custom_call" | custom-call | flops 100000000 | bytes 100000 | tf_op jit(solution)/shard_map/panel_solve/pallas_call | solution.py:239
  150.8 28.5 %trailing_update.1 = (f32[1024,16,128]{2,1,0:T(8,128)}, f32[16,128]{1,0:T(8,128)}) custom-call(s32[2]{0:T(128)S(1)} %pad_add_fusion.place, f32[1024,16,128]{2,1,0:T(8,128)} %bitcast.14, f32[16,256,256]{2,1,0:T(8,128)} %bitcast.15, bf16[1024,512]{1,0:T(8,128)(2,1)S(1)} %get-tuple-element.59.high, bf16[1024,512]{1,0:T(8,128)(2,1)S(1)} %get-tuple-element.60.low, ...), custom_call_target="tpu_custom_call" | custom-call | flops 100000000 | bytes 100000 | tf_op jit(solution)/shard_map/trailing_update/pallas_call | solution.py:292
  (46 shorter events, 1.1 us)
Async XLA Ops:
  7.2 143.6 %all-gather.3.cloned.1.call-start = ((), (), s32[]{:S(2)}) async-start(), calls=%async_computation | async-start | bytes 4456448 | tf_op jit(solution)/shard_map/all_gather | solution.py:376
  10.5 31.4 %copy-start.1 = (f32[256,256]{1,0:T(8,128)S(1)}, f32[256,256]{1,0:T(8,128)}, u32[]{:S(2)}) copy-start(f32[256,256]{1,0:T(8,128)} %get-tuple-element.41) | copy-start | bytes 786436
  10.5 14.5 %collective-permute-start = (f32[256,256]{1,0:T(8,128)}, f32[256,256]{1,0:T(8,128)S(1)}, u32[]{:S(2)}, u32[]{:S(2)}) collective-permute-start(f32[256,256]{1,0:T(8,128)} %get-tuple-element.34), channel_id=1, source_target_pairs={{0,112},{8,120},{1,113},{9,121},{2,114},{10,122},{3,115},{11,123},... | collective-permute-start | bytes 786440 | tf_op jit(solution)/shard_map/ppermute | solution.py:375
  19.8 6.6 %collective-permute-start.1 = (f32[256,256]{1,0:T(8,128)}, f32[256,256]{1,0:T(8,128)S(1)}, u32[]{:S(2)}, u32[]{:S(2)}) collective-permute-start(f32[256,256]{1,0:T(8,128)} %get-tuple-element.35), channel_id=1, source_target_pairs={{0,96},{8,104},{1,97},{9,105},{2,98},{10,106},{3,99},{11,107},{4,1... | collective-permute-start | bytes 786440 | tf_op jit(solution)/shard_map/ppermute | solution.py:375
  21.1 10.6 %collective-permute-start.7 = (f32[256,256]{1,0:T(8,128)}, f32[256,256]{1,0:T(8,128)S(1)}, u32[]{:S(2)}, u32[]{:S(2)}) collective-permute-start(f32[256,256]{1,0:T(8,128)} %get-tuple-element.42), channel_id=1, source_target_pairs={{8,0},{9,1}} | collective-permute-start | bytes 786440 | tf_op jit(solution)/shard_map/ppermute | solution.py:363
  22.4 11.7 %collective-permute-start.2 = (f32[256,256]{1,0:T(8,128)}, f32[256,256]{1,0:T(8,128)S(1)}, u32[]{:S(2)}, u32[]{:S(2)}) collective-permute-start(f32[256,256]{1,0:T(8,128)} %get-tuple-element.36), channel_id=1, source_target_pairs={{0,80},{8,88},{1,81},{9,89},{2,82},{10,90},{3,83},{11,91},{4,84},{... | collective-permute-start | bytes 786440 | tf_op jit(solution)/shard_map/ppermute | solution.py:375
  23.7 15.0 %collective-permute-start.3 = (f32[256,256]{1,0:T(8,128)}, f32[256,256]{1,0:T(8,128)S(1)}, u32[]{:S(2)}, u32[]{:S(2)}) collective-permute-start(f32[256,256]{1,0:T(8,128)} %get-tuple-element.37), channel_id=1, source_target_pairs={{0,64},{8,72},{1,65},{9,73},{2,66},{10,74},{3,67},{11,75},{4,68},{... | collective-permute-start | bytes 786440 | tf_op jit(solution)/shard_map/ppermute | solution.py:375
  25.0 13.7 %collective-permute-start.4 = (f32[256,256]{1,0:T(8,128)}, f32[256,256]{1,0:T(8,128)S(1)}, u32[]{:S(2)}, u32[]{:S(2)}) collective-permute-start(f32[256,256]{1,0:T(8,128)} %get-tuple-element.38), channel_id=1, source_target_pairs={{0,48},{8,56},{1,49},{9,57},{2,50},{10,58},{3,51},{11,59},{4,52},{... | collective-permute-start | bytes 786440 | tf_op jit(solution)/shard_map/ppermute | solution.py:375
  26.4 12.4 %collective-permute-start.5 = (f32[256,256]{1,0:T(8,128)}, f32[256,256]{1,0:T(8,128)S(1)}, u32[]{:S(2)}, u32[]{:S(2)}) collective-permute-start(f32[256,256]{1,0:T(8,128)} %get-tuple-element.39), channel_id=1, source_target_pairs={{0,32},{8,40},{1,33},{9,41},{2,34},{10,42},{3,35},{11,43},{4,36},{... | collective-permute-start | bytes 786440 | tf_op jit(solution)/shard_map/ppermute | solution.py:375
  31.7 10.2 %collective-permute-start.6 = (f32[256,256]{1,0:T(8,128)}, f32[256,256]{1,0:T(8,128)S(1)}, u32[]{:S(2)}, u32[]{:S(2)}) collective-permute-start(f32[256,256]{1,0:T(8,128)} %get-tuple-element.40), channel_id=1, source_target_pairs={{0,16},{8,24},{1,17},{9,25},{2,18},{10,26},{3,19},{11,27},{4,20},{... | collective-permute-start | bytes 786440 | tf_op jit(solution)/shard_map/ppermute | solution.py:375
  34.1 13.1 %collective-permute-start.8 = (f32[384,256]{1,0:T(8,128)S(1)}, f32[384,256]{1,0:T(8,128)S(1)}, u32[]{:S(2)}, u32[]{:S(2)}) collective-permute-start(f32[384,256]{1,0:T(8,128)S(1)} %maximum_select_fusion), channel_id=1, source_target_pairs={{0,2},{1,9}} | collective-permute-start | bytes 1179656 | tf_op jit(solution)/shard_map/ppermute | solution.py:339
  47.2 12.6 %collective-permute-start.11 = (f32[384,256]{1,0:T(8,128)S(1)}, f32[384,256]{1,0:T(8,128)S(1)}, u32[]{:S(2)}, u32[]{:S(2)}) collective-permute-start(f32[384,256]{1,0:T(8,128)S(1)} %broadcast_select_fusion.7), channel_id=1, source_target_pairs={{0,6},{2,4},{1,25},{9,17}} | collective-permute-start | bytes 1179656 | tf_op jit(solution)/shard_map/ppermute | solution.py:339
  59.9 8.6 %collective-permute-start.12 = (f32[384,256]{1,0:T(8,128)S(1)}, f32[384,256]{1,0:T(8,128)S(1)}, u32[]{:S(2)}, u32[]{:S(2)}) collective-permute-start(f32[384,256]{1,0:T(8,128)S(1)} %broadcast_select_fusion.2), channel_id=1, source_target_pairs={{0,8},{2,10},{4,12},{6,14},{1,33},{9,41},{17,49},{25,57}} | collective-permute-start | bytes 1179656 | tf_op jit(solution)/shard_map/ppermute | solution.py:339
  61.3 14.8 %copy-start.2 = (f32[4,1,256]{2,1,0:T(1,128)S(1)}, f32[4,1,256]{2,1,0:T(1,128)}, u32[]{:S(2)}) copy-start(f32[4,1,256]{2,1,0:T(1,128)} %param.3) | copy-start | bytes 12292
  68.6 6.0 %collective-permute-start.13 = (f32[384,256]{1,0:T(8,128)S(1)}, f32[384,256]{1,0:T(8,128)S(1)}, u32[]{:S(2)}, u32[]{:S(2)}) collective-permute-start(f32[384,256]{1,0:T(8,128)S(1)} %broadcast_select_fusion.3), channel_id=1, source_target_pairs={{0,24},{2,26},{4,28},{6,30},{8,16},{10,18},{12,20},{14,22},{1,97},... | collective-permute-start | bytes 1179656 | tf_op jit(solution)/shard_map/ppermute | solution.py:339
  74.6 12.0 %collective-permute-start.14 = (f32[384,256]{1,0:T(8,128)S(1)}, f32[384,256]{1,0:T(8,128)S(1)}, u32[]{:S(2)}, u32[]{:S(2)}) collective-permute-start(f32[384,256]{1,0:T(8,128)S(1)} %broadcast_select_fusion.4), channel_id=1, source_target_pairs={{0,32},{8,40},{16,48},{24,56},{2,34},{10,42},{18,50},{26,58},{4,36... | collective-permute-start | bytes 1179656 | tf_op jit(solution)/shard_map/ppermute | solution.py:339
  82.9 28.6 %collective-permute-start.10 = (f32[1024,256]{1,0:T(8,128)S(1)}, f32[1024,256]{1,0:T(8,128)S(1)}, u32[]{:S(2)}, u32[]{:S(2)}) collective-permute-start(f32[1024,256]{1,0:T(8,128)S(1)} %get-tuple-element.46), channel_id=1, source_target_pairs={{0,6},{1,7},{8,14},{9,15},{16,22},{17,23},{24,30},{25,31},{32,38},... | collective-permute-start | bytes 3145736 | tf_op jit(solution)/shard_map/ppermute | solution.py:391
  84.3 28.2 %collective-permute-start.9 = (f32[1024,256]{1,0:T(8,128)S(1)}, f32[1024,256]{1,0:T(8,128)}, u32[]{:S(2)}, u32[]{:S(2)}) collective-permute-start(f32[1024,256]{1,0:T(8,128)S(1)} %get-tuple-element.46), channel_id=1, source_target_pairs={{0,2},{1,3},{8,10},{9,11},{16,18},{17,19},{24,26},{25,27},{32,34},... | collective-permute-start | bytes 3145736 | tf_op jit(solution)/shard_map/ppermute | solution.py:390
  86.7 24.7 %collective-permute-start.15 = (f32[384,256]{1,0:T(8,128)S(1)}, f32[384,256]{1,0:T(8,128)S(1)}, u32[]{:S(2)}, u32[]{:S(2)}) collective-permute-start(f32[384,256]{1,0:T(8,128)S(1)} %broadcast_select_fusion.5), channel_id=1, source_target_pairs={{0,96},{8,104},{16,112},{24,120},{2,98},{10,106},{18,114},{26,122}... | collective-permute-start | bytes 1179656 | tf_op jit(solution)/shard_map/ppermute | solution.py:339
  88.0 3.0 %collective-permute-start.19 = (f32[16,128]{1,0:T(8,128)S(1)}, f32[16,128]{1,0:T(8,128)S(1)}, u32[]{:S(2)}, u32[]{:S(2)}) collective-permute-start(f32[16,128]{1,0:T(8,128)S(1)} %get-tuple-element.52), channel_id=1, source_target_pairs={{0,8},{8,0},{16,24},{24,16},{32,40},{40,32},{48,56},{56,48},{64,72... | collective-permute-start | bytes 24584 | tf_op jit(solution)/shard_map/ppermute | solution.py:381
  91.0 4.6 %collective-permute-start.20 = (f32[16,128]{1,0:T(8,128)S(1)}, f32[16,128]{1,0:T(8,128)S(1)}, u32[]{:S(2)}, u32[]{:S(2)}) collective-permute-start(f32[16,128]{1,0:T(8,128)S(1)} %add.51), channel_id=1, source_target_pairs={{0,24},{8,16},{16,8},{24,0},{32,56},{40,48},{48,40},{56,32},{64,88... | collective-permute-start | bytes 24584 | tf_op jit(solution)/shard_map/ppermute | solution.py:381
  95.6 3.5 %collective-permute-start.21 = (f32[16,128]{1,0:T(8,128)S(1)}, f32[16,128]{1,0:T(8,128)S(1)}, u32[]{:S(2)}, u32[]{:S(2)}) collective-permute-start(f32[16,128]{1,0:T(8,128)S(1)} %add.52), channel_id=1, source_target_pairs={{0,32},{8,40},{16,48},{24,56},{32,0},{40,8},{48,16},{56,24},{64,96... | collective-permute-start | bytes 24584 | tf_op jit(solution)/shard_map/ppermute | solution.py:381
  99.1 3.9 %collective-permute-start.22 = (f32[16,128]{1,0:T(8,128)S(1)}, f32[16,128]{1,0:T(8,128)S(1)}, u32[]{:S(2)}, u32[]{:S(2)}) collective-permute-start(f32[16,128]{1,0:T(8,128)S(1)} %add.53), channel_id=1, source_target_pairs={{0,96},{8,104},{16,112},{24,120},{32,64},{40,72},{48,80},{56,88},{... | collective-permute-start | bytes 24584 | tf_op jit(solution)/shard_map/ppermute | solution.py:381
  111.4 13.4 %collective-permute-start.18 = (f32[384,256]{1,0:T(8,128)S(1)}, f32[384,256]{1,0:T(8,128)S(1)}, u32[]{:S(2)}, u32[]{:S(2)}) collective-permute-start(f32[384,256]{1,0:T(8,128)S(1)} %broadcast_select_fusion.6.own), channel_id=1, source_target_pairs={{0,1},{1,0},{2,3},{3,2},{4,5},{5,4},{6,7},{7,6},{8,9},{9,8},{10,11... | collective-permute-start | bytes 1179656 | tf_op jit(solution)/shard_map/ppermute | solution.py:371
  111.5 1.0 copy-start
  113.6 19.5 %collective-permute-start.17 = (f32[512,256]{1,0:T(8,128)}, f32[512,256]{1,0:T(8,128)S(1)}, u32[]{:S(2)}, u32[]{:S(2)}) collective-permute-start(f32[512,256]{1,0:T(8,128)} %get-tuple-element.70), channel_id=1, source_target_pairs={{6,4},{7,5},{14,12},{15,13},{22,20},{23,21},{30,28},{31,29},{38,36... | collective-permute-start | bytes 1572872 | tf_op jit(solution)/shard_map/ppermute | solution.py:395
  114.3 18.8 %collective-permute-start.16 = (f32[512,256]{1,0:T(8,128)S(1)}, f32[512,256]{1,0:T(8,128)}, u32[]{:S(2)}, u32[]{:S(2)}) collective-permute-start(f32[512,256]{1,0:T(8,128)S(1)} %get-tuple-element.71), channel_id=1, source_target_pairs={{2,4},{3,5},{10,12},{11,13},{18,20},{19,21},{26,28},{27,29},{34,36... | collective-permute-start | bytes 1572872 | tf_op jit(solution)/shard_map/ppermute | solution.py:394
  115.8 2.6 %collective-permute-start.25 = (f32[16,256]{1,0:T(8,128)S(1)}, f32[16,256]{1,0:T(8,128)S(1)}, u32[]{:S(2)}, u32[]{:S(2)}) collective-permute-start(f32[16,256]{1,0:T(8,128)S(1)} %broadcast_in_dim.26), channel_id=1, source_target_pairs={{0,2},{1,3},{8,10},{9,11},{16,18},{17,19},{24,26},{25,27},{32,34},... | collective-permute-start | bytes 49160 | tf_op jit(solution)/shard_map/ppermute | solution.py:385
  117.0 7.0 %collective-permute-start.24 = (f32[16,256]{1,0:T(8,128)S(1)}, f32[16,256]{1,0:T(8,128)S(1)}, u32[]{:S(2)}, u32[]{:S(2)}) collective-permute-start(f32[16,256]{1,0:T(8,128)S(1)} %broadcast_in_dim.26), channel_id=1, source_target_pairs={{0,4},{1,5},{8,12},{9,13},{16,20},{17,21},{24,28},{25,29},{32,36},... | collective-permute-start | bytes 49160 | tf_op jit(solution)/shard_map/ppermute | solution.py:385
  118.4 6.5 %collective-permute-start.23 = (f32[16,256]{1,0:T(8,128)S(1)}, f32[16,256]{1,0:T(8,128)S(1)}, u32[]{:S(2)}, u32[]{:S(2)}) collective-permute-start(f32[16,256]{1,0:T(8,128)S(1)} %broadcast_in_dim.26), channel_id=1, source_target_pairs={{0,6},{1,7},{8,14},{9,15},{16,22},{17,23},{24,30},{25,31},{32,38},... | collective-permute-start | bytes 49160 | tf_op jit(solution)/shard_map/ppermute | solution.py:385
  133.3 10.9 %collective-permute-start.26 = (f32[1040,256]{1,0:T(8,128)S(1)}, f32[1040,256]{1,0:T(8,128)S(1)}, u32[]{:S(2)}, u32[]{:S(2)}) collective-permute-start(f32[1040,256]{1,0:T(8,128)S(1)} %pad_maximum_fusion.mine.own_sums), channel_id=1, source_target_pairs={{0,1},{1,0},{2,3},{3,2},{4,5},{5,4},{6,7},{7,6},{8,9},{9,8},{10,11... | collective-permute-start | bytes 3194888 | tf_op jit(solution)/shard_map/ppermute | solution.py:400
Sparse Core Ops, SparseCore 0:
  47.4 50.6 all-gather.2

commit v6 on v5

--- a/solution.py
+++ b/solution.py
@@ -277,13 +277,10 @@
             q = 2 * u + h
             value = flat[:, q, :] - product[0:rows, 128 * h : 128 * h + 128]
             out[:, q, :] = jnp.where(gone, 0.0, value)
-
-            @pl.when(step == 0)
-            def _():
-                kept = sums[pl.ds(8 * group + q, 1), :] - product[rows : rows + 1, 128 * h : 128 * h + 128]
-                if u == 0:
-                    kept = jnp.where((group == 0) & (col_index < 2), 0.0, kept)
-                checksum[pl.ds(8 * group + q, 1), :] = kept
+            kept = sums[q : q + 1, :] - product[rows : rows + 1, 128 * h : 128 * h + 128]
+            if u == 0:
+                kept = jnp.where((group == 0) & (col_index < 2), 0.0, kept)
+            checksum[q : q + 1, :] = kept
 
 
 def update_call(place, flat, across, high, low, sums, taken):
@@ -298,10 +295,10 @@
             pl.BlockSpec((8, NB, NB), lambda g, i: (g, 0, 0)),
             full(1024, 512),
             full(1024, 512),
-            full(16, 128),
+            pl.BlockSpec((8, 128), lambda g, i: (g, 0)),
             full(16, 512),
         ],
-        out_specs=(pl.BlockSpec((rows, 8, 128), lambda g, i: (i, g, 0)), full(16, 128)),
+        out_specs=(pl.BlockSpec((rows, 8, 128), lambda g, i: (i, g, 0)), pl.BlockSpec((8, 128), lambda g, i: (g, 0))),
         scratch_shapes=[pltpu.VMEM((4, 512, NB), BF16), pltpu.VMEM((4, 512, NB), BF16)],
         name="trailing_update", **FACTOR,
     )(place, flat, across, high, low, sums, taken)
@@ -322,7 +319,7 @@
     return device_at(*at)
 
 
-def spread(value, trees, here):
+def spread(value, trees, here, beside):
     holders = [[device_at(z, y, 0, c)] for (z, y), c, _ in trees]
     stages = []
     for at in range(3):
@@ -336,6 +333,8 @@
                     pairs += [(h, moved(h, dim, 1)) for h in held]
                 else:
                     pairs += [(h, moved(h, dim, -1)) for h in held] + [(moved(h, dim, 1), moved(h, dim, 2)) for h in held]
+            if stages:
+                value = beside(len(stages), value)
             arrived = lax.ppermute(value, ("row", "col"), pairs)
             value = jnp.where((away == 1) if half == 0 else (away >= 2), arrived, value)
             stages.append(value)
@@ -366,26 +365,35 @@
         jnp.concatenate([pieces[0], fetched[0:128]], axis=0),
         jnp.concatenate([fetched, pieces[9]], axis=0),
     )
-    tree = spread(corner, [((0, 0), 0, (2, 1, 0)), ((0, 0), 1, (1, 0, 2))], here)
+    column, sums = column_call(weights, after(flat, corner))
+    partial = [sums]
+
+    def beside(stage, value):
+        before = partial[-1]
+        if stage >= 2:
+            d = (1, 3, 4, 12)[stage - 2]
+            partial.append(before + lax.ppermute(after(before, value), "row", [(r, r ^ d) for r in range(16)]))
+        return after(value, before)
+
+    tree = spread(corner, [((0, 0), 0, (2, 1, 0)), ((0, 0), 1, (1, 0, 2))], here, beside)
+    sums = partial[-1]
     own = tree[-1]
     other = lax.ppermute(own, "col", swap_cores)
 
     piece = pieces[8]
     for j in range(1, 8):
-        piece = jnp.where(row // 2 == j, lax.ppermute(pieces[j], "row", [(0, 2 * j), (1, 2 * j + 1)]), piece)
-    across = lax.all_gather(after(piece, tree[0]), "row", axis=0)
+        piece = jnp.where(row // 2 == j, lax.ppermute(pieces[j] if j < 4 else after(pieces[j], fetched), "row", [(0, 2 * j), (1, 2 * j + 1)]), piece)
+    across = lax.all_gather(after(piece, (tree[0], column)), "row", axis=0)
     across = pltpu.with_memory_space_constraint(across, pltpu.HBM)
 
-    column, sums = column_call(weights, after(flat, corner))
-    for d, stage in ((1, 1), (3, 2), (4, 3), (12, 4)):
-        sums = sums + lax.ppermute(after(sums, tree[stage]), "row", [(r, r ^ d) for r in range(16)])
     near_sums = jnp.broadcast_to(sums[0:2].reshape(1, NB), (16, NB))
+    far_sums = [lax.ppermute(near_sums, "col", [(0, 2 * k), (1, 2 * k + 1)]) for k in (1, 2, 3)]
+    w00 = first_factor(place, own, other)
+    far_sums = after(far_sums, w00)
     panel_sums = near_sums
     for k in (1, 2, 3):
-        arrived = lax.ppermute(near_sums, "col", [(0, 2 * k), (1, 2 * k + 1)])
-        panel_sums = jnp.where(x == k, arrived, panel_sums)
-
-    w00 = first_factor(place, own, other)
+        panel_sums = jnp.where(x == k, far_sums[k - 1], panel_sums)
+
     l10, w11 = second_factor(place, w00, own, other)
     from_left = lax.ppermute(column, "col", [(0, 2), (1, 3)])
     from_right = lax.ppermute(column, "col", [(0, 6), (1, 7)])

time: 187 us -> 165 us (0.88)
  waiting for transfers between devices: 45.2 us -> 34.7 us
  Pallas kernels: 62.7 us -> 54.5 us
  starting transfers between devices: 59 us -> 55.8 us
    pallas_call x1, Pallas kernels: 28.5 us -> 20.3 us  [update_call(): pl.pallas_call(update_kernel, grid=(2, 1024 // rows), out_shape=(jax.Shap...]
    ppermute x6, starting transfers between devices: 16.3 us -> 10.1 us  [spread(): arrived = lax.ppermute(value, ('row', 'col'), pairs)]
    ppermute x14, waiting for transfers between devices: 10.4 us -> 5.91 us  [the longest x4 5.01 us: beside(): lax.ppermute(after(before, value), 'row', [(r, r ^ d) for r in range(16)])]
    ppermute x1, waiting for transfers between devices: 4.01 us -> 0.01 us  [shards(): fetched = lax.ppermute(pieces[0], ('row', 'col'), [(8, 0), (9, 1)])]
    ppermute x6, waiting for transfers between devices: 30.7 us -> 28.8 us  [spread(): arrived = lax.ppermute(value, ('row', 'col'), pairs)]
    ppermute x1, starting transfers between devices: 0.09 us -> 2.03 us  [shards(): other = lax.ppermute(own, 'col', swap_cores)]
  transfers between devices with their start and end apart: 28 -> 28, of which waited for: 12 -> 11; matrix products, arithmetic and copies ran while one was open for 2% -> 2% of each run, Pallas kernels for 17% -> 19%
where the time goes in v6:
time: 165 us; the launch traced here: 164 us
  starting transfers between devices  55.8 us (34%)
  Pallas kernels  54.5 us (33%)
  waiting for transfers between devices  34.7 us (21%)
  between operations  14.5 us (9%)
  other arithmetic  2.75 us (2%)
  local copies, waits for them, and re-layouts  1.95 us (1%)
    ppermute x6, waiting for transfers between devices, spread(): arrived = lax.ppermute(value, ('row', 'col'), pairs)  28.8 us
    pallas_call x1, Pallas kernels, update_call(): pl.pallas_call(update_kernel, grid=(2, 1024 // rows), out_shape=(jax.Shap...  20.3 us
    ppermute x7, starting transfers between devices, shards(): lax.ppermute(pieces[j] if j < 4 else after(pieces[j], fetched), 'row', [(...  15.8 us
    ppermute x4, starting transfers between devices, beside(): lax.ppermute(after(before, value), 'row', [(r, r ^ d) for r in range(16)])  10.2 us
    ppermute x6, starting transfers between devices, spread(): arrived = lax.ppermute(value, ('row', 'col'), pairs)  10.1 us
    pallas_call x1, Pallas kernels, second_factor(): pl.pallas_call(second_kernel, out_shape=(TILE, TILE), in_specs=[SMEM, VME...  9.32 us
    pallas_call x1, Pallas kernels, first_factor(): pl.pallas_call(first_kernel, out_shape=TILE, in_specs=[SMEM, VMEM, VMEM],...  8.22 us
    ppermute x3, starting transfers between devices, shards(): lax.ppermute(near_sums, 'col', [(0, 2 * k), (1, 2 * k + 1)])  7.91 us
  transfers between devices with their start and end apart: 28, of which 11 were waited for; matrix products, arithmetic and copies ran while one was open for 2% of the time, Pallas kernels for 19%

profile of v6, /device:TPU:1, one launch (start us, length us, event | category | flops | bytes accessed | tf_op | source)
XLA Modules:
  0.0 164.3 jit_solution(15094772453617887039)
XLA Ops:
  7.2 3.3 %corner_tiles.1 = (f32[256,256]{1,0:T(8,128)}, f32[256,256]{1,0:T(8,128)}, f32[256,256]{1,0:T(8,128)}, f32[256,256]{1,0:T(8,128)}, f32[256,256]{1,0:T(8,128)}, /...) custom-call(f32[1024,16,128]{2,1,0:T(8,128)} %bitcast.12), custom_call_target="tpu_custom_call" | custom-call | tf_op jit(solution)/shard_map/corner_tiles/pallas_call | solution.py:167
  10.5 1.3 collective-permute-start
  11.8 6.4 %collective-permute-start.5 = (f32[256,256]{1,0:T(8,128)}, f32[256,256]{1,0:T(8,128)S(1)}, u32[]{:S(2)}, u32[]{:S(2)}) collective-permute-start(f32[256,256]{1,0:T(8,128)} %get-tuple-element.55), channel_id=1, source_target_pairs={{0,48},{8,56},{1,49},{9,57},{2,50},{10,58},{3,51},{11,59},{4,52},{... | collective-permute-start | bytes 786440 | tf_op jit(solution)/shard_map/ppermute | solution.py:385
  18.2 1.3 collective-permute-start.6
  19.5 1.3 collective-permute-start.7
  21.0 1.5 collective-permute-start.1
  22.5 1.3 collective-permute-start.2
  23.8 2.0 %collective-permute-start.3 = (f32[256,256]{1,0:T(8,128)}, f32[256,256]{1,0:T(8,128)}, u32[]{:S(2)}, u32[]{:S(2)}) collective-permute-start(f32[256,256]{1,0:T(8,128)} %get-tuple-element.52), channel_id=1, source_target_pairs={{0,80},{8,88},{1,81},{9,89},{2,82},{10,90},{3,83},{11,91},{4,84},{... | collective-permute-start | bytes 786440 | tf_op jit(solution)/shard_map/ppermute | solution.py:385
  25.8 2.0 %collective-permute-start.4 = (f32[256,256]{1,0:T(8,128)}, f32[256,256]{1,0:T(8,128)}, u32[]{:S(2)}, u32[]{:S(2)}) collective-permute-start(f32[256,256]{1,0:T(8,128)} %get-tuple-element.54), channel_id=1, source_target_pairs={{0,64},{8,72},{1,65},{9,73},{2,66},{10,74},{3,67},{11,75},{4,68},{... | collective-permute-start | bytes 786440 | tf_op jit(solution)/shard_map/ppermute | solution.py:385
  27.8 1.0 maximum_select_fusion
  28.9 0.2 collective-permute-done.7
  29.1 3.5 %collective-permute-start.8 = (f32[384,256]{1,0:T(8,128)S(1)}, f32[384,256]{1,0:T(8,128)S(1)}, u32[]{:S(2)}, u32[]{:S(2)}) collective-permute-start(f32[384,256]{1,0:T(8,128)S(1)} %maximum_select_fusion), channel_id=1, source_target_pairs={{0,2},{1,9}} | collective-permute-start | bytes 1179656 | tf_op jit(solution)/shard_map/ppermute | solution.py:338
  32.7 6.9 %first_column.1 = (f32[1024,256]{1,0:T(8,128)S(1)}, f32[16,128]{1,0:T(8,128)S(1)}) custom-call(f32[1024]{0:T(1024)S(1)} %broadcast_select_fusion.8.weights, f32[1024,16,128]{2,1,0:T(8,128)} %bitcast.13), custom_call_target="tpu_custom_call" | custom-call | flops 100000000 | bytes 100000 | tf_op jit(solution)/shard_map/first_column/pallas_call | solution.py:194
  39.7 0.7 collective-permute-done.3
  40.3 0.8 select_select_fusion.1
  41.2 4.4 %collective-permute-done.8 = f32[384,256]{1,0:T(8,128)S(1)} collective-permute-done((f32[384,256]{1,0:T(8,128)S(1)}, f32[384,256]{1,0:T(8,128)S(1)}, u32[]{:S(2)}, u32[]{:S(2)}) %collective-permute-start.8) | collective-permute-done | bytes 393248 | tf_op jit(solution)/shard_map/ppermute | solution.py:338
  45.7 1.3 collective-permute-start.11
  47.0 4.7 %collective-permute-done.11 = f32[384,256]{1,0:T(8,128)S(1)} collective-permute-done((f32[384,256]{1,0:T(8,128)S(1)}, f32[384,256]{1,0:T(8,128)S(1)}, u32[]{:S(2)}, u32[]{:S(2)}) %collective-permute-start.11) | collective-permute-done | bytes 393248 | tf_op jit(solution)/shard_map/ppermute | solution.py:338
  51.7 1.3 collective-permute-start.12
  53.0 2.0 %collective-permute-start.13 = (f32[16,128]{1,0:T(8,128)S(1)}, f32[16,128]{1,0:T(8,128)S(1)}, u32[]{:S(2)}, u32[]{:S(2)}) collective-permute-start(f32[16,128]{1,0:T(8,128)S(1)} %get-tuple-element.66), channel_id=1, source_target_pairs={{0,8},{8,0},{16,24},{24,16},{32,40},{40,32},{48,56},{56,48},{64,72... | collective-permute-start | bytes 24584 | tf_op jit(solution)/shard_map/ppermute | solution.py:375
  55.0 1.0 collective-permute-done.13
  56.1 3.1 %collective-permute-done.12 = f32[384,256]{1,0:T(8,128)S(1)} collective-permute-done((f32[384,256]{1,0:T(8,128)S(1)}, f32[384,256]{1,0:T(8,128)S(1)}, u32[]{:S(2)}, u32[]{:S(2)}) %collective-permute-start.12) | collective-permute-done | bytes 393248 | tf_op jit(solution)/shard_map/ppermute | solution.py:338
  59.2 1.3 collective-permute-start.14
  60.5 3.2 %collective-permute-start.15 = (f32[16,128]{1,0:T(8,128)S(1)}, f32[16,128]{1,0:T(8,128)S(1)}, u32[]{:S(2)}, u32[]{:S(2)}) collective-permute-start(f32[16,128]{1,0:T(8,128)S(1)} %add.51), channel_id=1, source_target_pairs={{0,24},{8,16},{16,8},{24,0},{32,56},{40,48},{48,40},{56,32},{64,88... | collective-permute-start | bytes 24584 | tf_op jit(solution)/shard_map/ppermute | solution.py:375
  63.7 1.4 collective-permute-done.15
  65.2 2.7 %collective-permute-done.14 = f32[384,256]{1,0:T(8,128)S(1)} collective-permute-done((f32[384,256]{1,0:T(8,128)S(1)}, f32[384,256]{1,0:T(8,128)S(1)}, u32[]{:S(2)}, u32[]{:S(2)}) %collective-permute-start.14) | collective-permute-done | bytes 393248 | tf_op jit(solution)/shard_map/ppermute | solution.py:338
  67.9 1.3 collective-permute-start.16
  69.3 1.4 collective-permute-start.10
  70.6 2.3 %collective-permute-start.9 = (f32[1024,256]{1,0:T(8,128)S(1)}, f32[1024,256]{1,0:T(8,128)}, u32[]{:S(2)}, u32[]{:S(2)}) collective-permute-start(f32[1024,256]{1,0:T(8,128)S(1)} %get-tuple-element.61), channel_id=1, source_target_pairs={{0,2},{1,3},{8,10},{9,11},{16,18},{17,19},{24,26},{25,27},{32,34},... | collective-permute-start | bytes 3145736 | tf_op jit(solution)/shard_map/ppermute | solution.py:398
  72.9 1.5 collective-permute-start.17
  74.4 1.0 collective-permute-done.17
  75.5 1.3 collective-permute-start.18
  76.8 3.6 %collective-permute-start.22 = (f32[16,128]{1,0:T(8,128)S(1)}, f32[16,128]{1,0:T(8,128)S(1)}, u32[]{:S(2)}, u32[]{:S(2)}) collective-permute-start(f32[16,128]{1,0:T(8,128)S(1)} %add.53), channel_id=1, source_target_pairs={{0,96},{8,104},{16,112},{24,120},{32,64},{40,72},{48,80},{56,88},{... | collective-permute-start | bytes 24584 | tf_op jit(solution)/shard_map/ppermute | solution.py:375
  80.4 1.5 collective-permute-done.22
  81.9 13.9 %collective-permute-done.18 = f32[384,256]{1,0:T(8,128)S(1)} collective-permute-done((f32[384,256]{1,0:T(8,128)S(1)}, f32[384,256]{1,0:T(8,128)S(1)}, u32[]{:S(2)}, u32[]{:S(2)}) %collective-permute-start.18) | collective-permute-done | bytes 393248 | tf_op jit(solution)/shard_map/ppermute | solution.py:338
  95.9 2.0 %collective-permute-start.21 = (f32[384,256]{1,0:T(8,128)S(1)}, f32[384,256]{1,0:T(8,128)S(1)}, u32[]{:S(2)}, u32[]{:S(2)}) collective-permute-start(f32[384,256]{1,0:T(8,128)S(1)} %broadcast_select_fusion.6.own), channel_id=1, source_target_pairs={{0,1},{1,0},{2,3},{3,2},{4,5},{5,4},{6,7},{7,6},{8,9},{9,8},{10,11... | collective-permute-start | bytes 1179656 | tf_op jit(solution)/shard_map/ppermute | solution.py:381
  97.9 1.0 copy-done
  99.1 0.9 fusion
  99.9 0.7 collective-permute-start.20
  100.6 1.5 collective-permute-start.19
  102.1 5.3 %collective-permute-start.25 = (f32[16,256]{1,0:T(8,128)S(1)}, f32[16,256]{1,0:T(8,128)S(1)}, u32[]{:S(2)}, u32[]{:S(2)}) collective-permute-start(f32[16,256]{1,0:T(8,128)S(1)} %broadcast_in_dim.26), channel_id=1, source_target_pairs={{0,6},{1,7},{8,14},{9,15},{16,22},{17,23},{24,30},{25,31},{32,38},... | collective-permute-start | bytes 49160 | tf_op jit(solution)/shard_map/ppermute | solution.py:390
  107.5 1.3 collective-permute-start.24
  108.8 1.3 collective-permute-start.23
  110.1 8.2 %first_factor.1.w00 = f32[256,256]{1,0:T(8,128)S(1)} custom-call(s32[2]{0:T(128)S(1)} %pad_add_fusion.place, f32[384,256]{1,0:T(8,128)S(1)} %broadcast_select_fusion.6.own, f32[384,256]{1,0:T(8,128)S(1)} %collective-permute-done.21.other), custom_call_target="tpu_custom_call" | custom-call | flops 100000000 | bytes 100000 | tf_op jit(solution)/shard_map/first_factor/pallas_call | solution.py:144
  118.7 2.6 %collective-permute-start.26 = (f32[1040,256]{1,0:T(8,128)S(1)}, f32[1040,256]{1,0:T(8,128)S(1)}, u32[]{:S(2)}, u32[]{:S(2)}) collective-permute-start(f32[1040,256]{1,0:T(8,128)S(1)} %pad_maximum_fusion.mine.own_sums), channel_id=1, source_target_pairs={{0,1},{1,0},{2,3},{3,2},{4,5},{5,4},{6,7},{7,6},{8,9},{9,8},{10,11... | collective-permute-start | bytes 3194888 | tf_op jit(solution)/shard_map/ppermute | solution.py:408
  121.3 9.3 %second_factor.1 = (f32[256,256]{1,0:T(8,128)S(1)}, f32[256,256]{1,0:T(8,128)S(1)}) custom-call(s32[2]{0:T(128)S(1)} %pad_add_fusion.place, f32[256,256]{1,0:T(8,128)S(1)} %first_factor.1.w00, f32[384,256]{1,0:T(8,128)S(1)} %broadcast_select_fusion.6.own, f32[384,256]{1,0:T(8,128)S(1)} %collective-permute-done.21.other), custom_call_target="tpu_custom_call" | custom-call | flops 100000000 | bytes 100000 | tf_op jit(solution)/shard_map/second_factor/pallas_call | solution.py:151
  130.6 6.5 %panel_solve.1 = (f32[1024,512]{1,0:T(8,128)}, bf16[1024,512]{1,0:T(8,128)(2,1)S(1)}, bf16[1024,512]{1,0:T(8,128)(2,1)S(1)}, f32[16,512]{1,0:T(8,128)S(1)}) custom-call(s32[2]{0:T(128)S(1)} %pad_add_fusion.place, f32[1040,256]{1,0:T(8,128)S(1)} %pad_maximum_fusion.mine.own_sums, f32[1040,256]{1,0:T(8,128)S(1)} %collective-permute-done.26.theirs.other_sums, ...), custom_call_target="tpu_custom_call" | custom-call | flops 100000000 | bytes 100000 | tf_op jit(solution)/shard_map/panel_solve/pallas_call | solution.py:239
  137.1 20.3 %trailing_update.1 = (f32[1024,16,128]{2,1,0:T(8,128)}, f32[16,128]{1,0:T(8,128)}) custom-call(s32[2]{0:T(128)S(1)} %pad_add_fusion.place, f32[1024,16,128]{2,1,0:T(8,128)} %bitcast.14, f32[16,256,256]{2,1,0:T(8,128)} %bitcast.15, bf16[1024,512]{1,0:T(8,128)(2,1)S(1)} %get-tuple-element.83.high, bf16[1024,512]{1,0:T(8,128)(2,1)S(1)} %get-tuple-element.84.low, ...), custom_call_target="tpu_custom_call" | custom-call | flops 100000000 | bytes 100000 | tf_op jit(solution)/shard_map/trailing_update/pallas_call | solution.py:289
  (46 shorter events, 1.1 us)
Async XLA Ops:
  7.2 130.0 %all-gather.3.cloned.1.call-start = ((), (), s32[]{:S(2)}) async-start(), calls=%async_computation | async-start | bytes 4456448 | tf_op jit(solution)/shard_map/all_gather | solution.py:386
  10.5 22.1 %copy-start.2 = (f32[4,1,256]{2,1,0:T(1,128)S(1)}, f32[4,1,256]{2,1,0:T(1,128)}, u32[]{:S(2)}) copy-start(f32[4,1,256]{2,1,0:T(1,128)} %param.3) | copy-start | bytes 12292
  10.5 10.5 %collective-permute-start = (f32[256,256]{1,0:T(8,128)}, f32[256,256]{1,0:T(8,128)S(1)}, u32[]{:S(2)}, u32[]{:S(2)}) collective-permute-start(f32[256,256]{1,0:T(8,128)} %get-tuple-element.47), channel_id=1, source_target_pairs={{8,0},{9,1}} | collective-permute-start | bytes 786440 | tf_op jit(solution)/shard_map/ppermute | solution.py:362
  11.8 12.0 %collective-permute-start.5 = (f32[256,256]{1,0:T(8,128)}, f32[256,256]{1,0:T(8,128)S(1)}, u32[]{:S(2)}, u32[]{:S(2)}) collective-permute-start(f32[256,256]{1,0:T(8,128)} %get-tuple-element.55), channel_id=1, source_target_pairs={{0,48},{8,56},{1,49},{9,57},{2,50},{10,58},{3,51},{11,59},{4,52},{... | collective-permute-start | bytes 786440 | tf_op jit(solution)/shard_map/ppermute | solution.py:385
  18.2 7.6 %collective-permute-start.6 = (f32[256,256]{1,0:T(8,128)}, f32[256,256]{1,0:T(8,128)S(1)}, u32[]{:S(2)}, u32[]{:S(2)}) collective-permute-start(f32[256,256]{1,0:T(8,128)} %get-tuple-element.56), channel_id=1, source_target_pairs={{0,32},{8,40},{1,33},{9,41},{2,34},{10,42},{3,35},{11,43},{4,36},{... | collective-permute-start | bytes 786440 | tf_op jit(solution)/shard_map/ppermute | solution.py:385
  19.5 9.6 %collective-permute-start.7 = (f32[256,256]{1,0:T(8,128)}, f32[256,256]{1,0:T(8,128)S(1)}, u32[]{:S(2)}, u32[]{:S(2)}) collective-permute-start(f32[256,256]{1,0:T(8,128)} %get-tuple-element.57), channel_id=1, source_target_pairs={{0,16},{8,24},{1,17},{9,25},{2,18},{10,26},{3,19},{11,27},{4,20},{... | collective-permute-start | bytes 786440 | tf_op jit(solution)/shard_map/ppermute | solution.py:385
  21.0 18.7 %collective-permute-start.1 = (f32[256,256]{1,0:T(8,128)}, f32[256,256]{1,0:T(8,128)S(1)}, u32[]{:S(2)}, u32[]{:S(2)}) collective-permute-start(f32[256,256]{1,0:T(8,128)} %get-tuple-element.48), channel_id=1, source_target_pairs={{0,112},{8,120},{1,113},{9,121},{2,114},{10,122},{3,115},{11,123},... | collective-permute-start | bytes 786440 | tf_op jit(solution)/shard_map/ppermute | solution.py:385
  22.5 17.2 %collective-permute-start.2 = (f32[256,256]{1,0:T(8,128)}, f32[256,256]{1,0:T(8,128)S(1)}, u32[]{:S(2)}, u32[]{:S(2)}) collective-permute-start(f32[256,256]{1,0:T(8,128)} %get-tuple-element.50), channel_id=1, source_target_pairs={{0,96},{8,104},{1,97},{9,105},{2,98},{10,106},{3,99},{11,107},{4,1... | collective-permute-start | bytes 786440 | tf_op jit(solution)/shard_map/ppermute | solution.py:385
  23.8 16.5 %collective-permute-start.3 = (f32[256,256]{1,0:T(8,128)}, f32[256,256]{1,0:T(8,128)}, u32[]{:S(2)}, u32[]{:S(2)}) collective-permute-start(f32[256,256]{1,0:T(8,128)} %get-tuple-element.52), channel_id=1, source_target_pairs={{0,80},{8,88},{1,81},{9,89},{2,82},{10,90},{3,83},{11,91},{4,84},{... | collective-permute-start | bytes 786440 | tf_op jit(solution)/shard_map/ppermute | solution.py:385
  25.8 14.5 %collective-permute-start.4 = (f32[256,256]{1,0:T(8,128)}, f32[256,256]{1,0:T(8,128)}, u32[]{:S(2)}, u32[]{:S(2)}) collective-permute-start(f32[256,256]{1,0:T(8,128)} %get-tuple-element.54), channel_id=1, source_target_pairs={{0,64},{8,72},{1,65},{9,73},{2,66},{10,74},{3,67},{11,75},{4,68},{... | collective-permute-start | bytes 786440 | tf_op jit(solution)/shard_map/ppermute | solution.py:385
  29.1 16.5 %collective-permute-start.8 = (f32[384,256]{1,0:T(8,128)S(1)}, f32[384,256]{1,0:T(8,128)S(1)}, u32[]{:S(2)}, u32[]{:S(2)}) collective-permute-start(f32[384,256]{1,0:T(8,128)S(1)} %maximum_select_fusion), channel_id=1, source_target_pairs={{0,2},{1,9}} | collective-permute-start | bytes 1179656 | tf_op jit(solution)/shard_map/ppermute | solution.py:338
  32.7 7.6 %copy-start.1 = (f32[256,256]{1,0:T(8,128)S(1)}, f32[256,256]{1,0:T(8,128)}, u32[]{:S(2)}) copy-start(f32[256,256]{1,0:T(8,128)} %get-tuple-element.58) | copy-start | bytes 786436
  45.7 6.0 %collective-permute-start.11 = (f32[384,256]{1,0:T(8,128)S(1)}, f32[384,256]{1,0:T(8,128)S(1)}, u32[]{:S(2)}, u32[]{:S(2)}) collective-permute-start(f32[384,256]{1,0:T(8,128)S(1)} %broadcast_select_fusion.7), channel_id=1, source_target_pairs={{0,6},{2,4},{1,25},{9,17}} | collective-permute-start | bytes 1179656 | tf_op jit(solution)/shard_map/ppermute | solution.py:338
  51.7 7.4 %collective-permute-start.12 = (f32[384,256]{1,0:T(8,128)S(1)}, f32[384,256]{1,0:T(8,128)S(1)}, u32[]{:S(2)}, u32[]{:S(2)}) collective-permute-start(f32[384,256]{1,0:T(8,128)S(1)} %broadcast_select_fusion.2), channel_id=1, source_target_pairs={{0,8},{2,10},{4,12},{6,14},{1,33},{9,41},{17,49},{25,57}} | collective-permute-start | bytes 1179656 | tf_op jit(solution)/shard_map/ppermute | solution.py:338
  53.0 3.0 %collective-permute-start.13 = (f32[16,128]{1,0:T(8,128)S(1)}, f32[16,128]{1,0:T(8,128)S(1)}, u32[]{:S(2)}, u32[]{:S(2)}) collective-permute-start(f32[16,128]{1,0:T(8,128)S(1)} %get-tuple-element.66), channel_id=1, source_target_pairs={{0,8},{8,0},{16,24},{24,16},{32,40},{40,32},{48,56},{56,48},{64,72... | collective-permute-start | bytes 24584 | tf_op jit(solution)/shard_map/ppermute | solution.py:375
  59.2 8.7 %collective-permute-start.14 = (f32[384,256]{1,0:T(8,128)S(1)}, f32[384,256]{1,0:T(8,128)S(1)}, u32[]{:S(2)}, u32[]{:S(2)}) collective-permute-start(f32[384,256]{1,0:T(8,128)S(1)} %broadcast_select_fusion.3), channel_id=1, source_target_pairs={{0,24},{2,26},{4,28},{6,30},{8,16},{10,18},{12,20},{14,22},{1,97},... | collective-permute-start | bytes 1179656 | tf_op jit(solution)/shard_map/ppermute | solution.py:338
  60.5 4.6 %collective-permute-start.15 = (f32[16,128]{1,0:T(8,128)S(1)}, f32[16,128]{1,0:T(8,128)S(1)}, u32[]{:S(2)}, u32[]{:S(2)}) collective-permute-start(f32[16,128]{1,0:T(8,128)S(1)} %add.51), channel_id=1, source_target_pairs={{0,24},{8,16},{16,8},{24,0},{32,56},{40,48},{48,40},{56,32},{64,88... | collective-permute-start | bytes 24584 | tf_op jit(solution)/shard_map/ppermute | solution.py:375
  67.9 7.5 %collective-permute-start.16 = (f32[384,256]{1,0:T(8,128)S(1)}, f32[384,256]{1,0:T(8,128)S(1)}, u32[]{:S(2)}, u32[]{:S(2)}) collective-permute-start(f32[384,256]{1,0:T(8,128)S(1)} %broadcast_select_fusion.4), channel_id=1, source_target_pairs={{0,32},{8,40},{16,48},{24,56},{2,34},{10,42},{18,50},{26,58},{4,36... | collective-permute-start | bytes 1179656 | tf_op jit(solution)/shard_map/ppermute | solution.py:338
  69.3 28.6 %collective-permute-start.10 = (f32[1024,256]{1,0:T(8,128)S(1)}, f32[1024,256]{1,0:T(8,128)S(1)}, u32[]{:S(2)}, u32[]{:S(2)}) collective-permute-start(f32[1024,256]{1,0:T(8,128)S(1)} %get-tuple-element.61), channel_id=1, source_target_pairs={{0,6},{1,7},{8,14},{9,15},{16,22},{17,23},{24,30},{25,31},{32,38},... | collective-permute-start | bytes 3145736 | tf_op jit(solution)/shard_map/ppermute | solution.py:399
  70.6 28.3 %collective-permute-start.9 = (f32[1024,256]{1,0:T(8,128)S(1)}, f32[1024,256]{1,0:T(8,128)}, u32[]{:S(2)}, u32[]{:S(2)}) collective-permute-start(f32[1024,256]{1,0:T(8,128)S(1)} %get-tuple-element.61), channel_id=1, source_target_pairs={{0,2},{1,3},{8,10},{9,11},{16,18},{17,19},{24,26},{25,27},{32,34},... | collective-permute-start | bytes 3145736 | tf_op jit(solution)/shard_map/ppermute | solution.py:398
  72.9 2.5 %collective-permute-start.17 = (f32[16,128]{1,0:T(8,128)S(1)}, f32[16,128]{1,0:T(8,128)S(1)}, u32[]{:S(2)}, u32[]{:S(2)}) collective-permute-start(f32[16,128]{1,0:T(8,128)S(1)} %add.52), channel_id=1, source_target_pairs={{0,32},{8,40},{16,48},{24,56},{32,0},{40,8},{48,16},{56,24},{64,96... | collective-permute-start | bytes 24584 | tf_op jit(solution)/shard_map/ppermute | solution.py:375
  75.5 20.3 %collective-permute-start.18 = (f32[384,256]{1,0:T(8,128)S(1)}, f32[384,256]{1,0:T(8,128)S(1)}, u32[]{:S(2)}, u32[]{:S(2)}) collective-permute-start(f32[384,256]{1,0:T(8,128)S(1)} %broadcast_select_fusion.5), channel_id=1, source_target_pairs={{0,96},{8,104},{16,112},{24,120},{2,98},{10,106},{18,114},{26,122}... | collective-permute-start | bytes 1179656 | tf_op jit(solution)/shard_map/ppermute | solution.py:338
  76.8 5.1 %collective-permute-start.22 = (f32[16,128]{1,0:T(8,128)S(1)}, f32[16,128]{1,0:T(8,128)S(1)}, u32[]{:S(2)}, u32[]{:S(2)}) collective-permute-start(f32[16,128]{1,0:T(8,128)S(1)} %add.53), channel_id=1, source_target_pairs={{0,96},{8,104},{16,112},{24,120},{32,64},{40,72},{48,80},{56,88},{... | collective-permute-start | bytes 24584 | tf_op jit(solution)/shard_map/ppermute | solution.py:375
  95.9 12.9 %collective-permute-start.21 = (f32[384,256]{1,0:T(8,128)S(1)}, f32[384,256]{1,0:T(8,128)S(1)}, u32[]{:S(2)}, u32[]{:S(2)}) collective-permute-start(f32[384,256]{1,0:T(8,128)S(1)} %broadcast_select_fusion.6.own), channel_id=1, source_target_pairs={{0,1},{1,0},{2,3},{3,2},{4,5},{5,4},{6,7},{7,6},{8,9},{9,8},{10,11... | collective-permute-start | bytes 1179656 | tf_op jit(solution)/shard_map/ppermute | solution.py:381
  97.9 1.0 copy-start
  99.9 18.5 %collective-permute-start.20 = (f32[512,256]{1,0:T(8,128)}, f32[512,256]{1,0:T(8,128)S(1)}, u32[]{:S(2)}, u32[]{:S(2)}) collective-permute-start(f32[512,256]{1,0:T(8,128)} %get-tuple-element.94), channel_id=1, source_target_pairs={{6,4},{7,5},{14,12},{15,13},{22,20},{23,21},{30,28},{31,29},{38,36... | collective-permute-start | bytes 1572872 | tf_op jit(solution)/shard_map/ppermute | solution.py:403
  100.6 17.8 %collective-permute-start.19 = (f32[512,256]{1,0:T(8,128)S(1)}, f32[512,256]{1,0:T(8,128)}, u32[]{:S(2)}, u32[]{:S(2)}) collective-permute-start(f32[512,256]{1,0:T(8,128)S(1)} %get-tuple-element.95), channel_id=1, source_target_pairs={{2,4},{3,5},{10,12},{11,13},{18,20},{19,21},{26,28},{27,29},{34,36... | collective-permute-start | bytes 1572872 | tf_op jit(solution)/shard_map/ppermute | solution.py:402
  102.1 16.3 %collective-permute-start.25 = (f32[16,256]{1,0:T(8,128)S(1)}, f32[16,256]{1,0:T(8,128)S(1)}, u32[]{:S(2)}, u32[]{:S(2)}) collective-permute-start(f32[16,256]{1,0:T(8,128)S(1)} %broadcast_in_dim.26), channel_id=1, source_target_pairs={{0,6},{1,7},{8,14},{9,15},{16,22},{17,23},{24,30},{25,31},{32,38},... | collective-permute-start | bytes 49160 | tf_op jit(solution)/shard_map/ppermute | solution.py:390
  107.5 10.9 %collective-permute-start.24 = (f32[16,256]{1,0:T(8,128)S(1)}, f32[16,256]{1,0:T(8,128)S(1)}, u32[]{:S(2)}, u32[]{:S(2)}) collective-permute-start(f32[16,256]{1,0:T(8,128)S(1)} %broadcast_in_dim.26), channel_id=1, source_target_pairs={{0,4},{1,5},{8,12},{9,13},{16,20},{17,21},{24,28},{25,29},{32,36},... | collective-permute-start | bytes 49160 | tf_op jit(solution)/shard_map/ppermute | solution.py:390
  108.8 9.6 %collective-permute-start.23 = (f32[16,256]{1,0:T(8,128)S(1)}, f32[16,256]{1,0:T(8,128)S(1)}, u32[]{:S(2)}, u32[]{:S(2)}) collective-permute-start(f32[16,256]{1,0:T(8,128)S(1)} %broadcast_in_dim.26), channel_id=1, source_target_pairs={{0,2},{1,3},{8,10},{9,11},{16,18},{17,19},{24,26},{25,27},{32,34},... | collective-permute-start | bytes 49160 | tf_op jit(solution)/shard_map/ppermute | solution.py:390
  118.7 11.9 %collective-permute-start.26 = (f32[1040,256]{1,0:T(8,128)S(1)}, f32[1040,256]{1,0:T(8,128)S(1)}, u32[]{:S(2)}, u32[]{:S(2)}) collective-permute-start(f32[1040,256]{1,0:T(8,128)S(1)} %pad_maximum_fusion.mine.own_sums), channel_id=1, source_target_pairs={{0,1},{1,0},{2,3},{3,2},{4,5},{5,4},{6,7},{7,6},{8,9},{9,8},{10,11... | collective-permute-start | bytes 3194888 | tf_op jit(solution)/shard_map/ppermute | solution.py:408
Sparse Core Ops, SparseCore 0:
  45.8 51.5 all-gather.2

commit v7 on v6

--- a/solution.py
+++ b/solution.py
@@ -203,105 +203,129 @@
     )(weights, flat)
 
 
-def panel_kernel(place, mine, theirs, own_sums, other_sums, w00, l10, w11, panels, high, low, taken, factors):
-    step = pl.program_id(0)
-    even = place[1] % 2 == 0
-
-    @pl.when(step == 0)
-    def _():
-        for k, ref in enumerate((w00, l10, w11)):
-            factors[0, k], factors[1, k] = halves(ref[...])
-
+ROWS = 256
+
+
+def final_kernel(
+    place, flat, across, mine, theirs, w00, l10, w11, sums, out, panels, checksum,
+    block, right, solved, high, low, right_high, right_low, ready, factors, block_sem, right_sem, panel_sem, out_sem,
+):
+    row_index, col_index = place[0], place[1]
+    even = col_index % 2 == 0
+    blocks = [
+        pltpu.make_async_copy(flat.at[pl.ds(ROWS * i, ROWS)], block.at[pl.ds(ROWS * i, ROWS)], block_sem.at[i]) for i in range(4)
+    ]
+    rights = [pltpu.make_async_copy(across.at[pl.ds(8 * i, 8)], right.at[pl.ds(8 * i, 8)], right_sem.at[i]) for i in range(2)]
+    for copy in (rights[0], *blocks, rights[1]):
+        copy.start()
+
+    for k, ref in enumerate((w00, l10, w11)):
+        factors[0, k], factors[1, k] = halves(ref[...])
     f00, f10, f11 = [(factors[0, k], factors[1, k]) for k in range(3)]
-    own = jnp.concatenate([mine[...], own_sums[...]], axis=0)
-    other = jnp.concatenate([theirs[...], other_sums[...]], axis=0)
-    first = jnp.where(even, own, other)
-    second = jnp.where(even, other, own)
-    left = dot3(halves(first), f00, NT)
-    right = dot3(halves(second - dot3(halves(left), f10, NT)), f11, NT)
-    panels[:, 0:256] = left[0:512]
-    top = (step == 0) & (place[0] == 0) & (lax.broadcasted_iota(jnp.int32, (512, 1), 0) < NB)
-    panels[:, 256:512] = jnp.where(top, 0.0, right[0:512])
-    last = dot3(halves(right), f11, NN)
-    last_high, last_low = halves(last)
-    rest = dot3(halves(left - dot3((last_high, last_low), f10, NN)), f00, NN)
-    high[:, 256:512] = last_high[0:512]
-    low[:, 256:512] = last_low[0:512]
-    high[:, 0:256], low[:, 0:256] = halves(rest[0:512])
-    taken[:, 0:256] = rest[512:528]
-    taken[:, 256:512] = last[512:528]
-
-
-def panel_call(place, mine, theirs, w00, l10, w11):
-    full = lambda *shape: pl.BlockSpec(shape, lambda i: (0,) * len(shape))
-    part = lambda n: pl.BlockSpec((512, n), lambda i: (i, 0))
-    tail = pl.BlockSpec((16, NB), lambda i: (1024 // 16, 0))
-    return pl.pallas_call(
-        panel_kernel, grid=(2,),
-        out_shape=(
-            jax.ShapeDtypeStruct((1024, 512), F32),
-            jax.ShapeDtypeStruct((1024, 512), BF16),
-            jax.ShapeDtypeStruct((1024, 512), BF16),
-            jax.ShapeDtypeStruct((16, 512), F32),
-        ),
-        in_specs=[SMEM, part(NB), part(NB), tail, tail, full(NB, NB), full(NB, NB), full(NB, NB)],
-        out_specs=(part(512), part(512), part(512), full(16, 512)),
-        scratch_shapes=[pltpu.VMEM((2, 3, NB, NB), BF16)],
-        name="panel_solve", **FACTOR,
-    )(place, mine, theirs, mine, theirs, w00, l10, w11)
-
-
-def update_kernel(place, flat, across, high, low, sums, taken, out, checksum, right_high, right_low):
-    group, step = pl.program_id(0), pl.program_id(1)
-    row_index, col_index = place[0], place[1]
-
-    @pl.when(step == 0)
-    def _():
+    solves = []
+    for half in range(2):
+        rows = slice(512 * half, 512 * half + 512 + 16 * half)
+        first = jnp.where(even, mine[rows], theirs[rows])
+        second = jnp.where(even, theirs[rows], mine[rows])
+        left = dot3(halves(first), f00, NT)
+        bottom = dot3(halves(second - dot3(halves(left), f10, NT)), f11, NT)
+        solved[512 * half : 512 * half + 512, 0:256] = left[0:512]
+        if half == 0:
+            top = (row_index == 0) & (lax.broadcasted_iota(jnp.int32, (512, 1), 0) < NB)
+            solved[0:512, 256:512] = jnp.where(top, 0.0, bottom)
+        else:
+            solved[512:1024, 256:512] = bottom[0:512]
+        copy = pltpu.make_async_copy(
+            solved.at[pl.ds(512 * half, 512)], panels.at[pl.ds(512 * half, 512)], panel_sem.at[half]
+        )
+        copy.start()
+        solves.append(copy)
+        last = halves(dot3(halves(bottom), f11, NN))
+        high[rows, 256:512], low[rows, 256:512] = last
+        high[rows, 0:256], low[rows, 0:256] = halves(dot3(halves(left - dot3(last, f10, NN)), f00, NN))
+
+    def put(slot, group, step):
+        return pltpu.make_async_copy(
+            ready.at[slot], out.at[pl.ds(pl.multiple_of(step * ROWS, ROWS), ROWS), group], out_sem.at[slot]
+        )
+
+    for group in range(2):
+        rights[group].wait()
         for u in range(4):
             for h in range(2):
                 span = slice(NB * h, NB * h + NB)
-                right_high[u, span], right_low[u, span] = halves(across[2 * u + h])
-
-    rows = out.shape[0]
-    base = pl.multiple_of(step * rows, rows)
-    top = (step * rows + lax.broadcasted_iota(jnp.int32, (rows, 1), 0) < NB) & (row_index < 2)
-    y_high, y_low = halves(taken[...])
-    mine = (
-        jnp.concatenate([high[pl.ds(base, rows), :], y_high], axis=0),
-        jnp.concatenate([low[pl.ds(base, rows), :], y_low], axis=0),
-    )
-    for u in range(4):
-        product = dot3(mine, (right_high[u], right_low[u]), NN)
-        gone = top | ((group == 0) & (col_index < 2)) if u == 0 else top
-        for h in range(2):
-            q = 2 * u + h
-            value = flat[:, q, :] - product[0:rows, 128 * h : 128 * h + 128]
-            out[:, q, :] = jnp.where(gone, 0.0, value)
-            kept = sums[q : q + 1, :] - product[rows : rows + 1, 128 * h : 128 * h + 128]
-            if u == 0:
-                kept = jnp.where((group == 0) & (col_index < 2), 0.0, kept)
-            checksum[q : q + 1, :] = kept
-
-
-def update_call(place, flat, across, high, low, sums, taken):
-    rows = 256
-    full = lambda *shape: pl.BlockSpec(shape, lambda g, i: (0,) * len(shape))
+                right_high[u, span], right_low[u, span] = halves(right[8 * group + 2 * u + h])
+
+        def body(step, carry, group=group):
+            slot = step % 2
+            base = pl.multiple_of(step * ROWS, ROWS)
+            if group == 0:
+                for i in range(4):
+
+                    @pl.when(step == i)
+                    def _(i=i):
+                        blocks[i].wait()
+
+            @pl.when(step + 4 * group >= 2)
+            def _():
+                put(slot, group, step).wait()
+
+            g_high = jnp.concatenate([high[pl.ds(base, ROWS), :], high[1024:1040, :]], axis=0)
+            g_low = jnp.concatenate([low[pl.ds(base, ROWS), :], low[1024:1040, :]], axis=0)
+            top = (step * ROWS + lax.broadcasted_iota(jnp.int32, (ROWS, 1), 0) < NB) & (row_index < 2)
+            for u in range(4):
+                product = dot3((g_high, g_low), (right_high[u], right_low[u]), NN)
+                gone = top | (col_index < 2) if (group, u) == (0, 0) else top
+                for h in range(2):
+                    q = 2 * u + h
+                    lanes = slice(128 * h, 128 * h + 128)
+                    value = block[pl.ds(base, ROWS), group, q, :] - product[0:ROWS, lanes]
+                    ready[slot, :, q, :] = jnp.where(gone, 0.0, value)
+                    at = 8 * group + q
+                    kept = sums[at : at + 1, :] - product[ROWS : ROWS + 1, lanes]
+                    if (group, u) == (0, 0):
+                        kept = jnp.where(col_index < 2, 0.0, kept)
+                    checksum[at : at + 1, :] = kept
+            put(slot, group, step).start()
+            return carry
+
+        lax.fori_loop(0, 4, body, 0)
+    for slot in range(2):
+        put(slot, 1, 2 + slot).wait()
+    for copy in solves:
+        copy.wait()
+
+
+def final_call(place, flat, across, mine, theirs, w00, l10, w11, sums):
+    hbm = pl.BlockSpec(memory_space=pl.ANY)
     return pl.pallas_call(
-        update_kernel, grid=(2, 1024 // rows),
-        out_shape=(jax.ShapeDtypeStruct((1024, 16, 128), F32), jax.ShapeDtypeStruct((16, 128), F32)),
-        in_specs=[
-            SMEM,
-            pl.BlockSpec((rows, 8, 128), lambda g, i: (i, g, 0)),
-            pl.BlockSpec((8, NB, NB), lambda g, i: (g, 0, 0)),
-            full(1024, 512),
-            full(1024, 512),
-            pl.BlockSpec((8, 128), lambda g, i: (g, 0)),
-            full(16, 512),
+        final_kernel,
+        out_shape=(
+            jax.ShapeDtypeStruct((1024, 2, 8, 128), F32),
+            jax.ShapeDtypeStruct((1024, 512), F32),
+            jax.ShapeDtypeStruct((16, 128), F32),
+        ),
+        in_specs=[SMEM, hbm, hbm] + [VMEM] * 6,
+        out_specs=(hbm, hbm, VMEM),
+        scratch_shapes=[
+            pltpu.VMEM((1024, 2, 8, 128), F32),
+            pltpu.VMEM((16, NB, NB), F32),
+            pltpu.VMEM((1024, 512), F32),
+            pltpu.VMEM((1040, 512), BF16),
+            pltpu.VMEM((1040, 512), BF16),
+            pltpu.VMEM((4, 512, NB), BF16),
+            pltpu.VMEM((4, 512, NB), BF16),
+            pltpu.VMEM((2, ROWS, 8, 128), F32),
+            pltpu.VMEM((2, 3, NB, NB), BF16),
+            pltpu.SemaphoreType.DMA((4,)),
+            pltpu.SemaphoreType.DMA((2,)),
+            pltpu.SemaphoreType.DMA((2,)),
+            pltpu.SemaphoreType.DMA((2,)),
         ],
-        out_specs=(pl.BlockSpec((rows, 8, 128), lambda g, i: (i, g, 0)), pl.BlockSpec((8, 128), lambda g, i: (g, 0))),
-        scratch_shapes=[pltpu.VMEM((4, 512, NB), BF16), pltpu.VMEM((4, 512, NB), BF16)],
-        name="trailing_update", **FACTOR,
-    )(place, flat, across, high, low, sums, taken)
+        name="panels_and_trailing",
+        compiler_params=pltpu.CompilerParams(vmem_limit_bytes=40 * 1024 * 1024),
+        cost_estimate=SMALL,
+    )(place, flat, across, mine, theirs, w00, l10, w11, sums)
 
 
 def where_is(device):
@@ -370,12 +394,12 @@
 
     def beside(stage, value):
         before = partial[-1]
-        if stage >= 2:
-            d = (1, 3, 4, 12)[stage - 2]
+        if stage <= 4:
+            d = (1, 3, 4, 12)[stage - 1]
             partial.append(before + lax.ppermute(after(before, value), "row", [(r, r ^ d) for r in range(16)]))
         return after(value, before)
 
-    tree = spread(corner, [((0, 0), 0, (2, 1, 0)), ((0, 0), 1, (1, 0, 2))], here, beside)
+    tree = spread(corner, [((0, 0), 0, (2, 1, 0)), ((0, 0), 1, (0, 2, 1))], here, beside)
     sums = partial[-1]
     own = tree[-1]
     other = lax.ppermute(own, "col", swap_cores)
@@ -407,8 +431,8 @@
     mine = jnp.concatenate([upper, lower, panel_sums], axis=0)
     theirs = after(lax.ppermute(mine, "col", swap_cores), w11)
 
-    panels, high, low, taken = panel_call(place, mine, theirs, w00, l10, w11)
-    trailing, checksum = update_call(place, flat, across, high, low, sums, taken)
+    grouped = pltpu.with_memory_space_constraint(covariance.reshape(1024, 2, 8, 128), pltpu.HBM)
+    trailing, panels, checksum = final_call(place, grouped, across, mine, theirs, w00, l10, w11, sums)
     return (
         trailing.reshape(4, 1, NB, 8, 1, NB),
         panels.reshape(4, 1, NB, 512),

time: 165 us -> 162 us (0.982); the launches traced: 164 us -> 159 us
  waiting for transfers between devices: 34.7 us -> 26 us
  starting transfers between devices: 55.8 us -> 61.3 us
  Pallas kernels: 54.5 us -> 51.3 us
  local copies, waits for them, and re-layouts: 1.95 us -> 3.6 us
    ppermute x6, waiting for transfers between devices: 28.8 us -> 15 us  [spread(): arrived = lax.ppermute(value, ('row', 'col'), pairs)]
    ppermute x1, starting transfers between devices: 2.03 us -> 12.9 us  [shards(): other = lax.ppermute(own, 'col', swap_cores)]
    ppermute x4, starting transfers between devices: 10.2 us -> 4.35 us  [beside(): lax.ppermute(after(before, value), 'row', [(r, r ^ d) for r in range(16)])]
    ppermute x1, starting transfers between devices: 1.36 us -> 5.47 us  [shards(): from_right = lax.ppermute(column, 'col', [(0, 6), (1, 7)])]
    ppermute x4, waiting for transfers between devices: 5.01 us -> 8.7 us  [beside(): lax.ppermute(after(before, value), 'row', [(r, r ^ d) for r in range(16)])]
    pallas_call x2 -> x1, Pallas kernels: 26.8 us -> 23.6 us  [final_call(): pl.pallas_call(final_kernel, out_shape=(jax.ShapeDtypeStruct((1024, 2, 8,...]
    ppermute x1, starting transfers between devices: 2.58 us -> 0.56 us  [shards(): theirs = after(lax.ppermute(mine, 'col', swap_cores), w11)]
    ppermute x3, starting transfers between devices: 7.91 us -> 6.16 us  [shards(): lax.ppermute(near_sums, 'col', [(0, 2 * k), (1, 2 * k + 1)])]
  transfers between devices with their start and end apart: 28 -> 28, of which waited for: 11 -> 10; matrix products, arithmetic and copies ran while one was open for 2% -> 2% of each run, Pallas kernels for 19% -> 15%
where the time goes in v7:
time: 162 us; the launch traced here: 159 us
  starting transfers between devices  61.3 us (38%)
  Pallas kernels  51.3 us (32%)
  waiting for transfers between devices  26 us (16%)
  between operations  14.6 us (9%)
  local copies, waits for them, and re-layouts  3.6 us (2%)
  other arithmetic  2.73 us (2%)
    pallas_call x1, Pallas kernels, final_call(): pl.pallas_call(final_kernel, out_shape=(jax.ShapeDtypeStruct((1024, 2, 8,...  23.6 us
    ppermute x7, starting transfers between devices, shards(): lax.ppermute(pieces[j] if j < 4 else after(pieces[j], fetched), 'row', [(...  15.9 us
    ppermute x6, waiting for transfers between devices, spread(): arrived = lax.ppermute(value, ('row', 'col'), pairs)  15 us
    ppermute x1, starting transfers between devices, shards(): other = lax.ppermute(own, 'col', swap_cores)  12.9 us
    ppermute x6, starting transfers between devices, spread(): arrived = lax.ppermute(value, ('row', 'col'), pairs)  10.2 us
    pallas_call x1, Pallas kernels, second_factor(): pl.pallas_call(second_kernel, out_shape=(TILE, TILE), in_specs=[SMEM, VME...  9.31 us
    ppermute x4, waiting for transfers between devices, beside(): lax.ppermute(after(before, value), 'row', [(r, r ^ d) for r in range(16)])  8.7 us
    pallas_call x1, Pallas kernels, first_factor(): pl.pallas_call(first_kernel, out_shape=TILE, in_specs=[SMEM, VMEM, VMEM],...  8.22 us
  transfers between devices with their start and end apart: 28, of which 10 were waited for; matrix products, arithmetic and copies ran while one was open for 2% of the time, Pallas kernels for 15%

profile of v7, /device:TPU:1, one launch (start us, length us, event | category | flops | bytes accessed | tf_op | source)
XLA Modules:
  0.0 159.5 jit_solution(8179162630399319938)
XLA Ops:
  7.2 3.3 %corner_tiles.1 = (f32[256,256]{1,0:T(8,128)}, f32[256,256]{1,0:T(8,128)}, f32[256,256]{1,0:T(8,128)}, f32[256,256]{1,0:T(8,128)}, f32[256,256]{1,0:T(8,128)}, /...) custom-call(f32[1024,16,128]{2,1,0:T(8,128)} %bitcast.13), custom_call_target="tpu_custom_call" | custom-call | tf_op jit(solution)/shard_map/corner_tiles/pallas_call | solution.py:167
  10.5 1.3 collective-permute-start
  11.8 6.4 %collective-permute-start.5 = (f32[256,256]{1,0:T(8,128)}, f32[256,256]{1,0:T(8,128)S(1)}, u32[]{:S(2)}, u32[]{:S(2)}) collective-permute-start(f32[256,256]{1,0:T(8,128)} %get-tuple-element.52), channel_id=1, source_target_pairs={{0,48},{8,56},{1,49},{9,57},{2,50},{10,58},{3,51},{11,59},{4,52},{... | collective-permute-start | bytes 786440 | tf_op jit(solution)/shard_map/ppermute | solution.py:409
  18.2 1.3 collective-permute-start.6
  19.5 1.3 collective-permute-start.7
  21.0 1.5 collective-permute-start.1
  22.5 1.3 collective-permute-start.2
  23.9 2.0 %collective-permute-start.3 = (f32[256,256]{1,0:T(8,128)}, f32[256,256]{1,0:T(8,128)}, u32[]{:S(2)}, u32[]{:S(2)}) collective-permute-start(f32[256,256]{1,0:T(8,128)} %get-tuple-element.49), channel_id=1, source_target_pairs={{0,80},{8,88},{1,81},{9,89},{2,82},{10,90},{3,83},{11,91},{4,84},{... | collective-permute-start | bytes 786440 | tf_op jit(solution)/shard_map/ppermute | solution.py:409
  25.9 2.0 %collective-permute-start.4 = (f32[256,256]{1,0:T(8,128)}, f32[256,256]{1,0:T(8,128)}, u32[]{:S(2)}, u32[]{:S(2)}) collective-permute-start(f32[256,256]{1,0:T(8,128)} %get-tuple-element.51), channel_id=1, source_target_pairs={{0,64},{8,72},{1,65},{9,73},{2,66},{10,74},{3,67},{11,75},{4,68},{... | collective-permute-start | bytes 786440 | tf_op jit(solution)/shard_map/ppermute | solution.py:409
  27.9 1.0 maximum_select_fusion
  28.9 0.2 collective-permute-done.7
  29.1 2.1 %collective-permute-start.8 = (f32[384,256]{1,0:T(8,128)S(1)}, f32[384,256]{1,0:T(8,128)S(1)}, u32[]{:S(2)}, u32[]{:S(2)}) collective-permute-start(f32[384,256]{1,0:T(8,128)S(1)} %maximum_select_fusion), channel_id=1, source_target_pairs={{0,2},{1,33}} | collective-permute-start | bytes 1179656 | tf_op jit(solution)/shard_map/ppermute | solution.py:362
  31.4 6.9 %first_column.1 = (f32[1024,256]{1,0:T(8,128)S(1)}, f32[16,128]{1,0:T(8,128)S(1)}) custom-call(f32[1024]{0:T(1024)S(1)} %broadcast_select_fusion.8.weights, f32[1024,16,128]{2,1,0:T(8,128)} %bitcast.14), custom_call_target="tpu_custom_call" | custom-call | flops 100000000 | bytes 100000 | tf_op jit(solution)/shard_map/first_column/pallas_call | solution.py:194
  38.3 2.0 %collective-permute-done.3 = f32[256,256]{1,0:T(8,128)} collective-permute-done((f32[256,256]{1,0:T(8,128)}, f32[256,256]{1,0:T(8,128)}, u32[]{:S(2)}, u32[]{:S(2)}) %collective-permute-start.3) | collective-permute-done | bytes 262176 | tf_op jit(solution)/shard_map/ppermute | solution.py:409
  40.3 0.8 select_select_fusion.1
  41.3 1.3 collective-permute-start.11
  42.6 1.1 collective-permute-start.12
  43.7 1.5 collective-permute-done.12
  45.2 2.1 %collective-permute-done.11 = f32[384,256]{1,0:T(8,128)S(1)} collective-permute-done((f32[384,256]{1,0:T(8,128)S(1)}, f32[384,256]{1,0:T(8,128)S(1)}, u32[]{:S(2)}, u32[]{:S(2)}) %collective-permute-start.11) | collective-permute-done | bytes 393248 | tf_op jit(solution)/shard_map/ppermute | solution.py:362
  47.3 1.3 collective-permute-start.13
  48.8 3.7 %collective-permute-done.14 = f32[16,128]{1,0:T(8,128)S(1)} collective-permute-done((f32[16,128]{1,0:T(8,128)S(1)}, f32[16,128]{1,0:T(8,128)S(1)}, u32[]{:S(2)}, u32[]{:S(2)}) %collective-permute-start.14) | collective-permute-done | bytes 8224 | tf_op jit(solution)/shard_map/ppermute | solution.py:399
  52.5 0.9 collective-permute-done.13
  53.4 1.3 collective-permute-start.15
  54.8 2.5 %collective-permute-done.16 = f32[16,128]{1,0:T(8,128)S(1)} collective-permute-done((f32[16,128]{1,0:T(8,128)S(1)}, f32[16,128]{1,0:T(8,128)S(1)}, u32[]{:S(2)}, u32[]{:S(2)}) %collective-permute-start.16) | collective-permute-done | bytes 8224 | tf_op jit(solution)/shard_map/ppermute | solution.py:399
  57.3 2.1 %collective-permute-done.15 = f32[384,256]{1,0:T(8,128)S(1)} collective-permute-done((f32[384,256]{1,0:T(8,128)S(1)}, f32[384,256]{1,0:T(8,128)S(1)}, u32[]{:S(2)}, u32[]{:S(2)}) %collective-permute-start.15) | collective-permute-done | bytes 393248 | tf_op jit(solution)/shard_map/ppermute | solution.py:362
  59.4 2.1 %collective-permute-start.17 = (f32[384,256]{1,0:T(8,128)S(1)}, f32[384,256]{1,0:T(8,128)}, u32[]{:S(2)}, u32[]{:S(2)}) collective-permute-start(f32[384,256]{1,0:T(8,128)S(1)} %broadcast_select_fusion.4), channel_id=1, source_target_pairs={{0,32},{8,40},{16,48},{24,56},{2,34},{10,42},{18,50},{26,58},{4,36... | collective-permute-start | bytes 1179656 | tf_op jit(solution)/shard_map/ppermute | solution.py:362
  61.5 5.5 %collective-permute-start.10 = (f32[1024,256]{1,0:T(8,128)S(1)}, f32[1024,256]{1,0:T(8,128)S(1)}, u32[]{:S(2)}, u32[]{:S(2)}) collective-permute-start(f32[1024,256]{1,0:T(8,128)S(1)} %get-tuple-element.58), channel_id=1, source_target_pairs={{0,6},{1,7},{8,14},{9,15},{16,22},{17,23},{24,30},{25,31},{32,38},... | collective-permute-start | bytes 3145736 | tf_op jit(solution)/shard_map/ppermute | solution.py:423
  67.0 2.3 %collective-permute-start.9 = (f32[1024,256]{1,0:T(8,128)S(1)}, f32[1024,256]{1,0:T(8,128)}, u32[]{:S(2)}, u32[]{:S(2)}) collective-permute-start(f32[1024,256]{1,0:T(8,128)S(1)} %get-tuple-element.58), channel_id=1, source_target_pairs={{0,2},{1,3},{8,10},{9,11},{16,18},{17,19},{24,26},{25,27},{32,34},... | collective-permute-start | bytes 3145736 | tf_op jit(solution)/shard_map/ppermute | solution.py:422
  69.3 3.1 %collective-permute-start.18 = (f32[16,128]{1,0:T(8,128)S(1)}, f32[16,128]{1,0:T(8,128)S(1)}, u32[]{:S(2)}, u32[]{:S(2)}) collective-permute-start(f32[16,128]{1,0:T(8,128)S(1)} %add.53), channel_id=1, source_target_pairs={{0,96},{8,104},{16,112},{24,120},{32,64},{40,72},{48,80},{56,88},{... | collective-permute-start | bytes 24584 | tf_op jit(solution)/shard_map/ppermute | solution.py:399
  72.4 1.0 collective-permute-done.18
  73.5 2.1 %collective-permute-start.19 = (f32[384,256]{1,0:T(8,128)S(1)}, f32[384,256]{1,0:T(8,128)}, u32[]{:S(2)}, u32[]{:S(2)}) collective-permute-start(f32[384,256]{1,0:T(8,128)S(1)} %broadcast_select_fusion.5), channel_id=1, source_target_pairs={{0,96},{8,104},{16,112},{24,120},{2,98},{10,106},{18,114},{26,122}... | collective-permute-start | bytes 1179656 | tf_op jit(solution)/shard_map/ppermute | solution.py:362
  75.6 10.0 %collective-permute-done.19 = f32[384,256]{1,0:T(8,128)} collective-permute-done((f32[384,256]{1,0:T(8,128)S(1)}, f32[384,256]{1,0:T(8,128)}, u32[]{:S(2)}, u32[]{:S(2)}) %collective-permute-start.19) | collective-permute-done | bytes 393248 | tf_op jit(solution)/shard_map/ppermute | solution.py:362
  85.6 12.9 %collective-permute-start.22 = (f32[384,256]{1,0:T(8,128)S(1)}, f32[384,256]{1,0:T(8,128)S(1)}, u32[]{:S(2)}, u32[]{:S(2)}) collective-permute-start(f32[384,256]{1,0:T(8,128)S(1)} %broadcast_select_fusion.6.own), channel_id=1, source_target_pairs={{0,1},{1,0},{2,3},{3,2},{4,5},{5,4},{6,7},{7,6},{8,9},{9,8},{10,11... | collective-permute-start | bytes 1179656 | tf_op jit(solution)/shard_map/ppermute | solution.py:405
  98.5 1.0 copy-done.2
  99.5 0.2 select_select_fusion
  99.7 0.9 fusion
  100.5 0.7 collective-permute-start.21
  101.2 1.5 collective-permute-start.20
  102.7 3.6 %collective-permute-start.25 = (f32[16,256]{1,0:T(8,128)S(1)}, f32[16,256]{1,0:T(8,128)S(1)}, u32[]{:S(2)}, u32[]{:S(2)}) collective-permute-start(f32[16,256]{1,0:T(8,128)S(1)} %broadcast_in_dim.26), channel_id=1, source_target_pairs={{0,6},{1,7},{8,14},{9,15},{16,22},{17,23},{24,30},{25,31},{32,38},... | collective-permute-start | bytes 49160 | tf_op jit(solution)/shard_map/ppermute | solution.py:414
  106.3 1.3 collective-permute-start.24
  107.6 1.3 collective-permute-start.23
  109.0 8.2 %first_factor.1.w00 = f32[256,256]{1,0:T(8,128)S(1)} custom-call(s32[2]{0:T(128)S(1)} %pad_add_fusion.place, f32[384,256]{1,0:T(8,128)S(1)} %broadcast_select_fusion.6.own, f32[384,256]{1,0:T(8,128)S(1)} %collective-permute-done.22.other), custom_call_target="tpu_custom_call" | custom-call | flops 100000000 | bytes 100000 | tf_op jit(solution)/shard_map/first_factor/pallas_call | solution.py:144
  117.3 0.1 broadcast_select_fusion.1
  117.5 0.6 collective-permute-start.26
  118.1 9.3 %second_factor.1 = (f32[256,256]{1,0:T(8,128)S(1)}, f32[256,256]{1,0:T(8,128)S(1)}) custom-call(s32[2]{0:T(128)S(1)} %pad_add_fusion.place, f32[256,256]{1,0:T(8,128)S(1)} %first_factor.1.w00, f32[384,256]{1,0:T(8,128)S(1)} %broadcast_select_fusion.6.own, f32[384,256]{1,0:T(8,128)S(1)} %collective-permute-done.22.other), custom_call_target="tpu_custom_call" | custom-call | flops 100000000 | bytes 100000 | tf_op jit(solution)/shard_map/second_factor/pallas_call | solution.py:151
  127.4 0.7 copy-done
  128.1 0.9 copy-done.1
  129.0 23.6 %panels_and_trailing.1 = (f32[1024,2,8,128]{3,2,1,0:T(8,128)}, f32[1024,512]{1,0:T(8,128)}, f32[16,128]{1,0:T(8,128)}) custom-call(s32[2]{0:T(128)S(1)} %pad_add_fusion.place, f32[1024,2,8,128]{3,2,1,0:T(8,128)} %bitcast.15, f32[16,256,256]{2,1,0:T(8,128)} %bitcast.16, f32[1040,256]{1,0:T(8,128)S(1)} %pad_maximum_fusion.mine, ...), custom_call_target="tpu_custom_call" | custom-call | flops 100000000 | bytes 100000 | tf_op jit(solution)/shard_map/panels_and_trailing/pallas_call | solution.py:301
  (49 shorter events, 0.9 us)
Async XLA Ops:
  7.2 120.9 %all-gather.3.cloned.1.call-start = ((), (), s32[]{:S(2)}) async-start(), calls=%async_computation | async-start | bytes 4456448 | tf_op jit(solution)/shard_map/all_gather | solution.py:410
  10.5 20.7 %copy-start.4 = (f32[4,1,256]{2,1,0:T(1,128)S(1)}, f32[4,1,256]{2,1,0:T(1,128)}, u32[]{:S(2)}) copy-start(f32[4,1,256]{2,1,0:T(1,128)} %param.3) | copy-start | bytes 12292
  10.5 10.5 %collective-permute-start = (f32[256,256]{1,0:T(8,128)}, f32[256,256]{1,0:T(8,128)S(1)}, u32[]{:S(2)}, u32[]{:S(2)}) collective-permute-start(f32[256,256]{1,0:T(8,128)} %get-tuple-element.44), channel_id=1, source_target_pairs={{8,0},{9,1}} | collective-permute-start | bytes 786440 | tf_op jit(solution)/shard_map/ppermute | solution.py:386
  11.8 12.0 %collective-permute-start.5 = (f32[256,256]{1,0:T(8,128)}, f32[256,256]{1,0:T(8,128)S(1)}, u32[]{:S(2)}, u32[]{:S(2)}) collective-permute-start(f32[256,256]{1,0:T(8,128)} %get-tuple-element.52), channel_id=1, source_target_pairs={{0,48},{8,56},{1,49},{9,57},{2,50},{10,58},{3,51},{11,59},{4,52},{... | collective-permute-start | bytes 786440 | tf_op jit(solution)/shard_map/ppermute | solution.py:409
  18.2 7.6 %collective-permute-start.6 = (f32[256,256]{1,0:T(8,128)}, f32[256,256]{1,0:T(8,128)S(1)}, u32[]{:S(2)}, u32[]{:S(2)}) collective-permute-start(f32[256,256]{1,0:T(8,128)} %get-tuple-element.53), channel_id=1, source_target_pairs={{0,32},{8,40},{1,33},{9,41},{2,34},{10,42},{3,35},{11,43},{4,36},{... | collective-permute-start | bytes 786440 | tf_op jit(solution)/shard_map/ppermute | solution.py:409
  19.5 9.6 %collective-permute-start.7 = (f32[256,256]{1,0:T(8,128)}, f32[256,256]{1,0:T(8,128)S(1)}, u32[]{:S(2)}, u32[]{:S(2)}) collective-permute-start(f32[256,256]{1,0:T(8,128)} %get-tuple-element.54), channel_id=1, source_target_pairs={{0,16},{8,24},{1,17},{9,25},{2,18},{10,26},{3,19},{11,27},{4,20},{... | collective-permute-start | bytes 786440 | tf_op jit(solution)/shard_map/ppermute | solution.py:409
  21.0 17.3 %collective-permute-start.1 = (f32[256,256]{1,0:T(8,128)}, f32[256,256]{1,0:T(8,128)S(1)}, u32[]{:S(2)}, u32[]{:S(2)}) collective-permute-start(f32[256,256]{1,0:T(8,128)} %get-tuple-element.45), channel_id=1, source_target_pairs={{0,112},{8,120},{1,113},{9,121},{2,114},{10,122},{3,115},{11,123},... | collective-permute-start | bytes 786440 | tf_op jit(solution)/shard_map/ppermute | solution.py:409
  22.5 15.8 %collective-permute-start.2 = (f32[256,256]{1,0:T(8,128)}, f32[256,256]{1,0:T(8,128)S(1)}, u32[]{:S(2)}, u32[]{:S(2)}) collective-permute-start(f32[256,256]{1,0:T(8,128)} %get-tuple-element.47), channel_id=1, source_target_pairs={{0,96},{8,104},{1,97},{9,105},{2,98},{10,106},{3,99},{11,107},{4,1... | collective-permute-start | bytes 786440 | tf_op jit(solution)/shard_map/ppermute | solution.py:409
  23.9 16.5 %collective-permute-start.3 = (f32[256,256]{1,0:T(8,128)}, f32[256,256]{1,0:T(8,128)}, u32[]{:S(2)}, u32[]{:S(2)}) collective-permute-start(f32[256,256]{1,0:T(8,128)} %get-tuple-element.49), channel_id=1, source_target_pairs={{0,80},{8,88},{1,81},{9,89},{2,82},{10,90},{3,83},{11,91},{4,84},{... | collective-permute-start | bytes 786440 | tf_op jit(solution)/shard_map/ppermute | solution.py:409
  25.9 14.5 %collective-permute-start.4 = (f32[256,256]{1,0:T(8,128)}, f32[256,256]{1,0:T(8,128)}, u32[]{:S(2)}, u32[]{:S(2)}) collective-permute-start(f32[256,256]{1,0:T(8,128)} %get-tuple-element.51), channel_id=1, source_target_pairs={{0,64},{8,72},{1,65},{9,73},{2,66},{10,74},{3,67},{11,75},{4,68},{... | collective-permute-start | bytes 786440 | tf_op jit(solution)/shard_map/ppermute | solution.py:409
  29.1 12.1 %collective-permute-start.8 = (f32[384,256]{1,0:T(8,128)S(1)}, f32[384,256]{1,0:T(8,128)S(1)}, u32[]{:S(2)}, u32[]{:S(2)}) collective-permute-start(f32[384,256]{1,0:T(8,128)S(1)} %maximum_select_fusion), channel_id=1, source_target_pairs={{0,2},{1,33}} | collective-permute-start | bytes 1179656 | tf_op jit(solution)/shard_map/ppermute | solution.py:362
  31.4 9.0 %copy-start.3 = (f32[256,256]{1,0:T(8,128)S(1)}, f32[256,256]{1,0:T(8,128)}, u32[]{:S(2)}) copy-start(f32[256,256]{1,0:T(8,128)} %get-tuple-element.55) | copy-start | bytes 786436
  41.3 6.0 %collective-permute-start.11 = (f32[384,256]{1,0:T(8,128)S(1)}, f32[384,256]{1,0:T(8,128)S(1)}, u32[]{:S(2)}, u32[]{:S(2)}) collective-permute-start(f32[384,256]{1,0:T(8,128)S(1)} %broadcast_select_fusion.7), channel_id=1, source_target_pairs={{0,6},{2,4},{1,97},{33,65}} | collective-permute-start | bytes 1179656 | tf_op jit(solution)/shard_map/ppermute | solution.py:362
  42.6 2.6 %collective-permute-start.12 = (f32[16,128]{1,0:T(8,128)S(1)}, f32[16,128]{1,0:T(8,128)S(1)}, u32[]{:S(2)}, u32[]{:S(2)}) collective-permute-start(f32[16,128]{1,0:T(8,128)S(1)} %get-tuple-element.62), channel_id=1, source_target_pairs={{0,8},{8,0},{16,24},{24,16},{32,40},{40,32},{48,56},{56,48},{64,72... | collective-permute-start | bytes 24584 | tf_op jit(solution)/shard_map/ppermute | solution.py:399
  47.3 6.0 %collective-permute-start.13 = (f32[384,256]{1,0:T(8,128)S(1)}, f32[384,256]{1,0:T(8,128)S(1)}, u32[]{:S(2)}, u32[]{:S(2)}) collective-permute-start(f32[384,256]{1,0:T(8,128)S(1)} %broadcast_select_fusion.2), channel_id=1, source_target_pairs={{0,8},{2,10},{4,12},{6,14},{1,3},{33,35},{65,67},{97,99}} | collective-permute-start | bytes 1179656 | tf_op jit(solution)/shard_map/ppermute | solution.py:362
  48.7 3.8 %collective-permute-start.14 = (f32[16,128]{1,0:T(8,128)S(1)}, f32[16,128]{1,0:T(8,128)S(1)}, u32[]{:S(2)}, u32[]{:S(2)}) collective-permute-start(f32[16,128]{1,0:T(8,128)S(1)} %add.51), channel_id=1, source_target_pairs={{0,24},{8,16},{16,8},{24,0},{32,56},{40,48},{48,40},{56,32},{64,88... | collective-permute-start | bytes 24584 | tf_op jit(solution)/shard_map/ppermute | solution.py:399
  53.4 6.0 %collective-permute-start.15 = (f32[384,256]{1,0:T(8,128)S(1)}, f32[384,256]{1,0:T(8,128)S(1)}, u32[]{:S(2)}, u32[]{:S(2)}) collective-permute-start(f32[384,256]{1,0:T(8,128)S(1)} %broadcast_select_fusion.3), channel_id=1, source_target_pairs={{0,24},{2,26},{4,28},{6,30},{8,16},{10,18},{12,20},{14,22},{1,7},{... | collective-permute-start | bytes 1179656 | tf_op jit(solution)/shard_map/ppermute | solution.py:362
  54.7 2.6 %collective-permute-start.16 = (f32[16,128]{1,0:T(8,128)S(1)}, f32[16,128]{1,0:T(8,128)S(1)}, u32[]{:S(2)}, u32[]{:S(2)}) collective-permute-start(f32[16,128]{1,0:T(8,128)S(1)} %add.52), channel_id=1, source_target_pairs={{0,32},{8,40},{16,48},{24,56},{32,0},{40,8},{48,16},{56,24},{64,96... | collective-permute-start | bytes 24584 | tf_op jit(solution)/shard_map/ppermute | solution.py:399
  59.4 14.0 %collective-permute-start.17 = (f32[384,256]{1,0:T(8,128)S(1)}, f32[384,256]{1,0:T(8,128)}, u32[]{:S(2)}, u32[]{:S(2)}) collective-permute-start(f32[384,256]{1,0:T(8,128)S(1)} %broadcast_select_fusion.4), channel_id=1, source_target_pairs={{0,32},{8,40},{16,48},{24,56},{2,34},{10,42},{18,50},{26,58},{4,36... | collective-permute-start | bytes 1179656 | tf_op jit(solution)/shard_map/ppermute | solution.py:362
  61.5 37.0 %collective-permute-start.10 = (f32[1024,256]{1,0:T(8,128)S(1)}, f32[1024,256]{1,0:T(8,128)S(1)}, u32[]{:S(2)}, u32[]{:S(2)}) collective-permute-start(f32[1024,256]{1,0:T(8,128)S(1)} %get-tuple-element.58), channel_id=1, source_target_pairs={{0,6},{1,7},{8,14},{9,15},{16,22},{17,23},{24,30},{25,31},{32,38},... | collective-permute-start | bytes 3145736 | tf_op jit(solution)/shard_map/ppermute | solution.py:423
  67.0 32.5 %collective-permute-start.9 = (f32[1024,256]{1,0:T(8,128)S(1)}, f32[1024,256]{1,0:T(8,128)}, u32[]{:S(2)}, u32[]{:S(2)}) collective-permute-start(f32[1024,256]{1,0:T(8,128)S(1)} %get-tuple-element.58), channel_id=1, source_target_pairs={{0,2},{1,3},{8,10},{9,11},{16,18},{17,19},{24,26},{25,27},{32,34},... | collective-permute-start | bytes 3145736 | tf_op jit(solution)/shard_map/ppermute | solution.py:422
  69.3 4.2 %collective-permute-start.18 = (f32[16,128]{1,0:T(8,128)S(1)}, f32[16,128]{1,0:T(8,128)S(1)}, u32[]{:S(2)}, u32[]{:S(2)}) collective-permute-start(f32[16,128]{1,0:T(8,128)S(1)} %add.53), channel_id=1, source_target_pairs={{0,96},{8,104},{16,112},{24,120},{32,64},{40,72},{48,80},{56,88},{... | collective-permute-start | bytes 24584 | tf_op jit(solution)/shard_map/ppermute | solution.py:399
  73.5 12.0 %collective-permute-start.19 = (f32[384,256]{1,0:T(8,128)S(1)}, f32[384,256]{1,0:T(8,128)}, u32[]{:S(2)}, u32[]{:S(2)}) collective-permute-start(f32[384,256]{1,0:T(8,128)S(1)} %broadcast_select_fusion.5), channel_id=1, source_target_pairs={{0,96},{8,104},{16,112},{24,120},{2,98},{10,106},{18,114},{26,122}... | collective-permute-start | bytes 1179656 | tf_op jit(solution)/shard_map/ppermute | solution.py:362
  85.6 22.0 %collective-permute-start.22 = (f32[384,256]{1,0:T(8,128)S(1)}, f32[384,256]{1,0:T(8,128)S(1)}, u32[]{:S(2)}, u32[]{:S(2)}) collective-permute-start(f32[384,256]{1,0:T(8,128)S(1)} %broadcast_select_fusion.6.own), channel_id=1, source_target_pairs={{0,1},{1,0},{2,3},{3,2},{4,5},{5,4},{6,7},{7,6},{8,9},{9,8},{10,11... | collective-permute-start | bytes 1179656 | tf_op jit(solution)/shard_map/ppermute | solution.py:405
  98.5 1.0 copy-start.2
  100.5 16.7 %collective-permute-start.21 = (f32[512,256]{1,0:T(8,128)}, f32[512,256]{1,0:T(8,128)S(1)}, u32[]{:S(2)}, u32[]{:S(2)}) collective-permute-start(f32[512,256]{1,0:T(8,128)} %get-tuple-element.88), channel_id=1, source_target_pairs={{6,4},{7,5},{14,12},{15,13},{22,20},{23,21},{30,28},{31,29},{38,36... | collective-permute-start | bytes 1572872 | tf_op jit(solution)/shard_map/ppermute | solution.py:427
  101.2 16.0 %collective-permute-start.20 = (f32[512,256]{1,0:T(8,128)S(1)}, f32[512,256]{1,0:T(8,128)}, u32[]{:S(2)}, u32[]{:S(2)}) collective-permute-start(f32[512,256]{1,0:T(8,128)S(1)} %get-tuple-element.89), channel_id=1, source_target_pairs={{2,4},{3,5},{10,12},{11,13},{18,20},{19,21},{26,28},{27,29},{34,36... | collective-permute-start | bytes 1572872 | tf_op jit(solution)/shard_map/ppermute | solution.py:426
  102.7 14.5 %collective-permute-start.25 = (f32[16,256]{1,0:T(8,128)S(1)}, f32[16,256]{1,0:T(8,128)S(1)}, u32[]{:S(2)}, u32[]{:S(2)}) collective-permute-start(f32[16,256]{1,0:T(8,128)S(1)} %broadcast_in_dim.26), channel_id=1, source_target_pairs={{0,6},{1,7},{8,14},{9,15},{16,22},{17,23},{24,30},{25,31},{32,38},... | collective-permute-start | bytes 49160 | tf_op jit(solution)/shard_map/ppermute | solution.py:414
  106.3 10.9 %collective-permute-start.24 = (f32[16,256]{1,0:T(8,128)S(1)}, f32[16,256]{1,0:T(8,128)S(1)}, u32[]{:S(2)}, u32[]{:S(2)}) collective-permute-start(f32[16,256]{1,0:T(8,128)S(1)} %broadcast_in_dim.26), channel_id=1, source_target_pairs={{0,4},{1,5},{8,12},{9,13},{16,20},{17,21},{24,28},{25,29},{32,36},... | collective-permute-start | bytes 49160 | tf_op jit(solution)/shard_map/ppermute | solution.py:414
  107.6 9.6 %collective-permute-start.23 = (f32[16,256]{1,0:T(8,128)S(1)}, f32[16,256]{1,0:T(8,128)S(1)}, u32[]{:S(2)}, u32[]{:S(2)}) collective-permute-start(f32[16,256]{1,0:T(8,128)S(1)} %broadcast_in_dim.26), channel_id=1, source_target_pairs={{0,2},{1,3},{8,10},{9,11},{16,18},{17,19},{24,26},{25,27},{32,34},... | collective-permute-start | bytes 49160 | tf_op jit(solution)/shard_map/ppermute | solution.py:414
  117.5 10.6 %collective-permute-start.26 = (f32[1040,256]{1,0:T(8,128)S(1)}, f32[1040,256]{1,0:T(8,128)S(1)}, u32[]{:S(2)}, u32[]{:S(2)}) collective-permute-start(f32[1040,256]{1,0:T(8,128)S(1)} %pad_maximum_fusion.mine), channel_id=1, source_target_pairs={{0,1},{1,0},{2,3},{3,2},{4,5},{5,4},{6,7},{7,6},{8,9},{9,8},{10,11... | collective-permute-start | bytes 3194888 | tf_op jit(solution)/shard_map/ppermute | solution.py:432
  127.4 0.7 copy-start
  128.1 1.0 copy-start.1
Sparse Core Ops, SparseCore 0:
  41.4 55.7 all-gather.2

commit v8 on v7

--- a/solution.py
+++ b/solution.py
@@ -391,17 +391,21 @@
     )
     column, sums = column_call(weights, after(flat, corner))
     partial = [sums]
+    from_left = lax.ppermute(column, "col", [(0, 2), (1, 3)])
+    from_right = lax.ppermute(column, "col", [(0, 6), (1, 7)])
 
     def beside(stage, value):
         before = partial[-1]
         if stage <= 4:
             d = (1, 3, 4, 12)[stage - 1]
             partial.append(before + lax.ppermute(after(before, value), "row", [(r, r ^ d) for r in range(16)]))
-        return after(value, before)
-
-    tree = spread(corner, [((0, 0), 0, (2, 1, 0)), ((0, 0), 1, (0, 2, 1))], here, beside)
+        return after(value, (before, from_left, from_right) if stage == 4 else before)
+
+    tree = spread(corner, [((0, 0), 0, (2, 1, 0)), ((0, 0), 1, (1, 0, 2))], here, beside)
     sums = partial[-1]
-    own = tree[-1]
+    near_sums = jnp.broadcast_to(sums[0:2].reshape(1, NB), (16, NB))
+    far_sums = [lax.ppermute(near_sums, "col", [(0, 2 * k), (1, 2 * k + 1)]) for k in (1, 2, 3)]
+    own, far_sums = lax.optimization_barrier((tree[-1], far_sums))
     other = lax.ppermute(own, "col", swap_cores)
 
     piece = pieces[8]
@@ -410,19 +414,14 @@
     across = lax.all_gather(after(piece, (tree[0], column)), "row", axis=0)
     across = pltpu.with_memory_space_constraint(across, pltpu.HBM)
 
-    near_sums = jnp.broadcast_to(sums[0:2].reshape(1, NB), (16, NB))
-    far_sums = [lax.ppermute(near_sums, "col", [(0, 2 * k), (1, 2 * k + 1)]) for k in (1, 2, 3)]
     w00 = first_factor(place, own, other)
-    far_sums = after(far_sums, w00)
     panel_sums = near_sums
     for k in (1, 2, 3):
         panel_sums = jnp.where(x == k, far_sums[k - 1], panel_sums)
 
     l10, w11 = second_factor(place, w00, own, other)
-    from_left = lax.ppermute(column, "col", [(0, 2), (1, 3)])
-    from_right = lax.ppermute(column, "col", [(0, 6), (1, 7)])
-    from_left, from_right = after((from_left, from_right), tree[5])
     mine = jnp.where(x == 1, from_left, jnp.where(x == 3, from_right, column))
+    mine = after(mine, own)
     upper = lax.ppermute(mine[0:512], "col", [(2, 4), (3, 5)])
     lower = lax.ppermute(mine[512:1024], "col", [(6, 4), (7, 5)])
     upper, lower = after((upper, lower), w00)

time: 162 us -> 162 us (level)
    ppermute x6, waiting for transfers between devices: 15 us -> 10.6 us  [spread(): arrived = lax.ppermute(value, ('row', 'col'), pairs)]
    ppermute x1, starting transfers between devices: 5.47 us -> 1.36 us  [shards(): from_right = lax.ppermute(column, 'col', [(0, 6), (1, 7)])]
    ppermute x6, starting transfers between devices: 10.2 us -> 13.1 us  [spread(): arrived = lax.ppermute(value, ('row', 'col'), pairs)]
    ppermute x1, waiting for transfers between devices: 0.01 us -> 2.86 us  [shards(): from_right = lax.ppermute(column, 'col', [(0, 6), (1, 7)])]
  transfers between devices with their start and end apart: 28 -> 28, of which waited for: 10 -> 14; matrix products, arithmetic and copies ran while one was open for 2% -> 2% of each run, Pallas kernels for 15% -> 15%
where the time goes in v8:
time: 162 us; the launch traced here: 160 us
  starting transfers between devices  61.7 us (38%)
  Pallas kernels  51.3 us (32%)
  waiting for transfers between devices  27.1 us (17%)
  between operations  14.5 us (9%)
  other arithmetic  2.73 us (2%)
  local copies, waits for them, and re-layouts  2.63 us (2%)
    pallas_call x1, Pallas kernels, final_call(): pl.pallas_call(final_kernel, out_shape=(jax.ShapeDtypeStruct((1024, 2, 8,...  23.5 us
    ppermute x7, starting transfers between devices, shards(): lax.ppermute(pieces[j] if j < 4 else after(pieces[j], fetched), 'row', [(...  15.8 us
    ppermute x6, starting transfers between devices, spread(): arrived = lax.ppermute(value, ('row', 'col'), pairs)  13.1 us
    ppermute x1, starting transfers between devices, shards(): other = lax.ppermute(own, 'col', swap_cores)  12.7 us
    ppermute x6, waiting for transfers between devices, spread(): arrived = lax.ppermute(value, ('row', 'col'), pairs)  10.6 us
    ppermute x4, waiting for transfers between devices, beside(): lax.ppermute(after(before, value), 'row', [(r, r ^ d) for r in range(16)])  9.32 us
    pallas_call x1, Pallas kernels, second_factor(): pl.pallas_call(second_kernel, out_shape=(TILE, TILE), in_specs=[SMEM, VME...  9.31 us
    pallas_call x1, Pallas kernels, first_factor(): pl.pallas_call(first_kernel, out_shape=TILE, in_specs=[SMEM, VMEM, VMEM],...  8.22 us
  transfers between devices with their start and end apart: 28, of which 14 were waited for; matrix products, arithmetic and copies ran while one was open for 2% of the time, Pallas kernels for 15%

profile of v8, /device:TPU:1, one launch (start us, length us, event | category | flops | bytes accessed | tf_op | source)
XLA Modules:
  0.0 159.9 jit_solution(12899200329185862336)
XLA Ops:
  7.2 3.3 %corner_tiles.1 = (f32[256,256]{1,0:T(8,128)}, f32[256,256]{1,0:T(8,128)}, f32[256,256]{1,0:T(8,128)}, f32[256,256]{1,0:T(8,128)}, f32[256,256]{1,0:T(8,128)}, /...) custom-call(f32[1024,16,128]{2,1,0:T(8,128)} %bitcast.13), custom_call_target="tpu_custom_call" | custom-call | tf_op jit(solution)/shard_map/corner_tiles/pallas_call | solution.py:167
  10.5 1.3 collective-permute-start
  11.8 6.4 %collective-permute-start.5 = (f32[256,256]{1,0:T(8,128)}, f32[256,256]{1,0:T(8,128)S(1)}, u32[]{:S(2)}, u32[]{:S(2)}) collective-permute-start(f32[256,256]{1,0:T(8,128)} %get-tuple-element.52), channel_id=1, source_target_pairs={{0,48},{8,56},{1,49},{9,57},{2,50},{10,58},{3,51},{11,59},{4,52},{... | collective-permute-start | bytes 786440 | tf_op jit(solution)/shard_map/ppermute | solution.py:413
  18.2 1.3 collective-permute-start.6
  19.5 1.3 collective-permute-start.7
  21.0 1.5 collective-permute-start.1
  22.5 1.3 collective-permute-start.2
  23.9 2.0 %collective-permute-start.3 = (f32[256,256]{1,0:T(8,128)}, f32[256,256]{1,0:T(8,128)}, u32[]{:S(2)}, u32[]{:S(2)}) collective-permute-start(f32[256,256]{1,0:T(8,128)} %get-tuple-element.49), channel_id=1, source_target_pairs={{0,80},{8,88},{1,81},{9,89},{2,82},{10,90},{3,83},{11,91},{4,84},{... | collective-permute-start | bytes 786440 | tf_op jit(solution)/shard_map/ppermute | solution.py:413
  25.9 2.0 %collective-permute-start.4 = (f32[256,256]{1,0:T(8,128)}, f32[256,256]{1,0:T(8,128)}, u32[]{:S(2)}, u32[]{:S(2)}) collective-permute-start(f32[256,256]{1,0:T(8,128)} %get-tuple-element.51), channel_id=1, source_target_pairs={{0,64},{8,72},{1,65},{9,73},{2,66},{10,74},{3,67},{11,75},{4,68},{... | collective-permute-start | bytes 786440 | tf_op jit(solution)/shard_map/ppermute | solution.py:413
  27.9 1.0 maximum_select_fusion
  29.1 3.5 %collective-permute-start.8 = (f32[384,256]{1,0:T(8,128)S(1)}, f32[384,256]{1,0:T(8,128)S(1)}, u32[]{:S(2)}, u32[]{:S(2)}) collective-permute-start(f32[384,256]{1,0:T(8,128)S(1)} %maximum_select_fusion), channel_id=1, source_target_pairs={{0,2},{1,9}} | collective-permute-start | bytes 1179656 | tf_op jit(solution)/shard_map/ppermute | solution.py:362
  32.8 6.9 %first_column.1 = (f32[1024,256]{1,0:T(8,128)S(1)}, f32[16,128]{1,0:T(8,128)S(1)}) custom-call(f32[1024]{0:T(1024)S(1)} %broadcast_select_fusion.8.weights, f32[1024,16,128]{2,1,0:T(8,128)} %bitcast.14), custom_call_target="tpu_custom_call" | custom-call | flops 100000000 | bytes 100000 | tf_op jit(solution)/shard_map/first_column/pallas_call | solution.py:194
  39.7 0.7 collective-permute-done.3
  40.3 0.8 select_select_fusion.1
  41.2 4.4 %collective-permute-done.8 = f32[384,256]{1,0:T(8,128)S(1)} collective-permute-done((f32[384,256]{1,0:T(8,128)S(1)}, f32[384,256]{1,0:T(8,128)S(1)}, u32[]{:S(2)}, u32[]{:S(2)}) %collective-permute-start.8) | collective-permute-done | bytes 393248 | tf_op jit(solution)/shard_map/ppermute | solution.py:362
  45.7 1.3 collective-permute-start.11
  47.0 2.0 %collective-permute-start.12 = (f32[16,128]{1,0:T(8,128)S(1)}, f32[16,128]{1,0:T(8,128)S(1)}, u32[]{:S(2)}, u32[]{:S(2)}) collective-permute-start(f32[16,128]{1,0:T(8,128)S(1)} %get-tuple-element.62), channel_id=1, source_target_pairs={{0,8},{8,0},{16,24},{24,16},{32,40},{40,32},{48,56},{56,48},{64,72... | collective-permute-start | bytes 24584 | tf_op jit(solution)/shard_map/ppermute | solution.py:401
  49.0 1.0 collective-permute-done.12
  50.0 1.6 %collective-permute-done.11 = f32[384,256]{1,0:T(8,128)S(1)} collective-permute-done((f32[384,256]{1,0:T(8,128)S(1)}, f32[384,256]{1,0:T(8,128)S(1)}, u32[]{:S(2)}, u32[]{:S(2)}) %collective-permute-start.11) | collective-permute-done | bytes 393248 | tf_op jit(solution)/shard_map/ppermute | solution.py:362
  51.7 1.3 collective-permute-start.13
  53.0 1.4 collective-permute-start.10
  54.4 2.3 %collective-permute-start.9 = (f32[1024,256]{1,0:T(8,128)S(1)}, f32[1024,256]{1,0:T(8,128)}, u32[]{:S(2)}, u32[]{:S(2)}) collective-permute-start(f32[1024,256]{1,0:T(8,128)S(1)} %get-tuple-element.58), channel_id=1, source_target_pairs={{0,2},{1,3},{8,10},{9,11},{16,18},{17,19},{24,26},{25,27},{32,34},... | collective-permute-start | bytes 3145736 | tf_op jit(solution)/shard_map/ppermute | solution.py:394
  56.7 3.1 %collective-permute-start.14 = (f32[16,128]{1,0:T(8,128)S(1)}, f32[16,128]{1,0:T(8,128)S(1)}, u32[]{:S(2)}, u32[]{:S(2)}) collective-permute-start(f32[16,128]{1,0:T(8,128)S(1)} %add.51), channel_id=1, source_target_pairs={{0,24},{8,16},{16,8},{24,0},{32,56},{40,48},{48,40},{56,32},{64,88... | collective-permute-start | bytes 24584 | tf_op jit(solution)/shard_map/ppermute | solution.py:401
  59.8 1.4 collective-permute-done.14
  61.3 1.3 collective-permute-start.15
  62.9 2.8 %collective-permute-done.16 = f32[16,128]{1,0:T(8,128)S(1)} collective-permute-done((f32[16,128]{1,0:T(8,128)S(1)}, f32[16,128]{1,0:T(8,128)S(1)}, u32[]{:S(2)}, u32[]{:S(2)}) %collective-permute-start.16) | collective-permute-done | bytes 8224 | tf_op jit(solution)/shard_map/ppermute | solution.py:401
  65.7 3.1 %collective-permute-done.15 = f32[384,256]{1,0:T(8,128)S(1)} collective-permute-done((f32[384,256]{1,0:T(8,128)S(1)}, f32[384,256]{1,0:T(8,128)S(1)}, u32[]{:S(2)}, u32[]{:S(2)}) %collective-permute-start.15) | collective-permute-done | bytes 393248 | tf_op jit(solution)/shard_map/ppermute | solution.py:362
  68.8 2.9 %collective-permute-done.10 = f32[1024,256]{1,0:T(8,128)S(1)} collective-permute-done((f32[1024,256]{1,0:T(8,128)S(1)}, f32[1024,256]{1,0:T(8,128)S(1)}, u32[]{:S(2)}, u32[]{:S(2)}) %collective-permute-start.10) | collective-permute-done | bytes 1048608 | tf_op jit(solution)/shard_map/ppermute | solution.py:395
  71.7 1.4 collective-permute-done.9
  73.0 4.2 %collective-permute-start.17 = (f32[384,256]{1,0:T(8,128)S(1)}, f32[384,256]{1,0:T(8,128)S(1)}, u32[]{:S(2)}, u32[]{:S(2)}) collective-permute-start(f32[384,256]{1,0:T(8,128)S(1)} %broadcast_select_fusion.4), channel_id=1, source_target_pairs={{0,32},{8,40},{16,48},{24,56},{2,34},{10,42},{18,50},{26,58},{4,36... | collective-permute-start | bytes 1179656 | tf_op jit(solution)/shard_map/ppermute | solution.py:362
  77.4 4.1 %collective-permute-done.18 = f32[16,128]{1,0:T(8,128)S(1)} collective-permute-done((f32[16,128]{1,0:T(8,128)S(1)}, f32[16,128]{1,0:T(8,128)S(1)}, u32[]{:S(2)}, u32[]{:S(2)}) %collective-permute-start.18) | collective-permute-done | bytes 8224 | tf_op jit(solution)/shard_map/ppermute | solution.py:401
  81.5 1.4 collective-permute-done.17
  82.9 1.4 collective-permute-start.19
  84.6 1.3 collective-permute-start.22
  85.9 1.3 collective-permute-start.21
  87.2 4.2 %collective-permute-start.20 = (f32[16,256]{1,0:T(8,128)S(1)}, f32[16,256]{1,0:T(8,128)S(1)}, u32[]{:S(2)}, u32[]{:S(2)}) collective-permute-start(f32[16,256]{1,0:T(8,128)S(1)} %broadcast_in_dim.26), channel_id=1, source_target_pairs={{0,2},{1,3},{8,10},{9,11},{16,18},{17,19},{24,26},{25,27},{32,34},... | collective-permute-start | bytes 49160 | tf_op jit(solution)/shard_map/ppermute | solution.py:407
  91.5 0.8 collective-permute-done.20
  92.3 0.9 fusion
  93.2 0.7 collective-permute-start.24
  93.9 1.5 collective-permute-start.23
  95.3 12.7 %collective-permute-start.25 = (f32[384,256]{1,0:T(8,128)S(1)}, f32[384,256]{1,0:T(8,128)S(1)}, u32[]{:S(2)}, u32[]{:S(2)}) collective-permute-start(f32[384,256]{1,0:T(8,128)S(1)} %broadcast_select_fusion.6.own), channel_id=1, source_target_pairs={{0,1},{1,0},{2,3},{3,2},{4,5},{5,4},{6,7},{7,6},{8,9},{9,8},{10,11... | collective-permute-start | bytes 1179656 | tf_op jit(solution)/shard_map/ppermute | solution.py:409
  108.1 1.3 collective-permute-done.25.other
  109.4 8.2 %first_factor.1.w00 = f32[256,256]{1,0:T(8,128)S(1)} custom-call(s32[2]{0:T(128)S(1)} %pad_add_fusion.place, f32[384,256]{1,0:T(8,128)S(1)} %broadcast_select_fusion.6.own, f32[384,256]{1,0:T(8,128)S(1)} %collective-permute-done.25.other), custom_call_target="tpu_custom_call" | custom-call | flops 100000000 | bytes 100000 | tf_op jit(solution)/shard_map/first_factor/pallas_call | solution.py:144
  117.9 0.6 collective-permute-start.26
  118.5 9.3 %second_factor.1 = (f32[256,256]{1,0:T(8,128)S(1)}, f32[256,256]{1,0:T(8,128)S(1)}) custom-call(s32[2]{0:T(128)S(1)} %pad_add_fusion.place, f32[256,256]{1,0:T(8,128)S(1)} %first_factor.1.w00, f32[384,256]{1,0:T(8,128)S(1)} %broadcast_select_fusion.6.own, f32[384,256]{1,0:T(8,128)S(1)} %collective-permute-done.25.other), custom_call_target="tpu_custom_call" | custom-call | flops 100000000 | bytes 100000 | tf_op jit(solution)/shard_map/second_factor/pallas_call | solution.py:151
  127.8 0.7 copy-done
  128.5 0.9 copy-done.1
  129.5 23.5 %panels_and_trailing.1 = (f32[1024,2,8,128]{3,2,1,0:T(8,128)}, f32[1024,512]{1,0:T(8,128)}, f32[16,128]{1,0:T(8,128)}) custom-call(s32[2]{0:T(128)S(1)} %pad_add_fusion.place, f32[1024,2,8,128]{3,2,1,0:T(8,128)} %bitcast.15, f32[16,256,256]{2,1,0:T(8,128)} %bitcast.16, f32[1040,256]{1,0:T(8,128)S(1)} %pad_maximum_fusion.mine, ...), custom_call_target="tpu_custom_call" | custom-call | flops 100000000 | bytes 100000 | tf_op jit(solution)/shard_map/panels_and_trailing/pallas_call | solution.py:301
  (51 shorter events, 1.6 us)
Async XLA Ops:
  7.2 121.4 %all-gather.3.cloned.1.call-start = ((), (), s32[]{:S(2)}) async-start(), calls=%async_computation | async-start | bytes 4456448 | tf_op jit(solution)/shard_map/all_gather | solution.py:414
  10.5 22.1 %copy-start.5 = (f32[4,1,256]{2,1,0:T(1,128)S(1)}, f32[4,1,256]{2,1,0:T(1,128)}, u32[]{:S(2)}) copy-start(f32[4,1,256]{2,1,0:T(1,128)} %param.3) | copy-start | bytes 12292
  10.5 10.5 %collective-permute-start = (f32[256,256]{1,0:T(8,128)}, f32[256,256]{1,0:T(8,128)S(1)}, u32[]{:S(2)}, u32[]{:S(2)}) collective-permute-start(f32[256,256]{1,0:T(8,128)} %get-tuple-element.44), channel_id=1, source_target_pairs={{8,0},{9,1}} | collective-permute-start | bytes 786440 | tf_op jit(solution)/shard_map/ppermute | solution.py:386
  11.8 12.0 %collective-permute-start.5 = (f32[256,256]{1,0:T(8,128)}, f32[256,256]{1,0:T(8,128)S(1)}, u32[]{:S(2)}, u32[]{:S(2)}) collective-permute-start(f32[256,256]{1,0:T(8,128)} %get-tuple-element.52), channel_id=1, source_target_pairs={{0,48},{8,56},{1,49},{9,57},{2,50},{10,58},{3,51},{11,59},{4,52},{... | collective-permute-start | bytes 786440 | tf_op jit(solution)/shard_map/ppermute | solution.py:413
  18.2 7.6 %collective-permute-start.6 = (f32[256,256]{1,0:T(8,128)}, f32[256,256]{1,0:T(8,128)S(1)}, u32[]{:S(2)}, u32[]{:S(2)}) collective-permute-start(f32[256,256]{1,0:T(8,128)} %get-tuple-element.53), channel_id=1, source_target_pairs={{0,32},{8,40},{1,33},{9,41},{2,34},{10,42},{3,35},{11,43},{4,36},{... | collective-permute-start | bytes 786440 | tf_op jit(solution)/shard_map/ppermute | solution.py:413
  19.5 9.6 %collective-permute-start.7 = (f32[256,256]{1,0:T(8,128)}, f32[256,256]{1,0:T(8,128)S(1)}, u32[]{:S(2)}, u32[]{:S(2)}) collective-permute-start(f32[256,256]{1,0:T(8,128)} %get-tuple-element.54), channel_id=1, source_target_pairs={{0,16},{8,24},{1,17},{9,25},{2,18},{10,26},{3,19},{11,27},{4,20},{... | collective-permute-start | bytes 786440 | tf_op jit(solution)/shard_map/ppermute | solution.py:413
  21.0 18.7 %collective-permute-start.1 = (f32[256,256]{1,0:T(8,128)}, f32[256,256]{1,0:T(8,128)S(1)}, u32[]{:S(2)}, u32[]{:S(2)}) collective-permute-start(f32[256,256]{1,0:T(8,128)} %get-tuple-element.45), channel_id=1, source_target_pairs={{0,112},{8,120},{1,113},{9,121},{2,114},{10,122},{3,115},{11,123},... | collective-permute-start | bytes 786440 | tf_op jit(solution)/shard_map/ppermute | solution.py:413
  22.5 17.2 %collective-permute-start.2 = (f32[256,256]{1,0:T(8,128)}, f32[256,256]{1,0:T(8,128)S(1)}, u32[]{:S(2)}, u32[]{:S(2)}) collective-permute-start(f32[256,256]{1,0:T(8,128)} %get-tuple-element.47), channel_id=1, source_target_pairs={{0,96},{8,104},{1,97},{9,105},{2,98},{10,106},{3,99},{11,107},{4,1... | collective-permute-start | bytes 786440 | tf_op jit(solution)/shard_map/ppermute | solution.py:413
  23.9 16.5 %collective-permute-start.3 = (f32[256,256]{1,0:T(8,128)}, f32[256,256]{1,0:T(8,128)}, u32[]{:S(2)}, u32[]{:S(2)}) collective-permute-start(f32[256,256]{1,0:T(8,128)} %get-tuple-element.49), channel_id=1, source_target_pairs={{0,80},{8,88},{1,81},{9,89},{2,82},{10,90},{3,83},{11,91},{4,84},{... | collective-permute-start | bytes 786440 | tf_op jit(solution)/shard_map/ppermute | solution.py:413
  25.9 14.5 %collective-permute-start.4 = (f32[256,256]{1,0:T(8,128)}, f32[256,256]{1,0:T(8,128)}, u32[]{:S(2)}, u32[]{:S(2)}) collective-permute-start(f32[256,256]{1,0:T(8,128)} %get-tuple-element.51), channel_id=1, source_target_pairs={{0,64},{8,72},{1,65},{9,73},{2,66},{10,74},{3,67},{11,75},{4,68},{... | collective-permute-start | bytes 786440 | tf_op jit(solution)/shard_map/ppermute | solution.py:413
  29.1 16.5 %collective-permute-start.8 = (f32[384,256]{1,0:T(8,128)S(1)}, f32[384,256]{1,0:T(8,128)S(1)}, u32[]{:S(2)}, u32[]{:S(2)}) collective-permute-start(f32[384,256]{1,0:T(8,128)S(1)} %maximum_select_fusion), channel_id=1, source_target_pairs={{0,2},{1,9}} | collective-permute-start | bytes 1179656 | tf_op jit(solution)/shard_map/ppermute | solution.py:362
  32.7 7.6 %copy-start.4 = (f32[256,256]{1,0:T(8,128)S(1)}, f32[256,256]{1,0:T(8,128)}, u32[]{:S(2)}) copy-start(f32[256,256]{1,0:T(8,128)} %get-tuple-element.55) | copy-start | bytes 786436
  45.7 6.0 %collective-permute-start.11 = (f32[384,256]{1,0:T(8,128)S(1)}, f32[384,256]{1,0:T(8,128)S(1)}, u32[]{:S(2)}, u32[]{:S(2)}) collective-permute-start(f32[384,256]{1,0:T(8,128)S(1)} %broadcast_select_fusion.7), channel_id=1, source_target_pairs={{0,6},{2,4},{1,25},{9,17}} | collective-permute-start | bytes 1179656 | tf_op jit(solution)/shard_map/ppermute | solution.py:362
  47.0 3.0 %collective-permute-start.12 = (f32[16,128]{1,0:T(8,128)S(1)}, f32[16,128]{1,0:T(8,128)S(1)}, u32[]{:S(2)}, u32[]{:S(2)}) collective-permute-start(f32[16,128]{1,0:T(8,128)S(1)} %get-tuple-element.62), channel_id=1, source_target_pairs={{0,8},{8,0},{16,24},{24,16},{32,40},{40,32},{48,56},{56,48},{64,72... | collective-permute-start | bytes 24584 | tf_op jit(solution)/shard_map/ppermute | solution.py:401
  51.7 9.6 %collective-permute-start.13 = (f32[384,256]{1,0:T(8,128)S(1)}, f32[384,256]{1,0:T(8,128)S(1)}, u32[]{:S(2)}, u32[]{:S(2)}) collective-permute-start(f32[384,256]{1,0:T(8,128)S(1)} %broadcast_select_fusion.2), channel_id=1, source_target_pairs={{0,8},{2,10},{4,12},{6,14},{1,33},{9,41},{17,49},{25,57}} | collective-permute-start | bytes 1179656 | tf_op jit(solution)/shard_map/ppermute | solution.py:362
  53.0 18.6 %collective-permute-start.10 = (f32[1024,256]{1,0:T(8,128)S(1)}, f32[1024,256]{1,0:T(8,128)S(1)}, u32[]{:S(2)}, u32[]{:S(2)}) collective-permute-start(f32[1024,256]{1,0:T(8,128)S(1)} %get-tuple-element.58), channel_id=1, source_target_pairs={{0,6},{1,7},{8,14},{9,15},{16,22},{17,23},{24,30},{25,31},{32,38},... | collective-permute-start | bytes 3145736 | tf_op jit(solution)/shard_map/ppermute | solution.py:395
  54.4 18.6 %collective-permute-start.9 = (f32[1024,256]{1,0:T(8,128)S(1)}, f32[1024,256]{1,0:T(8,128)}, u32[]{:S(2)}, u32[]{:S(2)}) collective-permute-start(f32[1024,256]{1,0:T(8,128)S(1)} %get-tuple-element.58), channel_id=1, source_target_pairs={{0,2},{1,3},{8,10},{9,11},{16,18},{17,19},{24,26},{25,27},{32,34},... | collective-permute-start | bytes 3145736 | tf_op jit(solution)/shard_map/ppermute | solution.py:394
  56.7 4.6 %collective-permute-start.14 = (f32[16,128]{1,0:T(8,128)S(1)}, f32[16,128]{1,0:T(8,128)S(1)}, u32[]{:S(2)}, u32[]{:S(2)}) collective-permute-start(f32[16,128]{1,0:T(8,128)S(1)} %add.51), channel_id=1, source_target_pairs={{0,24},{8,16},{16,8},{24,0},{32,56},{40,48},{48,40},{56,32},{64,88... | collective-permute-start | bytes 24584 | tf_op jit(solution)/shard_map/ppermute | solution.py:401
  61.3 7.4 %collective-permute-start.15 = (f32[384,256]{1,0:T(8,128)S(1)}, f32[384,256]{1,0:T(8,128)S(1)}, u32[]{:S(2)}, u32[]{:S(2)}) collective-permute-start(f32[384,256]{1,0:T(8,128)S(1)} %broadcast_select_fusion.3), channel_id=1, source_target_pairs={{0,24},{2,26},{4,28},{6,30},{8,16},{10,18},{12,20},{14,22},{1,97},... | collective-permute-start | bytes 1179656 | tf_op jit(solution)/shard_map/ppermute | solution.py:362
  62.7 3.0 %collective-permute-start.16 = (f32[16,128]{1,0:T(8,128)S(1)}, f32[16,128]{1,0:T(8,128)S(1)}, u32[]{:S(2)}, u32[]{:S(2)}) collective-permute-start(f32[16,128]{1,0:T(8,128)S(1)} %add.52), channel_id=1, source_target_pairs={{0,32},{8,40},{16,48},{24,56},{32,0},{40,8},{48,16},{56,24},{64,96... | collective-permute-start | bytes 24584 | tf_op jit(solution)/shard_map/ppermute | solution.py:401
  71.7 9.8 %copy-start.2 = (f32[1024,256]{1,0:T(8,128)}, f32[1024,256]{1,0:T(8,128)S(1)}, u32[]{:S(2)}) copy-start(f32[1024,256]{1,0:T(8,128)S(1)} %collective-permute-done.10) | copy-start | bytes 3145732
  73.0 9.9 %collective-permute-start.17 = (f32[384,256]{1,0:T(8,128)S(1)}, f32[384,256]{1,0:T(8,128)S(1)}, u32[]{:S(2)}, u32[]{:S(2)}) collective-permute-start(f32[384,256]{1,0:T(8,128)S(1)} %broadcast_select_fusion.4), channel_id=1, source_target_pairs={{0,32},{8,40},{16,48},{24,56},{2,34},{10,42},{18,50},{26,58},{4,36... | collective-permute-start | bytes 1179656 | tf_op jit(solution)/shard_map/ppermute | solution.py:362
  77.3 4.2 %collective-permute-start.18 = (f32[16,128]{1,0:T(8,128)S(1)}, f32[16,128]{1,0:T(8,128)S(1)}, u32[]{:S(2)}, u32[]{:S(2)}) collective-permute-start(f32[16,128]{1,0:T(8,128)S(1)} %add.53), channel_id=1, source_target_pairs={{0,96},{8,104},{16,112},{24,120},{32,64},{40,72},{48,80},{56,88},{... | collective-permute-start | bytes 24584 | tf_op jit(solution)/shard_map/ppermute | solution.py:401
  82.9 1.5 copy-start.3
  82.9 8.5 %collective-permute-start.19 = (f32[384,256]{1,0:T(8,128)S(1)}, f32[384,256]{1,0:T(8,128)S(1)}, u32[]{:S(2)}, u32[]{:S(2)}) collective-permute-start(f32[384,256]{1,0:T(8,128)S(1)} %broadcast_select_fusion.5), channel_id=1, source_target_pairs={{0,96},{8,104},{16,112},{24,120},{2,98},{10,106},{18,114},{26,122}... | collective-permute-start | bytes 1179656 | tf_op jit(solution)/shard_map/ppermute | solution.py:362
  84.6 6.9 %collective-permute-start.22 = (f32[16,256]{1,0:T(8,128)S(1)}, f32[16,256]{1,0:T(8,128)S(1)}, u32[]{:S(2)}, u32[]{:S(2)}) collective-permute-start(f32[16,256]{1,0:T(8,128)S(1)} %broadcast_in_dim.26), channel_id=1, source_target_pairs={{0,6},{1,7},{8,14},{9,15},{16,22},{17,23},{24,30},{25,31},{32,38},... | collective-permute-start | bytes 49160 | tf_op jit(solution)/shard_map/ppermute | solution.py:407
  85.9 5.6 %collective-permute-start.21 = (f32[16,256]{1,0:T(8,128)S(1)}, f32[16,256]{1,0:T(8,128)S(1)}, u32[]{:S(2)}, u32[]{:S(2)}) collective-permute-start(f32[16,256]{1,0:T(8,128)S(1)} %broadcast_in_dim.26), channel_id=1, source_target_pairs={{0,4},{1,5},{8,12},{9,13},{16,20},{17,21},{24,28},{25,29},{32,36},... | collective-permute-start | bytes 49160 | tf_op jit(solution)/shard_map/ppermute | solution.py:407
  87.2 5.1 %collective-permute-start.20 = (f32[16,256]{1,0:T(8,128)S(1)}, f32[16,256]{1,0:T(8,128)S(1)}, u32[]{:S(2)}, u32[]{:S(2)}) collective-permute-start(f32[16,256]{1,0:T(8,128)S(1)} %broadcast_in_dim.26), channel_id=1, source_target_pairs={{0,2},{1,3},{8,10},{9,11},{16,18},{17,19},{24,26},{25,27},{32,34},... | collective-permute-start | bytes 49160 | tf_op jit(solution)/shard_map/ppermute | solution.py:407
  93.2 24.5 %collective-permute-start.24 = (f32[512,256]{1,0:T(8,128)}, f32[512,256]{1,0:T(8,128)S(1)}, u32[]{:S(2)}, u32[]{:S(2)}) collective-permute-start(f32[512,256]{1,0:T(8,128)} %get-tuple-element.88), channel_id=1, source_target_pairs={{6,4},{7,5},{14,12},{15,13},{22,20},{23,21},{30,28},{31,29},{38,36... | collective-permute-start | bytes 1572872 | tf_op jit(solution)/shard_map/ppermute | solution.py:426
  93.9 23.8 %collective-permute-start.23 = (f32[512,256]{1,0:T(8,128)S(1)}, f32[512,256]{1,0:T(8,128)}, u32[]{:S(2)}, u32[]{:S(2)}) collective-permute-start(f32[512,256]{1,0:T(8,128)S(1)} %get-tuple-element.89), channel_id=1, source_target_pairs={{2,4},{3,5},{10,12},{11,13},{18,20},{19,21},{26,28},{27,29},{34,36... | collective-permute-start | bytes 1572872 | tf_op jit(solution)/shard_map/ppermute | solution.py:425
  95.3 14.1 %collective-permute-start.25 = (f32[384,256]{1,0:T(8,128)S(1)}, f32[384,256]{1,0:T(8,128)S(1)}, u32[]{:S(2)}, u32[]{:S(2)}) collective-permute-start(f32[384,256]{1,0:T(8,128)S(1)} %broadcast_select_fusion.6.own), channel_id=1, source_target_pairs={{0,1},{1,0},{2,3},{3,2},{4,5},{5,4},{6,7},{7,6},{8,9},{9,8},{10,11... | collective-permute-start | bytes 1179656 | tf_op jit(solution)/shard_map/ppermute | solution.py:409
  117.9 10.7 %collective-permute-start.26 = (f32[1040,256]{1,0:T(8,128)S(1)}, f32[1040,256]{1,0:T(8,128)S(1)}, u32[]{:S(2)}, u32[]{:S(2)}) collective-permute-start(f32[1040,256]{1,0:T(8,128)S(1)} %pad_maximum_fusion.mine), channel_id=1, source_target_pairs={{0,1},{1,0},{2,3},{3,2},{4,5},{5,4},{6,7},{7,6},{8,9},{9,8},{10,11... | collective-permute-start | bytes 3194888 | tf_op jit(solution)/shard_map/ppermute | solution.py:431
  127.8 0.7 copy-start
  128.5 1.0 copy-start.1
Sparse Core Ops, SparseCore 0:
  45.8 51.3 all-gather.2

commit v9 on v8

--- a/solution.py
+++ b/solution.py
@@ -154,28 +154,33 @@
     )(place, w00, own, other)
 
 
-def corner_kernel(a, *pieces):
+def corner_kernel(near, far, column, *pieces):
     *pieces, flipped = pieces
-    flipped[...] = a[:, 1, :].T
-    for q in range(16):
-        value = a[:, q, :]
-        for ref in pieces[q // 2 :: 8]:
-            ref[:, 128 * (q % 2) : 128 * (q % 2) + 128] = value
+    for q in range(2):
+        column[:, 128 * q : 128 * q + 128] = near[:, q, :]
+
+    @pl.when(pl.program_id(0) == 0)
+    def _():
+        flipped[...] = near[:, 1, :].T
+        for q in range(16):
+            value = (near, far)[q // 8][:, q % 8, :]
+            for ref in pieces[q // 2 :: 8]:
+                ref[:, 128 * (q % 2) : 128 * (q % 2) + 128] = value
 
 
 def corner_call(flat):
+    whole = pl.BlockSpec((NB, NB), lambda i: (0, 0))
     return pl.pallas_call(
-        corner_kernel, grid=(2,), out_shape=(TILE,) * 9 + (jax.ShapeDtypeStruct((128, NB), F32),),
-        in_specs=[pl.BlockSpec((128, 16, 128), lambda i: (i, 0, 0))],
-        out_specs=(pl.BlockSpec((128, NB), lambda i: (i, 0)),) * 9 + (pl.BlockSpec((128, 128), lambda i: (0, i)),),
-        name="corner_tiles",
-    )(flat)
-
-
-def column_kernel(weights, a, column, sums):
+        corner_kernel, grid=(4,),
+        out_shape=(jax.ShapeDtypeStruct((1024, NB), F32),) + (TILE,) * 9 + (jax.ShapeDtypeStruct((128, NB), F32),),
+        in_specs=[pl.BlockSpec((NB, 8, 128), lambda i: (i, 0, 0)), pl.BlockSpec((NB, 8, 128), lambda i: (0, 1, 0))],
+        out_specs=(pl.BlockSpec((NB, NB), lambda i: (i, 0)),) + (whole,) * 9 + (pl.BlockSpec((128, NB), lambda i: (0, 0)),),
+        name="corner_tiles", **FACTOR,
+    )(flat, flat)
+
+
+def sums_kernel(weights, a, sums):
     step = pl.program_id(0)
-    for q in range(2):
-        column[:, 128 * q : 128 * q + 128] = a[:, q, :]
 
     @pl.when(step == 0)
     def _():
@@ -190,16 +195,12 @@
     sums[...] += lax.fori_loop(0, 16, body, jnp.zeros((16, 128), F32))
 
 
-def column_call(weights, flat):
+def sums_call(weights, flat):
     return pl.pallas_call(
-        column_kernel, grid=(8,),
-        out_shape=(jax.ShapeDtypeStruct((1024, NB), F32), jax.ShapeDtypeStruct((16, 128), F32)),
+        sums_kernel, grid=(8,), out_shape=jax.ShapeDtypeStruct((16, 128), F32),
         in_specs=[SMEM, pl.BlockSpec((128, 16, 128), lambda i: (i, 0, 0))],
-        out_specs=(
-            pl.BlockSpec((128, NB), lambda i: (i, 0)),
-            pl.BlockSpec((16, 128), lambda i: (0, 0)),
-        ),
-        name="first_column", **FACTOR,
+        out_specs=pl.BlockSpec((16, 128), lambda i: (0, 0)),
+        name="column_sums", **FACTOR,
     )(weights, flat)
 
 
@@ -272,20 +273,27 @@
 
             g_high = jnp.concatenate([high[pl.ds(base, ROWS), :], high[1024:1040, :]], axis=0)
             g_low = jnp.concatenate([low[pl.ds(base, ROWS), :], low[1024:1040, :]], axis=0)
-            top = (step * ROWS + lax.broadcasted_iota(jnp.int32, (ROWS, 1), 0) < NB) & (row_index < 2)
             for u in range(4):
                 product = dot3((g_high, g_low), (right_high[u], right_low[u]), NN)
-                gone = top | (col_index < 2) if (group, u) == (0, 0) else top
                 for h in range(2):
                     q = 2 * u + h
                     lanes = slice(128 * h, 128 * h + 128)
-                    value = block[pl.ds(base, ROWS), group, q, :] - product[0:ROWS, lanes]
-                    ready[slot, :, q, :] = jnp.where(gone, 0.0, value)
+                    ready[slot, :, q, :] = block[pl.ds(base, ROWS), group, q, :] - product[0:ROWS, lanes]
                     at = 8 * group + q
                     kept = sums[at : at + 1, :] - product[ROWS : ROWS + 1, lanes]
                     if (group, u) == (0, 0):
                         kept = jnp.where(col_index < 2, 0.0, kept)
                     checksum[at : at + 1, :] = kept
+            @pl.when((step == 0) & (row_index < 2))
+            def _():
+                ready[slot] = jnp.zeros((ROWS, 8, 128), F32)
+
+            if group == 0:
+
+                @pl.when(col_index < 2)
+                def _():
+                    ready[slot, :, 0:2, :] = jnp.zeros((ROWS, 2, 128), F32)
+
             put(slot, group, step).start()
             return carry
 
@@ -323,7 +331,7 @@
             pltpu.SemaphoreType.DMA((2,)),
         ],
         name="panels_and_trailing",
-        compiler_params=pltpu.CompilerParams(vmem_limit_bytes=40 * 1024 * 1024),
+        compiler_params=pltpu.CompilerParams(vmem_limit_bytes=30 * 1024 * 1024),
         cost_estimate=SMALL,
     )(place, flat, across, mine, theirs, w00, l10, w11, sums)
 
@@ -382,24 +390,28 @@
     place = jnp.stack([row, col]).astype(jnp.int32)
     swap_cores = [(c, c ^ 1) for c in range(8)]
 
-    pieces = corner_call(flat)
+    column, *pieces = corner_call(flat)
     fetched = lax.ppermute(pieces[0], ("row", "col"), [(8, 0), (9, 1)])
     corner = jnp.where(
         core == 0,
         jnp.concatenate([pieces[0], fetched[0:128]], axis=0),
         jnp.concatenate([fetched, pieces[9]], axis=0),
     )
-    column, sums = column_call(weights, after(flat, corner))
+    sums = sums_call(weights, after(flat, corner))
     partial = [sums]
     from_left = lax.ppermute(column, "col", [(0, 2), (1, 3)])
     from_right = lax.ppermute(column, "col", [(0, 6), (1, 7)])
+    mine = jnp.where(x == 1, from_left, jnp.where(x == 3, from_right, column))
+    upper = lax.ppermute(mine[0:512], "col", [(2, 4), (3, 5)])
+    lower = lax.ppermute(mine[512:1024], "col", [(6, 4), (7, 5)])
 
     def beside(stage, value):
         before = partial[-1]
         if stage <= 4:
             d = (1, 3, 4, 12)[stage - 1]
             partial.append(before + lax.ppermute(after(before, value), "row", [(r, r ^ d) for r in range(16)]))
-        return after(value, (before, from_left, from_right) if stage == 4 else before)
+        more = {1: (from_left, from_right), 4: (upper, lower)}.get(stage, ())
+        return after(value, (before, *more))
 
     tree = spread(corner, [((0, 0), 0, (2, 1, 0)), ((0, 0), 1, (1, 0, 2))], here, beside)
     sums = partial[-1]
@@ -411,7 +423,7 @@
     piece = pieces[8]
     for j in range(1, 8):
         piece = jnp.where(row // 2 == j, lax.ppermute(pieces[j] if j < 4 else after(pieces[j], fetched), "row", [(0, 2 * j), (1, 2 * j + 1)]), piece)
-    across = lax.all_gather(after(piece, (tree[0], column)), "row", axis=0)
+    across = lax.all_gather(after(piece, (tree[0], partial[0], from_left, from_right)), "row", axis=0)
     across = pltpu.with_memory_space_constraint(across, pltpu.HBM)
 
     w00 = first_factor(place, own, other)
@@ -420,11 +432,6 @@
         panel_sums = jnp.where(x == k, far_sums[k - 1], panel_sums)
 
     l10, w11 = second_factor(place, w00, own, other)
-    mine = jnp.where(x == 1, from_left, jnp.where(x == 3, from_right, column))
-    mine = after(mine, own)
-    upper = lax.ppermute(mine[0:512], "col", [(2, 4), (3, 5)])
-    lower = lax.ppermute(mine[512:1024], "col", [(6, 4), (7, 5)])
-    upper, lower = after((upper, lower), w00)
     upper = jnp.where(x == 2, upper, mine[0:512])
     lower = jnp.where(x == 2, lower, mine[512:1024])
     mine = jnp.concatenate([upper, lower, panel_sums], axis=0)

time: 162 us -> 169 us (1.043)
  starting transfers between devices: 61.7 us -> 79.3 us
  waiting for transfers between devices: 27.1 us -> 19.7 us
  local copies, waits for them, and re-layouts: 2.63 us -> 0.16 us
    ppermute x1, starting transfers between devices: 0.64 us -> 20.4 us  [shards(): theirs = after(lax.ppermute(mine, 'col', swap_cores), w11)]
    ppermute x1, starting transfers between devices: 12.7 us -> 0.27 us  [shards(): other = lax.ppermute(own, 'col', swap_cores)]
    ppermute x6, starting transfers between devices: 13.1 us -> 20.1 us  [spread(): arrived = lax.ppermute(value, ('row', 'col'), pairs)]
    ppermute x6, waiting for transfers between devices: 10.6 us -> 3.85 us  [spread(): arrived = lax.ppermute(value, ('row', 'col'), pairs)]
    ppermute x1, starting transfers between devices: 1.36 us -> 5.38 us  [shards(): from_right = lax.ppermute(column, 'col', [(0, 6), (1, 7)])]
    ppermute x7, starting transfers between devices: 15.8 us -> 17.9 us  [shards(): lax.ppermute(pieces[j] if j < 4 else after(pieces[j], fetched), 'row', [(...]
    ppermute x3, starting transfers between devices: 6.78 us -> 5.03 us  [shards(): lax.ppermute(near_sums, 'col', [(0, 2 * k), (1, 2 * k + 1)])]
  transfers between devices with their start and end apart: 28 -> 28, of which waited for: 14 -> 11; matrix products, arithmetic and copies ran while one was open for 2% -> 2% of each run, Pallas kernels for 15% -> 14%
where the time goes in v9:
time: 169 us; the launch traced here: 168 us
  starting transfers between devices  79.3 us (47%)
  Pallas kernels  51.9 us (31%)
  waiting for transfers between devices  19.7 us (12%)
  between operations  14.5 us (9%)
  other arithmetic  2.59 us (2%)
    pallas_call x1, Pallas kernels, final_call(): pl.pallas_call(final_kernel, out_shape=(jax.ShapeDtypeStruct((1024, 2, 8,...  23.1 us
    ppermute x1, starting transfers between devices, shards(): theirs = after(lax.ppermute(mine, 'col', swap_cores), w11)  20.4 us
    ppermute x6, starting transfers between devices, spread(): arrived = lax.ppermute(value, ('row', 'col'), pairs)  20.1 us
    ppermute x7, starting transfers between devices, shards(): lax.ppermute(pieces[j] if j < 4 else after(pieces[j], fetched), 'row', [(...  17.9 us
    pallas_call x1, Pallas kernels, second_factor(): pl.pallas_call(second_kernel, out_shape=(TILE, TILE), in_specs=[SMEM, VME...  9.31 us
    ppermute x4, waiting for transfers between devices, beside(): lax.ppermute(after(before, value), 'row', [(r, r ^ d) for r in range(16)])  8.27 us
    pallas_call x1, Pallas kernels, first_factor(): pl.pallas_call(first_kernel, out_shape=TILE, in_specs=[SMEM, VMEM, VMEM],...  8.22 us
    pallas_call x1, Pallas kernels, sums_call(): pl.pallas_call(sums_kernel, grid=(8,), out_shape=jax.ShapeDtypeStruct((16...  6.59 us
  transfers between devices with their start and end apart: 28, of which 11 were waited for; matrix products, arithmetic and copies ran while one was open for 2% of the time, Pallas kernels for 14%

profile of v9, /device:TPU:1, one launch (start us, length us, event | category | flops | bytes accessed | tf_op | source)
XLA Modules:
  0.0 168.1 jit_solution(10235535980742864942)
XLA Ops:
  7.2 4.7 %corner_tiles.1 = (f32[1024,256]{1,0:T(8,128)S(1)}, f32[256,256]{1,0:T(8,128)S(1)}, f32[256,256]{1,0:T(8,128)S(1)}, f32[256,256]{1,0:T(8,128)S(1)}, f32[256,256]...) custom-call(f32[1024,16,128]{2,1,0:T(8,128)} %bitcast.13, ...), custom_call_target="tpu_custom_call" | custom-call | flops 100000000 | bytes 100000 | tf_op jit(solution)/shard_map/corner_tiles/pallas_call | solution.py:173
  11.9 1.3 collective-permute-start
  13.2 6.4 %collective-permute-start.5 = (f32[256,256]{1,0:T(8,128)S(1)}, f32[256,256]{1,0:T(8,128)S(1)}, u32[]{:S(2)}, u32[]{:S(2)}) collective-permute-start(f32[256,256]{1,0:T(8,128)S(1)} %get-tuple-element.48), channel_id=1, source_target_pairs={{0,48},{8,56},{1,49},{9,57},{2,50},{10,58},{3,51},{11,59},{4,52},{... | collective-permute-start | bytes 786440 | tf_op jit(solution)/shard_map/ppermute | solution.py:425
  19.6 1.3 collective-permute-start.6
  20.9 2.0 %collective-permute-start.7 = (f32[256,256]{1,0:T(8,128)S(1)}, f32[256,256]{1,0:T(8,128)}, u32[]{:S(2)}, u32[]{:S(2)}) collective-permute-start(f32[256,256]{1,0:T(8,128)S(1)} %get-tuple-element.50), channel_id=1, source_target_pairs={{0,16},{8,24},{1,17},{9,25},{2,18},{10,26},{3,19},{11,27},{4,20},{... | collective-permute-start | bytes 786440 | tf_op jit(solution)/shard_map/ppermute | solution.py:425
  22.9 2.2 %collective-permute-start.1 = (f32[256,256]{1,0:T(8,128)S(1)}, f32[256,256]{1,0:T(8,128)}, u32[]{:S(2)}, u32[]{:S(2)}) collective-permute-start(f32[256,256]{1,0:T(8,128)S(1)} %get-tuple-element.41), channel_id=1, source_target_pairs={{0,112},{8,120},{1,113},{9,121},{2,114},{10,122},{3,115},{11,123},... | collective-permute-start | bytes 786440 | tf_op jit(solution)/shard_map/ppermute | solution.py:425
  25.1 5.4 %collective-permute-start.10 = (f32[1024,256]{1,0:T(8,128)S(1)}, f32[1024,256]{1,0:T(8,128)}, u32[]{:S(2)}, u32[]{:S(2)}) collective-permute-start(f32[1024,256]{1,0:T(8,128)S(1)} %get-tuple-element.54), channel_id=1, source_target_pairs={{0,6},{1,7},{8,14},{9,15},{16,22},{17,23},{24,30},{25,31},{32,38},... | collective-permute-start | bytes 3145736 | tf_op jit(solution)/shard_map/ppermute | solution.py:403
  30.5 2.3 %collective-permute-start.9 = (f32[1024,256]{1,0:T(8,128)S(1)}, f32[1024,256]{1,0:T(8,128)}, u32[]{:S(2)}, u32[]{:S(2)}) collective-permute-start(f32[1024,256]{1,0:T(8,128)S(1)} %get-tuple-element.54), channel_id=1, source_target_pairs={{0,2},{1,3},{8,10},{9,11},{16,18},{17,19},{24,26},{25,27},{32,34},... | collective-permute-start | bytes 3145736 | tf_op jit(solution)/shard_map/ppermute | solution.py:402
  32.8 2.0 %collective-permute-start.2 = (f32[256,256]{1,0:T(8,128)S(1)}, f32[256,256]{1,0:T(8,128)}, u32[]{:S(2)}, u32[]{:S(2)}) collective-permute-start(f32[256,256]{1,0:T(8,128)S(1)} %get-tuple-element.43), channel_id=1, source_target_pairs={{0,96},{8,104},{1,97},{9,105},{2,98},{10,106},{3,99},{11,107},{4,1... | collective-permute-start | bytes 786440 | tf_op jit(solution)/shard_map/ppermute | solution.py:425
  34.8 0.1 broadcast_in_dim.22
  35.0 2.0 %collective-permute-start.3 = (f32[256,256]{1,0:T(8,128)S(1)}, f32[256,256]{1,0:T(8,128)}, u32[]{:S(2)}, u32[]{:S(2)}) collective-permute-start(f32[256,256]{1,0:T(8,128)S(1)} %get-tuple-element.45), channel_id=1, source_target_pairs={{0,80},{8,88},{1,81},{9,89},{2,82},{10,90},{3,83},{11,91},{4,84},{... | collective-permute-start | bytes 786440 | tf_op jit(solution)/shard_map/ppermute | solution.py:425
  37.0 2.0 %collective-permute-start.4 = (f32[256,256]{1,0:T(8,128)S(1)}, f32[256,256]{1,0:T(8,128)}, u32[]{:S(2)}, u32[]{:S(2)}) collective-permute-start(f32[256,256]{1,0:T(8,128)S(1)} %get-tuple-element.47), channel_id=1, source_target_pairs={{0,64},{8,72},{1,65},{9,73},{2,66},{10,74},{3,67},{11,75},{4,68},{... | collective-permute-start | bytes 786440 | tf_op jit(solution)/shard_map/ppermute | solution.py:425
  39.0 2.3 %collective-permute-start.8 = (f32[384,256]{1,0:T(8,128)S(1)}, f32[384,256]{1,0:T(8,128)S(1)}, u32[]{:S(2)}, u32[]{:S(2)}) collective-permute-start(f32[384,256]{1,0:T(8,128)S(1)} %maximum_select_fusion), channel_id=1, source_target_pairs={{0,2},{1,9}} | collective-permute-start | bytes 1179656 | tf_op jit(solution)/shard_map/ppermute | solution.py:370
  41.5 6.6 %column_sums.1 = f32[16,128]{1,0:T(8,128)S(1)} custom-call(f32[1024]{0:T(1024)S(1)} %broadcast_select_fusion.8.weights, f32[1024,16,128]{2,1,0:T(8,128)} %bitcast.15), custom_call_target="tpu_custom_call" | custom-call | flops 100000000 | bytes 100000 | tf_op jit(solution)/shard_map/column_sums/pallas_call | solution.py:199
  48.1 0.9 select_select_fusion.1
  49.1 1.9 %collective-permute-done.10 = f32[1024,256]{1,0:T(8,128)} collective-permute-done((f32[1024,256]{1,0:T(8,128)S(1)}, f32[1024,256]{1,0:T(8,128)}, u32[]{:S(2)}, u32[]{:S(2)}) %collective-permute-start.10) | collective-permute-done | bytes 1048608 | tf_op jit(solution)/shard_map/ppermute | solution.py:403
  51.0 2.3 %collective-permute-done.9 = f32[1024,256]{1,0:T(8,128)} collective-permute-done((f32[1024,256]{1,0:T(8,128)S(1)}, f32[1024,256]{1,0:T(8,128)}, u32[]{:S(2)}, u32[]{:S(2)}) %collective-permute-start.9) | collective-permute-done | bytes 1048608 | tf_op jit(solution)/shard_map/ppermute | solution.py:402
  53.3 1.3 collective-permute-start.13
  54.6 0.5 collective-permute-start.14
  55.1 2.1 %collective-permute-done.14 = f32[16,128]{1,0:T(8,128)S(1)} collective-permute-done((f32[16,128]{1,0:T(8,128)S(1)}, f32[16,128]{1,0:T(8,128)S(1)}, u32[]{:S(2)}, u32[]{:S(2)}) %collective-permute-start.14) | collective-permute-done | bytes 8224 | tf_op jit(solution)/shard_map/ppermute | solution.py:412
  57.2 2.1 %collective-permute-done.13 = f32[384,256]{1,0:T(8,128)S(1)} collective-permute-done((f32[384,256]{1,0:T(8,128)S(1)}, f32[384,256]{1,0:T(8,128)S(1)}, u32[]{:S(2)}, u32[]{:S(2)}) %collective-permute-start.13) | collective-permute-done | bytes 393248 | tf_op jit(solution)/shard_map/ppermute | solution.py:370
  59.4 1.3 collective-permute-start.15
  60.7 0.2 select_select_fusion
  61.0 0.7 collective-permute-start.11
  61.7 3.2 %collective-permute-start.16 = (f32[16,128]{1,0:T(8,128)S(1)}, f32[16,128]{1,0:T(8,128)S(1)}, u32[]{:S(2)}, u32[]{:S(2)}) collective-permute-start(f32[16,128]{1,0:T(8,128)S(1)} %add.51), channel_id=1, source_target_pairs={{0,24},{8,16},{16,8},{24,0},{32,56},{40,48},{48,40},{56,32},{64,88... | collective-permute-start | bytes 24584 | tf_op jit(solution)/shard_map/ppermute | solution.py:412
  64.9 1.0 collective-permute-done.16
  66.0 2.1 %collective-permute-start.17 = (f32[384,256]{1,0:T(8,128)S(1)}, f32[384,256]{1,0:T(8,128)}, u32[]{:S(2)}, u32[]{:S(2)}) collective-permute-start(f32[384,256]{1,0:T(8,128)S(1)} %broadcast_select_fusion.3), channel_id=1, source_target_pairs={{0,24},{2,26},{4,28},{6,30},{8,16},{10,18},{12,20},{14,22},{1,97},... | collective-permute-start | bytes 1179656 | tf_op jit(solution)/shard_map/ppermute | solution.py:370
  68.0 0.9 broadcast_select_fusion.1
  68.9 0.7 collective-permute-start.12
  69.6 1.4 collective-permute-start.18
  71.1 1.4 collective-permute-done.18
  72.5 0.9 collective-permute-done.17
  73.4 5.8 %collective-permute-start.19 = (f32[384,256]{1,0:T(8,128)S(1)}, f32[384,256]{1,0:T(8,128)S(1)}, u32[]{:S(2)}, u32[]{:S(2)}) collective-permute-start(f32[384,256]{1,0:T(8,128)S(1)} %broadcast_select_fusion.4), channel_id=1, source_target_pairs={{0,32},{8,40},{16,48},{24,56},{2,34},{10,42},{18,50},{26,58},{4,36... | collective-permute-start | bytes 1179656 | tf_op jit(solution)/shard_map/ppermute | solution.py:370
  79.3 0.1 collective-permute-start.20
  79.4 3.7 %collective-permute-done.20 = f32[16,128]{1,0:T(8,128)S(1)} collective-permute-done((f32[16,128]{1,0:T(8,128)S(1)}, f32[16,128]{1,0:T(8,128)S(1)}, u32[]{:S(2)}, u32[]{:S(2)}) %collective-permute-start.20) | collective-permute-done | bytes 8224 | tf_op jit(solution)/shard_map/ppermute | solution.py:412
  83.1 0.9 collective-permute-done.19
  84.0 7.2 %collective-permute-start.21 = (f32[384,256]{1,0:T(8,128)S(1)}, f32[384,256]{1,0:T(8,128)S(1)}, u32[]{:S(2)}, u32[]{:S(2)}) collective-permute-start(f32[384,256]{1,0:T(8,128)S(1)} %broadcast_select_fusion.5), channel_id=1, source_target_pairs={{0,96},{8,104},{16,112},{24,120},{2,98},{10,106},{18,114},{26,122}... | collective-permute-start | bytes 1179656 | tf_op jit(solution)/shard_map/ppermute | solution.py:370
  91.4 1.3 collective-permute-start.24
  92.7 2.5 %collective-permute-start.23 = (f32[16,256]{1,0:T(8,128)S(1)}, f32[16,256]{1,0:T(8,128)S(1)}, u32[]{:S(2)}, u32[]{:S(2)}) collective-permute-start(f32[16,256]{1,0:T(8,128)S(1)} %broadcast_in_dim.26), channel_id=1, source_target_pairs={{0,4},{1,5},{8,12},{9,13},{16,20},{17,21},{24,28},{25,29},{32,36},... | collective-permute-start | bytes 49160 | tf_op jit(solution)/shard_map/ppermute | solution.py:419
  95.1 1.3 collective-permute-start.22
  96.5 0.8 collective-permute-done.22
  97.3 20.4 %collective-permute-start.25 = (f32[1040,256]{1,0:T(8,128)S(1)}, f32[1040,256]{1,0:T(8,128)S(1)}, u32[]{:S(2)}, u32[]{:S(2)}) collective-permute-start(f32[1040,256]{1,0:T(8,128)S(1)} %pad_maximum_fusion.mine), channel_id=1, source_target_pairs={{0,1},{1,0},{2,3},{3,2},{4,5},{5,4},{6,7},{7,6},{8,9},{9,8},{10,11... | collective-permute-start | bytes 3194888 | tf_op jit(solution)/shard_map/ppermute | solution.py:438
  117.7 0.3 collective-permute-start.26
  118.0 0.1 pad_add_fusion.place
  118.0 2.5 %collective-permute-done.26.other = f32[384,256]{1,0:T(8,128)S(1)} collective-permute-done((f32[384,256]{1,0:T(8,128)S(1)}, f32[384,256]{1,0:T(8,128)S(1)}, u32[]{:S(2)}, u32[]{:S(2)}) %collective-permute-start.26) | collective-permute-done | bytes 393248 | tf_op jit(solution)/shard_map/ppermute | solution.py:421
  120.6 8.2 %first_factor.1.w00 = f32[256,256]{1,0:T(8,128)S(1)} custom-call(s32[2]{0:T(128)S(1)} %pad_add_fusion.place, f32[384,256]{1,0:T(8,128)S(1)} %broadcast_select_fusion.6.own, f32[384,256]{1,0:T(8,128)S(1)} %collective-permute-done.26.other), custom_call_target="tpu_custom_call" | custom-call | flops 100000000 | bytes 100000 | tf_op jit(solution)/shard_map/first_factor/pallas_call | solution.py:144
  128.8 9.3 %second_factor.1 = (f32[256,256]{1,0:T(8,128)S(1)}, f32[256,256]{1,0:T(8,128)S(1)}) custom-call(s32[2]{0:T(128)S(1)} %pad_add_fusion.place, f32[256,256]{1,0:T(8,128)S(1)} %first_factor.1.w00, f32[384,256]{1,0:T(8,128)S(1)} %broadcast_select_fusion.6.own, f32[384,256]{1,0:T(8,128)S(1)} %collective-permute-done.26.other), custom_call_target="tpu_custom_call" | custom-call | flops 100000000 | bytes 100000 | tf_op jit(solution)/shard_map/second_factor/pallas_call | solution.py:151
  138.2 23.1 %panels_and_trailing.1 = (f32[1024,2,8,128]{3,2,1,0:T(8,128)}, f32[1024,512]{1,0:T(8,128)}, f32[16,128]{1,0:T(8,128)}) custom-call(s32[2]{0:T(128)S(1)} %pad_add_fusion.place, f32[1024,2,8,128]{3,2,1,0:T(8,128)} %bitcast.16, f32[16,256,256]{2,1,0:T(8,128)} %bitcast.17, f32[1040,256]{1,0:T(8,128)S(1)} %pad_maximum_fusion.mine, ...), custom_call_target="tpu_custom_call" | custom-call | flops 100000000 | bytes 100000 | tf_op jit(solution)/shard_map/panels_and_trailing/pallas_call | solution.py:309
  (46 shorter events, 0.7 us)
Async XLA Ops:
  7.2 131.0 %all-gather.3.cloned.1.call-start = ((), (), s32[]{:S(2)}) async-start(), calls=%async_computation | async-start | bytes 4456448 | tf_op jit(solution)/shard_map/all_gather | solution.py:426
  11.9 29.5 %copy-start.2 = (f32[4,1,256]{2,1,0:T(1,128)S(1)}, f32[4,1,256]{2,1,0:T(1,128)}, u32[]{:S(2)}) copy-start(f32[4,1,256]{2,1,0:T(1,128)} %param.3) | copy-start | bytes 12292
  11.9 11.0 %collective-permute-start = (f32[256,256]{1,0:T(8,128)S(1)}, f32[256,256]{1,0:T(8,128)S(1)}, u32[]{:S(2)}, u32[]{:S(2)}) collective-permute-start(f32[256,256]{1,0:T(8,128)S(1)} %get-tuple-element.40), channel_id=1, source_target_pairs={{8,0},{9,1}} | collective-permute-start | bytes 786440 | tf_op jit(solution)/shard_map/ppermute | solution.py:394
  13.2 17.3 %collective-permute-start.5 = (f32[256,256]{1,0:T(8,128)S(1)}, f32[256,256]{1,0:T(8,128)S(1)}, u32[]{:S(2)}, u32[]{:S(2)}) collective-permute-start(f32[256,256]{1,0:T(8,128)S(1)} %get-tuple-element.48), channel_id=1, source_target_pairs={{0,48},{8,56},{1,49},{9,57},{2,50},{10,58},{3,51},{11,59},{4,52},{... | collective-permute-start | bytes 786440 | tf_op jit(solution)/shard_map/ppermute | solution.py:425
  19.6 13.2 %collective-permute-start.6 = (f32[256,256]{1,0:T(8,128)S(1)}, f32[256,256]{1,0:T(8,128)S(1)}, u32[]{:S(2)}, u32[]{:S(2)}) collective-permute-start(f32[256,256]{1,0:T(8,128)S(1)} %get-tuple-element.49), channel_id=1, source_target_pairs={{0,32},{8,40},{1,33},{9,41},{2,34},{10,42},{3,35},{11,43},{4,36},{... | collective-permute-start | bytes 786440 | tf_op jit(solution)/shard_map/ppermute | solution.py:425
  20.9 14.0 %collective-permute-start.7 = (f32[256,256]{1,0:T(8,128)S(1)}, f32[256,256]{1,0:T(8,128)}, u32[]{:S(2)}, u32[]{:S(2)}) collective-permute-start(f32[256,256]{1,0:T(8,128)S(1)} %get-tuple-element.50), channel_id=1, source_target_pairs={{0,16},{8,24},{1,17},{9,25},{2,18},{10,26},{3,19},{11,27},{4,20},{... | collective-permute-start | bytes 786440 | tf_op jit(solution)/shard_map/ppermute | solution.py:425
  22.9 14.1 %collective-permute-start.1 = (f32[256,256]{1,0:T(8,128)S(1)}, f32[256,256]{1,0:T(8,128)}, u32[]{:S(2)}, u32[]{:S(2)}) collective-permute-start(f32[256,256]{1,0:T(8,128)S(1)} %get-tuple-element.41), channel_id=1, source_target_pairs={{0,112},{8,120},{1,113},{9,121},{2,114},{10,122},{3,115},{11,123},... | collective-permute-start | bytes 786440 | tf_op jit(solution)/shard_map/ppermute | solution.py:425
  25.1 25.9 %collective-permute-start.10 = (f32[1024,256]{1,0:T(8,128)S(1)}, f32[1024,256]{1,0:T(8,128)}, u32[]{:S(2)}, u32[]{:S(2)}) collective-permute-start(f32[1024,256]{1,0:T(8,128)S(1)} %get-tuple-element.54), channel_id=1, source_target_pairs={{0,6},{1,7},{8,14},{9,15},{16,22},{17,23},{24,30},{25,31},{32,38},... | collective-permute-start | bytes 3145736 | tf_op jit(solution)/shard_map/ppermute | solution.py:403
  30.5 22.8 %collective-permute-start.9 = (f32[1024,256]{1,0:T(8,128)S(1)}, f32[1024,256]{1,0:T(8,128)}, u32[]{:S(2)}, u32[]{:S(2)}) collective-permute-start(f32[1024,256]{1,0:T(8,128)S(1)} %get-tuple-element.54), channel_id=1, source_target_pairs={{0,2},{1,3},{8,10},{9,11},{16,18},{17,19},{24,26},{25,27},{32,34},... | collective-permute-start | bytes 3145736 | tf_op jit(solution)/shard_map/ppermute | solution.py:402
  32.8 2.0 %copy-start = (f32[256,256]{1,0:T(8,128)}, f32[256,256]{1,0:T(8,128)S(1)}, u32[]{:S(2)}) copy-start(f32[256,256]{1,0:T(8,128)S(1)} %collective-permute-done.6) | copy-start | bytes 786436
  32.8 6.2 %collective-permute-start.2 = (f32[256,256]{1,0:T(8,128)S(1)}, f32[256,256]{1,0:T(8,128)}, u32[]{:S(2)}, u32[]{:S(2)}) collective-permute-start(f32[256,256]{1,0:T(8,128)S(1)} %get-tuple-element.43), channel_id=1, source_target_pairs={{0,96},{8,104},{1,97},{9,105},{2,98},{10,106},{3,99},{11,107},{4,1... | collective-permute-start | bytes 786440 | tf_op jit(solution)/shard_map/ppermute | solution.py:425
  35.0 13.1 %collective-permute-start.3 = (f32[256,256]{1,0:T(8,128)S(1)}, f32[256,256]{1,0:T(8,128)}, u32[]{:S(2)}, u32[]{:S(2)}) collective-permute-start(f32[256,256]{1,0:T(8,128)S(1)} %get-tuple-element.45), channel_id=1, source_target_pairs={{0,80},{8,88},{1,81},{9,89},{2,82},{10,90},{3,83},{11,91},{4,84},{... | collective-permute-start | bytes 786440 | tf_op jit(solution)/shard_map/ppermute | solution.py:425
  37.0 11.1 %collective-permute-start.4 = (f32[256,256]{1,0:T(8,128)S(1)}, f32[256,256]{1,0:T(8,128)}, u32[]{:S(2)}, u32[]{:S(2)}) collective-permute-start(f32[256,256]{1,0:T(8,128)S(1)} %get-tuple-element.47), channel_id=1, source_target_pairs={{0,64},{8,72},{1,65},{9,73},{2,66},{10,74},{3,67},{11,75},{4,68},{... | collective-permute-start | bytes 786440 | tf_op jit(solution)/shard_map/ppermute | solution.py:425
  39.0 10.0 %collective-permute-start.8 = (f32[384,256]{1,0:T(8,128)S(1)}, f32[384,256]{1,0:T(8,128)S(1)}, u32[]{:S(2)}, u32[]{:S(2)}) collective-permute-start(f32[384,256]{1,0:T(8,128)S(1)} %maximum_select_fusion), channel_id=1, source_target_pairs={{0,2},{1,9}} | collective-permute-start | bytes 1179656 | tf_op jit(solution)/shard_map/ppermute | solution.py:370
  41.5 6.6 %copy-start.1 = (f32[256,256]{1,0:T(8,128)S(1)}, f32[256,256]{1,0:T(8,128)}, u32[]{:S(2)}) copy-start(f32[256,256]{1,0:T(8,128)} %copy-done) | copy-start | bytes 786436
  53.3 6.0 %collective-permute-start.13 = (f32[384,256]{1,0:T(8,128)S(1)}, f32[384,256]{1,0:T(8,128)S(1)}, u32[]{:S(2)}, u32[]{:S(2)}) collective-permute-start(f32[384,256]{1,0:T(8,128)S(1)} %broadcast_select_fusion.7), channel_id=1, source_target_pairs={{0,6},{2,4},{1,25},{9,17}} | collective-permute-start | bytes 1179656 | tf_op jit(solution)/shard_map/ppermute | solution.py:370
  54.6 2.6 %collective-permute-start.14 = (f32[16,128]{1,0:T(8,128)S(1)}, f32[16,128]{1,0:T(8,128)S(1)}, u32[]{:S(2)}, u32[]{:S(2)}) collective-permute-start(f32[16,128]{1,0:T(8,128)S(1)} %column_sums.1), channel_id=1, source_target_pairs={{0,8},{8,0},{16,24},{24,16},{32,40},{40,32},{48,56},{56,48},{64,72... | collective-permute-start | bytes 24584 | tf_op jit(solution)/shard_map/ppermute | solution.py:412
  59.4 6.5 %collective-permute-start.15 = (f32[384,256]{1,0:T(8,128)S(1)}, f32[384,256]{1,0:T(8,128)S(1)}, u32[]{:S(2)}, u32[]{:S(2)}) collective-permute-start(f32[384,256]{1,0:T(8,128)S(1)} %broadcast_select_fusion.2), channel_id=1, source_target_pairs={{0,8},{2,10},{4,12},{6,14},{1,33},{9,41},{17,49},{25,57}} | collective-permute-start | bytes 1179656 | tf_op jit(solution)/shard_map/ppermute | solution.py:370
  61.0 7.1 %collective-permute-start.11 = (f32[512,256]{1,0:T(8,128)S(1)}, f32[512,256]{1,0:T(8,128)S(1)}, u32[]{:S(2)}, u32[]{:S(2)}) collective-permute-start(f32[512,256]{1,0:T(8,128)S(1)} %slice.19), channel_id=1, source_target_pairs={{2,4},{3,5},{10,12},{11,13},{18,20},{19,21},{26,28},{27,29},{34,36... | collective-permute-start | bytes 1572872 | tf_op jit(solution)/shard_map/ppermute | solution.py:405
  61.7 4.2 %collective-permute-start.16 = (f32[16,128]{1,0:T(8,128)S(1)}, f32[16,128]{1,0:T(8,128)S(1)}, u32[]{:S(2)}, u32[]{:S(2)}) collective-permute-start(f32[16,128]{1,0:T(8,128)S(1)} %add.51), channel_id=1, source_target_pairs={{0,24},{8,16},{16,8},{24,0},{32,56},{40,48},{48,40},{56,32},{64,88... | collective-permute-start | bytes 24584 | tf_op jit(solution)/shard_map/ppermute | solution.py:412
  66.0 7.4 %collective-permute-start.17 = (f32[384,256]{1,0:T(8,128)S(1)}, f32[384,256]{1,0:T(8,128)}, u32[]{:S(2)}, u32[]{:S(2)}) collective-permute-start(f32[384,256]{1,0:T(8,128)S(1)} %broadcast_select_fusion.3), channel_id=1, source_target_pairs={{0,24},{2,26},{4,28},{6,30},{8,16},{10,18},{12,20},{14,22},{1,97},... | collective-permute-start | bytes 1179656 | tf_op jit(solution)/shard_map/ppermute | solution.py:370
  68.9 4.5 %collective-permute-start.12 = (f32[512,256]{1,0:T(8,128)}, f32[512,256]{1,0:T(8,128)S(1)}, u32[]{:S(2)}, u32[]{:S(2)}) collective-permute-start(f32[512,256]{1,0:T(8,128)} %get-tuple-element.79), channel_id=1, source_target_pairs={{6,4},{7,5},{14,12},{15,13},{22,20},{23,21},{30,28},{31,29},{38,36... | collective-permute-start | bytes 1572872 | tf_op jit(solution)/shard_map/ppermute | solution.py:406
  69.6 2.9 %collective-permute-start.18 = (f32[16,128]{1,0:T(8,128)S(1)}, f32[16,128]{1,0:T(8,128)S(1)}, u32[]{:S(2)}, u32[]{:S(2)}) collective-permute-start(f32[16,128]{1,0:T(8,128)S(1)} %add.52), channel_id=1, source_target_pairs={{0,32},{8,40},{16,48},{24,56},{32,0},{40,8},{48,16},{56,24},{64,96... | collective-permute-start | bytes 24584 | tf_op jit(solution)/shard_map/ppermute | solution.py:412
  73.4 10.5 %collective-permute-start.19 = (f32[384,256]{1,0:T(8,128)S(1)}, f32[384,256]{1,0:T(8,128)S(1)}, u32[]{:S(2)}, u32[]{:S(2)}) collective-permute-start(f32[384,256]{1,0:T(8,128)S(1)} %broadcast_select_fusion.4), channel_id=1, source_target_pairs={{0,32},{8,40},{16,48},{24,56},{2,34},{10,42},{18,50},{26,58},{4,36... | collective-permute-start | bytes 1179656 | tf_op jit(solution)/shard_map/ppermute | solution.py:370
  79.3 3.8 %collective-permute-start.20 = (f32[16,128]{1,0:T(8,128)S(1)}, f32[16,128]{1,0:T(8,128)S(1)}, u32[]{:S(2)}, u32[]{:S(2)}) collective-permute-start(f32[16,128]{1,0:T(8,128)S(1)} %add.53), channel_id=1, source_target_pairs={{0,96},{8,104},{16,112},{24,120},{32,64},{40,72},{48,80},{56,88},{... | collective-permute-start | bytes 24584 | tf_op jit(solution)/shard_map/ppermute | solution.py:412
  84.0 12.4 %collective-permute-start.21 = (f32[384,256]{1,0:T(8,128)S(1)}, f32[384,256]{1,0:T(8,128)S(1)}, u32[]{:S(2)}, u32[]{:S(2)}) collective-permute-start(f32[384,256]{1,0:T(8,128)S(1)} %broadcast_select_fusion.5), channel_id=1, source_target_pairs={{0,96},{8,104},{16,112},{24,120},{2,98},{10,106},{18,114},{26,122}... | collective-permute-start | bytes 1179656 | tf_op jit(solution)/shard_map/ppermute | solution.py:370
  91.4 5.1 %collective-permute-start.24 = (f32[16,256]{1,0:T(8,128)S(1)}, f32[16,256]{1,0:T(8,128)S(1)}, u32[]{:S(2)}, u32[]{:S(2)}) collective-permute-start(f32[16,256]{1,0:T(8,128)S(1)} %broadcast_in_dim.26), channel_id=1, source_target_pairs={{0,6},{1,7},{8,14},{9,15},{16,22},{17,23},{24,30},{25,31},{32,38},... | collective-permute-start | bytes 49160 | tf_op jit(solution)/shard_map/ppermute | solution.py:419
  92.7 3.8 %collective-permute-start.23 = (f32[16,256]{1,0:T(8,128)S(1)}, f32[16,256]{1,0:T(8,128)S(1)}, u32[]{:S(2)}, u32[]{:S(2)}) collective-permute-start(f32[16,256]{1,0:T(8,128)S(1)} %broadcast_in_dim.26), channel_id=1, source_target_pairs={{0,4},{1,5},{8,12},{9,13},{16,20},{17,21},{24,28},{25,29},{32,36},... | collective-permute-start | bytes 49160 | tf_op jit(solution)/shard_map/ppermute | solution.py:419
  95.1 2.1 %collective-permute-start.22 = (f32[16,256]{1,0:T(8,128)S(1)}, f32[16,256]{1,0:T(8,128)S(1)}, u32[]{:S(2)}, u32[]{:S(2)}) collective-permute-start(f32[16,256]{1,0:T(8,128)S(1)} %broadcast_in_dim.26), channel_id=1, source_target_pairs={{0,2},{1,3},{8,10},{9,11},{16,18},{17,19},{24,26},{25,27},{32,34},... | collective-permute-start | bytes 49160 | tf_op jit(solution)/shard_map/ppermute | solution.py:419
  97.3 40.8 %collective-permute-start.25 = (f32[1040,256]{1,0:T(8,128)S(1)}, f32[1040,256]{1,0:T(8,128)S(1)}, u32[]{:S(2)}, u32[]{:S(2)}) collective-permute-start(f32[1040,256]{1,0:T(8,128)S(1)} %pad_maximum_fusion.mine), channel_id=1, source_target_pairs={{0,1},{1,0},{2,3},{3,2},{4,5},{5,4},{6,7},{7,6},{8,9},{9,8},{10,11... | collective-permute-start | bytes 3194888 | tf_op jit(solution)/shard_map/ppermute | solution.py:438
  117.7 2.9 %collective-permute-start.26 = (f32[384,256]{1,0:T(8,128)S(1)}, f32[384,256]{1,0:T(8,128)S(1)}, u32[]{:S(2)}, u32[]{:S(2)}) collective-permute-start(f32[384,256]{1,0:T(8,128)S(1)} %broadcast_select_fusion.6.own), channel_id=1, source_target_pairs={{0,1},{1,0},{2,3},{3,2},{4,5},{5,4},{6,7},{7,6},{8,9},{9,8},{10,11... | collective-permute-start | bytes 1179656 | tf_op jit(solution)/shard_map/ppermute | solution.py:421
Sparse Core Ops, SparseCore 0:
  53.4 52.8 all-gather.2

commit v10 on v8

--- a/solution.py
+++ b/solution.py
@@ -272,20 +272,27 @@
 
             g_high = jnp.concatenate([high[pl.ds(base, ROWS), :], high[1024:1040, :]], axis=0)
             g_low = jnp.concatenate([low[pl.ds(base, ROWS), :], low[1024:1040, :]], axis=0)
-            top = (step * ROWS + lax.broadcasted_iota(jnp.int32, (ROWS, 1), 0) < NB) & (row_index < 2)
             for u in range(4):
                 product = dot3((g_high, g_low), (right_high[u], right_low[u]), NN)
-                gone = top | (col_index < 2) if (group, u) == (0, 0) else top
                 for h in range(2):
                     q = 2 * u + h
                     lanes = slice(128 * h, 128 * h + 128)
-                    value = block[pl.ds(base, ROWS), group, q, :] - product[0:ROWS, lanes]
-                    ready[slot, :, q, :] = jnp.where(gone, 0.0, value)
+                    ready[slot, :, q, :] = block[pl.ds(base, ROWS), group, q, :] - product[0:ROWS, lanes]
                     at = 8 * group + q
                     kept = sums[at : at + 1, :] - product[ROWS : ROWS + 1, lanes]
                     if (group, u) == (0, 0):
                         kept = jnp.where(col_index < 2, 0.0, kept)
                     checksum[at : at + 1, :] = kept
+            @pl.when((step == 0) & (row_index < 2))
+            def _():
+                ready[slot] = jnp.zeros((ROWS, 8, 128), F32)
+
+            if group == 0:
+
+                @pl.when(col_index < 2)
+                def _():
+                    ready[slot, :, 0:2, :] = jnp.zeros((ROWS, 2, 128), F32)
+
             put(slot, group, step).start()
             return carry
 
@@ -323,7 +330,7 @@
             pltpu.SemaphoreType.DMA((2,)),
         ],
         name="panels_and_trailing",
-        compiler_params=pltpu.CompilerParams(vmem_limit_bytes=40 * 1024 * 1024),
+        compiler_params=pltpu.CompilerParams(vmem_limit_bytes=30 * 1024 * 1024),
         cost_estimate=SMALL,
     )(place, flat, across, mine, theirs, w00, l10, w11, sums)
 
@@ -401,7 +408,7 @@
             partial.append(before + lax.ppermute(after(before, value), "row", [(r, r ^ d) for r in range(16)]))
         return after(value, (before, from_left, from_right) if stage == 4 else before)
 
-    tree = spread(corner, [((0, 0), 0, (2, 1, 0)), ((0, 0), 1, (1, 0, 2))], here, beside)
+    tree = spread(corner, [((0, 0), 0, (0, 1, 2)), ((0, 0), 1, (0, 2, 1))], here, beside)
     sums = partial[-1]
     near_sums = jnp.broadcast_to(sums[0:2].reshape(1, NB), (16, NB))
     far_sums = [lax.ppermute(near_sums, "col", [(0, 2 * k), (1, 2 * k + 1)]) for k in (1, 2, 3)]

time: 162 us -> 162 us (level)
  starting transfers between devices: 61.7 us -> 45.4 us
  waiting for transfers between devices: 27.1 us -> 42.8 us
    ppermute x6, waiting for transfers between devices: 10.6 us -> 29 us  [spread(): arrived = lax.ppermute(value, ('row', 'col'), pairs)]
    ppermute x1, starting transfers between devices: 12.7 us -> 0.01 us  [shards(): other = lax.ppermute(own, 'col', swap_cores)]
    ppermute x6, starting transfers between devices: 13.1 us -> 8.83 us  [spread(): arrived = lax.ppermute(value, ('row', 'col'), pairs)]
    ppermute x1, waiting for transfers between devices: 2.86 us -> 0.01 us  [shards(): from_right = lax.ppermute(column, 'col', [(0, 6), (1, 7)])]
  transfers between devices with their start and end apart: 28 -> 28, of which waited for: 14 -> 11; matrix products, arithmetic and copies ran while one was open for 2% -> 2% of each run, Pallas kernels for 15% -> 15%
where the time goes in v10:
time: 162 us; the launch traced here: 159 us
  Pallas kernels  50.7 us (31%)
  starting transfers between devices  45.4 us (28%)
  waiting for transfers between devices  42.8 us (26%)
  between operations  14.5 us (9%)
  other arithmetic  2.73 us (2%)
  local copies, waits for them, and re-layouts  2.63 us (2%)
    ppermute x6, waiting for transfers between devices, spread(): arrived = lax.ppermute(value, ('row', 'col'), pairs)  29 us
    pallas_call x1, Pallas kernels, final_call(): pl.pallas_call(final_kernel, out_shape=(jax.ShapeDtypeStruct((1024, 2, 8,...  23 us
    ppermute x7, starting transfers between devices, shards(): lax.ppermute(pieces[j] if j < 4 else after(pieces[j], fetched), 'row', [(...  15.8 us
    pallas_call x1, Pallas kernels, second_factor(): pl.pallas_call(second_kernel, out_shape=(TILE, TILE), in_specs=[SMEM, VME...  9.31 us
    ppermute x4, waiting for transfers between devices, beside(): lax.ppermute(after(before, value), 'row', [(r, r ^ d) for r in range(16)])  9.09 us
    ppermute x6, starting transfers between devices, spread(): arrived = lax.ppermute(value, ('row', 'col'), pairs)  8.83 us
    pallas_call x1, Pallas kernels, first_factor(): pl.pallas_call(first_kernel, out_shape=TILE, in_specs=[SMEM, VMEM, VMEM],...  8.22 us
    ppermute x3, starting transfers between devices, shards(): lax.ppermute(near_sums, 'col', [(0, 2 * k), (1, 2 * k + 1)])  7.93 us
  transfers between devices with their start and end apart: 28, of which 11 were waited for; matrix products, arithmetic and copies ran while one was open for 2% of the time, Pallas kernels for 15%

profile of v10, /device:TPU:1, one launch (start us, length us, event | category | flops | bytes accessed | tf_op | source)
XLA Modules:
  0.0 158.8 jit_solution(5391561023413705964)
XLA Ops:
  7.2 3.3 %corner_tiles.1 = (f32[256,256]{1,0:T(8,128)}, f32[256,256]{1,0:T(8,128)}, f32[256,256]{1,0:T(8,128)}, f32[256,256]{1,0:T(8,128)}, f32[256,256]{1,0:T(8,128)}, /...) custom-call(f32[1024,16,128]{2,1,0:T(8,128)} %bitcast.13), custom_call_target="tpu_custom_call" | custom-call | tf_op jit(solution)/shard_map/corner_tiles/pallas_call | solution.py:167
  10.5 1.3 collective-permute-start
  11.8 6.4 %collective-permute-start.5 = (f32[256,256]{1,0:T(8,128)}, f32[256,256]{1,0:T(8,128)S(1)}, u32[]{:S(2)}, u32[]{:S(2)}) collective-permute-start(f32[256,256]{1,0:T(8,128)} %get-tuple-element.52), channel_id=1, source_target_pairs={{0,48},{8,56},{1,49},{9,57},{2,50},{10,58},{3,51},{11,59},{4,52},{... | collective-permute-start | bytes 786440 | tf_op jit(solution)/shard_map/ppermute | solution.py:420
  18.2 1.3 collective-permute-start.6
  19.5 1.3 collective-permute-start.7
  21.0 1.5 collective-permute-start.1
  22.5 1.3 collective-permute-start.2
  23.9 2.0 %collective-permute-start.3 = (f32[256,256]{1,0:T(8,128)}, f32[256,256]{1,0:T(8,128)}, u32[]{:S(2)}, u32[]{:S(2)}) collective-permute-start(f32[256,256]{1,0:T(8,128)} %get-tuple-element.49), channel_id=1, source_target_pairs={{0,80},{8,88},{1,81},{9,89},{2,82},{10,90},{3,83},{11,91},{4,84},{... | collective-permute-start | bytes 786440 | tf_op jit(solution)/shard_map/ppermute | solution.py:420
  25.9 2.0 %collective-permute-start.4 = (f32[256,256]{1,0:T(8,128)}, f32[256,256]{1,0:T(8,128)}, u32[]{:S(2)}, u32[]{:S(2)}) collective-permute-start(f32[256,256]{1,0:T(8,128)} %get-tuple-element.51), channel_id=1, source_target_pairs={{0,64},{8,72},{1,65},{9,73},{2,66},{10,74},{3,67},{11,75},{4,68},{... | collective-permute-start | bytes 786440 | tf_op jit(solution)/shard_map/ppermute | solution.py:420
  27.9 1.0 maximum_select_fusion
  28.9 0.2 collective-permute-done.7
  29.1 2.1 %collective-permute-start.8 = (f32[384,256]{1,0:T(8,128)S(1)}, f32[384,256]{1,0:T(8,128)S(1)}, u32[]{:S(2)}, u32[]{:S(2)}) collective-permute-start(f32[384,256]{1,0:T(8,128)S(1)} %maximum_select_fusion), channel_id=1, source_target_pairs={{0,32},{1,33}} | collective-permute-start | bytes 1179656 | tf_op jit(solution)/shard_map/ppermute | solution.py:369
  31.3 6.9 %first_column.1 = (f32[1024,256]{1,0:T(8,128)S(1)}, f32[16,128]{1,0:T(8,128)S(1)}) custom-call(f32[1024]{0:T(1024)S(1)} %broadcast_select_fusion.8.weights, f32[1024,16,128]{2,1,0:T(8,128)} %bitcast.14), custom_call_target="tpu_custom_call" | custom-call | flops 100000000 | bytes 100000 | tf_op jit(solution)/shard_map/first_column/pallas_call | solution.py:194
  38.2 2.1 %collective-permute-done.3 = f32[256,256]{1,0:T(8,128)} collective-permute-done((f32[256,256]{1,0:T(8,128)}, f32[256,256]{1,0:T(8,128)}, u32[]{:S(2)}, u32[]{:S(2)}) %collective-permute-start.3) | collective-permute-done | bytes 262176 | tf_op jit(solution)/shard_map/ppermute | solution.py:420
  40.3 0.8 select_select_fusion.1
  41.3 1.3 collective-permute-start.11
  42.6 1.1 collective-permute-start.12
  43.7 1.5 collective-permute-done.12
  45.2 4.5 %collective-permute-done.11 = f32[384,256]{1,0:T(8,128)S(1)} collective-permute-done((f32[384,256]{1,0:T(8,128)S(1)}, f32[384,256]{1,0:T(8,128)S(1)}, u32[]{:S(2)}, u32[]{:S(2)}) %collective-permute-start.11) | collective-permute-done | bytes 393248 | tf_op jit(solution)/shard_map/ppermute | solution.py:369
  49.7 1.3 collective-permute-start.13
  51.1 1.4 collective-permute-start.10
  52.4 2.3 %collective-permute-start.9 = (f32[1024,256]{1,0:T(8,128)S(1)}, f32[1024,256]{1,0:T(8,128)}, u32[]{:S(2)}, u32[]{:S(2)}) collective-permute-start(f32[1024,256]{1,0:T(8,128)S(1)} %get-tuple-element.58), channel_id=1, source_target_pairs={{0,2},{1,3},{8,10},{9,11},{16,18},{17,19},{24,26},{25,27},{32,34},... | collective-permute-start | bytes 3145736 | tf_op jit(solution)/shard_map/ppermute | solution.py:401
  54.8 3.7 %collective-permute-done.14 = f32[16,128]{1,0:T(8,128)S(1)} collective-permute-done((f32[16,128]{1,0:T(8,128)S(1)}, f32[16,128]{1,0:T(8,128)S(1)}, u32[]{:S(2)}, u32[]{:S(2)}) %collective-permute-start.14) | collective-permute-done | bytes 8224 | tf_op jit(solution)/shard_map/ppermute | solution.py:408
  58.5 1.3 collective-permute-start.15
  59.8 0.7 collective-permute-start.16
  60.5 2.3 %collective-permute-done.16 = f32[16,128]{1,0:T(8,128)S(1)} collective-permute-done((f32[16,128]{1,0:T(8,128)S(1)}, f32[16,128]{1,0:T(8,128)S(1)}, u32[]{:S(2)}, u32[]{:S(2)}) %collective-permute-start.16) | collective-permute-done | bytes 8224 | tf_op jit(solution)/shard_map/ppermute | solution.py:408
  62.8 16.7 %collective-permute-done.15 = f32[384,256]{1,0:T(8,128)S(1)} collective-permute-done((f32[384,256]{1,0:T(8,128)S(1)}, f32[384,256]{1,0:T(8,128)S(1)}, u32[]{:S(2)}, u32[]{:S(2)}) %collective-permute-start.15) | collective-permute-done | bytes 393248 | tf_op jit(solution)/shard_map/ppermute | solution.py:369
  79.6 1.3 collective-permute-start.17
  80.9 3.5 %collective-permute-start.18 = (f32[16,128]{1,0:T(8,128)S(1)}, f32[16,128]{1,0:T(8,128)S(1)}, u32[]{:S(2)}, u32[]{:S(2)}) collective-permute-start(f32[16,128]{1,0:T(8,128)S(1)} %add.53), channel_id=1, source_target_pairs={{0,96},{8,104},{16,112},{24,120},{32,64},{40,72},{48,80},{56,88},{... | collective-permute-start | bytes 24584 | tf_op jit(solution)/shard_map/ppermute | solution.py:408
  84.4 1.6 collective-permute-done.18
  86.0 7.7 %collective-permute-done.17 = f32[384,256]{1,0:T(8,128)S(1)} collective-permute-done((f32[384,256]{1,0:T(8,128)S(1)}, f32[384,256]{1,0:T(8,128)S(1)}, u32[]{:S(2)}, u32[]{:S(2)}) %collective-permute-start.17) | collective-permute-done | bytes 393248 | tf_op jit(solution)/shard_map/ppermute | solution.py:369
  93.8 1.4 collective-permute-start.19
  95.3 0.2 select_select_fusion
  95.5 5.3 %collective-permute-start.22 = (f32[16,256]{1,0:T(8,128)S(1)}, f32[16,256]{1,0:T(8,128)S(1)}, u32[]{:S(2)}, u32[]{:S(2)}) collective-permute-start(f32[16,256]{1,0:T(8,128)S(1)} %broadcast_in_dim.26), channel_id=1, source_target_pairs={{0,6},{1,7},{8,14},{9,15},{16,22},{17,23},{24,30},{25,31},{32,38},... | collective-permute-start | bytes 49160 | tf_op jit(solution)/shard_map/ppermute | solution.py:414
  100.9 1.3 collective-permute-start.21
  102.2 1.3 collective-permute-start.20
  103.6 0.8 collective-permute-done.20
  104.3 0.9 fusion
  105.2 0.7 collective-permute-start.24
  105.9 1.5 collective-permute-start.23
  107.4 1.6 %collective-permute-done.25.other = f32[384,256]{1,0:T(8,128)S(1)} collective-permute-done((f32[384,256]{1,0:T(8,128)S(1)}, f32[384,256]{1,0:T(8,128)S(1)}, u32[]{:S(2)}, u32[]{:S(2)}) %collective-permute-start.25) | collective-permute-done | bytes 393248 | tf_op jit(solution)/shard_map/ppermute | solution.py:416
  109.1 8.2 %first_factor.1.w00 = f32[256,256]{1,0:T(8,128)S(1)} custom-call(s32[2]{0:T(128)S(1)} %pad_add_fusion.place, f32[384,256]{1,0:T(8,128)S(1)} %broadcast_select_fusion.6.own, f32[384,256]{1,0:T(8,128)S(1)} %collective-permute-done.25.other), custom_call_target="tpu_custom_call" | custom-call | flops 100000000 | bytes 100000 | tf_op jit(solution)/shard_map/first_factor/pallas_call | solution.py:144
  117.3 0.1 broadcast_select_fusion.1
  117.6 0.4 collective-permute-start.26
  118.0 9.3 %second_factor.1 = (f32[256,256]{1,0:T(8,128)S(1)}, f32[256,256]{1,0:T(8,128)S(1)}) custom-call(s32[2]{0:T(128)S(1)} %pad_add_fusion.place, f32[256,256]{1,0:T(8,128)S(1)} %first_factor.1.w00, f32[384,256]{1,0:T(8,128)S(1)} %broadcast_select_fusion.6.own, f32[384,256]{1,0:T(8,128)S(1)} %collective-permute-done.25.other), custom_call_target="tpu_custom_call" | custom-call | flops 100000000 | bytes 100000 | tf_op jit(solution)/shard_map/second_factor/pallas_call | solution.py:151
  127.3 0.7 copy-done
  128.0 0.9 copy-done.1
  128.9 23.0 %panels_and_trailing.1 = (f32[1024,2,8,128]{3,2,1,0:T(8,128)}, f32[1024,512]{1,0:T(8,128)}, f32[16,128]{1,0:T(8,128)}) custom-call(s32[2]{0:T(128)S(1)} %pad_add_fusion.place, f32[1024,2,8,128]{3,2,1,0:T(8,128)} %bitcast.15, f32[16,256,256]{2,1,0:T(8,128)} %bitcast.16, f32[1040,256]{1,0:T(8,128)S(1)} %pad_maximum_fusion.mine, ...), custom_call_target="tpu_custom_call" | custom-call | flops 100000000 | bytes 100000 | tf_op jit(solution)/shard_map/panels_and_trailing/pallas_call | solution.py:308
  (51 shorter events, 0.7 us)
Async XLA Ops:
  7.2 120.8 %all-gather.3.cloned.1.call-start = ((), (), s32[]{:S(2)}) async-start(), calls=%async_computation | async-start | bytes 4456448 | tf_op jit(solution)/shard_map/all_gather | solution.py:421
  10.5 20.7 %copy-start.5 = (f32[4,1,256]{2,1,0:T(1,128)S(1)}, f32[4,1,256]{2,1,0:T(1,128)}, u32[]{:S(2)}) copy-start(f32[4,1,256]{2,1,0:T(1,128)} %param.3) | copy-start | bytes 12292
  10.5 10.5 %collective-permute-start = (f32[256,256]{1,0:T(8,128)}, f32[256,256]{1,0:T(8,128)S(1)}, u32[]{:S(2)}, u32[]{:S(2)}) collective-permute-start(f32[256,256]{1,0:T(8,128)} %get-tuple-element.44), channel_id=1, source_target_pairs={{8,0},{9,1}} | collective-permute-start | bytes 786440 | tf_op jit(solution)/shard_map/ppermute | solution.py:393
  11.8 12.0 %collective-permute-start.5 = (f32[256,256]{1,0:T(8,128)}, f32[256,256]{1,0:T(8,128)S(1)}, u32[]{:S(2)}, u32[]{:S(2)}) collective-permute-start(f32[256,256]{1,0:T(8,128)} %get-tuple-element.52), channel_id=1, source_target_pairs={{0,48},{8,56},{1,49},{9,57},{2,50},{10,58},{3,51},{11,59},{4,52},{... | collective-permute-start | bytes 786440 | tf_op jit(solution)/shard_map/ppermute | solution.py:420
  18.2 7.6 %collective-permute-start.6 = (f32[256,256]{1,0:T(8,128)}, f32[256,256]{1,0:T(8,128)S(1)}, u32[]{:S(2)}, u32[]{:S(2)}) collective-permute-start(f32[256,256]{1,0:T(8,128)} %get-tuple-element.53), channel_id=1, source_target_pairs={{0,32},{8,40},{1,33},{9,41},{2,34},{10,42},{3,35},{11,43},{4,36},{... | collective-permute-start | bytes 786440 | tf_op jit(solution)/shard_map/ppermute | solution.py:420
  19.5 9.6 %collective-permute-start.7 = (f32[256,256]{1,0:T(8,128)}, f32[256,256]{1,0:T(8,128)S(1)}, u32[]{:S(2)}, u32[]{:S(2)}) collective-permute-start(f32[256,256]{1,0:T(8,128)} %get-tuple-element.54), channel_id=1, source_target_pairs={{0,16},{8,24},{1,17},{9,25},{2,18},{10,26},{3,19},{11,27},{4,20},{... | collective-permute-start | bytes 786440 | tf_op jit(solution)/shard_map/ppermute | solution.py:420
  21.0 17.3 %collective-permute-start.1 = (f32[256,256]{1,0:T(8,128)}, f32[256,256]{1,0:T(8,128)S(1)}, u32[]{:S(2)}, u32[]{:S(2)}) collective-permute-start(f32[256,256]{1,0:T(8,128)} %get-tuple-element.45), channel_id=1, source_target_pairs={{0,112},{8,120},{1,113},{9,121},{2,114},{10,122},{3,115},{11,123},... | collective-permute-start | bytes 786440 | tf_op jit(solution)/shard_map/ppermute | solution.py:420
  22.5 15.7 %collective-permute-start.2 = (f32[256,256]{1,0:T(8,128)}, f32[256,256]{1,0:T(8,128)S(1)}, u32[]{:S(2)}, u32[]{:S(2)}) collective-permute-start(f32[256,256]{1,0:T(8,128)} %get-tuple-element.47), channel_id=1, source_target_pairs={{0,96},{8,104},{1,97},{9,105},{2,98},{10,106},{3,99},{11,107},{4,1... | collective-permute-start | bytes 786440 | tf_op jit(solution)/shard_map/ppermute | solution.py:420
  23.9 16.5 %collective-permute-start.3 = (f32[256,256]{1,0:T(8,128)}, f32[256,256]{1,0:T(8,128)}, u32[]{:S(2)}, u32[]{:S(2)}) collective-permute-start(f32[256,256]{1,0:T(8,128)} %get-tuple-element.49), channel_id=1, source_target_pairs={{0,80},{8,88},{1,81},{9,89},{2,82},{10,90},{3,83},{11,91},{4,84},{... | collective-permute-start | bytes 786440 | tf_op jit(solution)/shard_map/ppermute | solution.py:420
  25.9 14.5 %collective-permute-start.4 = (f32[256,256]{1,0:T(8,128)}, f32[256,256]{1,0:T(8,128)}, u32[]{:S(2)}, u32[]{:S(2)}) collective-permute-start(f32[256,256]{1,0:T(8,128)} %get-tuple-element.51), channel_id=1, source_target_pairs={{0,64},{8,72},{1,65},{9,73},{2,66},{10,74},{3,67},{11,75},{4,68},{... | collective-permute-start | bytes 786440 | tf_op jit(solution)/shard_map/ppermute | solution.py:420
  29.1 12.1 %collective-permute-start.8 = (f32[384,256]{1,0:T(8,128)S(1)}, f32[384,256]{1,0:T(8,128)S(1)}, u32[]{:S(2)}, u32[]{:S(2)}) collective-permute-start(f32[384,256]{1,0:T(8,128)S(1)} %maximum_select_fusion), channel_id=1, source_target_pairs={{0,32},{1,33}} | collective-permute-start | bytes 1179656 | tf_op jit(solution)/shard_map/ppermute | solution.py:369
  31.3 9.0 %copy-start.4 = (f32[256,256]{1,0:T(8,128)S(1)}, f32[256,256]{1,0:T(8,128)}, u32[]{:S(2)}) copy-start(f32[256,256]{1,0:T(8,128)} %get-tuple-element.55) | copy-start | bytes 786436
  41.3 8.4 %collective-permute-start.11 = (f32[384,256]{1,0:T(8,128)S(1)}, f32[384,256]{1,0:T(8,128)S(1)}, u32[]{:S(2)}, u32[]{:S(2)}) collective-permute-start(f32[384,256]{1,0:T(8,128)S(1)} %broadcast_select_fusion.7), channel_id=1, source_target_pairs={{0,96},{32,64},{1,97},{33,65}} | collective-permute-start | bytes 1179656 | tf_op jit(solution)/shard_map/ppermute | solution.py:369
  42.6 2.6 %collective-permute-start.12 = (f32[16,128]{1,0:T(8,128)S(1)}, f32[16,128]{1,0:T(8,128)S(1)}, u32[]{:S(2)}, u32[]{:S(2)}) collective-permute-start(f32[16,128]{1,0:T(8,128)S(1)} %get-tuple-element.62), channel_id=1, source_target_pairs={{0,8},{8,0},{16,24},{24,16},{32,40},{40,32},{48,56},{56,48},{64,72... | collective-permute-start | bytes 24584 | tf_op jit(solution)/shard_map/ppermute | solution.py:408
  49.7 8.7 %collective-permute-start.13 = (f32[384,256]{1,0:T(8,128)S(1)}, f32[384,256]{1,0:T(8,128)S(1)}, u32[]{:S(2)}, u32[]{:S(2)}) collective-permute-start(f32[384,256]{1,0:T(8,128)S(1)} %broadcast_select_fusion.2), channel_id=1, source_target_pairs={{0,8},{32,40},{64,72},{96,104},{1,3},{33,35},{65,67},{97,99}} | collective-permute-start | bytes 1179656 | tf_op jit(solution)/shard_map/ppermute | solution.py:369
  51.1 28.5 %collective-permute-start.10 = (f32[1024,256]{1,0:T(8,128)S(1)}, f32[1024,256]{1,0:T(8,128)S(1)}, u32[]{:S(2)}, u32[]{:S(2)}) collective-permute-start(f32[1024,256]{1,0:T(8,128)S(1)} %get-tuple-element.58), channel_id=1, source_target_pairs={{0,6},{1,7},{8,14},{9,15},{16,22},{17,23},{24,30},{25,31},{32,38},... | collective-permute-start | bytes 3145736 | tf_op jit(solution)/shard_map/ppermute | solution.py:402
  52.4 27.2 %collective-permute-start.9 = (f32[1024,256]{1,0:T(8,128)S(1)}, f32[1024,256]{1,0:T(8,128)}, u32[]{:S(2)}, u32[]{:S(2)}) collective-permute-start(f32[1024,256]{1,0:T(8,128)S(1)} %get-tuple-element.58), channel_id=1, source_target_pairs={{0,2},{1,3},{8,10},{9,11},{16,18},{17,19},{24,26},{25,27},{32,34},... | collective-permute-start | bytes 3145736 | tf_op jit(solution)/shard_map/ppermute | solution.py:401
  54.7 3.7 %collective-permute-start.14 = (f32[16,128]{1,0:T(8,128)S(1)}, f32[16,128]{1,0:T(8,128)S(1)}, u32[]{:S(2)}, u32[]{:S(2)}) collective-permute-start(f32[16,128]{1,0:T(8,128)S(1)} %add.51), channel_id=1, source_target_pairs={{0,24},{8,16},{16,8},{24,0},{32,56},{40,48},{48,40},{56,32},{64,88... | collective-permute-start | bytes 24584 | tf_op jit(solution)/shard_map/ppermute | solution.py:408
  58.5 21.0 %collective-permute-start.15 = (f32[384,256]{1,0:T(8,128)S(1)}, f32[384,256]{1,0:T(8,128)S(1)}, u32[]{:S(2)}, u32[]{:S(2)}) collective-permute-start(f32[384,256]{1,0:T(8,128)S(1)} %broadcast_select_fusion.3), channel_id=1, source_target_pairs={{0,24},{32,56},{64,88},{96,120},{8,16},{40,48},{72,80},{104,112},{... | collective-permute-start | bytes 1179656 | tf_op jit(solution)/shard_map/ppermute | solution.py:369
  59.8 3.0 %collective-permute-start.16 = (f32[16,128]{1,0:T(8,128)S(1)}, f32[16,128]{1,0:T(8,128)S(1)}, u32[]{:S(2)}, u32[]{:S(2)}) collective-permute-start(f32[16,128]{1,0:T(8,128)S(1)} %add.52), channel_id=1, source_target_pairs={{0,32},{8,40},{16,48},{24,56},{32,0},{40,8},{48,16},{56,24},{64,96... | collective-permute-start | bytes 24584 | tf_op jit(solution)/shard_map/ppermute | solution.py:408
  79.6 6.4 %copy-start.2 = (f32[1024,256]{1,0:T(8,128)}, f32[1024,256]{1,0:T(8,128)S(1)}, u32[]{:S(2)}) copy-start(f32[1024,256]{1,0:T(8,128)S(1)} %collective-permute-done.10) | copy-start | bytes 3145732
  79.6 14.1 %collective-permute-start.17 = (f32[384,256]{1,0:T(8,128)S(1)}, f32[384,256]{1,0:T(8,128)S(1)}, u32[]{:S(2)}, u32[]{:S(2)}) collective-permute-start(f32[384,256]{1,0:T(8,128)S(1)} %broadcast_select_fusion.4), channel_id=1, source_target_pairs={{0,2},{8,10},{16,18},{24,26},{32,34},{40,42},{48,50},{56,58},{64,6... | collective-permute-start | bytes 1179656 | tf_op jit(solution)/shard_map/ppermute | solution.py:369
  80.9 5.1 %collective-permute-start.18 = (f32[16,128]{1,0:T(8,128)S(1)}, f32[16,128]{1,0:T(8,128)S(1)}, u32[]{:S(2)}, u32[]{:S(2)}) collective-permute-start(f32[16,128]{1,0:T(8,128)S(1)} %add.53), channel_id=1, source_target_pairs={{0,96},{8,104},{16,112},{24,120},{32,64},{40,72},{48,80},{56,88},{... | collective-permute-start | bytes 24584 | tf_op jit(solution)/shard_map/ppermute | solution.py:408
  93.8 1.5 copy-start.3
  93.8 9.7 %collective-permute-start.19 = (f32[384,256]{1,0:T(8,128)S(1)}, f32[384,256]{1,0:T(8,128)S(1)}, u32[]{:S(2)}, u32[]{:S(2)}) collective-permute-start(f32[384,256]{1,0:T(8,128)S(1)} %broadcast_select_fusion.5), channel_id=1, source_target_pairs={{0,6},{8,14},{16,22},{24,30},{32,38},{40,46},{48,54},{56,62},{64,7... | collective-permute-start | bytes 1179656 | tf_op jit(solution)/shard_map/ppermute | solution.py:369
  95.5 8.0 %collective-permute-start.22 = (f32[16,256]{1,0:T(8,128)S(1)}, f32[16,256]{1,0:T(8,128)S(1)}, u32[]{:S(2)}, u32[]{:S(2)}) collective-permute-start(f32[16,256]{1,0:T(8,128)S(1)} %broadcast_in_dim.26), channel_id=1, source_target_pairs={{0,6},{1,7},{8,14},{9,15},{16,22},{17,23},{24,30},{25,31},{32,38},... | collective-permute-start | bytes 49160 | tf_op jit(solution)/shard_map/ppermute | solution.py:414
  100.9 2.7 %collective-permute-start.21 = (f32[16,256]{1,0:T(8,128)S(1)}, f32[16,256]{1,0:T(8,128)S(1)}, u32[]{:S(2)}, u32[]{:S(2)}) collective-permute-start(f32[16,256]{1,0:T(8,128)S(1)} %broadcast_in_dim.26), channel_id=1, source_target_pairs={{0,4},{1,5},{8,12},{9,13},{16,20},{17,21},{24,28},{25,29},{32,36},... | collective-permute-start | bytes 49160 | tf_op jit(solution)/shard_map/ppermute | solution.py:414
  102.2 2.1 %collective-permute-start.20 = (f32[16,256]{1,0:T(8,128)S(1)}, f32[16,256]{1,0:T(8,128)S(1)}, u32[]{:S(2)}, u32[]{:S(2)}) collective-permute-start(f32[16,256]{1,0:T(8,128)S(1)} %broadcast_in_dim.26), channel_id=1, source_target_pairs={{0,2},{1,3},{8,10},{9,11},{16,18},{17,19},{24,26},{25,27},{32,34},... | collective-permute-start | bytes 49160 | tf_op jit(solution)/shard_map/ppermute | solution.py:414
  105.2 12.1 %collective-permute-start.24 = (f32[512,256]{1,0:T(8,128)}, f32[512,256]{1,0:T(8,128)S(1)}, u32[]{:S(2)}, u32[]{:S(2)}) collective-permute-start(f32[512,256]{1,0:T(8,128)} %get-tuple-element.88), channel_id=1, source_target_pairs={{6,4},{7,5},{14,12},{15,13},{22,20},{23,21},{30,28},{31,29},{38,36... | collective-permute-start | bytes 1572872 | tf_op jit(solution)/shard_map/ppermute | solution.py:433
  105.9 11.4 %collective-permute-start.23 = (f32[512,256]{1,0:T(8,128)S(1)}, f32[512,256]{1,0:T(8,128)}, u32[]{:S(2)}, u32[]{:S(2)}) collective-permute-start(f32[512,256]{1,0:T(8,128)S(1)} %get-tuple-element.89), channel_id=1, source_target_pairs={{2,4},{3,5},{10,12},{11,13},{18,20},{19,21},{26,28},{27,29},{34,36... | collective-permute-start | bytes 1572872 | tf_op jit(solution)/shard_map/ppermute | solution.py:432
  107.3 1.7 %collective-permute-start.25 = (f32[384,256]{1,0:T(8,128)S(1)}, f32[384,256]{1,0:T(8,128)S(1)}, u32[]{:S(2)}, u32[]{:S(2)}) collective-permute-start(f32[384,256]{1,0:T(8,128)S(1)} %broadcast_select_fusion.6.own), channel_id=1, source_target_pairs={{0,1},{1,0},{2,3},{3,2},{4,5},{5,4},{6,7},{7,6},{8,9},{9,8},{10,11... | collective-permute-start | bytes 1179656 | tf_op jit(solution)/shard_map/ppermute | solution.py:416
  117.6 10.4 %collective-permute-start.26 = (f32[1040,256]{1,0:T(8,128)S(1)}, f32[1040,256]{1,0:T(8,128)S(1)}, u32[]{:S(2)}, u32[]{:S(2)}) collective-permute-start(f32[1040,256]{1,0:T(8,128)S(1)} %pad_maximum_fusion.mine), channel_id=1, source_target_pairs={{0,1},{1,0},{2,3},{3,2},{4,5},{5,4},{6,7},{7,6},{8,9},{9,8},{10,11... | collective-permute-start | bytes 3194888 | tf_op jit(solution)/shard_map/ppermute | solution.py:438
  127.3 0.7 copy-start
  128.0 1.0 copy-start.1
Sparse Core Ops, SparseCore 0:
  41.4 55.7 all-gather.2

commit v11 on v10

--- a/solution.py
+++ b/solution.py
@@ -406,7 +406,7 @@
         if stage <= 4:
             d = (1, 3, 4, 12)[stage - 1]
             partial.append(before + lax.ppermute(after(before, value), "row", [(r, r ^ d) for r in range(16)]))
-        return after(value, (before, from_left, from_right) if stage == 4 else before)
+        return after(value, (before, from_left, from_right) if stage == 5 else before)
 
     tree = spread(corner, [((0, 0), 0, (0, 1, 2)), ((0, 0), 1, (0, 2, 1))], here, beside)
     sums = partial[-1]

time: 162 us -> 156 us (0.963); the launches traced: 159 us -> 155 us
  waiting for transfers between devices: 42.8 us -> 31.2 us
  starting transfers between devices: 45.4 us -> 52.7 us
    ppermute x6, waiting for transfers between devices: 29 us -> 9.09 us  [spread(): arrived = lax.ppermute(value, ('row', 'col'), pairs)]
    ppermute x1, waiting for transfers between devices: 0.01 us -> 9.84 us  [shards(): from_right = lax.ppermute(column, 'col', [(0, 6), (1, 7)])]
    ppermute x1, starting transfers between devices: 0.01 us -> 2.91 us  [shards(): other = lax.ppermute(own, 'col', swap_cores)]
    ppermute x1, starting transfers between devices: 2.31 us -> 4.19 us  [shards(): from_left = lax.ppermute(column, 'col', [(0, 2), (1, 3)])]
  transfers between devices with their start and end apart: 28 -> 28, of which waited for: 11 -> 12; matrix products, arithmetic and copies ran while one was open for 2% -> 2% of each run, Pallas kernels for 15% -> 16%
where the time goes in v11:
time: 156 us; the launch traced here: 155 us
  starting transfers between devices  52.7 us (34%)
  Pallas kernels  50.7 us (32%)
  waiting for transfers between devices  31.2 us (20%)
  between operations  14.5 us (9%)
  other arithmetic  2.73 us (2%)
  local copies, waits for them, and re-layouts  2.62 us (2%)
    pallas_call x1, Pallas kernels, final_call(): pl.pallas_call(final_kernel, out_shape=(jax.ShapeDtypeStruct((1024, 2, 8,...  23 us
    ppermute x7, starting transfers between devices, shards(): lax.ppermute(pieces[j] if j < 4 else after(pieces[j], fetched), 'row', [(...  15.8 us
    ppermute x1, waiting for transfers between devices, shards(): from_right = lax.ppermute(column, 'col', [(0, 6), (1, 7)])  9.84 us
    pallas_call x1, Pallas kernels, second_factor(): pl.pallas_call(second_kernel, out_shape=(TILE, TILE), in_specs=[SMEM, VME...  9.31 us
    ppermute x6, waiting for transfers between devices, spread(): arrived = lax.ppermute(value, ('row', 'col'), pairs)  9.09 us
    ppermute x3, starting transfers between devices, shards(): lax.ppermute(near_sums, 'col', [(0, 2 * k), (1, 2 * k + 1)])  8.93 us
    ppermute x6, starting transfers between devices, spread(): arrived = lax.ppermute(value, ('row', 'col'), pairs)  8.68 us
    ppermute x4, waiting for transfers between devices, beside(): lax.ppermute(after(before, value), 'row', [(r, r ^ d) for r in range(16)])  8.37 us
  transfers between devices with their start and end apart: 28, of which 12 were waited for; matrix products, arithmetic and copies ran while one was open for 2% of the time, Pallas kernels for 16%

profile of v11, /device:TPU:1, one launch (start us, length us, event | category | flops | bytes accessed | tf_op | source)
XLA Modules:
  0.0 154.6 jit_solution(8832231052985986517)
XLA Ops:
  7.2 3.3 %corner_tiles.1 = (f32[256,256]{1,0:T(8,128)}, f32[256,256]{1,0:T(8,128)}, f32[256,256]{1,0:T(8,128)}, f32[256,256]{1,0:T(8,128)}, f32[256,256]{1,0:T(8,128)}, /...) custom-call(f32[1024,16,128]{2,1,0:T(8,128)} %bitcast.13), custom_call_target="tpu_custom_call" | custom-call | tf_op jit(solution)/shard_map/corner_tiles/pallas_call | solution.py:167
  10.5 1.3 collective-permute-start
  11.8 6.4 %collective-permute-start.5 = (f32[256,256]{1,0:T(8,128)}, f32[256,256]{1,0:T(8,128)S(1)}, u32[]{:S(2)}, u32[]{:S(2)}) collective-permute-start(f32[256,256]{1,0:T(8,128)} %get-tuple-element.52), channel_id=1, source_target_pairs={{0,48},{8,56},{1,49},{9,57},{2,50},{10,58},{3,51},{11,59},{4,52},{... | collective-permute-start | bytes 786440 | tf_op jit(solution)/shard_map/ppermute | solution.py:420
  18.2 1.3 collective-permute-start.6
  19.5 1.3 collective-permute-start.7
  21.0 1.5 collective-permute-start.1
  22.5 1.3 collective-permute-start.2
  23.8 2.0 %collective-permute-start.3 = (f32[256,256]{1,0:T(8,128)}, f32[256,256]{1,0:T(8,128)}, u32[]{:S(2)}, u32[]{:S(2)}) collective-permute-start(f32[256,256]{1,0:T(8,128)} %get-tuple-element.49), channel_id=1, source_target_pairs={{0,80},{8,88},{1,81},{9,89},{2,82},{10,90},{3,83},{11,91},{4,84},{... | collective-permute-start | bytes 786440 | tf_op jit(solution)/shard_map/ppermute | solution.py:420
  25.8 2.0 %collective-permute-start.4 = (f32[256,256]{1,0:T(8,128)}, f32[256,256]{1,0:T(8,128)}, u32[]{:S(2)}, u32[]{:S(2)}) collective-permute-start(f32[256,256]{1,0:T(8,128)} %get-tuple-element.51), channel_id=1, source_target_pairs={{0,64},{8,72},{1,65},{9,73},{2,66},{10,74},{3,67},{11,75},{4,68},{... | collective-permute-start | bytes 786440 | tf_op jit(solution)/shard_map/ppermute | solution.py:420
  27.8 1.0 maximum_select_fusion
  28.9 0.2 collective-permute-done.7
  29.1 2.1 %collective-permute-start.8 = (f32[384,256]{1,0:T(8,128)S(1)}, f32[384,256]{1,0:T(8,128)S(1)}, u32[]{:S(2)}, u32[]{:S(2)}) collective-permute-start(f32[384,256]{1,0:T(8,128)S(1)} %maximum_select_fusion), channel_id=1, source_target_pairs={{0,32},{1,33}} | collective-permute-start | bytes 1179656 | tf_op jit(solution)/shard_map/ppermute | solution.py:369
  31.3 6.9 %first_column.1 = (f32[1024,256]{1,0:T(8,128)S(1)}, f32[16,128]{1,0:T(8,128)S(1)}) custom-call(f32[1024]{0:T(1024)S(1)} %broadcast_select_fusion.8.weights, f32[1024,16,128]{2,1,0:T(8,128)} %bitcast.14), custom_call_target="tpu_custom_call" | custom-call | flops 100000000 | bytes 100000 | tf_op jit(solution)/shard_map/first_column/pallas_call | solution.py:194
  38.2 2.1 %collective-permute-done.3 = f32[256,256]{1,0:T(8,128)} collective-permute-done((f32[256,256]{1,0:T(8,128)}, f32[256,256]{1,0:T(8,128)}, u32[]{:S(2)}, u32[]{:S(2)}) %collective-permute-start.3) | collective-permute-done | bytes 262176 | tf_op jit(solution)/shard_map/ppermute | solution.py:420
  40.3 0.8 select_select_fusion.1
  41.3 1.3 collective-permute-start.11
  42.6 1.1 collective-permute-start.12
  43.6 1.5 collective-permute-done.12
  45.2 4.5 %collective-permute-done.11 = f32[384,256]{1,0:T(8,128)S(1)} collective-permute-done((f32[384,256]{1,0:T(8,128)S(1)}, f32[384,256]{1,0:T(8,128)S(1)}, u32[]{:S(2)}, u32[]{:S(2)}) %collective-permute-start.11) | collective-permute-done | bytes 393248 | tf_op jit(solution)/shard_map/ppermute | solution.py:369
  49.7 1.3 collective-permute-start.13
  51.2 3.6 %collective-permute-done.14 = f32[16,128]{1,0:T(8,128)S(1)} collective-permute-done((f32[16,128]{1,0:T(8,128)S(1)}, f32[16,128]{1,0:T(8,128)S(1)}, u32[]{:S(2)}, u32[]{:S(2)}) %collective-permute-start.14) | collective-permute-done | bytes 8224 | tf_op jit(solution)/shard_map/ppermute | solution.py:408
  54.9 0.9 collective-permute-done.13
  55.8 1.3 collective-permute-start.15
  57.1 2.3 %collective-permute-start.10 = (f32[1024,256]{1,0:T(8,128)S(1)}, f32[1024,256]{1,0:T(8,128)}, u32[]{:S(2)}, u32[]{:S(2)}) collective-permute-start(f32[1024,256]{1,0:T(8,128)S(1)} %get-tuple-element.58), channel_id=1, source_target_pairs={{0,6},{1,7},{8,14},{9,15},{16,22},{17,23},{24,30},{25,31},{32,38},... | collective-permute-start | bytes 3145736 | tf_op jit(solution)/shard_map/ppermute | solution.py:402
  59.4 4.2 %collective-permute-start.9 = (f32[1024,256]{1,0:T(8,128)S(1)}, f32[1024,256]{1,0:T(8,128)}, u32[]{:S(2)}, u32[]{:S(2)}) collective-permute-start(f32[1024,256]{1,0:T(8,128)S(1)} %get-tuple-element.58), channel_id=1, source_target_pairs={{0,2},{1,3},{8,10},{9,11},{16,18},{17,19},{24,26},{25,27},{32,34},... | collective-permute-start | bytes 3145736 | tf_op jit(solution)/shard_map/ppermute | solution.py:401
  63.6 0.6 collective-permute-start.16
  64.2 2.2 %collective-permute-done.16 = f32[16,128]{1,0:T(8,128)S(1)} collective-permute-done((f32[16,128]{1,0:T(8,128)S(1)}, f32[16,128]{1,0:T(8,128)S(1)}, u32[]{:S(2)}, u32[]{:S(2)}) %collective-permute-start.16) | collective-permute-done | bytes 8224 | tf_op jit(solution)/shard_map/ppermute | solution.py:408
  66.5 1.3 collective-permute-start.17
  67.8 4.0 %collective-permute-start.18 = (f32[16,128]{1,0:T(8,128)S(1)}, f32[16,128]{1,0:T(8,128)S(1)}, u32[]{:S(2)}, u32[]{:S(2)}) collective-permute-start(f32[16,128]{1,0:T(8,128)S(1)} %add.53), channel_id=1, source_target_pairs={{0,96},{8,104},{16,112},{24,120},{32,64},{40,72},{48,80},{56,88},{... | collective-permute-start | bytes 24584 | tf_op jit(solution)/shard_map/ppermute | solution.py:408
  71.8 1.0 collective-permute-done.18
  72.9 9.8 %collective-permute-done.10 = f32[1024,256]{1,0:T(8,128)} collective-permute-done((f32[1024,256]{1,0:T(8,128)S(1)}, f32[1024,256]{1,0:T(8,128)}, u32[]{:S(2)}, u32[]{:S(2)}) %collective-permute-start.10) | collective-permute-done | bytes 1048608 | tf_op jit(solution)/shard_map/ppermute | solution.py:402
  82.7 0.3 collective-permute-done.9
  83.0 1.3 collective-permute-start.19
  84.6 6.3 %collective-permute-start.22 = (f32[16,256]{1,0:T(8,128)S(1)}, f32[16,256]{1,0:T(8,128)S(1)}, u32[]{:S(2)}, u32[]{:S(2)}) collective-permute-start(f32[16,256]{1,0:T(8,128)S(1)} %broadcast_in_dim.26), channel_id=1, source_target_pairs={{0,6},{1,7},{8,14},{9,15},{16,22},{17,23},{24,30},{25,31},{32,38},... | collective-permute-start | bytes 49160 | tf_op jit(solution)/shard_map/ppermute | solution.py:414
  91.0 1.3 collective-permute-start.21
  92.3 1.3 collective-permute-start.20
  93.6 3.7 %collective-permute-done.19 = f32[384,256]{1,0:T(8,128)S(1)} collective-permute-done((f32[384,256]{1,0:T(8,128)S(1)}, f32[384,256]{1,0:T(8,128)S(1)}, u32[]{:S(2)}, u32[]{:S(2)}) %collective-permute-start.19) | collective-permute-done | bytes 393248 | tf_op jit(solution)/shard_map/ppermute | solution.py:369
  97.3 0.9 fusion
  98.2 0.7 collective-permute-start.24
  98.9 1.5 collective-permute-start.23
  100.3 2.9 %collective-permute-start.25 = (f32[384,256]{1,0:T(8,128)S(1)}, f32[384,256]{1,0:T(8,128)S(1)}, u32[]{:S(2)}, u32[]{:S(2)}) collective-permute-start(f32[384,256]{1,0:T(8,128)S(1)} %broadcast_select_fusion.6.own), channel_id=1, source_target_pairs={{0,1},{1,0},{2,3},{3,2},{4,5},{5,4},{6,7},{7,6},{8,9},{9,8},{10,11... | collective-permute-start | bytes 1179656 | tf_op jit(solution)/shard_map/ppermute | solution.py:416
  103.3 1.3 collective-permute-done.25.other
  104.6 8.2 %first_factor.1.w00 = f32[256,256]{1,0:T(8,128)S(1)} custom-call(s32[2]{0:T(128)S(1)} %pad_add_fusion.place, f32[384,256]{1,0:T(8,128)S(1)} %broadcast_select_fusion.6.own, f32[384,256]{1,0:T(8,128)S(1)} %collective-permute-done.25.other), custom_call_target="tpu_custom_call" | custom-call | flops 100000000 | bytes 100000 | tf_op jit(solution)/shard_map/first_factor/pallas_call | solution.py:144
  113.1 0.6 collective-permute-start.26
  113.7 9.3 %second_factor.1 = (f32[256,256]{1,0:T(8,128)S(1)}, f32[256,256]{1,0:T(8,128)S(1)}) custom-call(s32[2]{0:T(128)S(1)} %pad_add_fusion.place, f32[256,256]{1,0:T(8,128)S(1)} %first_factor.1.w00, f32[384,256]{1,0:T(8,128)S(1)} %broadcast_select_fusion.6.own, f32[384,256]{1,0:T(8,128)S(1)} %collective-permute-done.25.other), custom_call_target="tpu_custom_call" | custom-call | flops 100000000 | bytes 100000 | tf_op jit(solution)/shard_map/second_factor/pallas_call | solution.py:151
  123.1 0.7 copy-done
  123.8 0.9 copy-done.1
  124.7 23.0 %panels_and_trailing.1 = (f32[1024,2,8,128]{3,2,1,0:T(8,128)}, f32[1024,512]{1,0:T(8,128)}, f32[16,128]{1,0:T(8,128)}) custom-call(s32[2]{0:T(128)S(1)} %pad_add_fusion.place, f32[1024,2,8,128]{3,2,1,0:T(8,128)} %bitcast.15, f32[16,256,256]{2,1,0:T(8,128)} %bitcast.16, f32[1040,256]{1,0:T(8,128)S(1)} %pad_maximum_fusion.mine, ...), custom_call_target="tpu_custom_call" | custom-call | flops 100000000 | bytes 100000 | tf_op jit(solution)/shard_map/panels_and_trailing/pallas_call | solution.py:308
  (47 shorter events, 1.1 us)
Async XLA Ops:
  7.2 116.6 %all-gather.3.cloned.1.call-start = ((), (), s32[]{:S(2)}) async-start(), calls=%async_computation | async-start | bytes 4456448 | tf_op jit(solution)/shard_map/all_gather | solution.py:421
  10.5 20.7 %copy-start.3 = (f32[4,1,256]{2,1,0:T(1,128)S(1)}, f32[4,1,256]{2,1,0:T(1,128)}, u32[]{:S(2)}) copy-start(f32[4,1,256]{2,1,0:T(1,128)} %param.3) | copy-start | bytes 12292
  10.5 10.5 %collective-permute-start = (f32[256,256]{1,0:T(8,128)}, f32[256,256]{1,0:T(8,128)S(1)}, u32[]{:S(2)}, u32[]{:S(2)}) collective-permute-start(f32[256,256]{1,0:T(8,128)} %get-tuple-element.44), channel_id=1, source_target_pairs={{8,0},{9,1}} | collective-permute-start | bytes 786440 | tf_op jit(solution)/shard_map/ppermute | solution.py:393
  11.8 12.0 %collective-permute-start.5 = (f32[256,256]{1,0:T(8,128)}, f32[256,256]{1,0:T(8,128)S(1)}, u32[]{:S(2)}, u32[]{:S(2)}) collective-permute-start(f32[256,256]{1,0:T(8,128)} %get-tuple-element.52), channel_id=1, source_target_pairs={{0,48},{8,56},{1,49},{9,57},{2,50},{10,58},{3,51},{11,59},{4,52},{... | collective-permute-start | bytes 786440 | tf_op jit(solution)/shard_map/ppermute | solution.py:420
  18.2 7.6 %collective-permute-start.6 = (f32[256,256]{1,0:T(8,128)}, f32[256,256]{1,0:T(8,128)S(1)}, u32[]{:S(2)}, u32[]{:S(2)}) collective-permute-start(f32[256,256]{1,0:T(8,128)} %get-tuple-element.53), channel_id=1, source_target_pairs={{0,32},{8,40},{1,33},{9,41},{2,34},{10,42},{3,35},{11,43},{4,36},{... | collective-permute-start | bytes 786440 | tf_op jit(solution)/shard_map/ppermute | solution.py:420
  19.5 9.6 %collective-permute-start.7 = (f32[256,256]{1,0:T(8,128)}, f32[256,256]{1,0:T(8,128)S(1)}, u32[]{:S(2)}, u32[]{:S(2)}) collective-permute-start(f32[256,256]{1,0:T(8,128)} %get-tuple-element.54), channel_id=1, source_target_pairs={{0,16},{8,24},{1,17},{9,25},{2,18},{10,26},{3,19},{11,27},{4,20},{... | collective-permute-start | bytes 786440 | tf_op jit(solution)/shard_map/ppermute | solution.py:420
  21.0 17.2 %collective-permute-start.1 = (f32[256,256]{1,0:T(8,128)}, f32[256,256]{1,0:T(8,128)S(1)}, u32[]{:S(2)}, u32[]{:S(2)}) collective-permute-start(f32[256,256]{1,0:T(8,128)} %get-tuple-element.45), channel_id=1, source_target_pairs={{0,112},{8,120},{1,113},{9,121},{2,114},{10,122},{3,115},{11,123},... | collective-permute-start | bytes 786440 | tf_op jit(solution)/shard_map/ppermute | solution.py:420
  22.5 15.7 %collective-permute-start.2 = (f32[256,256]{1,0:T(8,128)}, f32[256,256]{1,0:T(8,128)S(1)}, u32[]{:S(2)}, u32[]{:S(2)}) collective-permute-start(f32[256,256]{1,0:T(8,128)} %get-tuple-element.47), channel_id=1, source_target_pairs={{0,96},{8,104},{1,97},{9,105},{2,98},{10,106},{3,99},{11,107},{4,1... | collective-permute-start | bytes 786440 | tf_op jit(solution)/shard_map/ppermute | solution.py:420
  23.8 16.5 %collective-permute-start.3 = (f32[256,256]{1,0:T(8,128)}, f32[256,256]{1,0:T(8,128)}, u32[]{:S(2)}, u32[]{:S(2)}) collective-permute-start(f32[256,256]{1,0:T(8,128)} %get-tuple-element.49), channel_id=1, source_target_pairs={{0,80},{8,88},{1,81},{9,89},{2,82},{10,90},{3,83},{11,91},{4,84},{... | collective-permute-start | bytes 786440 | tf_op jit(solution)/shard_map/ppermute | solution.py:420
  25.8 14.5 %collective-permute-start.4 = (f32[256,256]{1,0:T(8,128)}, f32[256,256]{1,0:T(8,128)}, u32[]{:S(2)}, u32[]{:S(2)}) collective-permute-start(f32[256,256]{1,0:T(8,128)} %get-tuple-element.51), channel_id=1, source_target_pairs={{0,64},{8,72},{1,65},{9,73},{2,66},{10,74},{3,67},{11,75},{4,68},{... | collective-permute-start | bytes 786440 | tf_op jit(solution)/shard_map/ppermute | solution.py:420
  29.1 12.1 %collective-permute-start.8 = (f32[384,256]{1,0:T(8,128)S(1)}, f32[384,256]{1,0:T(8,128)S(1)}, u32[]{:S(2)}, u32[]{:S(2)}) collective-permute-start(f32[384,256]{1,0:T(8,128)S(1)} %maximum_select_fusion), channel_id=1, source_target_pairs={{0,32},{1,33}} | collective-permute-start | bytes 1179656 | tf_op jit(solution)/shard_map/ppermute | solution.py:369
  31.3 9.0 %copy-start.2 = (f32[256,256]{1,0:T(8,128)S(1)}, f32[256,256]{1,0:T(8,128)}, u32[]{:S(2)}) copy-start(f32[256,256]{1,0:T(8,128)} %get-tuple-element.55) | copy-start | bytes 786436
  41.3 8.4 %collective-permute-start.11 = (f32[384,256]{1,0:T(8,128)S(1)}, f32[384,256]{1,0:T(8,128)S(1)}, u32[]{:S(2)}, u32[]{:S(2)}) collective-permute-start(f32[384,256]{1,0:T(8,128)S(1)} %broadcast_select_fusion.7), channel_id=1, source_target_pairs={{0,96},{32,64},{1,97},{33,65}} | collective-permute-start | bytes 1179656 | tf_op jit(solution)/shard_map/ppermute | solution.py:369
  42.6 2.6 %collective-permute-start.12 = (f32[16,128]{1,0:T(8,128)S(1)}, f32[16,128]{1,0:T(8,128)S(1)}, u32[]{:S(2)}, u32[]{:S(2)}) collective-permute-start(f32[16,128]{1,0:T(8,128)S(1)} %get-tuple-element.62), channel_id=1, source_target_pairs={{0,8},{8,0},{16,24},{24,16},{32,40},{40,32},{48,56},{56,48},{64,72... | collective-permute-start | bytes 24584 | tf_op jit(solution)/shard_map/ppermute | solution.py:408
  49.7 6.0 %collective-permute-start.13 = (f32[384,256]{1,0:T(8,128)S(1)}, f32[384,256]{1,0:T(8,128)S(1)}, u32[]{:S(2)}, u32[]{:S(2)}) collective-permute-start(f32[384,256]{1,0:T(8,128)S(1)} %broadcast_select_fusion.2), channel_id=1, source_target_pairs={{0,8},{32,40},{64,72},{96,104},{1,3},{33,35},{65,67},{97,99}} | collective-permute-start | bytes 1179656 | tf_op jit(solution)/shard_map/ppermute | solution.py:369
  51.1 3.8 %collective-permute-start.14 = (f32[16,128]{1,0:T(8,128)S(1)}, f32[16,128]{1,0:T(8,128)S(1)}, u32[]{:S(2)}, u32[]{:S(2)}) collective-permute-start(f32[16,128]{1,0:T(8,128)S(1)} %add.51), channel_id=1, source_target_pairs={{0,24},{8,16},{16,8},{24,0},{32,56},{40,48},{48,40},{56,32},{64,88... | collective-permute-start | bytes 24584 | tf_op jit(solution)/shard_map/ppermute | solution.py:408
  55.8 10.6 %collective-permute-start.15 = (f32[384,256]{1,0:T(8,128)S(1)}, f32[384,256]{1,0:T(8,128)S(1)}, u32[]{:S(2)}, u32[]{:S(2)}) collective-permute-start(f32[384,256]{1,0:T(8,128)S(1)} %broadcast_select_fusion.3), channel_id=1, source_target_pairs={{0,24},{32,56},{64,88},{96,120},{8,16},{40,48},{72,80},{104,112},{... | collective-permute-start | bytes 1179656 | tf_op jit(solution)/shard_map/ppermute | solution.py:369
  57.1 25.6 %collective-permute-start.10 = (f32[1024,256]{1,0:T(8,128)S(1)}, f32[1024,256]{1,0:T(8,128)}, u32[]{:S(2)}, u32[]{:S(2)}) collective-permute-start(f32[1024,256]{1,0:T(8,128)S(1)} %get-tuple-element.58), channel_id=1, source_target_pairs={{0,6},{1,7},{8,14},{9,15},{16,22},{17,23},{24,30},{25,31},{32,38},... | collective-permute-start | bytes 3145736 | tf_op jit(solution)/shard_map/ppermute | solution.py:402
  59.4 23.6 %collective-permute-start.9 = (f32[1024,256]{1,0:T(8,128)S(1)}, f32[1024,256]{1,0:T(8,128)}, u32[]{:S(2)}, u32[]{:S(2)}) collective-permute-start(f32[1024,256]{1,0:T(8,128)S(1)} %get-tuple-element.58), channel_id=1, source_target_pairs={{0,2},{1,3},{8,10},{9,11},{16,18},{17,19},{24,26},{25,27},{32,34},... | collective-permute-start | bytes 3145736 | tf_op jit(solution)/shard_map/ppermute | solution.py:401
  63.6 2.8 %collective-permute-start.16 = (f32[16,128]{1,0:T(8,128)S(1)}, f32[16,128]{1,0:T(8,128)S(1)}, u32[]{:S(2)}, u32[]{:S(2)}) collective-permute-start(f32[16,128]{1,0:T(8,128)S(1)} %add.52), channel_id=1, source_target_pairs={{0,32},{8,40},{16,48},{24,56},{32,0},{40,8},{48,16},{56,24},{64,96... | collective-permute-start | bytes 24584 | tf_op jit(solution)/shard_map/ppermute | solution.py:408
  66.5 6.4 %collective-permute-start.17 = (f32[384,256]{1,0:T(8,128)S(1)}, f32[384,256]{1,0:T(8,128)S(1)}, u32[]{:S(2)}, u32[]{:S(2)}) collective-permute-start(f32[384,256]{1,0:T(8,128)S(1)} %broadcast_select_fusion.4), channel_id=1, source_target_pairs={{0,2},{8,10},{16,18},{24,26},{32,34},{40,42},{48,50},{56,58},{64,6... | collective-permute-start | bytes 1179656 | tf_op jit(solution)/shard_map/ppermute | solution.py:369
  67.8 5.0 %collective-permute-start.18 = (f32[16,128]{1,0:T(8,128)S(1)}, f32[16,128]{1,0:T(8,128)S(1)}, u32[]{:S(2)}, u32[]{:S(2)}) collective-permute-start(f32[16,128]{1,0:T(8,128)S(1)} %add.53), channel_id=1, source_target_pairs={{0,96},{8,104},{16,112},{24,120},{32,64},{40,72},{48,80},{56,88},{... | collective-permute-start | bytes 24584 | tf_op jit(solution)/shard_map/ppermute | solution.py:408
  83.0 14.2 %collective-permute-start.19 = (f32[384,256]{1,0:T(8,128)S(1)}, f32[384,256]{1,0:T(8,128)S(1)}, u32[]{:S(2)}, u32[]{:S(2)}) collective-permute-start(f32[384,256]{1,0:T(8,128)S(1)} %broadcast_select_fusion.5), channel_id=1, source_target_pairs={{0,6},{8,14},{16,22},{24,30},{32,38},{40,46},{48,54},{56,62},{64,7... | collective-permute-start | bytes 1179656 | tf_op jit(solution)/shard_map/ppermute | solution.py:369
  84.6 12.7 %collective-permute-start.22 = (f32[16,256]{1,0:T(8,128)S(1)}, f32[16,256]{1,0:T(8,128)S(1)}, u32[]{:S(2)}, u32[]{:S(2)}) collective-permute-start(f32[16,256]{1,0:T(8,128)S(1)} %broadcast_in_dim.26), channel_id=1, source_target_pairs={{0,6},{1,7},{8,14},{9,15},{16,22},{17,23},{24,30},{25,31},{32,38},... | collective-permute-start | bytes 49160 | tf_op jit(solution)/shard_map/ppermute | solution.py:414
  91.0 6.4 %collective-permute-start.21 = (f32[16,256]{1,0:T(8,128)S(1)}, f32[16,256]{1,0:T(8,128)S(1)}, u32[]{:S(2)}, u32[]{:S(2)}) collective-permute-start(f32[16,256]{1,0:T(8,128)S(1)} %broadcast_in_dim.26), channel_id=1, source_target_pairs={{0,4},{1,5},{8,12},{9,13},{16,20},{17,21},{24,28},{25,29},{32,36},... | collective-permute-start | bytes 49160 | tf_op jit(solution)/shard_map/ppermute | solution.py:414
  92.3 5.1 %collective-permute-start.20 = (f32[16,256]{1,0:T(8,128)S(1)}, f32[16,256]{1,0:T(8,128)S(1)}, u32[]{:S(2)}, u32[]{:S(2)}) collective-permute-start(f32[16,256]{1,0:T(8,128)S(1)} %broadcast_in_dim.26), channel_id=1, source_target_pairs={{0,2},{1,3},{8,10},{9,11},{16,18},{17,19},{24,26},{25,27},{32,34},... | collective-permute-start | bytes 49160 | tf_op jit(solution)/shard_map/ppermute | solution.py:414
  98.2 14.6 %collective-permute-start.24 = (f32[512,256]{1,0:T(8,128)}, f32[512,256]{1,0:T(8,128)S(1)}, u32[]{:S(2)}, u32[]{:S(2)}) collective-permute-start(f32[512,256]{1,0:T(8,128)} %get-tuple-element.88), channel_id=1, source_target_pairs={{6,4},{7,5},{14,12},{15,13},{22,20},{23,21},{30,28},{31,29},{38,36... | collective-permute-start | bytes 1572872 | tf_op jit(solution)/shard_map/ppermute | solution.py:433
  98.9 14.0 %collective-permute-start.23 = (f32[512,256]{1,0:T(8,128)S(1)}, f32[512,256]{1,0:T(8,128)}, u32[]{:S(2)}, u32[]{:S(2)}) collective-permute-start(f32[512,256]{1,0:T(8,128)S(1)} %get-tuple-element.89), channel_id=1, source_target_pairs={{2,4},{3,5},{10,12},{11,13},{18,20},{19,21},{26,28},{27,29},{34,36... | collective-permute-start | bytes 1572872 | tf_op jit(solution)/shard_map/ppermute | solution.py:432
  100.3 4.3 %collective-permute-start.25 = (f32[384,256]{1,0:T(8,128)S(1)}, f32[384,256]{1,0:T(8,128)S(1)}, u32[]{:S(2)}, u32[]{:S(2)}) collective-permute-start(f32[384,256]{1,0:T(8,128)S(1)} %broadcast_select_fusion.6.own), channel_id=1, source_target_pairs={{0,1},{1,0},{2,3},{3,2},{4,5},{5,4},{6,7},{7,6},{8,9},{9,8},{10,11... | collective-permute-start | bytes 1179656 | tf_op jit(solution)/shard_map/ppermute | solution.py:416
  113.1 10.7 %collective-permute-start.26 = (f32[1040,256]{1,0:T(8,128)S(1)}, f32[1040,256]{1,0:T(8,128)S(1)}, u32[]{:S(2)}, u32[]{:S(2)}) collective-permute-start(f32[1040,256]{1,0:T(8,128)S(1)} %pad_maximum_fusion.mine), channel_id=1, source_target_pairs={{0,1},{1,0},{2,3},{3,2},{4,5},{5,4},{6,7},{7,6},{8,9},{9,8},{10,11... | collective-permute-start | bytes 3194888 | tf_op jit(solution)/shard_map/ppermute | solution.py:438
  123.0 0.7 copy-start
  123.8 1.0 copy-start.1
Sparse Core Ops, SparseCore 0:
  41.4 55.9 all-gather.2

commit v12 on v11

--- a/solution.py
+++ b/solution.py
@@ -408,7 +408,7 @@
             partial.append(before + lax.ppermute(after(before, value), "row", [(r, r ^ d) for r in range(16)]))
         return after(value, (before, from_left, from_right) if stage == 5 else before)
 
-    tree = spread(corner, [((0, 0), 0, (0, 1, 2)), ((0, 0), 1, (0, 2, 1))], here, beside)
+    tree = spread(corner, [((0, 0), 0, (2, 0, 1)), ((0, 0), 1, (0, 2, 1))], here, beside)
     sums = partial[-1]
     near_sums = jnp.broadcast_to(sums[0:2].reshape(1, NB), (16, NB))
     far_sums = [lax.ppermute(near_sums, "col", [(0, 2 * k), (1, 2 * k + 1)]) for k in (1, 2, 3)]

time: 156 us -> 158 us (1.013)
  the two profiles are of different devices: /device:TPU:1 before, /device:TPU:93 now
where the time goes in v12:
time: 158 us; the launch traced here: 157 us
  waiting for transfers between devices  53.9 us (34%)
  Pallas kernels  50.3 us (32%)
  starting transfers between devices  31.2 us (20%)
  between operations  14.6 us (9%)
  other arithmetic  4.7 us (3%)
  local copies, waits for them, and re-layouts  2.62 us (2%)
    pallas_call x1, Pallas kernels, final_call(): pl.pallas_call(final_kernel, out_shape=(jax.ShapeDtypeStruct((1024, 2, 8,...  22.6 us
    ppermute x7, waiting for transfers between devices, shards(): lax.ppermute(pieces[j] if j < 4 else after(pieces[j], fetched), 'row', [(...  13.2 us
    ppermute x4, waiting for transfers between devices, beside(): lax.ppermute(after(before, value), 'row', [(r, r ^ d) for r in range(16)])  10.7 us
    ppermute x6, waiting for transfers between devices, spread(): arrived = lax.ppermute(value, ('row', 'col'), pairs)  10.6 us
    ppermute x3, waiting for transfers between devices, shards(): lax.ppermute(near_sums, 'col', [(0, 2 * k), (1, 2 * k + 1)])  9.74 us
    pallas_call x1, Pallas kernels, second_factor(): pl.pallas_call(second_kernel, out_shape=(TILE, TILE), in_specs=[SMEM, VME...  9.31 us
    ppermute x1, starting transfers between devices, shards(): other = lax.ppermute(own, 'col', swap_cores)  8.48 us
    ppermute x1, waiting for transfers between devices, shards(): lower = lax.ppermute(mine[512:1024], 'col', [(6, 4), (7, 5)])  8.47 us
  transfers between devices with their start and end apart: 28, of which 9 were waited for; matrix products, arithmetic and copies ran while one was open for 4% of the time, Pallas kernels for 16%

profile of v12, /device:TPU:93, one launch (start us, length us, event | category | flops | bytes accessed | tf_op | source)
XLA Modules:
  0.0 157.3 jit_solution(2784036555515887485)
XLA Ops:
  7.2 3.3 %corner_tiles.1 = (f32[256,256]{1,0:T(8,128)}, f32[256,256]{1,0:T(8,128)}, f32[256,256]{1,0:T(8,128)}, f32[256,256]{1,0:T(8,128)}, f32[256,256]{1,0:T(8,128)}, /...) custom-call(f32[1024,16,128]{2,1,0:T(8,128)} %bitcast.13), custom_call_target="tpu_custom_call" | custom-call | tf_op jit(solution)/shard_map/corner_tiles/pallas_call | solution.py:167
  10.5 0.7 collective-permute-start
  11.2 0.7 collective-permute-start.5
  11.9 0.7 collective-permute-start.6
  12.6 0.7 collective-permute-start.7
  13.4 0.7 collective-permute-start.1
  14.0 0.7 collective-permute-start.2
  14.8 1.3 collective-permute-start.3
  16.1 1.4 collective-permute-start.4
  17.4 1.0 maximum_select_fusion
  18.5 0.7 collective-permute-start.8
  19.3 6.9 %first_column.1 = (f32[1024,256]{1,0:T(8,128)S(1)}, f32[16,128]{1,0:T(8,128)S(1)}) custom-call(f32[1024]{0:T(1024)S(1)} %broadcast_select_fusion.8.weights, f32[1024,16,128]{2,1,0:T(8,128)} %bitcast.14), custom_call_target="tpu_custom_call" | custom-call | flops 100000000 | bytes 100000 | tf_op jit(solution)/shard_map/first_column/pallas_call | solution.py:194
  26.2 13.2 %collective-permute-done.3 = f32[256,256]{1,0:T(8,128)} collective-permute-done((f32[256,256]{1,0:T(8,128)}, f32[256,256]{1,0:T(8,128)}, u32[]{:S(2)}, u32[]{:S(2)}) %collective-permute-start.3) | collective-permute-done | bytes 262176 | tf_op jit(solution)/shard_map/ppermute | solution.py:420
  39.4 1.8 %select_select_fusion.1 = f32[256,256]{1,0:T(8,128)} fusion(f32[256,256]{1,0:T(8,128)S(1)} %collective-permute-done.1, f32[256,256]{1,0:T(8,128)S(1)} %collective-permute-done.2, f32[256,256]{1,0:T(8,128)} %collective-permute-done.3, f32[256,256]{1,0:T(8,128)} %collective-permute-done.4, f32[256,256]{1,0:T(8,128)S(1)} %collective-permute-done.5, ...), kind=kLoop, calls=%fused_computation.3 | loop fusion | flops 458752 | bytes 2359303 | tf_op jit(solution)/shard_map/jit(_where)/select_n | solution.py:420
  41.3 0.7 collective-permute-start.11
  42.0 0.5 collective-permute-start.12
  42.5 2.0 %collective-permute-done.12 = f32[16,128]{1,0:T(8,128)S(1)} collective-permute-done((f32[16,128]{1,0:T(8,128)S(1)}, f32[16,128]{1,0:T(8,128)S(1)}, u32[]{:S(2)}, u32[]{:S(2)}) %collective-permute-start.12) | collective-permute-done | bytes 8224 | tf_op jit(solution)/shard_map/ppermute | solution.py:408
  44.6 0.7 collective-permute-start.13
  45.3 0.1 collective-permute-start.14
  45.4 3.7 %collective-permute-done.14 = f32[16,128]{1,0:T(8,128)S(1)} collective-permute-done((f32[16,128]{1,0:T(8,128)S(1)}, f32[16,128]{1,0:T(8,128)S(1)}, u32[]{:S(2)}, u32[]{:S(2)}) %collective-permute-start.14) | collective-permute-done | bytes 8224 | tf_op jit(solution)/shard_map/ppermute | solution.py:408
  49.2 0.7 collective-permute-start.15
  49.8 0.7 collective-permute-start.10
  50.6 1.7 %collective-permute-start.9 = (f32[1024,256]{1,0:T(8,128)S(1)}, f32[1024,256]{1,0:T(8,128)}, u32[]{:S(2)}, u32[]{:S(2)}) collective-permute-start(f32[1024,256]{1,0:T(8,128)S(1)} %get-tuple-element.58), channel_id=1, source_target_pairs={{0,2},{1,3},{8,10},{9,11},{16,18},{17,19},{24,26},{25,27},{32,34},... | collective-permute-start | bytes 3145736 | tf_op jit(solution)/shard_map/ppermute | solution.py:401
  52.3 2.5 %collective-permute-done.16 = f32[16,128]{1,0:T(8,128)S(1)} collective-permute-done((f32[16,128]{1,0:T(8,128)S(1)}, f32[16,128]{1,0:T(8,128)S(1)}, u32[]{:S(2)}, u32[]{:S(2)}) %collective-permute-start.16) | collective-permute-done | bytes 8224 | tf_op jit(solution)/shard_map/ppermute | solution.py:408
  54.8 0.7 collective-permute-start.17
  55.5 0.1 collective-permute-start.18
  55.7 2.4 %collective-permute-done.18 = f32[16,128]{1,0:T(8,128)S(1)} collective-permute-done((f32[16,128]{1,0:T(8,128)S(1)}, f32[16,128]{1,0:T(8,128)S(1)}, u32[]{:S(2)}, u32[]{:S(2)}) %collective-permute-start.18) | collective-permute-done | bytes 8224 | tf_op jit(solution)/shard_map/ppermute | solution.py:408
  58.2 1.3 collective-permute-start.19
  59.5 0.2 select_select_fusion
  59.7 0.7 collective-permute-start.22
  60.4 1.3 collective-permute-start.21
  61.7 0.7 collective-permute-start.20
  62.4 10.5 %collective-permute-done.19 = f32[384,256]{1,0:T(8,128)S(1)} collective-permute-done((f32[384,256]{1,0:T(8,128)S(1)}, f32[384,256]{1,0:T(8,128)S(1)}, u32[]{:S(2)}, u32[]{:S(2)}) %collective-permute-start.19) | collective-permute-done | bytes 393248 | tf_op jit(solution)/shard_map/ppermute | solution.py:369
  73.0 9.7 %collective-permute-done.21 = f32[16,256]{1,0:T(8,128)S(1)} collective-permute-done((f32[16,256]{1,0:T(8,128)S(1)}, f32[16,256]{1,0:T(8,128)S(1)}, u32[]{:S(2)}, u32[]{:S(2)}) %collective-permute-start.21) | collective-permute-done | bytes 16416 | tf_op jit(solution)/shard_map/ppermute | solution.py:414
  82.7 0.9 fusion
  83.6 1.3 collective-permute-start.24
  84.9 1.3 collective-permute-start.23
  86.2 8.5 %collective-permute-start.25 = (f32[384,256]{1,0:T(8,128)S(1)}, f32[384,256]{1,0:T(8,128)S(1)}, u32[]{:S(2)}, u32[]{:S(2)}) collective-permute-start(f32[384,256]{1,0:T(8,128)S(1)} %broadcast_select_fusion.6.own), channel_id=1, source_target_pairs={{0,1},{1,0},{2,3},{3,2},{4,5},{5,4},{6,7},{7,6},{8,9},{9,8},{10,11... | collective-permute-start | bytes 1179656 | tf_op jit(solution)/shard_map/ppermute | solution.py:416
  94.6 0.1 pad_add_fusion.place
  94.7 1.3 collective-permute-done.25.other
  96.0 8.2 %first_factor.1.w00 = f32[256,256]{1,0:T(8,128)S(1)} custom-call(s32[2]{0:T(128)S(1)} %pad_add_fusion.place, f32[384,256]{1,0:T(8,128)S(1)} %broadcast_select_fusion.6.own, f32[384,256]{1,0:T(8,128)S(1)} %collective-permute-done.25.other), custom_call_target="tpu_custom_call" | custom-call | flops 100000000 | bytes 100000 | tf_op jit(solution)/shard_map/first_factor/pallas_call | solution.py:144
  104.2 8.5 %collective-permute-done.24 = f32[512,256]{1,0:T(8,128)S(1)} collective-permute-done((f32[512,256]{1,0:T(8,128)}, f32[512,256]{1,0:T(8,128)S(1)}, u32[]{:S(2)}, u32[]{:S(2)}) %collective-permute-start.24) | collective-permute-done | bytes 524320 | tf_op jit(solution)/shard_map/ppermute | solution.py:433
  112.7 1.2 broadcast_select_fusion.1
  114.0 2.9 %collective-permute-start.26 = (f32[1040,256]{1,0:T(8,128)S(1)}, f32[1040,256]{1,0:T(8,128)S(1)}, u32[]{:S(2)}, u32[]{:S(2)}) collective-permute-start(f32[1040,256]{1,0:T(8,128)S(1)} %pad_maximum_fusion.mine), channel_id=1, source_target_pairs={{0,1},{1,0},{2,3},{3,2},{4,5},{5,4},{6,7},{7,6},{8,9},{9,8},{10,11... | collective-permute-start | bytes 3194888 | tf_op jit(solution)/shard_map/ppermute | solution.py:438
  116.9 9.3 %second_factor.1 = (f32[256,256]{1,0:T(8,128)S(1)}, f32[256,256]{1,0:T(8,128)S(1)}) custom-call(s32[2]{0:T(128)S(1)} %pad_add_fusion.place, f32[256,256]{1,0:T(8,128)S(1)} %first_factor.1.w00, f32[384,256]{1,0:T(8,128)S(1)} %broadcast_select_fusion.6.own, f32[384,256]{1,0:T(8,128)S(1)} %collective-permute-done.25.other), custom_call_target="tpu_custom_call" | custom-call | flops 100000000 | bytes 100000 | tf_op jit(solution)/shard_map/second_factor/pallas_call | solution.py:151
  126.2 0.7 copy-done
  126.9 0.9 copy-done.1
  127.8 22.6 %panels_and_trailing.1 = (f32[1024,2,8,128]{3,2,1,0:T(8,128)}, f32[1024,512]{1,0:T(8,128)}, f32[16,128]{1,0:T(8,128)}) custom-call(s32[2]{0:T(128)S(1)} %pad_add_fusion.place, f32[1024,2,8,128]{3,2,1,0:T(8,128)} %bitcast.15, f32[16,256,256]{2,1,0:T(8,128)} %bitcast.16, f32[1040,256]{1,0:T(8,128)S(1)} %pad_maximum_fusion.mine, ...), custom_call_target="tpu_custom_call" | custom-call | flops 100000000 | bytes 100000 | tf_op jit(solution)/shard_map/panels_and_trailing/pallas_call | solution.py:308
  (47 shorter events, 0.6 us)
Async XLA Ops:
  7.2 119.7 %all-gather.3.cloned.1.call-start = ((), (), s32[]{:S(2)}) async-start(), calls=%async_computation | async-start | bytes 4456448 | tf_op jit(solution)/shard_map/all_gather | solution.py:421
  10.5 8.7 %copy-start.3 = (f32[4,1,256]{2,1,0:T(1,128)S(1)}, f32[4,1,256]{2,1,0:T(1,128)}, u32[]{:S(2)}) copy-start(f32[4,1,256]{2,1,0:T(1,128)} %param.3) | copy-start | bytes 12292
  10.5 2.9 %collective-permute-start = (f32[256,256]{1,0:T(8,128)}, f32[256,256]{1,0:T(8,128)S(1)}, u32[]{:S(2)}, u32[]{:S(2)}) collective-permute-start(f32[256,256]{1,0:T(8,128)} %get-tuple-element.44), channel_id=1, source_target_pairs={{8,0},{9,1}} | collective-permute-start | bytes 786440 | tf_op jit(solution)/shard_map/ppermute | solution.py:393
  11.2 3.6 %collective-permute-start.5 = (f32[256,256]{1,0:T(8,128)}, f32[256,256]{1,0:T(8,128)S(1)}, u32[]{:S(2)}, u32[]{:S(2)}) collective-permute-start(f32[256,256]{1,0:T(8,128)} %get-tuple-element.52), channel_id=1, source_target_pairs={{0,48},{8,56},{1,49},{9,57},{2,50},{10,58},{3,51},{11,59},{4,52},{... | collective-permute-start | bytes 786440 | tf_op jit(solution)/shard_map/ppermute | solution.py:420
  11.9 4.2 %collective-permute-start.6 = (f32[256,256]{1,0:T(8,128)}, f32[256,256]{1,0:T(8,128)S(1)}, u32[]{:S(2)}, u32[]{:S(2)}) collective-permute-start(f32[256,256]{1,0:T(8,128)} %get-tuple-element.53), channel_id=1, source_target_pairs={{0,32},{8,40},{1,33},{9,41},{2,34},{10,42},{3,35},{11,43},{4,36},{... | collective-permute-start | bytes 786440 | tf_op jit(solution)/shard_map/ppermute | solution.py:420
  12.6 5.9 %collective-permute-start.7 = (f32[256,256]{1,0:T(8,128)}, f32[256,256]{1,0:T(8,128)S(1)}, u32[]{:S(2)}, u32[]{:S(2)}) collective-permute-start(f32[256,256]{1,0:T(8,128)} %get-tuple-element.54), channel_id=1, source_target_pairs={{0,16},{8,24},{1,17},{9,25},{2,18},{10,26},{3,19},{11,27},{4,20},{... | collective-permute-start | bytes 786440 | tf_op jit(solution)/shard_map/ppermute | solution.py:420
  13.4 12.8 %collective-permute-start.1 = (f32[256,256]{1,0:T(8,128)}, f32[256,256]{1,0:T(8,128)S(1)}, u32[]{:S(2)}, u32[]{:S(2)}) collective-permute-start(f32[256,256]{1,0:T(8,128)} %get-tuple-element.45), channel_id=1, source_target_pairs={{0,112},{8,120},{1,113},{9,121},{2,114},{10,122},{3,115},{11,123},... | collective-permute-start | bytes 786440 | tf_op jit(solution)/shard_map/ppermute | solution.py:420
  14.0 12.2 %collective-permute-start.2 = (f32[256,256]{1,0:T(8,128)}, f32[256,256]{1,0:T(8,128)S(1)}, u32[]{:S(2)}, u32[]{:S(2)}) collective-permute-start(f32[256,256]{1,0:T(8,128)} %get-tuple-element.47), channel_id=1, source_target_pairs={{0,96},{8,104},{1,97},{9,105},{2,98},{10,106},{3,99},{11,107},{4,1... | collective-permute-start | bytes 786440 | tf_op jit(solution)/shard_map/ppermute | solution.py:420
  14.8 24.6 %collective-permute-start.3 = (f32[256,256]{1,0:T(8,128)}, f32[256,256]{1,0:T(8,128)}, u32[]{:S(2)}, u32[]{:S(2)}) collective-permute-start(f32[256,256]{1,0:T(8,128)} %get-tuple-element.49), channel_id=1, source_target_pairs={{0,80},{8,88},{1,81},{9,89},{2,82},{10,90},{3,83},{11,91},{4,84},{... | collective-permute-start | bytes 786440 | tf_op jit(solution)/shard_map/ppermute | solution.py:420
  16.1 23.3 %collective-permute-start.4 = (f32[256,256]{1,0:T(8,128)}, f32[256,256]{1,0:T(8,128)}, u32[]{:S(2)}, u32[]{:S(2)}) collective-permute-start(f32[256,256]{1,0:T(8,128)} %get-tuple-element.51), channel_id=1, source_target_pairs={{0,64},{8,72},{1,65},{9,73},{2,66},{10,74},{3,67},{11,75},{4,68},{... | collective-permute-start | bytes 786440 | tf_op jit(solution)/shard_map/ppermute | solution.py:420
  18.5 22.7 %collective-permute-start.8 = (f32[384,256]{1,0:T(8,128)S(1)}, f32[384,256]{1,0:T(8,128)S(1)}, u32[]{:S(2)}, u32[]{:S(2)}) collective-permute-start(f32[384,256]{1,0:T(8,128)S(1)} %maximum_select_fusion), channel_id=1, source_target_pairs={{0,2},{1,33}} | collective-permute-start | bytes 1179656 | tf_op jit(solution)/shard_map/ppermute | solution.py:369
  19.3 20.1 %copy-start.2 = (f32[256,256]{1,0:T(8,128)S(1)}, f32[256,256]{1,0:T(8,128)}, u32[]{:S(2)}) copy-start(f32[256,256]{1,0:T(8,128)} %get-tuple-element.55) | copy-start | bytes 786436
  41.3 3.3 %collective-permute-start.11 = (f32[384,256]{1,0:T(8,128)S(1)}, f32[384,256]{1,0:T(8,128)S(1)}, u32[]{:S(2)}, u32[]{:S(2)}) collective-permute-start(f32[384,256]{1,0:T(8,128)S(1)} %broadcast_select_fusion.7), channel_id=1, source_target_pairs={{0,6},{2,4},{1,97},{33,65}} | collective-permute-start | bytes 1179656 | tf_op jit(solution)/shard_map/ppermute | solution.py:369
  42.0 2.6 %collective-permute-start.12 = (f32[16,128]{1,0:T(8,128)S(1)}, f32[16,128]{1,0:T(8,128)S(1)}, u32[]{:S(2)}, u32[]{:S(2)}) collective-permute-start(f32[16,128]{1,0:T(8,128)S(1)} %get-tuple-element.62), channel_id=1, source_target_pairs={{0,8},{8,0},{16,24},{24,16},{32,40},{40,32},{48,56},{56,48},{64,72... | collective-permute-start | bytes 24584 | tf_op jit(solution)/shard_map/ppermute | solution.py:408
  44.6 4.5 %collective-permute-start.13 = (f32[384,256]{1,0:T(8,128)S(1)}, f32[384,256]{1,0:T(8,128)S(1)}, u32[]{:S(2)}, u32[]{:S(2)}) collective-permute-start(f32[384,256]{1,0:T(8,128)S(1)} %broadcast_select_fusion.2), channel_id=1, source_target_pairs={{0,32},{2,34},{4,36},{6,38},{1,3},{33,35},{65,67},{97,99}} | collective-permute-start | bytes 1179656 | tf_op jit(solution)/shard_map/ppermute | solution.py:369
  45.3 3.8 %collective-permute-start.14 = (f32[16,128]{1,0:T(8,128)S(1)}, f32[16,128]{1,0:T(8,128)S(1)}, u32[]{:S(2)}, u32[]{:S(2)}) collective-permute-start(f32[16,128]{1,0:T(8,128)S(1)} %add.51), channel_id=1, source_target_pairs={{0,24},{8,16},{16,8},{24,0},{32,56},{40,48},{48,40},{56,32},{64,88... | collective-permute-start | bytes 24584 | tf_op jit(solution)/shard_map/ppermute | solution.py:408
  49.2 5.6 %collective-permute-start.15 = (f32[384,256]{1,0:T(8,128)S(1)}, f32[384,256]{1,0:T(8,128)S(1)}, u32[]{:S(2)}, u32[]{:S(2)}) collective-permute-start(f32[384,256]{1,0:T(8,128)S(1)} %broadcast_select_fusion.3), channel_id=1, source_target_pairs={{0,96},{2,98},{4,100},{6,102},{32,64},{34,66},{36,68},{38,70},{1,7... | collective-permute-start | bytes 1179656 | tf_op jit(solution)/shard_map/ppermute | solution.py:369
  49.8 8.3 %collective-permute-start.10 = (f32[1024,256]{1,0:T(8,128)S(1)}, f32[1024,256]{1,0:T(8,128)S(1)}, u32[]{:S(2)}, u32[]{:S(2)}) collective-permute-start(f32[1024,256]{1,0:T(8,128)S(1)} %get-tuple-element.58), channel_id=1, source_target_pairs={{0,6},{1,7},{8,14},{9,15},{16,22},{17,23},{24,30},{25,31},{32,38},... | collective-permute-start | bytes 3145736 | tf_op jit(solution)/shard_map/ppermute | solution.py:402
  50.6 7.6 %collective-permute-start.9 = (f32[1024,256]{1,0:T(8,128)S(1)}, f32[1024,256]{1,0:T(8,128)}, u32[]{:S(2)}, u32[]{:S(2)}) collective-permute-start(f32[1024,256]{1,0:T(8,128)S(1)} %get-tuple-element.58), channel_id=1, source_target_pairs={{0,2},{1,3},{8,10},{9,11},{16,18},{17,19},{24,26},{25,27},{32,34},... | collective-permute-start | bytes 3145736 | tf_op jit(solution)/shard_map/ppermute | solution.py:401
  52.3 2.5 %collective-permute-start.16 = (f32[16,128]{1,0:T(8,128)S(1)}, f32[16,128]{1,0:T(8,128)S(1)}, u32[]{:S(2)}, u32[]{:S(2)}) collective-permute-start(f32[16,128]{1,0:T(8,128)S(1)} %add.52), channel_id=1, source_target_pairs={{0,32},{8,40},{16,48},{24,56},{32,0},{40,8},{48,16},{56,24},{64,96... | collective-permute-start | bytes 24584 | tf_op jit(solution)/shard_map/ppermute | solution.py:408
  54.8 3.3 %collective-permute-start.17 = (f32[384,256]{1,0:T(8,128)S(1)}, f32[384,256]{1,0:T(8,128)S(1)}, u32[]{:S(2)}, u32[]{:S(2)}) collective-permute-start(f32[384,256]{1,0:T(8,128)S(1)} %broadcast_select_fusion.4), channel_id=1, source_target_pairs={{0,8},{32,40},{64,72},{96,104},{2,10},{34,42},{66,74},{98,106},{4,... | collective-permute-start | bytes 1179656 | tf_op jit(solution)/shard_map/ppermute | solution.py:369
  55.5 2.6 %collective-permute-start.18 = (f32[16,128]{1,0:T(8,128)S(1)}, f32[16,128]{1,0:T(8,128)S(1)}, u32[]{:S(2)}, u32[]{:S(2)}) collective-permute-start(f32[16,128]{1,0:T(8,128)S(1)} %add.53), channel_id=1, source_target_pairs={{0,96},{8,104},{16,112},{24,120},{32,64},{40,72},{48,80},{56,88},{... | collective-permute-start | bytes 24584 | tf_op jit(solution)/shard_map/ppermute | solution.py:408
  58.2 14.7 %collective-permute-start.19 = (f32[384,256]{1,0:T(8,128)S(1)}, f32[384,256]{1,0:T(8,128)S(1)}, u32[]{:S(2)}, u32[]{:S(2)}) collective-permute-start(f32[384,256]{1,0:T(8,128)S(1)} %broadcast_select_fusion.5), channel_id=1, source_target_pairs={{0,24},{32,56},{64,88},{96,120},{2,26},{34,58},{66,90},{98,122},{4... | collective-permute-start | bytes 1179656 | tf_op jit(solution)/shard_map/ppermute | solution.py:369
  59.7 13.2 %collective-permute-start.22 = (f32[16,256]{1,0:T(8,128)S(1)}, f32[16,256]{1,0:T(8,128)S(1)}, u32[]{:S(2)}, u32[]{:S(2)}) collective-permute-start(f32[16,256]{1,0:T(8,128)S(1)} %broadcast_in_dim.26), channel_id=1, source_target_pairs={{0,6},{1,7},{8,14},{9,15},{16,22},{17,23},{24,30},{25,31},{32,38},... | collective-permute-start | bytes 49160 | tf_op jit(solution)/shard_map/ppermute | solution.py:414
  60.4 22.3 %collective-permute-start.21 = (f32[16,256]{1,0:T(8,128)S(1)}, f32[16,256]{1,0:T(8,128)S(1)}, u32[]{:S(2)}, u32[]{:S(2)}) collective-permute-start(f32[16,256]{1,0:T(8,128)S(1)} %broadcast_in_dim.26), channel_id=1, source_target_pairs={{0,4},{1,5},{8,12},{9,13},{16,20},{17,21},{24,28},{25,29},{32,36},... | collective-permute-start | bytes 49160 | tf_op jit(solution)/shard_map/ppermute | solution.py:414
  61.7 21.0 %collective-permute-start.20 = (f32[16,256]{1,0:T(8,128)S(1)}, f32[16,256]{1,0:T(8,128)S(1)}, u32[]{:S(2)}, u32[]{:S(2)}) collective-permute-start(f32[16,256]{1,0:T(8,128)S(1)} %broadcast_in_dim.26), channel_id=1, source_target_pairs={{0,2},{1,3},{8,10},{9,11},{16,18},{17,19},{24,26},{25,27},{32,34},... | collective-permute-start | bytes 49160 | tf_op jit(solution)/shard_map/ppermute | solution.py:414
  83.6 29.1 %collective-permute-start.24 = (f32[512,256]{1,0:T(8,128)}, f32[512,256]{1,0:T(8,128)S(1)}, u32[]{:S(2)}, u32[]{:S(2)}) collective-permute-start(f32[512,256]{1,0:T(8,128)} %get-tuple-element.88), channel_id=1, source_target_pairs={{6,4},{7,5},{14,12},{15,13},{22,20},{23,21},{30,28},{31,29},{38,36... | collective-permute-start | bytes 1572872 | tf_op jit(solution)/shard_map/ppermute | solution.py:433
  84.9 27.8 %collective-permute-start.23 = (f32[512,256]{1,0:T(8,128)S(1)}, f32[512,256]{1,0:T(8,128)}, u32[]{:S(2)}, u32[]{:S(2)}) collective-permute-start(f32[512,256]{1,0:T(8,128)S(1)} %get-tuple-element.89), channel_id=1, source_target_pairs={{2,4},{3,5},{10,12},{11,13},{18,20},{19,21},{26,28},{27,29},{34,36... | collective-permute-start | bytes 1572872 | tf_op jit(solution)/shard_map/ppermute | solution.py:432
  86.2 9.8 %collective-permute-start.25 = (f32[384,256]{1,0:T(8,128)S(1)}, f32[384,256]{1,0:T(8,128)S(1)}, u32[]{:S(2)}, u32[]{:S(2)}) collective-permute-start(f32[384,256]{1,0:T(8,128)S(1)} %broadcast_select_fusion.6.own), channel_id=1, source_target_pairs={{0,1},{1,0},{2,3},{3,2},{4,5},{5,4},{6,7},{7,6},{8,9},{9,8},{10,11... | collective-permute-start | bytes 1179656 | tf_op jit(solution)/shard_map/ppermute | solution.py:416
  114.0 12.9 %collective-permute-start.26 = (f32[1040,256]{1,0:T(8,128)S(1)}, f32[1040,256]{1,0:T(8,128)S(1)}, u32[]{:S(2)}, u32[]{:S(2)}) collective-permute-start(f32[1040,256]{1,0:T(8,128)S(1)} %pad_maximum_fusion.mine), channel_id=1, source_target_pairs={{0,1},{1,0},{2,3},{3,2},{4,5},{5,4},{6,7},{7,6},{8,9},{9,8},{10,11... | collective-permute-start | bytes 3194888 | tf_op jit(solution)/shard_map/ppermute | solution.py:438
  126.2 0.7 copy-start
  126.9 1.0 copy-start.1
Sparse Core Ops, SparseCore 0:
  41.4 55.5 all-gather.2

commit v13 on v12

--- a/solution.py
+++ b/solution.py
@@ -428,7 +428,7 @@
 
     l10, w11 = second_factor(place, w00, own, other)
     mine = jnp.where(x == 1, from_left, jnp.where(x == 3, from_right, column))
-    mine = after(mine, own)
+    mine = after(mine, tree[4])
     upper = lax.ppermute(mine[0:512], "col", [(2, 4), (3, 5)])
     lower = lax.ppermute(mine[512:1024], "col", [(6, 4), (7, 5)])
     upper, lower = after((upper, lower), w00)

time: 158 us -> 159 us (level)
  the two profiles are of different devices: /device:TPU:93 before, /device:TPU:49 now
where the time goes in v13:
time: 159 us
  Pallas kernels  50.6 us (32%)
  waiting for transfers between devices  47.7 us (30%)
  starting transfers between devices  40.4 us (25%)
  between operations  14.6 us (9%)
  other arithmetic  2.73 us (2%)
  local copies, waits for them, and re-layouts  2.62 us (2%)
    ppermute x6, waiting for transfers between devices, spread(): arrived = lax.ppermute(value, ('row', 'col'), pairs)  30.9 us
    pallas_call x1, Pallas kernels, final_call(): pl.pallas_call(final_kernel, out_shape=(jax.ShapeDtypeStruct((1024, 2, 8,...  22.9 us
    ppermute x4, starting transfers between devices, beside(): lax.ppermute(after(before, value), 'row', [(r, r ^ d) for r in range(16)])  11.6 us
    pallas_call x1, Pallas kernels, second_factor(): pl.pallas_call(second_kernel, out_shape=(TILE, TILE), in_specs=[SMEM, VME...  9.31 us
    pallas_call x1, Pallas kernels, first_factor(): pl.pallas_call(first_kernel, out_shape=TILE, in_specs=[SMEM, VMEM, VMEM],...  8.22 us
    ppermute x7, waiting for transfers between devices, shards(): lax.ppermute(pieces[j] if j < 4 else after(pieces[j], fetched), 'row', [(...  7.52 us
    ppermute x3, starting transfers between devices, shards(): lax.ppermute(near_sums, 'col', [(0, 2 * k), (1, 2 * k + 1)])  6.93 us
    pallas_call x1, Pallas kernels, column_call(): pl.pallas_call(column_kernel, grid=(8,), out_shape=(jax.ShapeDtypeStruct(...  6.89 us
  transfers between devices with their start and end apart: 28, of which 8 were waited for; matrix products, arithmetic and copies ran while one was open for 2% of the time, Pallas kernels for 15%

profile of v13, /device:TPU:49, one launch (start us, length us, event | category | flops | bytes accessed | tf_op | source)
XLA Modules:
  0.0 158.6 jit_solution(12455985888744715377)
XLA Ops:
  7.2 3.3 %corner_tiles.1 = (f32[256,256]{1,0:T(8,128)}, f32[256,256]{1,0:T(8,128)}, f32[256,256]{1,0:T(8,128)}, f32[256,256]{1,0:T(8,128)}, f32[256,256]{1,0:T(8,128)}, /...) custom-call(f32[1024,16,128]{2,1,0:T(8,128)} %bitcast.13), custom_call_target="tpu_custom_call" | custom-call | tf_op jit(solution)/shard_map/corner_tiles/pallas_call | solution.py:167
  10.5 0.7 collective-permute-start
  11.2 1.3 collective-permute-start.5
  12.5 0.7 collective-permute-start.6
  13.2 0.7 collective-permute-start.7
  13.9 0.1 broadcast_in_dim.22
  14.0 0.7 collective-permute-start.1
  14.7 0.7 collective-permute-start.2
  15.4 7.5 %collective-permute-done.5 = f32[256,256]{1,0:T(8,128)S(1)} collective-permute-done((f32[256,256]{1,0:T(8,128)}, f32[256,256]{1,0:T(8,128)S(1)}, u32[]{:S(2)}, u32[]{:S(2)}) %collective-permute-start.5) | collective-permute-done | bytes 262176 | tf_op jit(solution)/shard_map/ppermute | solution.py:420
  22.9 1.4 collective-permute-start.3
  24.2 1.4 collective-permute-start.4
  25.6 1.0 maximum_select_fusion
  26.6 0.7 collective-permute-start.8
  27.5 6.9 %first_column.1 = (f32[1024,256]{1,0:T(8,128)S(1)}, f32[16,128]{1,0:T(8,128)S(1)}) custom-call(f32[1024]{0:T(1024)S(1)} %broadcast_select_fusion.8.weights, f32[1024,16,128]{2,1,0:T(8,128)} %bitcast.14), custom_call_target="tpu_custom_call" | custom-call | flops 100000000 | bytes 100000 | tf_op jit(solution)/shard_map/first_column/pallas_call | solution.py:194
  34.4 0.9 select_select_fusion.1
  35.3 0.7 collective-permute-start.11
  36.0 2.3 %collective-permute-start.12 = (f32[16,128]{1,0:T(8,128)S(1)}, f32[16,128]{1,0:T(8,128)S(1)}, u32[]{:S(2)}, u32[]{:S(2)}) collective-permute-start(f32[16,128]{1,0:T(8,128)S(1)} %get-tuple-element.62), channel_id=1, source_target_pairs={{0,8},{8,0},{16,24},{24,16},{32,40},{40,32},{48,56},{56,48},{64,72... | collective-permute-start | bytes 24584 | tf_op jit(solution)/shard_map/ppermute | solution.py:408
  38.3 1.0 collective-permute-done.12
  39.4 0.7 collective-permute-start.13
  40.1 4.6 %collective-permute-start.10 = (f32[1024,256]{1,0:T(8,128)S(1)}, f32[1024,256]{1,0:T(8,128)}, u32[]{:S(2)}, u32[]{:S(2)}) collective-permute-start(f32[1024,256]{1,0:T(8,128)S(1)} %get-tuple-element.58), channel_id=1, source_target_pairs={{0,6},{1,7},{8,14},{9,15},{16,22},{17,23},{24,30},{25,31},{32,38},... | collective-permute-start | bytes 3145736 | tf_op jit(solution)/shard_map/ppermute | solution.py:402
  44.8 2.3 %collective-permute-start.9 = (f32[1024,256]{1,0:T(8,128)S(1)}, f32[1024,256]{1,0:T(8,128)}, u32[]{:S(2)}, u32[]{:S(2)}) collective-permute-start(f32[1024,256]{1,0:T(8,128)S(1)} %get-tuple-element.58), channel_id=1, source_target_pairs={{0,2},{1,3},{8,10},{9,11},{16,18},{17,19},{24,26},{25,27},{32,34},... | collective-permute-start | bytes 3145736 | tf_op jit(solution)/shard_map/ppermute | solution.py:401
  47.1 2.5 %collective-permute-done.14 = f32[16,128]{1,0:T(8,128)S(1)} collective-permute-done((f32[16,128]{1,0:T(8,128)S(1)}, f32[16,128]{1,0:T(8,128)S(1)}, u32[]{:S(2)}, u32[]{:S(2)}) %collective-permute-start.14) | collective-permute-done | bytes 8224 | tf_op jit(solution)/shard_map/ppermute | solution.py:408
  49.6 0.7 collective-permute-start.15
  50.3 2.8 %collective-permute-start.16 = (f32[16,128]{1,0:T(8,128)S(1)}, f32[16,128]{1,0:T(8,128)S(1)}, u32[]{:S(2)}, u32[]{:S(2)}) collective-permute-start(f32[16,128]{1,0:T(8,128)S(1)} %add.52), channel_id=1, source_target_pairs={{0,32},{8,40},{16,48},{24,56},{32,0},{40,8},{48,16},{56,24},{64,96... | collective-permute-start | bytes 24584 | tf_op jit(solution)/shard_map/ppermute | solution.py:408
  53.1 1.3 collective-permute-done.16
  54.5 0.7 collective-permute-start.17
  55.3 6.5 %collective-permute-start.20 = (f32[16,128]{1,0:T(8,128)S(1)}, f32[16,128]{1,0:T(8,128)S(1)}, u32[]{:S(2)}, u32[]{:S(2)}) collective-permute-start(f32[16,128]{1,0:T(8,128)S(1)} %add.53), channel_id=1, source_target_pairs={{0,96},{8,104},{16,112},{24,120},{32,64},{40,72},{48,80},{56,88},{... | collective-permute-start | bytes 24584 | tf_op jit(solution)/shard_map/ppermute | solution.py:408
  61.7 0.6 collective-permute-done.10
  62.4 2.3 %collective-permute-done.9 = f32[1024,256]{1,0:T(8,128)} collective-permute-done((f32[1024,256]{1,0:T(8,128)S(1)}, f32[1024,256]{1,0:T(8,128)}, u32[]{:S(2)}, u32[]{:S(2)}) %collective-permute-start.9) | collective-permute-done | bytes 1048608 | tf_op jit(solution)/shard_map/ppermute | solution.py:401
  64.7 0.2 select_select_fusion
  65.0 1.3 collective-permute-start.21
  66.3 4.4 %collective-permute-start.24 = (f32[16,256]{1,0:T(8,128)S(1)}, f32[16,256]{1,0:T(8,128)S(1)}, u32[]{:S(2)}, u32[]{:S(2)}) collective-permute-start(f32[16,256]{1,0:T(8,128)S(1)} %broadcast_in_dim.26), channel_id=1, source_target_pairs={{0,6},{1,7},{8,14},{9,15},{16,22},{17,23},{24,30},{25,31},{32,38},... | collective-permute-start | bytes 49160 | tf_op jit(solution)/shard_map/ppermute | solution.py:414
  70.6 1.3 collective-permute-start.23
  71.9 1.3 collective-permute-start.22
  73.2 0.9 fusion
  74.1 0.7 collective-permute-start.19
  74.8 30.9 %collective-permute-done.21 = f32[384,256]{1,0:T(8,128)S(1)} collective-permute-done((f32[384,256]{1,0:T(8,128)S(1)}, f32[384,256]{1,0:T(8,128)S(1)}, u32[]{:S(2)}, u32[]{:S(2)}) %collective-permute-start.21) | collective-permute-done | bytes 393248 | tf_op jit(solution)/shard_map/ppermute | solution.py:369
  105.6 1.5 collective-permute-start.18
  107.2 0.2 collective-permute-start.25
  107.4 0.1 pad_add_fusion.place
  107.5 1.5 collective-permute-done.25.other
  109.0 8.2 %first_factor.1.w00 = f32[256,256]{1,0:T(8,128)S(1)} custom-call(s32[2]{0:T(128)S(1)} %pad_add_fusion.place, f32[384,256]{1,0:T(8,128)S(1)} %broadcast_select_fusion.2.own, f32[384,256]{1,0:T(8,128)S(1)} %collective-permute-done.25.other), custom_call_target="tpu_custom_call" | custom-call | flops 100000000 | bytes 100000 | tf_op jit(solution)/shard_map/first_factor/pallas_call | solution.py:144
  117.2 0.1 broadcast_select_fusion.1
  117.5 0.4 collective-permute-start.26
  117.9 9.3 %second_factor.1 = (f32[256,256]{1,0:T(8,128)S(1)}, f32[256,256]{1,0:T(8,128)S(1)}) custom-call(s32[2]{0:T(128)S(1)} %pad_add_fusion.place, f32[256,256]{1,0:T(8,128)S(1)} %first_factor.1.w00, f32[384,256]{1,0:T(8,128)S(1)} %broadcast_select_fusion.2.own, f32[384,256]{1,0:T(8,128)S(1)} %collective-permute-done.25.other), custom_call_target="tpu_custom_call" | custom-call | flops 100000000 | bytes 100000 | tf_op jit(solution)/shard_map/second_factor/pallas_call | solution.py:151
  127.2 0.7 copy-done
  127.9 0.9 copy-done.1
  128.9 22.9 %panels_and_trailing.1 = (f32[1024,2,8,128]{3,2,1,0:T(8,128)}, f32[1024,512]{1,0:T(8,128)}, f32[16,128]{1,0:T(8,128)}) custom-call(s32[2]{0:T(128)S(1)} %pad_add_fusion.place, f32[1024,2,8,128]{3,2,1,0:T(8,128)} %bitcast.15, f32[16,256,256]{2,1,0:T(8,128)} %bitcast.16, f32[1040,256]{1,0:T(8,128)S(1)} %pad_maximum_fusion.mine, ...), custom_call_target="tpu_custom_call" | custom-call | flops 100000000 | bytes 100000 | tf_op jit(solution)/shard_map/panels_and_trailing/pallas_call | solution.py:308
  (47 shorter events, 0.6 us)
Async XLA Ops:
  7.2 120.8 %all-gather.3.cloned.1.call-start = ((), (), s32[]{:S(2)}) async-start(), calls=%async_computation | async-start | bytes 4456448 | tf_op jit(solution)/shard_map/all_gather | solution.py:421
  10.5 16.8 %copy-start.3 = (f32[4,1,256]{2,1,0:T(1,128)S(1)}, f32[4,1,256]{2,1,0:T(1,128)}, u32[]{:S(2)}) copy-start(f32[4,1,256]{2,1,0:T(1,128)} %param.3) | copy-start | bytes 12292
  10.5 3.5 %collective-permute-start = (f32[256,256]{1,0:T(8,128)}, f32[256,256]{1,0:T(8,128)S(1)}, u32[]{:S(2)}, u32[]{:S(2)}) collective-permute-start(f32[256,256]{1,0:T(8,128)} %get-tuple-element.44), channel_id=1, source_target_pairs={{8,0},{9,1}} | collective-permute-start | bytes 786440 | tf_op jit(solution)/shard_map/ppermute | solution.py:393
  11.2 11.7 %collective-permute-start.5 = (f32[256,256]{1,0:T(8,128)}, f32[256,256]{1,0:T(8,128)S(1)}, u32[]{:S(2)}, u32[]{:S(2)}) collective-permute-start(f32[256,256]{1,0:T(8,128)} %get-tuple-element.52), channel_id=1, source_target_pairs={{0,48},{8,56},{1,49},{9,57},{2,50},{10,58},{3,51},{11,59},{4,52},{... | collective-permute-start | bytes 786440 | tf_op jit(solution)/shard_map/ppermute | solution.py:420
  12.5 11.7 %collective-permute-start.6 = (f32[256,256]{1,0:T(8,128)}, f32[256,256]{1,0:T(8,128)S(1)}, u32[]{:S(2)}, u32[]{:S(2)}) collective-permute-start(f32[256,256]{1,0:T(8,128)} %get-tuple-element.53), channel_id=1, source_target_pairs={{0,32},{8,40},{1,33},{9,41},{2,34},{10,42},{3,35},{11,43},{4,36},{... | collective-permute-start | bytes 786440 | tf_op jit(solution)/shard_map/ppermute | solution.py:420
  13.2 13.4 %collective-permute-start.7 = (f32[256,256]{1,0:T(8,128)}, f32[256,256]{1,0:T(8,128)S(1)}, u32[]{:S(2)}, u32[]{:S(2)}) collective-permute-start(f32[256,256]{1,0:T(8,128)} %get-tuple-element.54), channel_id=1, source_target_pairs={{0,16},{8,24},{1,17},{9,25},{2,18},{10,26},{3,19},{11,27},{4,20},{... | collective-permute-start | bytes 786440 | tf_op jit(solution)/shard_map/ppermute | solution.py:420
  14.0 20.4 %collective-permute-start.1 = (f32[256,256]{1,0:T(8,128)}, f32[256,256]{1,0:T(8,128)S(1)}, u32[]{:S(2)}, u32[]{:S(2)}) collective-permute-start(f32[256,256]{1,0:T(8,128)} %get-tuple-element.45), channel_id=1, source_target_pairs={{0,112},{8,120},{1,113},{9,121},{2,114},{10,122},{3,115},{11,123},... | collective-permute-start | bytes 786440 | tf_op jit(solution)/shard_map/ppermute | solution.py:420
  14.7 19.7 %collective-permute-start.2 = (f32[256,256]{1,0:T(8,128)}, f32[256,256]{1,0:T(8,128)S(1)}, u32[]{:S(2)}, u32[]{:S(2)}) collective-permute-start(f32[256,256]{1,0:T(8,128)} %get-tuple-element.47), channel_id=1, source_target_pairs={{0,96},{8,104},{1,97},{9,105},{2,98},{10,106},{3,99},{11,107},{4,1... | collective-permute-start | bytes 786440 | tf_op jit(solution)/shard_map/ppermute | solution.py:420
  22.9 11.5 %collective-permute-start.3 = (f32[256,256]{1,0:T(8,128)}, f32[256,256]{1,0:T(8,128)}, u32[]{:S(2)}, u32[]{:S(2)}) collective-permute-start(f32[256,256]{1,0:T(8,128)} %get-tuple-element.49), channel_id=1, source_target_pairs={{0,80},{8,88},{1,81},{9,89},{2,82},{10,90},{3,83},{11,91},{4,84},{... | collective-permute-start | bytes 786440 | tf_op jit(solution)/shard_map/ppermute | solution.py:420
  24.2 10.2 %collective-permute-start.4 = (f32[256,256]{1,0:T(8,128)}, f32[256,256]{1,0:T(8,128)}, u32[]{:S(2)}, u32[]{:S(2)}) collective-permute-start(f32[256,256]{1,0:T(8,128)} %get-tuple-element.51), channel_id=1, source_target_pairs={{0,64},{8,72},{1,65},{9,73},{2,66},{10,74},{3,67},{11,75},{4,68},{... | collective-permute-start | bytes 786440 | tf_op jit(solution)/shard_map/ppermute | solution.py:420
  26.6 8.6 %collective-permute-start.8 = (f32[384,256]{1,0:T(8,128)S(1)}, f32[384,256]{1,0:T(8,128)S(1)}, u32[]{:S(2)}, u32[]{:S(2)}) collective-permute-start(f32[384,256]{1,0:T(8,128)S(1)} %maximum_select_fusion), channel_id=1, source_target_pairs={{0,2},{1,33}} | collective-permute-start | bytes 1179656 | tf_op jit(solution)/shard_map/ppermute | solution.py:369
  27.4 7.0 %copy-start.2 = (f32[256,256]{1,0:T(8,128)S(1)}, f32[256,256]{1,0:T(8,128)}, u32[]{:S(2)}) copy-start(f32[256,256]{1,0:T(8,128)} %get-tuple-element.55) | copy-start | bytes 786436
  35.3 4.0 %collective-permute-start.11 = (f32[384,256]{1,0:T(8,128)S(1)}, f32[384,256]{1,0:T(8,128)S(1)}, u32[]{:S(2)}, u32[]{:S(2)}) collective-permute-start(f32[384,256]{1,0:T(8,128)S(1)} %broadcast_select_fusion.7), channel_id=1, source_target_pairs={{0,6},{2,4},{1,97},{33,65}} | collective-permute-start | bytes 1179656 | tf_op jit(solution)/shard_map/ppermute | solution.py:369
  36.0 3.3 %collective-permute-start.12 = (f32[16,128]{1,0:T(8,128)S(1)}, f32[16,128]{1,0:T(8,128)S(1)}, u32[]{:S(2)}, u32[]{:S(2)}) collective-permute-start(f32[16,128]{1,0:T(8,128)S(1)} %get-tuple-element.62), channel_id=1, source_target_pairs={{0,8},{8,0},{16,24},{24,16},{32,40},{40,32},{48,56},{56,48},{64,72... | collective-permute-start | bytes 24584 | tf_op jit(solution)/shard_map/ppermute | solution.py:408
  39.4 10.1 %collective-permute-start.13 = (f32[384,256]{1,0:T(8,128)S(1)}, f32[384,256]{1,0:T(8,128)S(1)}, u32[]{:S(2)}, u32[]{:S(2)}) collective-permute-start(f32[384,256]{1,0:T(8,128)S(1)} %broadcast_select_fusion.3), channel_id=1, source_target_pairs={{0,32},{2,34},{4,36},{6,38},{1,3},{33,35},{65,67},{97,99}} | collective-permute-start | bytes 1179656 | tf_op jit(solution)/shard_map/ppermute | solution.py:369
  40.1 22.2 %collective-permute-start.10 = (f32[1024,256]{1,0:T(8,128)S(1)}, f32[1024,256]{1,0:T(8,128)}, u32[]{:S(2)}, u32[]{:S(2)}) collective-permute-start(f32[1024,256]{1,0:T(8,128)S(1)} %get-tuple-element.58), channel_id=1, source_target_pairs={{0,6},{1,7},{8,14},{9,15},{16,22},{17,23},{24,30},{25,31},{32,38},... | collective-permute-start | bytes 3145736 | tf_op jit(solution)/shard_map/ppermute | solution.py:402
  44.8 19.9 %collective-permute-start.9 = (f32[1024,256]{1,0:T(8,128)S(1)}, f32[1024,256]{1,0:T(8,128)}, u32[]{:S(2)}, u32[]{:S(2)}) collective-permute-start(f32[1024,256]{1,0:T(8,128)S(1)} %get-tuple-element.58), channel_id=1, source_target_pairs={{0,2},{1,3},{8,10},{9,11},{16,18},{17,19},{24,26},{25,27},{32,34},... | collective-permute-start | bytes 3145736 | tf_op jit(solution)/shard_map/ppermute | solution.py:401
  47.1 2.5 %collective-permute-start.14 = (f32[16,128]{1,0:T(8,128)S(1)}, f32[16,128]{1,0:T(8,128)S(1)}, u32[]{:S(2)}, u32[]{:S(2)}) collective-permute-start(f32[16,128]{1,0:T(8,128)S(1)} %add.51), channel_id=1, source_target_pairs={{0,24},{8,16},{16,8},{24,0},{32,56},{40,48},{48,40},{56,32},{64,88... | collective-permute-start | bytes 24584 | tf_op jit(solution)/shard_map/ppermute | solution.py:408
  49.6 4.8 %collective-permute-start.15 = (f32[384,256]{1,0:T(8,128)S(1)}, f32[384,256]{1,0:T(8,128)S(1)}, u32[]{:S(2)}, u32[]{:S(2)}) collective-permute-start(f32[384,256]{1,0:T(8,128)S(1)} %broadcast_select_fusion.4), channel_id=1, source_target_pairs={{0,96},{2,98},{4,100},{6,102},{32,64},{34,66},{36,68},{38,70},{1,7... | collective-permute-start | bytes 1179656 | tf_op jit(solution)/shard_map/ppermute | solution.py:369
  50.3 4.1 %collective-permute-start.16 = (f32[16,128]{1,0:T(8,128)S(1)}, f32[16,128]{1,0:T(8,128)S(1)}, u32[]{:S(2)}, u32[]{:S(2)}) collective-permute-start(f32[16,128]{1,0:T(8,128)S(1)} %add.52), channel_id=1, source_target_pairs={{0,32},{8,40},{16,48},{24,56},{32,0},{40,8},{48,16},{56,24},{64,96... | collective-permute-start | bytes 24584 | tf_op jit(solution)/shard_map/ppermute | solution.py:408
  54.5 10.4 %collective-permute-start.17 = (f32[384,256]{1,0:T(8,128)S(1)}, f32[384,256]{1,0:T(8,128)S(1)}, u32[]{:S(2)}, u32[]{:S(2)}) collective-permute-start(f32[384,256]{1,0:T(8,128)S(1)} %broadcast_select_fusion.5), channel_id=1, source_target_pairs={{0,8},{32,40},{64,72},{96,104},{2,10},{34,42},{66,74},{98,106},{4,... | collective-permute-start | bytes 1179656 | tf_op jit(solution)/shard_map/ppermute | solution.py:369
  55.3 9.6 %collective-permute-start.20 = (f32[16,128]{1,0:T(8,128)S(1)}, f32[16,128]{1,0:T(8,128)S(1)}, u32[]{:S(2)}, u32[]{:S(2)}) collective-permute-start(f32[16,128]{1,0:T(8,128)S(1)} %add.53), channel_id=1, source_target_pairs={{0,96},{8,104},{16,112},{24,120},{32,64},{40,72},{48,80},{56,88},{... | collective-permute-start | bytes 24584 | tf_op jit(solution)/shard_map/ppermute | solution.py:408
  65.0 40.7 %collective-permute-start.21 = (f32[384,256]{1,0:T(8,128)S(1)}, f32[384,256]{1,0:T(8,128)S(1)}, u32[]{:S(2)}, u32[]{:S(2)}) collective-permute-start(f32[384,256]{1,0:T(8,128)S(1)} %broadcast_select_fusion.6), channel_id=1, source_target_pairs={{0,24},{32,56},{64,88},{96,120},{2,26},{34,58},{66,90},{98,122},{4... | collective-permute-start | bytes 1179656 | tf_op jit(solution)/shard_map/ppermute | solution.py:369
  66.3 40.9 %collective-permute-start.24 = (f32[16,256]{1,0:T(8,128)S(1)}, f32[16,256]{1,0:T(8,128)S(1)}, u32[]{:S(2)}, u32[]{:S(2)}) collective-permute-start(f32[16,256]{1,0:T(8,128)S(1)} %broadcast_in_dim.26), channel_id=1, source_target_pairs={{0,6},{1,7},{8,14},{9,15},{16,22},{17,23},{24,30},{25,31},{32,38},... | collective-permute-start | bytes 49160 | tf_op jit(solution)/shard_map/ppermute | solution.py:414
  70.6 36.5 %collective-permute-start.23 = (f32[16,256]{1,0:T(8,128)S(1)}, f32[16,256]{1,0:T(8,128)S(1)}, u32[]{:S(2)}, u32[]{:S(2)}) collective-permute-start(f32[16,256]{1,0:T(8,128)S(1)} %broadcast_in_dim.26), channel_id=1, source_target_pairs={{0,4},{1,5},{8,12},{9,13},{16,20},{17,21},{24,28},{25,29},{32,36},... | collective-permute-start | bytes 49160 | tf_op jit(solution)/shard_map/ppermute | solution.py:414
  71.9 35.2 %collective-permute-start.22 = (f32[16,256]{1,0:T(8,128)S(1)}, f32[16,256]{1,0:T(8,128)S(1)}, u32[]{:S(2)}, u32[]{:S(2)}) collective-permute-start(f32[16,256]{1,0:T(8,128)S(1)} %broadcast_in_dim.26), channel_id=1, source_target_pairs={{0,2},{1,3},{8,10},{9,11},{16,18},{17,19},{24,26},{25,27},{32,34},... | collective-permute-start | bytes 49160 | tf_op jit(solution)/shard_map/ppermute | solution.py:414
  74.1 43.1 %collective-permute-start.19 = (f32[512,256]{1,0:T(8,128)}, f32[512,256]{1,0:T(8,128)S(1)}, u32[]{:S(2)}, u32[]{:S(2)}) collective-permute-start(f32[512,256]{1,0:T(8,128)} %get-tuple-element.88), channel_id=1, source_target_pairs={{6,4},{7,5},{14,12},{15,13},{22,20},{23,21},{30,28},{31,29},{38,36... | collective-permute-start | bytes 1572872 | tf_op jit(solution)/shard_map/ppermute | solution.py:433
  105.6 11.6 %collective-permute-start.18 = (f32[512,256]{1,0:T(8,128)S(1)}, f32[512,256]{1,0:T(8,128)}, u32[]{:S(2)}, u32[]{:S(2)}) collective-permute-start(f32[512,256]{1,0:T(8,128)S(1)} %get-tuple-element.89), channel_id=1, source_target_pairs={{2,4},{3,5},{10,12},{11,13},{18,20},{19,21},{26,28},{27,29},{34,36... | collective-permute-start | bytes 1572872 | tf_op jit(solution)/shard_map/ppermute | solution.py:432
  107.2 1.8 %collective-permute-start.25 = (f32[384,256]{1,0:T(8,128)S(1)}, f32[384,256]{1,0:T(8,128)S(1)}, u32[]{:S(2)}, u32[]{:S(2)}) collective-permute-start(f32[384,256]{1,0:T(8,128)S(1)} %broadcast_select_fusion.2.own), channel_id=1, source_target_pairs={{0,1},{1,0},{2,3},{3,2},{4,5},{5,4},{6,7},{7,6},{8,9},{9,8},{10,11... | collective-permute-start | bytes 1179656 | tf_op jit(solution)/shard_map/ppermute | solution.py:416
  117.5 10.4 %collective-permute-start.26 = (f32[1040,256]{1,0:T(8,128)S(1)}, f32[1040,256]{1,0:T(8,128)S(1)}, u32[]{:S(2)}, u32[]{:S(2)}) collective-permute-start(f32[1040,256]{1,0:T(8,128)S(1)} %pad_maximum_fusion.mine), channel_id=1, source_target_pairs={{0,1},{1,0},{2,3},{3,2},{4,5},{5,4},{6,7},{7,6},{8,9},{9,8},{10,11... | collective-permute-start | bytes 3194888 | tf_op jit(solution)/shard_map/ppermute | solution.py:438
  127.2 0.7 copy-start
  127.9 1.0 copy-start.1
Sparse Core Ops, SparseCore 0:
  35.5 67.0 all-gather.2
